TPU v7x, 128 devices: a whole 4x4x4 slice. The times are simulated.
128 devices in a mesh: grid: 32 (over z, x, core), pert: 4 (over y).
Axes of the slice: x: 4, y: 4, z: 4, core: 2. Of those that a mesh axis runs over, the one named last changes fastest.
Arguments:
- basis_values: bfloat16 [131072, 1024], P(('grid', 'pert')), may hold values from -6 to 6
- point_coords: float32 [3, 131072], P(None, 'grid'), may hold values from 0 to 4
- point_weights: float32 [131072], P('grid'), may hold values from 0.005 to 0.05
- xc_kernel: float32 [131072], P('grid'), may hold values from -2 to -0.5
- gauss_widths: float32 [64], replicated, may hold values from 0.3 to 3
- atom_coords: float32 [3, 256], replicated, may hold values from 0 to 4
- resp_density: bfloat16 [4, 128, 256, 256], P('pert', 'grid'), may hold values from -0.0059814453 to 0.0059814453
- tile_list: int32 [64, 16], P('grid'), may hold values from 0 to 127, as said below
- tile_home: int32 [128], replicated, may hold values from 0 to 127, as said below
- atom_list: int32 [64, 16], P('grid'), may hold values from 0 to 255, all different within a row
- atom_home: int32 [256], replicated, may hold values from 0 to 255, each once
Outputs:
- hamiltonian: float32 [4, 128, 256, 256], P('pert', 'grid')
- coefficients: float32 [4, 256, 64], P('pert', 'grid')
- potential: float32 [4, 131072], P('pert', 'grid')
Inputs may be any that keep to these rules, and one draw needn't show every extreme that they name: `tile_list`: the 2 batches of one index of grid, rows of aligned blocks of 2, name 32 different tiles; at most 2 of them have tile_home in any one aligned block of 4 positions, and exactly 2 in at least one such block. `tile_home`: each tile has one stored position. `atom_list`: the 16 atoms of a batch are different; every atom is a neighbour of some batch, and atoms are shared: the 64 batches name 1024 slots, four or more for each atom on average, so that an atom is in general a neighbour of batches on several indices of grid.
All inputs are finite; a program needn't handle non-finite values.
Results may differ from a plain program's by a relative error of at most 0.0015.
Values may be sent and summed in bfloat16 or wider, within the bound.
No kernel may reach another device: no remote copies, remote signals or barrier semaphores. Data moves between devices by JAX's collectives and lax.ppermute only.
A program may use at most 192 MiB of HBM per device.

v0:
```python
import jax
import jax.numpy as jnp
from jax import lax
from jax.sharding import PartitionSpec as P

SOFTEN = 0.25
ROOT_TWO = 1.4142135623730951


def pair_dist(coords_rows, atom_pos):
    delta = coords_rows[:, :, None] - atom_pos[:, None, :]
    return jnp.sum(delta * delta, axis=0) + SOFTEN


def per_device(
    basis_values,
    point_coords,
    point_weights,
    xc_kernel,
    gauss_widths,
    atom_coords,
    resp_density,
    tile_list,
    tile_home,
    atom_list,
    atom_home,
):
    groups = lax.axis_size("grid")
    local_perts = resp_density.shape[0]
    tile_dev = resp_density.shape[1]
    blk_side = resp_density.shape[2]
    batches_here = tile_list.shape[0]
    pair_count = tile_list.shape[1]
    neighbors = atom_list.shape[1]
    moments = gauss_widths.shape[0]
    natoms = atom_home.shape[0]
    ntiles = tile_home.shape[0]
    nbasis = basis_values.shape[1]
    blocks = nbasis // blk_side
    points = point_weights.shape[0] // batches_here
    requests = batches_here * pair_count
    capacity = max(2, (requests + groups - 1) // groups)
    basis_rows = lax.all_gather(basis_values, "pert", axis=0, tiled=True)
    wanted = tile_list.reshape(requests)
    tile_match = wanted[:, None] == jnp.arange(ntiles, dtype=jnp.int32)[None, :]
    tile_homes = jnp.sum(jnp.where(tile_match, tile_home[None, :], 0), axis=1)
    owners = tile_homes // tile_dev
    local_slot = tile_homes % tile_dev
    request_ids = jnp.arange(requests)
    earlier = (owners[:, None] == owners[None, :]) & (request_ids[None, :] < request_ids[:, None])
    rank_in_owner = jnp.sum(earlier.astype(jnp.int32), axis=1)
    slot_of = owners * capacity + rank_in_owner
    slot_hits = slot_of[None, :] == jnp.arange(groups * capacity, dtype=jnp.int32)[:, None]
    asked_slots = (jnp.sum(jnp.where(slot_hits, local_slot[None, :] + 1, 0), axis=1) - 1).reshape(
        groups, capacity
    )
    asked = lax.all_to_all(asked_slots, "grid", split_axis=0, concat_axis=0, tiled=True)
    picked = jnp.clip(asked, 0, tile_dev - 1).reshape(groups * capacity)
    replies = jnp.take(resp_density, picked, axis=1).reshape(
        local_perts, groups, capacity, blk_side, blk_side
    )
    arrived = lax.all_to_all(replies, "grid", split_axis=1, concat_axis=1, tiled=True)
    my_tiles = jnp.take(
        arrived.reshape(local_perts, groups * capacity, blk_side, blk_side), slot_of, axis=1
    )
    spread = 2.0 * gauss_widths * gauss_widths
    erf_scale = ROOT_TWO * gauss_widths
    atom_range = jnp.arange(natoms, dtype=jnp.int32)
    contrib = jnp.zeros((local_perts, natoms, moments), jnp.float32)
    geometry = []
    responses = []
    for batch_index in range(batches_here):
        row_start = batch_index * points
        phi_rows = basis_rows[row_start : row_start + points]
        tile_block = my_tiles[:, batch_index * pair_count : (batch_index + 1) * pair_count]
        dens_matrix = (
            tile_block.reshape(local_perts, blocks, blocks, blk_side, blk_side)
            .transpose(0, 1, 3, 2, 4)
            .reshape(local_perts, nbasis, nbasis)
        )
        mixed_rows = jnp.einsum(
            "rb,pbc->prc", phi_rows, dens_matrix, preferred_element_type=jnp.float32
        )
        response = jnp.sum(mixed_rows * phi_rows[None], axis=2)
        atom_match = atom_list[batch_index][:, None] == atom_range[None, :]
        atom_pos = jnp.dot(
            atom_coords, atom_match.astype(jnp.float32).T, precision=lax.Precision.HIGHEST
        )
        atom_homes = jnp.sum(jnp.where(atom_match, atom_home[None, :], 0), axis=1)
        dist_sq = pair_dist(point_coords[:, row_start : row_start + points], atom_pos)
        gaussians = jnp.exp(-dist_sq[:, :, None] / spread).reshape(points, neighbors * moments)
        weight_rows = point_weights[row_start : row_start + points]
        partial_value = jnp.dot(
            weight_rows[None, :] * response, gaussians, precision=lax.Precision.HIGHEST
        )
        contrib = contrib.at[:, atom_homes].add(
            partial_value.reshape(local_perts, neighbors, moments)
        )
        geometry.append((dist_sq, atom_homes))
        responses.append(response)
    own_coeffs = lax.psum_scatter(contrib, "grid", scatter_dimension=1, tiled=True)
    all_coeffs = lax.all_gather(own_coeffs, "grid", axis=1, tiled=True)
    ham_tiles = []
    potentials = []
    for batch_index in range(batches_here):
        row_start = batch_index * points
        phi_rows = basis_rows[row_start : row_start + points]
        dist_sq, atom_homes = geometry[batch_index]
        distance = jnp.sqrt(dist_sq)
        kernel = (lax.erf(distance[:, :, None] / erf_scale) / distance[:, :, None]).reshape(
            points, neighbors * moments
        )
        coeff_vec = jnp.take(all_coeffs, atom_homes, axis=1).reshape(
            local_perts, neighbors * moments
        )
        hartree = jnp.einsum("pk,rk->pr", coeff_vec, kernel, precision=lax.Precision.HIGHEST)
        weight_rows = point_weights[row_start : row_start + points]
        potential = (
            hartree + xc_kernel[row_start : row_start + points][None, :] * responses[batch_index]
        )
        scaled = (phi_rows[None] * (weight_rows[None, :] * potential)[:, :, None]).astype(
            jnp.bfloat16
        )
        ham_matrix = jnp.einsum("rb,prc->pbc", phi_rows, scaled, preferred_element_type=jnp.float32)
        ham_tiles.append(
            ham_matrix.reshape(local_perts, blocks, blk_side, blocks, blk_side)
            .transpose(0, 1, 3, 2, 4)
            .reshape(local_perts, pair_count, blk_side, blk_side)
        )
        potentials.append(potential)
    all_ham = jnp.concatenate(ham_tiles, axis=1)
    outgoing = (
        jnp.zeros((local_perts, groups * capacity, blk_side, blk_side), jnp.float32)
        .at[:, slot_of]
        .set(all_ham)
    )
    incoming = lax.all_to_all(
        outgoing.reshape(local_perts, groups, capacity, blk_side, blk_side),
        "grid",
        split_axis=1,
        concat_axis=1,
        tiled=True,
    )
    owner_match = (
        asked.reshape(groups * capacity)[None, :] == jnp.arange(tile_dev, dtype=jnp.int32)[:, None]
    ).astype(jnp.float32)
    hamiltonian = jnp.einsum(
        "ts,psxy->ptxy",
        owner_match,
        incoming.reshape(local_perts, groups * capacity, blk_side, blk_side),
        precision=lax.Precision.HIGHEST,
    )
    return (hamiltonian, own_coeffs, jnp.concatenate(potentials, axis=1))


def solution(mesh):
    placed = (
        P(("grid", "pert"), None),
        P(None, "grid"),
        P("grid"),
        P("grid"),
        P(),
        P(),
        P("pert", "grid", None, None),
        P("grid", None),
        P(),
        P("grid", None),
        P(),
    )
    return jax.shard_map(
        per_device,
        mesh=mesh,
        in_specs=placed,
        out_specs=(P("pert", "grid", None, None), P("pert", "grid", None), P("pert", "grid")),
        check_vma=False,
    )
```

profile of v0, /device:TPU:0, one launch (start us, length us, event | category | flops | bytes accessed | tf_op | source)
XLA Modules:
  0.0 709.6 jit_solution(2485374846548148243)
XLA Ops:
  7.2 4.0 copy.45
  11.2 0.8 eq.86
  12.0 0.8 select_reduce_fusion.3
  13.3 15.5 %all_to_all.19 = s32[32,1,2]{2,1,0:T(1,128)S(1)} all-to-all(s32[32,1,2]{2,1,0:T(1,128)S(1)} %bitcast.175), channel_id=1, replica_groups=mesh['grid'=32,'pert'=4] {'grid'}, dimensions={0} | all-to-all | bytes 512 | tf_op jit(solution)/shard_map/all_to_all | solution.py:57
  29.2 0.7 fusion.44
  30.3 5.4 gather_fusion
  35.7 7.6 %broadcast_select_fusion = bf16[1,32,2,256,256]{4,3,2,0,1:T(8,128)(2,1)} fusion(bf16[1,32,2,256,256]{4,3,2,0,1:T(8,128)(2,1)} %bitcast.155, pred[32,2]{1,0:T(8,128)(4,1)S(1)} %copy.48), kind=kLoop, calls=%fused_computation.26 | loop fusion | flops 4194304 | bytes 16777280 | tf_op jit(solution)/shard_map/jit(_take)/select_n | solution.py:59
  43.3 5.1 all-to-all-start.1
  49.3 7.4 %fusion.8 = (f32[2048,1024]{0,1:T(8,128)}, f32[2048,1024]{0,1:T(8,128)}) fusion(f32[2048,16]{0,1:T(8,128)S(1)} %get-tuple-element.34, f32[1024]{0:T(1024)S(1)} %div.137, f32[2048,16]{0,1:T(8,128)S(1)} %get-tuple-element.32), kind=kLoop, calls=%fused_computation.23 | loop fusion | flops 4194304 | bytes 17043456 | tf_op jit(solution)/shard_map/exp | solution.py:91
  56.9 7.8 %fusion.1 = (f32[2048,16,64]{0,2,1:T(8,128)}, f32[2048,16,64]{0,2,1:T(8,128)}) fusion(f32[64]{0:T(128)S(1)} %get-tuple-element.48, f32[2048,16]{0,1:T(8,128)S(1)} %get-tuple-element.31, f32[2048,16]{0,1:T(8,128)S(1)} %get-tuple-element.33), kind=kLoop, calls=%fused_computation.14 | loop fusion | flops 8388608 | bytes 17039616 | tf_op jit(solution)/shard_map/div | solution.py:110
  64.7 89.6 %all-to-all-done.1 = bf16[1,32,2,256,256]{4,3,2,0,1:T(8,128)(2,1)} async-done(((bf16[1,32,2,256,256]{4,3,2,0,1:T(8,128)(2,1)}), bf16[1,32,2,256,256]{4,3,2,0,1:T(8,128)(2,1)}, u32[]{:S(2)}, u32[]{:S(2)}) %all-to-all-start.1) | async-done | bytes 8388640 | tf_op jit(solution)/shard_map/all_to_all | solution.py:62
  154.3 6.2 gather_fusion.1
  160.6 2.6 bitcast_select_fusion
  163.7 1.6 copy.49
  165.8 1.6 copy.50
  167.4 1.8 copy.61
  169.3 7.9 %fusion.3 = f32[2048]{0:T(1024)S(1)} fusion(bf16[1024,1024]{1,0:T(8,128)(2,1)S(1)} %bitcast.170, bf16[4096,1024]{0,1:T(8,128)(2,1)} %all-gather.2.cloned.1.call-done), kind=kOutput, calls=%fused_computation.16 | convolution fusion | flops 4301256704 | bytes 10493952 | tf_op jit(solution)/shard_map/rb,pbc->prc/dot_general | solution.py:81
  177.3 5.5 fusion.6
  182.8 9.9 %fusion.47 = f32[1,16,64]{2,0,1:T(1,128)S(1)} fusion(f32[2048,1,1]{0,1,2:T(1,128)S(1)} %bitcast.182, f32[16,64,2048]{2,1,0:T(8,128)S(1)} %bitcast.163), kind=kOutput, calls=%fused_computation.118 | convolution fusion | flops 25165824 | bytes 8400896 | tf_op jit(solution)/shard_map/dot_general | solution.py:93
  192.8 10.1 %fusion.48 = f32[1,16,64]{2,0,1:T(1,128)S(1)} fusion(f32[2048,1,1]{0,1,2:T(1,128)S(1)} %bitcast.181, f32[16,64,2048]{2,1,0:T(8,128)S(1)} %bitcast.160), kind=kOutput, calls=%fused_computation.119 | convolution fusion | flops 25165824 | bytes 8400896 | tf_op jit(solution)/shard_map/dot_general | solution.py:93
  202.9 0.7 scatter_custom_fusion
  203.6 0.7 scatter_fusion
  204.3 0.6 copy-done.3
  205.0 0.6 dynamic-slice
  206.3 97.2 %all-reduce.3.cloned.1.call-done = f32[1,256,64]{2,1,0:T(8,128)} async-done(((f32[1,256,64]{2,1,0:T(8,128)}), f32[1,256,64]{2,1,0:T(8,128)}) %all-reduce.3.cloned.1.call-update) | async-done | bytes 65552
  303.5 0.7 constant_dynamic-slice_fusion
  304.2 25.1 %all_gather.7 = f32[1,256,64]{2,1,0:T(8,128)S(1)} all-gather(f32[1,8,64]{2,1,0:T(8,128)S(1)} %constant_dynamic-slice_fusion), channel_id=1, replica_groups=mesh['grid'=32,'pert'=4] {'grid'}, dimensions={1}, use_global_device_ids=true | all-gather | bytes 67584 | tf_op jit(solution)/shard_map/all_gather | solution.py:102
  329.3 0.6 gather_fusion.3
  330.0 0.6 gather_fusion.2
  330.7 6.5 fusion.50
  337.2 6.5 fusion.49
  343.8 6.2 fusion.20
  349.9 5.6 reshape.479
  355.6 5.2 copy.51
  360.8 10.0 %fusion.25 = f32[1,1024,1024]{1,2,0:T(8,128)} fusion(bf16[4096,1024]{0,1:T(8,128)(2,1)} %all-gather.2.cloned.1.call-done, f32[2048]{0:T(1024)S(1)} %get-tuple-element.37), kind=kOutput, calls=%fused_computation.37 | convolution fusion | flops 4301258752 | bytes 12591104 | tf_op jit(solution)/shard_map/rb,prc->pbc/dot_general | solution.py:124
  370.8 5.6 reshape.482
  376.4 5.5 copy.52
  381.9 7.6 %maximum_bitcast_fusion = f32[32,256,256]{2,1,0:T(8,128)} fusion(f32[1,16,256,256]{3,2,1,0:T(8,128)} %bitcast.165, f32[1,16,256,256]{3,2,1,0:T(8,128)} %bitcast.164), kind=kLoop, calls=%fused_computation.21 | loop fusion | flops 2097152 | bytes 16777216 | tf_op jit(solution)/shard_map/concatenate | solution.py:131
  389.5 7.8 %broadcast.485 = f32[64,256,256]{2,1,0:T(8,128)} broadcast(f32[]{:T(128)} %constant.50.clone.1), dimensions={} | broadcast | bytes 16777220 | tf_op jit(solution)/shard_map/broadcast_in_dim | solution.py:133
  397.3 15.4 %scatter_fusion.1 = f32[64,256,256]{2,1,0:T(8,128)} fusion(f32[64,256,256]{2,1,0:T(8,128)} %broadcast.485, s32[32]{0:T(128)S(1)} %fusion.39, f32[32,256,256]{2,1,0:T(8,128)} %maximum_bitcast_fusion), kind=kCustom, calls=%fused_computation.6 | custom fusion | bytes 25165952 | tf_op jit(solution)/shard_map/scatter | solution.py:135
  412.7 28.5 %copy.53 = f32[1,32,2,256,256]{4,2,3,0,1:T(2,128)} copy(f32[1,32,2,256,256]{4,3,2,1,0:T(8,128)} %bitcast.154) | data formatting | bytes 33554432 | tf_op jit(solution)/shard_map/reshape | solution.py:138
  441.2 5.2 all-to-all-start.2
  446.5 0.6 pad_maximum_fusion
  447.1 212.6 %all-to-all-done.2 = f32[1,32,2,256,256]{4,2,3,0,1:T(2,128)} async-done(((f32[1,32,2,256,256]{4,2,3,0,1:T(2,128)}), f32[1,32,2,256,256]{4,2,3,0,1:T(2,128)}, u32[]{:S(2)}, u32[]{:S(2)}) %all-to-all-start.2) | async-done | bytes 16777248 | tf_op jit(solution)/shard_map/all_to_all | solution.py:137
  659.6 12.2 %copy.54 = f32[1,32,2,256,256]{4,2,1,3,0:T(2,128)} copy(f32[1,32,2,256,256]{4,2,3,0,1:T(2,128)} %all-to-all-done.2) | data formatting | bytes 33554432 | tf_op jit(solution)/shard_map/all_to_all | solution.py:137
  671.9 20.6 %reshape.485 = f32[64,256,256]{2,0,1:T(8,128)} reshape(f32[1,32,2,256,256]{4,2,1,3,0:T(2,128)} %copy.54) | data formatting | bytes 33554432 | tf_op jit(solution)/shard_map/reshape.45
  692.5 9.0 %convolution_bitcast_fusion = f32[1,4,256,256]{3,1,2,0:T(4,128)S(1)} fusion(f32[64,256,256]{2,0,1:T(8,128)} %reshape.485, s32[64]{0:T(128)S(1)} %all_to_all.15), kind=kOutput, calls=%fused_computation.38 | convolution fusion | flops 201326848 | bytes 17826048 | tf_op jit(solution)/shard_map/ts,psxy->ptxy/dot_general | solution.py:147
  701.4 1.2 copy.55
  (87 shorter events, 3.7 us)
Async XLA Ops:
  7.2 23.2 %copy-start = (bf16[1,4,256,256]{3,2,1,0:T(8,128)(2,1)S(1)}, bf16[1,4,256,256]{3,2,1,0:T(8,128)(2,1)}, u32[]{:S(2)}) copy-start(bf16[1,4,256,256]{3,2,1,0:T(8,128)(2,1)} %param.19) | copy-start | bytes 1572868
  7.2 162.1 %all-gather.2.cloned.1.call-start = ((), (), s32[]{:S(2)}) async-start(), calls=%async_computation.3 | async-start | bytes 10485760 | tf_op jit(solution)/shard_map/all_gather | solution.py:43
  43.3 5.2 copy-start.12
  43.3 5.3 copy-start.9
  43.3 5.3 copy-start.11
  43.3 5.7 copy-start.4
  43.3 111.0 %all-to-all-start.1 = ((bf16[1,32,2,256,256]{4,3,2,0,1:T(8,128)(2,1)}), bf16[1,32,2,256,256]{4,3,2,0,1:T(8,128)(2,1)}, u32[]{:S(2)}, u32[]{:S(2)}) async-start(bf16[1,32,2,256,256]{4,3,2,0,1:T(8,128)(2,1)} %broadcast_select_fusion), calls=%async_computation.1 | async-start | bytes 16777216 | tf_op jit(solution)/shard_map/all_to_all | solution.py:62
  48.5 255.1 %all-reduce.3.cloned.1.call-start = ((), (), s32[]{:S(2)}) async-start(), calls=%async_computation.4 | async-start | bytes 262144
  49.3 7.4 %copy-start.8 = (s32[256]{0:T(256)S(1)}, s32[256]{0:T(256)}, u32[]{:S(2)}) copy-start(s32[256]{0:T(256)} %param.23) | copy-start | bytes 3076
  169.3 7.9 %copy-start.2 = (bf16[128,8,4,256]{3,1,2,0:T(8,128)(2,1)S(1)}, bf16[128,8,4,256]{3,1,2,0:T(8,128)(2,1)}, u32[]{:S(2)}) copy-start(bf16[128,8,4,256]{3,1,2,0:T(8,128)(2,1)} %copy.61) | copy-start | bytes 6291460
  169.3 7.9 %copy-start.10 = (bf16[4096,1024]{0,1:T(8,128)(2,1)S(1)}, bf16[4096,1024]{0,1:T(8,128)(2,1)}, u32[]{:S(2)}) copy-start(bf16[4096,1024]{0,1:T(8,128)(2,1)} %all-gather.2.cloned.1.call-done) | copy-start | bytes 25165828
  169.3 13.5 %slice-start.2 = ((s8[8388608]{0:T(1024)(128)(4,1)}), s8[4194304]{0:T(1024)(128)(4,1)S(1)}, s32[]{:S(2)}) async-start(s8[8388608]{0:T(1024)(128)(4,1)} %bitcast.161), calls=%async_computation.7 | async-start | bytes 8388608
  177.2 15.6 %slice-start = ((s8[8388608]{0:T(1024)(128)(4,1)}), s8[4194304]{0:T(1024)(128)(4,1)S(1)}, s32[]{:S(2)}) async-start(s8[8388608]{0:T(1024)(128)(4,1)} %bitcast.158), calls=%async_computation.5 | async-start | bytes 8388608
  177.2 5.5 copy-start.5
  177.3 5.5 slice-start.3
  177.3 15.5 %slice-start.1 = ((s8[8388608]{0:T(1024)(128)(4,1)}), s8[4194304]{0:T(1024)(128)(4,1)S(1)}, s32[]{:S(2)}) async-start(s8[8388608]{0:T(1024)(128)(4,1)} %bitcast.158), calls=%async_computation.6 | async-start | bytes 8388608
  182.8 22.2 %copy-start.13 = (u32[128]{0:T(128)S(1)}, u32[128]{0:T(128)}, u32[]{:S(2)}) copy-start(u32[128]{0:T(128)} %constant.91) | copy-start | bytes 1540
  204.3 0.7 copy-start.3
  304.2 39.5 %copy-start.6 = (f32[1,8,64]{2,1,0:T(8,128)}, f32[1,8,64]{2,1,0:T(8,128)S(1)}, u32[]{:S(2)}) copy-start(f32[1,8,64]{2,1,0:T(8,128)S(1)} %constant_dynamic-slice_fusion) | copy-start | bytes 6148
  330.7 13.0 %copy-start.7 = (f32[4096]{0:T(1024)S(1)}, f32[4096]{0:T(1024)}, u32[]{:S(2)}) copy-start(f32[4096]{0:T(1024)} %param.16) | copy-start | bytes 49156
  330.7 13.0 %slice-start.4 = ((s8[8388608]{0:T(1024)(128)(4,1)}), s8[4194304]{0:T(1024)(128)(4,1)S(1)}, s32[]{:S(2)}) async-start(s8[8388608]{0:T(1024)(128)(4,1)} %bitcast.184), calls=%async_computation.9 | async-start | bytes 8388608
  337.2 6.5 slice-start.5
  441.2 218.5 %all-to-all-start.2 = ((f32[1,32,2,256,256]{4,2,3,0,1:T(2,128)}), f32[1,32,2,256,256]{4,2,3,0,1:T(2,128)}, u32[]{:S(2)}, u32[]{:S(2)}) async-start(f32[1,32,2,256,256]{4,2,3,0,1:T(2,128)} %copy.53), calls=%async_computation.2 | async-start | bytes 33554432 | tf_op jit(solution)/shard_map/all_to_all | solution.py:137
  671.9 30.7 %copy-start.1 = (bf16[1,4,256,256]{3,2,1,0:T(8,128)(2,1)S(1)}, bf16[1,4,256,256]{3,2,1,0:T(8,128)(2,1)}, u32[]{:S(2)}) copy-start(bf16[1,4,256,256]{3,2,1,0:T(8,128)(2,1)} %param.19) | copy-start | bytes 1572868
Sparse Core Ops, SparseCore 0:
  11.4 85.5 all-gather.1
  205.1 98.3 all-reduce.2
where the time goes:
time: 715 us; the launch traced here: 710 us
  waiting for transfers between devices  399 us (56%)
  local copies, waits for them, and re-layouts  134 us (19%)
  matrix products  71.9 us (10%)
  blocking collectives  40.5 us (6%)
  other arithmetic  37.6 us (5%)
  between operations  15.4 us (2%)
  starting transfers between devices  10.4 us (1%)
    all_to_all x1, waiting for transfers between devices, per_device(): lax.all_to_all(outgoing.reshape(local_perts, groups, capacity, blk_side,...  213 us
    unnamed x3, waiting for transfers between devices  97.3 us
    all_to_all x1, waiting for transfers between devices, per_device(): lax.all_to_all(replies, 'grid', split_axis=1, concat_axis=1, tiled=True)  89.6 us
    reshape x1, local copies, waits for them, and re-layouts, per_device(): outgoing.reshape(local_perts, groups, capacity, blk_side, blk_side)  28.5 us
    all_gather x1, blocking collectives, per_device(): all_coeffs = lax.all_gather(own_coeffs, 'grid', axis=1, tiled=True)  25.1 us
    reshape x4, local copies, waits for them, and re-layouts, per_device(): ham_matrix.reshape(local_perts, blocks, blk_side, blocks, blk_side)  21.9 us
    another operation x3, local copies, waits for them, and re-layouts  20.7 us
    dot_general x2, matrix products, per_device(): jnp.dot(weight_rows[None, :] * response, gaussians, precision=lax.Precisi...  20.1 us
  transfers between devices with their start and end apart: 4, of which 3 were waited for; matrix products, arithmetic and copies ran while one was open for 7% of the time, Pallas kernels for 0%

commit v1 on v0

v1 whole, which is shorter than its diff:
```python
import jax
import jax.numpy as jnp
from jax import lax
from jax.experimental import pallas as pl
from jax.experimental.pallas import tpu as pltpu
from jax.sharding import PartitionSpec as P

SOFTEN = 0.25
ROOT_TWO = 1.4142135623730951
HALF = 512
PIECES = 8
BLK = 256
NB = 4
PHI_MAX_SQ = 36.0
KERNEL_MAX = 2.0
F16_TOP = 32000.0
HIGH = lax.Precision.HIGHEST


def ring(shift):
    return [(i, (i + shift) % 4) for i in range(4)]


def grid_perm(dz, dx, dc):
    def at(z, x, c):
        return ((z % 4) * 4 + x % 4) * 2 + c

    return [
        (at(z, x, c), at(z + dz, x + dx, c ^ dc))
        for z in range(4)
        for x in range(4)
        for c in range(2)
    ]


def load_pieces(piece_refs, held, sems):
    for i, ref in enumerate(piece_refs):
        pltpu.make_async_copy(ref, held.at[i], sems.at[i]).start()


def density_body(order, where, *refs):
    pieces = refs[:PIECES]
    tiles, table, weights, rho, pacc, held, dmat, tbuf, psem, dsem, tsem = refs[PIECES:]
    for b in range(2):
        for t in range(16):
            pltpu.make_async_copy(
                tiles.at[where[b * 16 + t]],
                dmat.at[b, pl.ds((t // 4) * BLK, BLK), pl.ds((t % 4) * BLK, BLK)],
                dsem.at[b],
            ).start()
    load_pieces(pieces, held, psem)
    pltpu.make_async_copy(table.at[order[0]], tbuf.at[0], tsem.at[0]).start()
    pacc[...] = jnp.zeros_like(pacc)
    for b in range(2):
        pltpu.make_async_copy(dmat.at[b], dmat.at[b], dsem.at[b]).wait()

    def step(i, _):
        slot = lax.rem(i, 2)

        @pl.when(i + 1 < PIECES)
        def _():
            pltpu.make_async_copy(
                table.at[order[i + 1]], tbuf.at[1 - slot], tsem.at[1 - slot]
            ).start()

        pi = order[i]
        b = pi // 4
        pltpu.make_async_copy(held.at[i], held.at[i], psem.at[i]).wait()
        piece = held[i]
        total = jnp.zeros((1, HALF), jnp.float32)
        for block in range(NB):
            rows = pl.ds(block * BLK, BLK)
            mixed = jnp.dot(dmat[b, rows, :], piece, preferred_element_type=jnp.float32)
            total = total + jnp.sum(
                mixed * held[i, rows, :].astype(jnp.float32), axis=0, keepdims=True
            )
        rho[pi] = total
        weighted = weights[pi] * total
        pltpu.make_async_copy(table.at[pi], tbuf.at[slot], tsem.at[slot]).wait()
        for block in range(8):
            rows = pl.ds(block * 128, 128)
            part = pacc[b, rows, :]
            for lane in range(HALF // 128):
                cols = slice(lane * 128, (lane + 1) * 128)
                part = part + tbuf[slot, rows, cols] * weighted[:, cols]
            pacc[b, rows, :] = part
        return 0

    lax.fori_loop(0, PIECES, step, 0)


def ham_body(order, *refs):
    pieces = refs[:PIECES]
    (table, coeff, weights, xc, rho, pot, ham, held, tbuf, scaled, psem, tsem) = refs[PIECES:]
    load_pieces(pieces, held, psem)
    pltpu.make_async_copy(table.at[order[0]], tbuf.at[0], tsem.at[0]).start()
    ham[...] = jnp.zeros_like(ham)

    def step(i, _):
        slot = lax.rem(i, 2)

        @pl.when(i + 1 < PIECES)
        def _():
            pltpu.make_async_copy(
                table.at[order[i + 1]], tbuf.at[1 - slot], tsem.at[1 - slot]
            ).start()

        pi = order[i]
        b = pi // 4
        pltpu.make_async_copy(table.at[pi], tbuf.at[slot], tsem.at[slot]).wait()
        sums = []
        for lane in range(HALF // 128):
            cols = slice(lane * 128, (lane + 1) * 128)
            part = jnp.zeros((8, 128), jnp.float32)
            for block in range(16):
                rows = pl.ds(block * 64, 64)
                prod = tbuf[slot, rows, cols] * coeff[b, rows, :]
                part = part + jnp.sum(prod.reshape(8, 8, 128), axis=0)
            sums.append(jnp.sum(part, axis=0, keepdims=True))
        hartree = jnp.concatenate(sums, axis=1)
        potential = hartree + xc[pi] * rho[pi]
        pot[pi] = potential
        scale_row = weights[pi] * potential
        pltpu.make_async_copy(held.at[i], held.at[i], psem.at[i]).wait()
        scaled[...] = (held[i].astype(jnp.float32) * scale_row).astype(jnp.bfloat16)
        for block in range(NB):
            rows = pl.ds(block * BLK, BLK)
            part = lax.dot_general(
                held[i, rows, :],
                scaled[...],
                (((1,), (1,)), ((), ())),
                preferred_element_type=jnp.float32,
            )
            for col in range(NB):
                at = b * 16 + block * NB + col
                ham[at] = ham[at] + part[:, col * BLK : (col + 1) * BLK]
        return 0

    lax.fori_loop(0, PIECES, step, 0)


def any_spec():
    return pl.BlockSpec(memory_space=pl.ANY)


def vmem_spec():
    return pl.BlockSpec(memory_space=pltpu.VMEM)


def smem_spec():
    return pl.BlockSpec(memory_space=pltpu.SMEM)


def density_call(order, where, pieces, tiles, table, weights):
    nbasis = NB * BLK
    return pl.pallas_call(
        density_body,
        out_shape=(
            jax.ShapeDtypeStruct((PIECES, 1, HALF), jnp.float32),
            jax.ShapeDtypeStruct((2, nbasis, 128), jnp.float32),
        ),
        in_specs=[smem_spec(), smem_spec()] + [any_spec()] * (PIECES + 2) + [vmem_spec()],
        out_specs=(vmem_spec(), vmem_spec()),
        scratch_shapes=[
            pltpu.VMEM((PIECES, nbasis, HALF), jnp.bfloat16),
            pltpu.VMEM((2, nbasis, nbasis), jnp.bfloat16),
            pltpu.VMEM((2, nbasis, HALF), jnp.float32),
            pltpu.SemaphoreType.DMA((PIECES,)),
            pltpu.SemaphoreType.DMA((2,)),
            pltpu.SemaphoreType.DMA((2,)),
        ],
        compiler_params=pltpu.CompilerParams(vmem_limit_bytes=40 << 20),
        cost_estimate=pl.CostEstimate(
            flops=2 * 4096 * 1024 * 1024, bytes_accessed=32 << 20, transcendentals=0
        ),
        name="density",
    )(order, where, *pieces, tiles, table, weights)


def ham_call(order, pieces, table, coeff, weights, xc, rho):
    nbasis = NB * BLK
    return pl.pallas_call(
        ham_body,
        out_shape=(
            jax.ShapeDtypeStruct((PIECES, 1, HALF), jnp.float32),
            jax.ShapeDtypeStruct((2 * NB * NB, BLK, BLK), jnp.float32),
        ),
        in_specs=[smem_spec()] + [any_spec()] * (PIECES + 1) + [vmem_spec()] * 4,
        out_specs=(vmem_spec(), vmem_spec()),
        scratch_shapes=[
            pltpu.VMEM((PIECES, nbasis, HALF), jnp.bfloat16),
            pltpu.VMEM((2, nbasis, HALF), jnp.float32),
            pltpu.VMEM((nbasis, HALF), jnp.bfloat16),
            pltpu.SemaphoreType.DMA((PIECES,)),
            pltpu.SemaphoreType.DMA((2,)),
        ],
        compiler_params=pltpu.CompilerParams(vmem_limit_bytes=48 << 20),
        cost_estimate=pl.CostEstimate(
            flops=2 * 4096 * 1024 * 1024, bytes_accessed=32 << 20, transcendentals=0
        ),
        name="ham",
    )(order, *pieces, table, coeff, weights, xc, rho)


def ring_sum(parts, axis_name, send_up, send_down, split_axis):
    far = parts[2]
    half = far.shape[split_axis] // 2
    low = lax.slice_in_dim(far, 0, half, axis=split_axis)
    high = lax.slice_in_dim(far, half, 2 * half, axis=split_axis)
    from_below = lax.ppermute(low, axis_name, send_up)
    from_above = lax.ppermute(high, axis_name, send_down)

    def cut(x, lo, hi):
        return lax.slice_in_dim(x, lo, hi, axis=split_axis)

    def plus(a, b):
        return (a.astype(jnp.float32) + b.astype(jnp.float32)).astype(jnp.float16)

    up = lax.concatenate(
        [plus(cut(parts[1], 0, half), from_below), cut(parts[1], half, 2 * half)], split_axis
    )
    down = lax.concatenate(
        [cut(parts[3], 0, half), plus(cut(parts[3], half, 2 * half), from_above)], split_axis
    )
    got_below = lax.ppermute(up, axis_name, send_up)
    got_above = lax.ppermute(down, axis_name, send_down)
    return (
        parts[0].astype(jnp.float32)
        + got_below.astype(jnp.float32)
        + got_above.astype(jnp.float32)
    )


def per_device(
    basis_values,
    point_coords,
    point_weights,
    xc_kernel,
    gauss_widths,
    atom_coords,
    resp_density,
    tile_list,
    tile_home,
    atom_list,
    atom_home,
):
    groups = lax.axis_size("grid")
    me = lax.axis_index("grid")
    plane = lax.axis_index("pert")
    my_z, my_x, my_c = me // 8, (me // 2) % 4, me % 2
    tile_dev = resp_density.shape[1]
    neighbors = atom_list.shape[1]
    moments = gauss_widths.shape[0]
    natoms = atom_home.shape[0]
    ntiles = tile_home.shape[0]
    slots_here = 2 * neighbors

    own = [basis_values[:HALF].T, basis_values[HALF:].T]
    below0 = lax.ppermute(own[0], "pert", ring(1))
    above1 = lax.ppermute(own[1], "pert", ring(3))
    below1 = lax.ppermute(own[1], "pert", ring(1))
    above0 = lax.ppermute(own[0], "pert", ring(3))
    far0 = lax.ppermute(below0, "pert", ring(1))
    far1 = lax.ppermute(above1, "pert", ring(3))
    pieces = [own[0], own[1], below0, below1, above0, above1, far0, far1]
    steps = jnp.array([0, 0, 3, 3, 1, 1, 2, 2], jnp.int32)
    halves = jnp.array([0, 1] * 4, jnp.int32)
    order = ((plane + steps) % 4) * 2 + halves

    tiles = lax.all_gather(resp_density[0], "grid", axis=0, tiled=True)
    wanted = tile_list.reshape(-1)
    tile_match = wanted[:, None] == jnp.arange(ntiles, dtype=jnp.int32)[None, :]
    homes = jnp.sum(jnp.where(tile_match, tile_home[None, :], 0), axis=1)
    homes_beside = lax.ppermute(homes, "grid", grid_perm(0, 0, 1))

    atom_match = atom_list[:, :, None] == jnp.arange(natoms, dtype=jnp.int32)
    atom_pos = jnp.sum(jnp.where(atom_match[None], atom_coords[:, None, None, :], 0.0), axis=3)
    atom_homes = jnp.sum(jnp.where(atom_match, atom_home, 0), axis=2).reshape(-1)
    delta = point_coords.reshape(3, 2, 4, 1, HALF) - atom_pos[:, :, None, :, None]
    dist_sq = (jnp.sum(delta * delta, axis=0) + SOFTEN).reshape(PIECES, neighbors, 1, HALF)
    spread = (2.0 * gauss_widths * gauss_widths)[None, None, :, None]
    erf_scale = (ROOT_TWO * gauss_widths)[None, None, :, None]
    gauss = jnp.exp(-dist_sq / spread).reshape(PIECES, neighbors * moments, HALF)
    distance = jnp.sqrt(dist_sq)
    hart = (lax.erf(distance / erf_scale) / distance).reshape(PIECES, neighbors * moments, HALF)
    weights = point_weights.reshape(PIECES, 1, HALF)
    xc = xc_kernel.reshape(PIECES, 1, HALF)

    rho, pacc = density_call(order, homes, pieces, tiles, gauss, weights)
    partial_value = jnp.sum(pacc, axis=2).reshape(slots_here, moments)
    top = jnp.max(jnp.abs(xc * rho))
    extra = jnp.concatenate(
        [atom_homes.astype(jnp.float32), jnp.full((moments - slots_here,), top)]
    )
    payload = jnp.concatenate([partial_value, extra[None, :]], axis=0)
    sent = jnp.broadcast_to(payload[None], (groups, slots_here + 1, moments))
    got = lax.all_to_all(sent, "grid", split_axis=0, concat_axis=0, tiled=True)
    all_partial = got[:, :slots_here].reshape(groups * slots_here, moments)
    all_homes = got[:, slots_here, :slots_here].reshape(-1)
    rows = jnp.concatenate(
        [jnp.arange(natoms, dtype=jnp.float32), atom_homes.astype(jnp.float32)]
    )
    select = (rows[:, None] == all_homes[None, :]).astype(jnp.float32)
    summed = jnp.dot(select, all_partial, precision=HIGH)
    all_coeffs, my_coeffs = summed[:natoms], summed[natoms:]
    atom_dev = natoms // groups
    own_coeffs = lax.dynamic_slice_in_dim(all_coeffs, me * atom_dev, atom_dev, axis=0)
    coeff = jnp.broadcast_to(
        my_coeffs.reshape(2, neighbors * moments, 1), (2, neighbors * moments, 128)
    )
    pot_bound = jnp.max(got[:, slots_here, slots_here]) + KERNEL_MAX * neighbors * jnp.max(
        jnp.sum(jnp.abs(all_coeffs), axis=1)
    )
    ham_bound = PHI_MAX_SQ * 2048 * 0.05 * groups * pot_bound * 1.01 + 1e-20

    pot, ham = ham_call(order, pieces, hart, coeff, weights, xc, rho)

    mine = (ham * (F16_TOP / ham_bound)).astype(jnp.float16)
    beside = lax.ppermute(mine, "grid", grid_perm(0, 0, 1))
    dz = jnp.arange(4, dtype=jnp.int32)[:, None, None]
    dx = jnp.arange(4, dtype=jnp.int32)[None, :, None]
    place = jnp.arange(tile_dev, dtype=jnp.int32)[None, None, :]
    slot_home = (
        ((((my_z + dz) % 4) * 4 + (my_x + dx) % 4) * 2 + my_c) * tile_dev + place
    ).reshape(-1)

    def placed(tiles_of, homes_of):
        match = slot_home[:, None] == homes_of[None, :]
        index = jnp.sum(jnp.where(match, jnp.arange(slots_here, dtype=jnp.int32), 0), axis=1)
        found = jnp.any(match, axis=1)
        return jnp.where(found[:, None, None], jnp.take(tiles_of, index, axis=0), 0).astype(
            jnp.float32
        )

    dense = (placed(mine, homes) + placed(beside, homes_beside)).astype(jnp.float16)
    dense = dense.reshape(4, 4, tile_dev, BLK, BLK)
    z_up, z_down = grid_perm(1, 0, 0), grid_perm(-1, 0, 0)
    x_up, x_down = grid_perm(0, 1, 0), grid_perm(0, -1, 0)
    half = BLK // 2
    upper = dense[:, :, :, :half]
    lower = dense[:, :, :, half:]
    upper = ring_sum([upper[d] for d in range(4)], "grid", z_up, z_down, 0)
    lower = ring_sum([lower[:, d] for d in range(4)], "grid", x_up, x_down, 0)
    upper = upper.astype(jnp.float16)
    lower = lower.astype(jnp.float16)
    upper = ring_sum([upper[d] for d in range(4)], "grid", x_up, x_down, 0)
    lower = ring_sum([lower[d] for d in range(4)], "grid", z_up, z_down, 0)
    hamiltonian = jnp.concatenate([upper, lower], axis=1) * (ham_bound / F16_TOP)
    return (hamiltonian[None], own_coeffs[None], pot.reshape(1, -1))


def solution(mesh):
    placed = (
        P(("grid", "pert"), None),
        P(None, "grid"),
        P("grid"),
        P("grid"),
        P(),
        P(),
        P("pert", "grid", None, None),
        P("grid", None),
        P(),
        P("grid", None),
        P(),
    )
    return jax.shard_map(
        per_device,
        mesh=mesh,
        in_specs=placed,
        out_specs=(P("pert", "grid", None, None), P("pert", "grid", None), P("pert", "grid")),
        check_vma=False,
    )
```

time: 715 us -> 290 us (0.41)
  waiting for transfers between devices: 399 us -> 96.9 us
  local copies, waits for them, and re-layouts: 134 us -> 41.2 us
  matrix products: 71.9 us -> 1.97 us
  blocking collectives: 40.5 us -> 0 us
  Pallas kernels: 0 us -> 35.6 us
  starting transfers between devices: 10.4 us -> 44.8 us
  other arithmetic: 37.6 us -> 52.9 us
    all_to_all x2 -> x1, waiting for transfers between devices: 302 us -> 0.34 us  [per_device(): got = lax.all_to_all(sent, 'grid', split_axis=0, concat_axis=0, tiled=True)]
    unnamed x3 -> x1, waiting for transfers between devices: 97.3 us -> 0.68 us
    ppermute x0 -> x24, waiting for transfers between devices: none -> 95.5 us  [the longest x4 22.7 us: ring_sum(): got_below = lax.ppermute(up, axis_name, send_up)]
    dot_general x11 -> x1, matrix products: 71.9 us -> 1.97 us  [per_device(): summed = jnp.dot(select, all_partial, precision=HIGH)]
    reshape x5 -> x1, local copies, waits for them, and re-layouts: 50.4 us -> 0.08 us  [per_device(): partial_value = jnp.sum(pacc, axis=2).reshape(slots_here, moments)]
    ppermute x0 -> x24, starting transfers between devices: none -> 36.8 us  [the longest x4 12.7 us: ring_sum(): got_above = lax.ppermute(down, axis_name, send_down)]
    pallas_call x0 -> x2, Pallas kernels: none -> 35.6 us  [the longest x1 21 us: ham_call(): pl.pallas_call(ham_body, out_shape=(jax.ShapeDtypeStruct((PIECES, 1, HALF...]
    all_gather x1 -> x0, blocking collectives: 25.1 us -> none  [per_device(): all_coeffs = lax.all_gather(own_coeffs, 'grid', axis=1, tiled=True)]
  transfers between devices with their start and end apart: 4 -> 26, of which waited for: 3 -> 17; matrix products, arithmetic and copies ran while one was open for 7% -> 13% of each run, Pallas kernels for 0% -> 0%
where the time goes in v1:
time: 290 us; the launch traced here: 289 us
  waiting for transfers between devices  96.9 us (33%)
  other arithmetic  52.9 us (18%)
  starting transfers between devices  44.8 us (15%)
  local copies, waits for them, and re-layouts  41.2 us (14%)
  Pallas kernels  35.6 us (12%)
  between operations  15.8 us (5%)
    ppermute x4, waiting for transfers between devices, ring_sum(): got_below = lax.ppermute(up, axis_name, send_up)  22.7 us
    pallas_call x1, Pallas kernels, ham_call(): pl.pallas_call(ham_body, out_shape=(jax.ShapeDtypeStruct((PIECES, 1, HALF...  21 us
    ppermute x1, waiting for transfers between devices, per_device(): far0 = lax.ppermute(below0, 'pert', ring(1))  19.4 us
    ppermute x1, waiting for transfers between devices, per_device(): below0 = lax.ppermute(own[0], 'pert', ring(1))  18.7 us
    gather x2, local copies, waits for them, and re-layouts, placed(): jnp.take(tiles_of, index, axis=0)  17.9 us
    pallas_call x1, Pallas kernels, density_call(): pl.pallas_call(density_body, out_shape=(jax.ShapeDtypeStruct((PIECES, 1,...  14.7 us
    ppermute x4, starting transfers between devices, ring_sum(): got_above = lax.ppermute(down, axis_name, send_down)  12.7 us
    unnamed x38, local copies, waits for them, and re-layouts  11.6 us
  transfers between devices with their start and end apart: 26, of which 17 were waited for; matrix products, arithmetic and copies ran while one was open for 13% of the time, Pallas kernels for 0%

profile of v1, /device:TPU:0, one launch (start us, length us, event | category | flops | bytes accessed | tf_op | source)
XLA Modules:
  0.0 289.2 jit_solution(6015162266080208256)
XLA Ops:
  8.0 2.7 fusion.29
  11.2 1.8 collective-permute-start
  12.9 1.5 copy.75
  14.4 1.6 collective-permute-start.3
  16.5 2.8 collective-permute-start.2
  19.8 18.7 %collective-permute-done.refs_2_ = bf16[1024,512]{1,0:T(8,128)(2,1)S(1)} collective-permute-done((bf16[1024,512]{1,0:T(8,128)(2,1)S(1)}, bf16[1024,512]{1,0:T(8,128)(2,1)S(1)}, u32[]{:S(2)}, u32[]{:S(2)}) %collective-permute-start) | collective-permute-done | bytes 1048608 | tf_op jit(solution)/shard_map/ppermute | solution.py:259
  39.0 1.7 collective-permute-done.3.refs_5_
  40.6 2.8 collective-permute-start.5
  44.5 8.1 %fusion.refs_9_ = f32[8,1024,512]{2,1,0:T(8,128)} fusion(f32[1024]{0:T(1024)S(1)} %div.84, f32[8,16,512]{2,1,0:T(8,128)S(1)} %bitcast.153), kind=kLoop, calls=%fused_computation.5 | loop fusion | flops 4194304 | bytes 17043456 | tf_op jit(solution)/shard_map/exp | solution.py:283
  52.8 8.2 %collective-permute-done.1.refs_3_ = bf16[1024,512]{1,0:T(8,128)(2,1)} collective-permute-done((bf16[1024,512]{1,0:T(8,128)(2,1)S(1)}, bf16[1024,512]{1,0:T(8,128)(2,1)}, u32[]{:S(2)}, u32[]{:S(2)}) %collective-permute-start.1) | collective-permute-done | bytes 1048608 | tf_op jit(solution)/shard_map/ppermute | solution.py:261
  61.1 2.0 collective-permute-done.2.refs_4_
  63.1 19.4 %collective-permute-done.4.refs_6_ = bf16[1024,512]{1,0:T(8,128)(2,1)S(1)} collective-permute-done((bf16[1024,512]{1,0:T(8,128)(2,1)S(1)}, bf16[1024,512]{1,0:T(8,128)(2,1)S(1)}, u32[]{:S(2)}, u32[]{:S(2)}) %collective-permute-start.4) | collective-permute-done | bytes 1048608 | tf_op jit(solution)/shard_map/ppermute | solution.py:263
  85.5 1.2 copy-done.1
  86.7 1.2 copy-done.3
  87.9 14.7 %density.1 = (f32[8,1,512]{2,1,0:T(1,128)S(1)}, f32[2,1024,128]{2,1,0:T(8,128)S(1)}) custom-call(s32[8]{0:T(128)S(1)} %fusion.25.order, s32[32]{0:T(128)S(1)} %select_reduce_fusion.2.where, bf16[1024,512]{1,0:T(8,128)(2,1)S(1)} %bitcast.136, bf16[1024,512]{1,0:T(8,128)(2,1)S(1)} %bitcast.140, bf16[1024,512]{1,0:T(8,128)(2,1)S(1)} %collective-permute-done.refs_2_, ...), custom_call_target="tpu_custom_call" | custom-call | flops 8589934592 | bytes 33554432 | tf_op jit(solution)/shard_map/density/pallas_call | solution.py:156
  103.6 1.6 reduce_sum.76
  107.4 2.1 reshape.303
  109.6 8.0 %all-to-all-start = ((f32[32,1,2112]{2,1,0:T(1,128)}), f32[32,1,2112]{2,1,0:T(1,128)S(1)}, u32[]{:S(2)}, u32[]{:S(2)}) async-start(f32[32,1,2112]{2,1,0:T(1,128)} %reshape.303), calls=%async_computation | async-start | bytes 557056 | tf_op jit(solution)/shard_map/all_to_all | solution.py:297
  117.7 8.3 %bitcast_divide_fusion.refs_8_ = f32[8,1024,512]{2,1,0:T(8,128)} fusion(f32[1024]{0:T(1024)S(1)} %div.77, f32[8,16,512]{2,1,0:T(8,128)} %bitcast.152), kind=kLoop, calls=%fused_computation.2 | loop fusion | flops 8388608 | bytes 17043456 | tf_op jit(solution)/shard_map/div | solution.py:285
  126.9 2.1 reduce.5
  128.9 1.9 reshape.304
  130.9 1.9 slice.263
  133.7 1.6 slice_reduce_fusion
  135.4 2.0 fusion.5
  139.5 1.4 broadcast_in_dim.128.refs_9_
  140.9 21.0 %ham.1 = (f32[8,1,512]{2,1,0:T(1,128)}, f32[32,256,256]{2,1,0:T(8,128)}) custom-call(s32[8]{0:T(128)S(1)} %fusion.25.order, bf16[1024,512]{1,0:T(8,128)(2,1)S(1)} %bitcast.137, bf16[1024,512]{1,0:T(8,128)(2,1)S(1)} %bitcast.141, bf16[1024,512]{1,0:T(8,128)(2,1)S(1)} %collective-permute-done.refs_2_, bf16[1024,512]{1,0:T(8,128)(2,1)} %collective-permute-done.1.refs_3_, ...), custom_call_target="tpu_custom_call" | custom-call | flops 8589934592 | bytes 33554432 | tf_op jit(solution)/shard_map/ham/pallas_call | solution.py:182
  161.9 6.4 %multiply_convert_fusion = f16[32,256,256]{2,1,0:T(8,128)(2,1)} fusion(f32[32,256,256]{2,1,0:T(8,128)} %get-tuple-element.10, f32[]{:T(128)S(6)} %div.87), kind=kLoop, calls=%fused_computation.9 | loop fusion | flops 4194304 | bytes 12582916 | tf_op jit(solution)/shard_map/convert_element_type | solution.py:318
  169.0 6.7 %collective-permute-done.6 = s32[32]{0:T(128)S(1)} collective-permute-done((s32[32]{0:T(128)S(1)}, s32[32]{0:T(128)S(1)}, u32[]{:S(2)}, u32[]{:S(2)}) %collective-permute-start.6) | collective-permute-done | bytes 160 | tf_op jit(solution)/shard_map/ppermute | solution.py:274
  176.0 8.9 %gather_fusion = f16[64,256,256]{2,1,0:T(8,128)(2,1)} fusion(f16[32,256,256]{2,1,0:T(8,128)(2,1)} %multiply_convert_fusion, s32[1024]{0:T(1024)S(1)} %pad_clamp_fusion.1), kind=kCustom, calls=%fused_computation.clone | custom fusion | bytes 16777472 | tf_op jit(solution)/shard_map/jit(_take)/gather | solution.py:331
  185.0 8.9 %gather_fusion.1 = f16[64,256,256]{2,1,0:T(8,128)(2,1)} fusion(f16[32,256,256]{2,1,0:T(8,128)(2,1)} %collective-permute-done.7, s32[1024]{0:T(1024)S(1)} %pad_clamp_fusion), kind=kCustom, calls=%fused_computation.1.clone | custom fusion | bytes 16777472 | tf_op jit(solution)/shard_map/jit(_take)/gather | solution.py:331
  193.9 10.6 %add_convert_fusion = f16[64,256,256]{2,1,0:T(8,128)(2,1)S(1)} fusion(f16[64,256,256]{2,1,0:T(8,128)(2,1)} %gather_fusion.1, f16[64,256,256]{2,1,0:T(8,128)(2,1)} %gather_fusion, pred[64]{0:T(512)(128)(4,1)S(1)} %compare_and_fusion, pred[64]{0:T(512)(128)(4,1)S(1)} %compare_and_fusion.1, pred[64]{0:T(512)(128)(4,1)S(1)} %get-tuple-element.13, ...), kind=kLoop, calls=%fused_computation.6 | loop fusion | flops 33554432 | bytes 25166080 | tf_op jit(solution)/shard_map/convert_element_type | solution.py:335
  205.6 2.6 collective-permute-start.10
  208.2 1.5 collective-permute-start.16
  209.7 1.8 collective-permute-start.18
  211.5 8.4 %collective-permute-done.10 = f16[2,4,128,256]{3,2,1,0:T(8,128)(2,1)S(1)} collective-permute-done((f16[2,4,128,256]{3,2,1,0:T(8,128)(2,1)S(1)}, f16[2,4,128,256]{3,2,1,0:T(8,128)(2,1)S(1)}, u32[]{:S(2)}, u32[]{:S(2)}) %collective-permute-start.10) | collective-permute-done | bytes 524320 | tf_op jit(solution)/shard_map/ppermute | solution.py:211
  219.8 3.3 %collective-permute-done.16 = f16[2,4,128,256]{3,2,1,0:T(8,128)(2,1)S(1)} collective-permute-done((f16[2,4,128,256]{3,2,1,0:T(8,128)(2,1)S(1)}, f16[2,4,128,256]{3,2,1,0:T(8,128)(2,1)S(1)}, u32[]{:S(2)}, u32[]{:S(2)}) %collective-permute-start.16) | collective-permute-done | bytes 524320 | tf_op jit(solution)/shard_map/ppermute | solution.py:210
  223.1 2.7 collective-permute-done.8
  227.7 3.0 %collective-permute-start.19 = (f16[4,4,128,256]{3,2,1,0:T(8,128)(2,1)S(1)}, f16[4,4,128,256]{3,2,1,0:T(8,128)(2,1)}, u32[]{:S(2)}, u32[]{:S(2)}) collective-permute-start(f16[4,4,128,256]{3,2,1,0:T(8,128)(2,1)S(1)} %pad_maximum_fusion.3), channel_id=1, source_target_pairs={{0,24},{4,28},{8,0},{12,4},{16,8},{20,12},{24,16},{28,20},{32,56},... | collective-permute-start | bytes 3145736 | tf_op jit(solution)/shard_map/ppermute | solution.py:226
  231.4 1.2 pad_maximum_fusion.1
  232.6 3.2 %collective-permute-start.11 = (f16[4,4,128,256]{3,2,1,0:T(8,128)(2,1)}, f16[4,4,128,256]{3,2,1,0:T(8,128)(2,1)}, u32[]{:S(2)}, u32[]{:S(2)}) collective-permute-start(f16[4,4,128,256]{3,2,1,0:T(8,128)(2,1)} %pad_maximum_fusion.1), channel_id=1, source_target_pairs={{0,96},{4,100},{8,104},{12,108},{16,112},{20,116},{24,120},{28,124... | collective-permute-start | bytes 3145736 | tf_op jit(solution)/shard_map/ppermute | solution.py:226
  235.8 16.1 %collective-permute-done.17 = f16[4,4,128,256]{3,2,1,0:T(8,128)(2,1)} collective-permute-done((f16[4,4,128,256]{3,2,1,0:T(8,128)(2,1)S(1)}, f16[4,4,128,256]{3,2,1,0:T(8,128)(2,1)}, u32[]{:S(2)}, u32[]{:S(2)}) %collective-permute-start.17) | collective-permute-done | bytes 1048608 | tf_op jit(solution)/shard_map/ppermute | solution.py:225
  251.9 3.6 %collective-permute-done.9 = f16[4,4,128,256]{3,2,1,0:T(8,128)(2,1)} collective-permute-done((f16[4,4,128,256]{3,2,1,0:T(8,128)(2,1)S(1)}, f16[4,4,128,256]{3,2,1,0:T(8,128)(2,1)}, u32[]{:S(2)}, u32[]{:S(2)}) %collective-permute-start.9) | collective-permute-done | bytes 1048608 | tf_op jit(solution)/shard_map/ppermute | solution.py:225
  256.3 4.3 %fusion.4 = (f16[4,4,128,256]{3,2,1,0:T(8,128)(2,1)S(1)}, f16[4,4,128,256]{3,2,1,0:T(8,128)(2,1)S(1)}) fusion(f16[4,4,128,256]{3,2,1,0:T(8,128)(2,1)} %collective-permute-done.11, f16[4,4,128,256]{3,2,1,0:T(8,128)(2,1)} %collective-permute-done.9, f16[4,4,4,256,256]{4,3,2,1,0:T(8,128)(2,1)} %bitcast.149, f16[4,4,128,256]{3,2,1,0:T(8,128)(2,1)} %collective-permute-done.19, ...), kind=kLoop, calls=%fused_computation.15 | loop fusion | flops 6291456 | bytes 8388608 | tf_op jit(solution)/shard_map/convert_element_type | solution.py:344
  260.8 3.2 %collective-permute-start.14 = (f16[2,128,256]{2,1,0:T(8,128)(2,1)S(1)}, f16[2,128,256]{2,1,0:T(8,128)(2,1)S(1)}, u32[]{:S(2)}, u32[]{:S(2)}) collective-permute-start(f16[2,128,256]{2,1,0:T(8,128)(2,1)S(1)} %get-tuple-element.35), channel_id=1, source_target_pairs={{0,24},{4,28},{8,0},{12,4},{16,8},{20,12},{24,16},{28,20},{32,56},... | collective-permute-start | bytes 393224 | tf_op jit(solution)/shard_map/ppermute | solution.py:211
  264.2 3.8 %collective-permute-start.22 = (f16[2,128,256]{2,1,0:T(8,128)(2,1)S(1)}, f16[2,128,256]{2,1,0:T(8,128)(2,1)S(1)}, u32[]{:S(2)}, u32[]{:S(2)}) collective-permute-start(f16[2,128,256]{2,1,0:T(8,128)(2,1)S(1)} %get-tuple-element.41), channel_id=1, source_target_pairs={{0,96},{4,100},{8,104},{12,108},{16,112},{20,116},{24,120},{28,124... | collective-permute-start | bytes 393224 | tf_op jit(solution)/shard_map/ppermute | solution.py:211
  268.9 3.2 %collective-permute-start.15 = (f16[4,128,256]{2,1,0:T(8,128)(2,1)}, f16[4,128,256]{2,1,0:T(8,128)(2,1)S(1)}, u32[]{:S(2)}, u32[]{:S(2)}) collective-permute-start(f16[4,128,256]{2,1,0:T(8,128)(2,1)} %pad_maximum_fusion.5), channel_id=1, source_target_pairs={{0,24},{4,28},{8,0},{12,4},{16,8},{20,12},{24,16},{28,20},{32,56},... | collective-permute-start | bytes 786440 | tf_op jit(solution)/shard_map/ppermute | solution.py:226
  273.8 3.2 %collective-permute-start.23 = (f16[4,128,256]{2,1,0:T(8,128)(2,1)}, f16[4,128,256]{2,1,0:T(8,128)(2,1)S(1)}, u32[]{:S(2)}, u32[]{:S(2)}) collective-permute-start(f16[4,128,256]{2,1,0:T(8,128)(2,1)} %pad_maximum_fusion.7), channel_id=1, source_target_pairs={{0,96},{4,100},{8,104},{12,108},{16,112},{20,116},{24,120},{28,124... | collective-permute-start | bytes 786440 | tf_op jit(solution)/shard_map/ppermute | solution.py:226
  277.9 2.9 %collective-permute-done.21 = f16[4,128,256]{2,1,0:T(8,128)(2,1)S(1)} collective-permute-done((f16[4,128,256]{2,1,0:T(8,128)(2,1)}, f16[4,128,256]{2,1,0:T(8,128)(2,1)S(1)}, u32[]{:S(2)}, u32[]{:S(2)}) %collective-permute-start.21) | collective-permute-done | bytes 262176 | tf_op jit(solution)/shard_map/ppermute | solution.py:225
  (122 shorter events, 23.8 us)
Async XLA Ops:
  7.2 12.1 %copy-start.14 = (s32[2,16]{1,0:T(2,128)S(1)}, s32[2,16]{1,0:T(2,128)}, u32[]{:S(2)}) copy-start(s32[2,16]{1,0:T(2,128)} %param.22) | copy-start | bytes 388
  7.2 12.2 %copy-start.8 = (f32[3,4096]{1,0:T(4,128)S(1)}, f32[3,4096]{1,0:T(4,128)}, u32[]{:S(2)}) copy-start(f32[3,4096]{1,0:T(4,128)} %param.16) | copy-start | bytes 147460
  7.2 12.3 %copy-start.15 = (f32[64]{0:T(128)S(1)}, f32[64]{0:T(128)}, u32[]{:S(2)}) copy-start(f32[64]{0:T(128)} %param.19) | copy-start | bytes 772
  7.2 12.3 %copy-start.9 = (s32[2,16]{1,0:T(2,128)S(1)}, s32[2,16]{1,0:T(2,128)}, u32[]{:S(2)}) copy-start(s32[2,16]{1,0:T(2,128)} %param.24) | copy-start | bytes 388
  7.2 12.3 %copy-start.11 = (s32[256]{0:T(256)S(1)}, s32[256]{0:T(256)}, u32[]{:S(2)}) copy-start(s32[256]{0:T(256)} %param.25) | copy-start | bytes 3076
  7.2 36.3 %copy-start.10 = (f32[3,256]{1,0:T(4,128)S(1)}, f32[3,256]{1,0:T(4,128)}, u32[]{:S(2)}) copy-start(f32[3,256]{1,0:T(4,128)} %param.20) | copy-start | bytes 9220
  7.2 78.3 %all-gather.3.cloned.1.call-start = ((), (), s32[]{:S(2)}) async-start(), calls=%async_computation.1 | async-start | bytes 17301504 | tf_op jit(solution)/shard_map/all_gather | solution.py:270
  11.2 27.3 %collective-permute-start = (bf16[1024,512]{1,0:T(8,128)(2,1)S(1)}, bf16[1024,512]{1,0:T(8,128)(2,1)S(1)}, u32[]{:S(2)}, u32[]{:S(2)}) collective-permute-start(bf16[1024,512]{1,0:T(8,128)(2,1)S(1)} %bitcast.134), channel_id=1, source_target_pairs={{0,1},{1,2},{2,3},{3,0},{4,5},{5,6},{6,7},{7,4},{8,9},{9,10},{10,1... | collective-permute-start | bytes 3145736 | tf_op jit(solution)/shard_map/ppermute | solution.py:259
  14.4 26.2 %collective-permute-start.3 = (bf16[1024,512]{1,0:T(8,128)(2,1)S(1)}, bf16[1024,512]{1,0:T(8,128)(2,1)}, u32[]{:S(2)}, u32[]{:S(2)}) collective-permute-start(bf16[1024,512]{1,0:T(8,128)(2,1)S(1)} %bitcast.138), channel_id=1, source_target_pairs={{0,3},{1,0},{2,1},{3,2},{4,7},{5,4},{6,5},{7,6},{8,11},{9,8},{10,9... | collective-permute-start | bytes 3145736 | tf_op jit(solution)/shard_map/ppermute | solution.py:260
  16.1 45.0 %collective-permute-start.1 = (bf16[1024,512]{1,0:T(8,128)(2,1)S(1)}, bf16[1024,512]{1,0:T(8,128)(2,1)}, u32[]{:S(2)}, u32[]{:S(2)}) collective-permute-start(bf16[1024,512]{1,0:T(8,128)(2,1)S(1)} %bitcast.139), channel_id=1, source_target_pairs={{0,1},{1,2},{2,3},{3,0},{4,5},{5,6},{6,7},{7,4},{8,9},{9,10},{10,1... | collective-permute-start | bytes 3145736 | tf_op jit(solution)/shard_map/ppermute | solution.py:261
  16.5 46.6 %collective-permute-start.2 = (bf16[1024,512]{1,0:T(8,128)(2,1)S(1)}, bf16[1024,512]{1,0:T(8,128)(2,1)}, u32[]{:S(2)}, u32[]{:S(2)}) collective-permute-start(bf16[1024,512]{1,0:T(8,128)(2,1)S(1)} %bitcast.135), channel_id=1, source_target_pairs={{0,3},{1,0},{2,1},{3,2},{4,7},{5,4},{6,5},{7,6},{8,11},{9,8},{10,9... | collective-permute-start | bytes 3145736 | tf_op jit(solution)/shard_map/ppermute | solution.py:262
  38.5 44.0 %collective-permute-start.4 = (bf16[1024,512]{1,0:T(8,128)(2,1)S(1)}, bf16[1024,512]{1,0:T(8,128)(2,1)S(1)}, u32[]{:S(2)}, u32[]{:S(2)}) collective-permute-start(bf16[1024,512]{1,0:T(8,128)(2,1)S(1)} %collective-permute-done.refs_2_), channel_id=1, source_target_pairs={{0,1},{1,2},{2,3},{3,0},{4,5},{5,6},{6,7},{7,4},{8,9},{9,10},{10,1... | collective-permute-start | bytes 3145736 | tf_op jit(solution)/shard_map/ppermute | solution.py:263
  40.6 43.4 %collective-permute-start.5 = (bf16[1024,512]{1,0:T(8,128)(2,1)}, bf16[1024,512]{1,0:T(8,128)(2,1)S(1)}, u32[]{:S(2)}, u32[]{:S(2)}) collective-permute-start(bf16[1024,512]{1,0:T(8,128)(2,1)} %collective-permute-done.3.refs_5_), channel_id=1, source_target_pairs={{0,3},{1,0},{2,1},{3,2},{4,7},{5,4},{6,5},{7,6},{8,11},{9,8},{10,9... | collective-permute-start | bytes 3145736 | tf_op jit(solution)/shard_map/ppermute | solution.py:264
  44.5 8.1 %copy-start.16 = (s32[128]{0:T(128)S(1)}, s32[128]{0:T(128)}, u32[]{:S(2)}) copy-start(s32[128]{0:T(128)} %param.23) | copy-start | bytes 1540
  44.5 8.3 %copy-start.12 = (s32[8]{0:T(128)S(1)}, s32[8]{0:T(128)}, u32[]{:S(2)}) copy-start(s32[8]{0:T(128)} %constant.125.clone) | copy-start | bytes 100
  44.5 8.3 %copy-start.13 = (s32[8]{0:T(128)S(1)}, s32[8]{0:T(128)}, u32[]{:S(2)}) copy-start(s32[8]{0:T(128)} %constant.126.clone) | copy-start | bytes 100
  44.5 41.0 %copy-start.5 = (f32[4096]{0:T(1024)S(1)}, f32[4096]{0:T(1024)}, u32[]{:S(2)}) copy-start(f32[4096]{0:T(1024)} %param.17) | copy-start | bytes 49156
  82.5 1.0 copy-start
  84.1 1.0 copy-start.2
  85.5 1.2 copy-start.1
  86.7 1.2 copy-start.3
  87.9 17.3 %copy-start.6 = (f32[4096]{0:T(1024)S(1)}, f32[4096]{0:T(1024)}, u32[]{:S(2)}) copy-start(f32[4096]{0:T(1024)} %param.18) | copy-start | bytes 49156
  102.6 1.0 copy-start.4
  109.6 16.8 %all-to-all-start = ((f32[32,1,2112]{2,1,0:T(1,128)}), f32[32,1,2112]{2,1,0:T(1,128)S(1)}, u32[]{:S(2)}, u32[]{:S(2)}) async-start(f32[32,1,2112]{2,1,0:T(1,128)} %reshape.303), calls=%async_computation | async-start | bytes 557056 | tf_op jit(solution)/shard_map/all_to_all | solution.py:297
  168.3 16.7 %collective-permute-start.7 = (f16[32,256,256]{2,1,0:T(8,128)(2,1)}, f16[32,256,256]{2,1,0:T(8,128)(2,1)}, u32[]{:S(2)}, u32[]{:S(2)}) collective-permute-start(f16[32,256,256]{2,1,0:T(8,128)(2,1)} %multiply_convert_fusion), channel_id=1, source_target_pairs={{0,4},{4,0},{8,12},{12,8},{16,20},{20,16},{24,28},{28,24},{32,36},... | collective-permute-start | bytes 12582920 | tf_op jit(solution)/shard_map/ppermute | solution.py:319
  168.6 7.2 %collective-permute-start.6 = (s32[32]{0:T(128)S(1)}, s32[32]{0:T(128)S(1)}, u32[]{:S(2)}, u32[]{:S(2)}) collective-permute-start(s32[32]{0:T(128)S(1)} %select_reduce_fusion.2.where), channel_id=1, source_target_pairs={{0,4},{4,0},{8,12},{12,8},{16,20},{20,16},{24,28},{28,24},{32,36},... | collective-permute-start | bytes 392 | tf_op jit(solution)/shard_map/ppermute | solution.py:274
  204.5 22.6 %copy-start.7 = (f16[64,256,256]{2,1,0:T(8,128)(2,1)}, f16[64,256,256]{2,1,0:T(8,128)(2,1)S(1)}, u32[]{:S(2)}) copy-start(f16[64,256,256]{2,1,0:T(8,128)(2,1)S(1)} %add_convert_fusion) | copy-start | bytes 25165828
  205.6 14.2 %collective-permute-start.10 = (f16[2,4,128,256]{3,2,1,0:T(8,128)(2,1)S(1)}, f16[2,4,128,256]{3,2,1,0:T(8,128)(2,1)S(1)}, u32[]{:S(2)}, u32[]{:S(2)}) collective-permute-start(f16[2,4,128,256]{3,2,1,0:T(8,128)(2,1)S(1)} %get-tuple-element.23), channel_id=1, source_target_pairs={{0,96},{4,100},{8,104},{12,108},{16,112},{20,116},{24,120},{28,124... | collective-permute-start | bytes 1572872 | tf_op jit(solution)/shard_map/ppermute | solution.py:211
  208.2 14.9 %collective-permute-start.16 = (f16[2,4,128,256]{3,2,1,0:T(8,128)(2,1)S(1)}, f16[2,4,128,256]{3,2,1,0:T(8,128)(2,1)S(1)}, u32[]{:S(2)}, u32[]{:S(2)}) collective-permute-start(f16[2,4,128,256]{3,2,1,0:T(8,128)(2,1)S(1)} %get-tuple-element.26), channel_id=1, source_target_pairs={{0,8},{4,12},{8,16},{12,20},{16,24},{20,28},{24,0},{28,4},{32,40},... | collective-permute-start | bytes 1572872 | tf_op jit(solution)/shard_map/ppermute | solution.py:210
  209.7 13.4 %collective-permute-start.18 = (f16[2,4,128,256]{3,2,1,0:T(8,128)(2,1)S(1)}, f16[2,4,128,256]{3,2,1,0:T(8,128)(2,1)S(1)}, u32[]{:S(2)}, u32[]{:S(2)}) collective-permute-start(f16[2,4,128,256]{3,2,1,0:T(8,128)(2,1)S(1)} %get-tuple-element.29), channel_id=1, source_target_pairs={{0,24},{4,28},{8,0},{12,4},{16,8},{20,12},{24,16},{28,20},{32,56},... | collective-permute-start | bytes 1572872 | tf_op jit(solution)/shard_map/ppermute | solution.py:211
  211.5 14.3 %collective-permute-start.8 = (f16[2,4,128,256]{3,2,1,0:T(8,128)(2,1)S(1)}, f16[2,4,128,256]{3,2,1,0:T(8,128)(2,1)S(1)}, u32[]{:S(2)}, u32[]{:S(2)}) collective-permute-start(f16[2,4,128,256]{3,2,1,0:T(8,128)(2,1)S(1)} %get-tuple-element.22), channel_id=1, source_target_pairs={{0,32},{4,36},{8,40},{12,44},{16,48},{20,52},{24,56},{28,60},{32,6... | collective-permute-start | bytes 1572872 | tf_op jit(solution)/shard_map/ppermute | solution.py:210
  227.1 24.9 %collective-permute-start.17 = (f16[4,4,128,256]{3,2,1,0:T(8,128)(2,1)S(1)}, f16[4,4,128,256]{3,2,1,0:T(8,128)(2,1)}, u32[]{:S(2)}, u32[]{:S(2)}) collective-permute-start(f16[4,4,128,256]{3,2,1,0:T(8,128)(2,1)S(1)} %pad_maximum_fusion.2), channel_id=1, source_target_pairs={{0,8},{4,12},{8,16},{12,20},{16,24},{20,28},{24,0},{28,4},{32,40},... | collective-permute-start | bytes 3145736 | tf_op jit(solution)/shard_map/ppermute | solution.py:225
  227.7 24.2 %collective-permute-start.19 = (f16[4,4,128,256]{3,2,1,0:T(8,128)(2,1)S(1)}, f16[4,4,128,256]{3,2,1,0:T(8,128)(2,1)}, u32[]{:S(2)}, u32[]{:S(2)}) collective-permute-start(f16[4,4,128,256]{3,2,1,0:T(8,128)(2,1)S(1)} %pad_maximum_fusion.3), channel_id=1, source_target_pairs={{0,24},{4,28},{8,0},{12,4},{16,8},{20,12},{24,16},{28,20},{32,56},... | collective-permute-start | bytes 3145736 | tf_op jit(solution)/shard_map/ppermute | solution.py:226
  231.0 24.6 %collective-permute-start.9 = (f16[4,4,128,256]{3,2,1,0:T(8,128)(2,1)S(1)}, f16[4,4,128,256]{3,2,1,0:T(8,128)(2,1)}, u32[]{:S(2)}, u32[]{:S(2)}) collective-permute-start(f16[4,4,128,256]{3,2,1,0:T(8,128)(2,1)S(1)} %pad_maximum_fusion), channel_id=1, source_target_pairs={{0,32},{4,36},{8,40},{12,44},{16,48},{20,52},{24,56},{28,60},{32,6... | collective-permute-start | bytes 3145736 | tf_op jit(solution)/shard_map/ppermute | solution.py:225
  232.6 23.7 %collective-permute-start.11 = (f16[4,4,128,256]{3,2,1,0:T(8,128)(2,1)}, f16[4,4,128,256]{3,2,1,0:T(8,128)(2,1)}, u32[]{:S(2)}, u32[]{:S(2)}) collective-permute-start(f16[4,4,128,256]{3,2,1,0:T(8,128)(2,1)} %pad_maximum_fusion.1), channel_id=1, source_target_pairs={{0,96},{4,100},{8,104},{12,108},{16,112},{20,116},{24,120},{28,124... | collective-permute-start | bytes 3145736 | tf_op jit(solution)/shard_map/ppermute | solution.py:226
  260.7 7.3 %collective-permute-start.12 = (f16[2,128,256]{2,1,0:T(8,128)(2,1)S(1)}, f16[2,128,256]{2,1,0:T(8,128)(2,1)S(1)}, u32[]{:S(2)}, u32[]{:S(2)}) collective-permute-start(f16[2,128,256]{2,1,0:T(8,128)(2,1)S(1)} %get-tuple-element.34), channel_id=1, source_target_pairs={{0,8},{4,12},{8,16},{12,20},{16,24},{20,28},{24,0},{28,4},{32,40},... | collective-permute-start | bytes 393224 | tf_op jit(solution)/shard_map/ppermute | solution.py:210
  260.8 7.2 %collective-permute-start.14 = (f16[2,128,256]{2,1,0:T(8,128)(2,1)S(1)}, f16[2,128,256]{2,1,0:T(8,128)(2,1)S(1)}, u32[]{:S(2)}, u32[]{:S(2)}) collective-permute-start(f16[2,128,256]{2,1,0:T(8,128)(2,1)S(1)} %get-tuple-element.35), channel_id=1, source_target_pairs={{0,24},{4,28},{8,0},{12,4},{16,8},{20,12},{24,16},{28,20},{32,56},... | collective-permute-start | bytes 393224 | tf_op jit(solution)/shard_map/ppermute | solution.py:211
  264.1 8.1 %collective-permute-start.20 = (f16[2,128,256]{2,1,0:T(8,128)(2,1)S(1)}, f16[2,128,256]{2,1,0:T(8,128)(2,1)S(1)}, u32[]{:S(2)}, u32[]{:S(2)}) collective-permute-start(f16[2,128,256]{2,1,0:T(8,128)(2,1)S(1)} %get-tuple-element.40), channel_id=1, source_target_pairs={{0,32},{4,36},{8,40},{12,44},{16,48},{20,52},{24,56},{28,60},{32,6... | collective-permute-start | bytes 393224 | tf_op jit(solution)/shard_map/ppermute | solution.py:210
  264.2 8.0 %collective-permute-start.22 = (f16[2,128,256]{2,1,0:T(8,128)(2,1)S(1)}, f16[2,128,256]{2,1,0:T(8,128)(2,1)S(1)}, u32[]{:S(2)}, u32[]{:S(2)}) collective-permute-start(f16[2,128,256]{2,1,0:T(8,128)(2,1)S(1)} %get-tuple-element.41), channel_id=1, source_target_pairs={{0,96},{4,100},{8,104},{12,108},{16,112},{20,116},{24,120},{28,124... | collective-permute-start | bytes 393224 | tf_op jit(solution)/shard_map/ppermute | solution.py:211
  268.1 9.7 %collective-permute-start.13 = (f16[4,128,256]{2,1,0:T(8,128)(2,1)S(1)}, f16[4,128,256]{2,1,0:T(8,128)(2,1)S(1)}, u32[]{:S(2)}, u32[]{:S(2)}) collective-permute-start(f16[4,128,256]{2,1,0:T(8,128)(2,1)S(1)} %pad_maximum_fusion.4), channel_id=1, source_target_pairs={{0,8},{4,12},{8,16},{12,20},{16,24},{20,28},{24,0},{28,4},{32,40},... | collective-permute-start | bytes 786440 | tf_op jit(solution)/shard_map/ppermute | solution.py:225
  268.9 8.8 %collective-permute-start.15 = (f16[4,128,256]{2,1,0:T(8,128)(2,1)}, f16[4,128,256]{2,1,0:T(8,128)(2,1)S(1)}, u32[]{:S(2)}, u32[]{:S(2)}) collective-permute-start(f16[4,128,256]{2,1,0:T(8,128)(2,1)} %pad_maximum_fusion.5), channel_id=1, source_target_pairs={{0,24},{4,28},{8,0},{12,4},{16,8},{20,12},{24,16},{28,20},{32,56},... | collective-permute-start | bytes 786440 | tf_op jit(solution)/shard_map/ppermute | solution.py:226
  273.0 7.8 %collective-permute-start.21 = (f16[4,128,256]{2,1,0:T(8,128)(2,1)}, f16[4,128,256]{2,1,0:T(8,128)(2,1)S(1)}, u32[]{:S(2)}, u32[]{:S(2)}) collective-permute-start(f16[4,128,256]{2,1,0:T(8,128)(2,1)} %pad_maximum_fusion.6), channel_id=1, source_target_pairs={{0,32},{4,36},{8,40},{12,44},{16,48},{20,52},{24,56},{28,60},{32,6... | collective-permute-start | bytes 786440 | tf_op jit(solution)/shard_map/ppermute | solution.py:225
  273.8 7.4 %collective-permute-start.23 = (f16[4,128,256]{2,1,0:T(8,128)(2,1)}, f16[4,128,256]{2,1,0:T(8,128)(2,1)S(1)}, u32[]{:S(2)}, u32[]{:S(2)}) collective-permute-start(f16[4,128,256]{2,1,0:T(8,128)(2,1)} %pad_maximum_fusion.7), channel_id=1, source_target_pairs={{0,96},{4,100},{8,104},{12,108},{16,112},{20,116},{24,120},{28,124... | collective-permute-start | bytes 786440 | tf_op jit(solution)/shard_map/ppermute | solution.py:226
Sparse Core Ops, SparseCore 0:
  10.3 75.1 all-gather.2

commit v2 on v1

v2 whole, which is shorter than its diff:
```python
import jax
import jax.numpy as jnp
from jax import lax
from jax.experimental import pallas as pl
from jax.experimental.pallas import tpu as pltpu
from jax.sharding import PartitionSpec as P

SOFTEN = 0.25
ROOT_TWO = 1.4142135623730951
HALF = 512
PIECES = 8
BLK = 256
NB = 4
PHI_MAX_SQ = 36.0
KERNEL_MAX = 2.0
F16_TOP = 32000.0
PAY_ROWS = 24


def ring(shift):
    return [(i, (i + shift) % 4) for i in range(4)]


def grid_perm(dz, dx, dc):
    def at(z, x, c):
        return ((z % 4) * 4 + x % 4) * 2 + c

    return [
        (at(z, x, c), at(z + dz, x + dx, c ^ dc))
        for z in range(4)
        for x in range(4)
        for c in range(2)
    ]


def load_pieces(piece_refs, held, sems):
    for i, ref in enumerate(piece_refs):
        pltpu.make_async_copy(ref, held.at[i], sems.at[i]).start()


def split3(x):
    first = x.astype(jnp.bfloat16)
    rest = x - first.astype(jnp.float32)
    second = rest.astype(jnp.bfloat16)
    third = (rest - second.astype(jnp.float32)).astype(jnp.bfloat16)
    return first, second, third


def density_body(order, where, *refs):
    pieces = refs[:PIECES]
    (tiles, table, weights, xc, rho, sent, pacc, block_out, held, dmat, tbuf, psem, dsem, tsem) = (
        refs[PIECES:]
    )
    for b in range(2):
        for t in range(16):
            pltpu.make_async_copy(
                tiles.at[where[b * 16 + t]],
                dmat.at[b, pl.ds((t // 4) * BLK, BLK), pl.ds((t % 4) * BLK, BLK)],
                dsem.at[b],
            ).start()
    load_pieces(pieces, held, psem)
    pltpu.make_async_copy(table.at[order[0]], tbuf.at[0], tsem.at[0]).start()
    pacc[...] = jnp.zeros_like(pacc)
    block_out[...] = jnp.zeros_like(block_out)
    for b in range(2):
        pltpu.make_async_copy(dmat.at[b], dmat.at[b], dsem.at[b]).wait()

    def step(i, top):
        slot = lax.rem(i, 2)

        @pl.when(i + 1 < PIECES)
        def _():
            pltpu.make_async_copy(
                table.at[order[i + 1]], tbuf.at[1 - slot], tsem.at[1 - slot]
            ).start()

        pi = order[i]
        b = pi // 4
        pltpu.make_async_copy(held.at[i], held.at[i], psem.at[i]).wait()
        piece = held[i]
        total = jnp.zeros((1, HALF), jnp.float32)
        for block in range(NB):
            rows = pl.ds(block * BLK, BLK)
            mixed = jnp.dot(dmat[b, rows, :], piece, preferred_element_type=jnp.float32)
            total = total + jnp.sum(
                mixed * held[i, rows, :].astype(jnp.float32), axis=0, keepdims=True
            )
        rho[pi] = total
        weighted = weights[pi] * total
        pltpu.make_async_copy(table.at[pi], tbuf.at[slot], tsem.at[slot]).wait()
        for block in range(8):
            rows = pl.ds(block * 128, 128)
            part = pacc[b, rows, :]
            for lane in range(HALF // 128):
                cols = slice(lane * 128, (lane + 1) * 128)
                part = part + tbuf[slot, rows, cols] * weighted[:, cols]
            pacc[b, rows, :] = part
        return jnp.maximum(top, jnp.abs(xc[pi] * total))

    top = lax.fori_loop(0, PIECES, step, jnp.zeros((1, HALF), jnp.float32))
    ones = jnp.ones((8, 128), jnp.bfloat16)
    for b in range(2):
        total = jnp.zeros((8, NB * BLK), jnp.float32)
        for term in split3(pacc[b]):
            total = total + lax.dot_general(
                ones, term, (((1,), (1,)), ((), ())), preferred_element_type=jnp.float32
            )
        for r in range(8):
            block_out[pl.ds(b * 8 + r, 1), :] = total[0:1, r * 128 : (r + 1) * 128]
    block_out[pl.ds(16, 1), :] = jnp.broadcast_to(jnp.max(top, axis=1, keepdims=True), (1, 128))
    for dest in range(32):
        sent[dest] = block_out[...]


def potential_body(table, got, even, odd, weights, xc, rho, coeffs, pot, scale, bound, *scratch):
    tbuf, column, tsem = scratch
    for i in range(2):
        pltpu.make_async_copy(table.at[i], tbuf.at[i], tsem.at[i]).start()
    first = jnp.zeros((even.shape[0], 128), jnp.float32)
    second = jnp.zeros((even.shape[0], 128), jnp.float32)
    for term in split3(got[...]):
        first = first + jnp.dot(even[...], term, preferred_element_type=jnp.float32)
        second = second + jnp.dot(odd[...], term, preferred_element_type=jnp.float32)
    summed = first[:, :64] + second[:, 64:]
    natoms = coeffs.shape[0]
    coeffs[...] = summed[:natoms]
    turned = summed[natoms:].T
    for k in range(32):
        column[pl.ds(k * 64, 64), :] = jnp.broadcast_to(turned[:, k : k + 1], (64, 128))
    top = jnp.zeros((1, 128), jnp.float32)
    for k in range(32):
        top = jnp.maximum(top, got[pl.ds(k * PAY_ROWS + 16, 1), :])
    heavy = jnp.max(jnp.sum(jnp.abs(summed[:natoms]), axis=1, keepdims=True), axis=0, keepdims=True)
    bound[...] = top + jnp.broadcast_to(heavy, (1, 128)) * (KERNEL_MAX * 16)

    def step(i, _):
        slot = lax.rem(i, 3)

        @pl.when(i + 2 < PIECES)
        def _():
            ahead = lax.rem(i + 2, 3)
            pltpu.make_async_copy(table.at[i + 2], tbuf.at[ahead], tsem.at[ahead]).start()

        base = (i // 4) * 1024
        pltpu.make_async_copy(table.at[i], tbuf.at[slot], tsem.at[slot]).wait()
        parts = [jnp.zeros((8, 128), jnp.float32) for _ in range(HALF // 128)]
        for block in range(16):
            factor = column[pl.ds(base + block * 64, 64), :]
            for lane in range(HALF // 128):
                prod = tbuf[slot, block * 64 : (block + 1) * 64, lane * 128 : (lane + 1) * 128]
                parts[lane] = parts[lane] + jnp.sum((prod * factor).reshape(8, 8, 128), axis=0)
        hartree = jnp.concatenate([jnp.sum(p, axis=0, keepdims=True) for p in parts], axis=1)
        potential = hartree + xc[i] * rho[i]
        pot[i] = potential
        scale[i] = weights[i] * potential
        return 0

    lax.fori_loop(0, PIECES, step, 0)


def ham_body(order, listed, slots, starts, *refs):
    pieces = refs[: 2 * PIECES]
    scale_mine, scale_beside, out, held, dense, rows_of, psem, osem = refs[2 * PIECES :]
    for i in range(2 * PIECES):
        pi = order[i % PIECES]
        pltpu.make_async_copy(
            pieces[i],
            held.at[i // PIECES, pi // 4, :, pl.ds(pl.multiple_of((pi % 4) * HALF, HALF), HALF)],
            psem,
        ).start()
    for b in range(2):
        rows_of[0, b] = scale_mine[b]
        rows_of[1, b] = scale_beside[b]

    def clear(s, _):
        dense[s] = jnp.zeros((BLK, BLK), jnp.float32)
        return 0

    lax.fori_loop(0, dense.shape[0], clear, 0)
    pltpu.make_async_copy(held, held, psem).wait()

    def product(n, flag):
        code = listed[n]
        side, tile = code // 32, code % 32
        b, row, col = tile // 16, (tile // 4) % 4, tile % 4
        left = held[side, b, pl.ds(pl.multiple_of(row * BLK, BLK), BLK), :]
        right = held[side, b, pl.ds(pl.multiple_of(col * BLK, BLK), BLK), :]
        right = (right.astype(jnp.float32) * (rows_of[side, b] * flag)).astype(jnp.bfloat16)
        return lax.dot_general(
            left, right, (((1,), (1,)), ((), ())), preferred_element_type=jnp.float32
        )

    for quarter in range(4):
        begin, end = starts[quarter], starts[quarter + 1]

        def pair(k, _):
            n = begin + 2 * k
            other = jnp.minimum(n + 1, end - 1)
            one = product(n, 1.0)
            two = product(other, jnp.where(n + 1 < end, 1.0, 0.0).astype(jnp.float32))
            dense[slots[n]] += one
            dense[slots[other]] += two
            return 0

        lax.fori_loop(0, (end - begin + 1) // 2, pair, 0)
        part = pl.ds(quarter * 16, 16)
        pltpu.make_async_copy(dense.at[part], out.at[part], osem.at[quarter]).start()
    for quarter in range(4):
        part = pl.ds(quarter * 16, 16)
        pltpu.make_async_copy(dense.at[part], out.at[part], osem.at[quarter]).wait()


def any_spec():
    return pl.BlockSpec(memory_space=pl.ANY)


def vmem_spec():
    return pl.BlockSpec(memory_space=pltpu.VMEM)


def smem_spec():
    return pl.BlockSpec(memory_space=pltpu.SMEM)


def density_call(order, where, pieces, tiles, table, weights, xc):
    nbasis = NB * BLK
    return pl.pallas_call(
        density_body,
        out_shape=(
            jax.ShapeDtypeStruct((PIECES, 1, HALF), jnp.float32),
            jax.ShapeDtypeStruct((32, PAY_ROWS, 128), jnp.float32),
        ),
        in_specs=[smem_spec(), smem_spec()] + [any_spec()] * (PIECES + 2) + [vmem_spec()] * 2,
        out_specs=(vmem_spec(), vmem_spec()),
        scratch_shapes=[
            pltpu.VMEM((2, nbasis, 128), jnp.float32),
            pltpu.VMEM((PAY_ROWS, 128), jnp.float32),
            pltpu.VMEM((PIECES, nbasis, HALF), jnp.bfloat16),
            pltpu.VMEM((2, nbasis, nbasis), jnp.bfloat16),
            pltpu.VMEM((2, nbasis, HALF), jnp.float32),
            pltpu.SemaphoreType.DMA((PIECES,)),
            pltpu.SemaphoreType.DMA((2,)),
            pltpu.SemaphoreType.DMA((2,)),
        ],
        compiler_params=pltpu.CompilerParams(vmem_limit_bytes=36 << 20),
        cost_estimate=pl.CostEstimate(
            flops=2 * 4096 * 1024 * 1024, bytes_accessed=32 << 20, transcendentals=0
        ),
        name="density",
    )(order, where, *pieces, tiles, table, weights, xc)


def potential_call(table, got, even, odd, weights, xc, rho, natoms):
    row = jax.ShapeDtypeStruct((PIECES, 1, HALF), jnp.float32)
    return pl.pallas_call(
        potential_body,
        out_shape=(
            jax.ShapeDtypeStruct((natoms, 64), jnp.float32),
            row,
            row,
            jax.ShapeDtypeStruct((1, 128), jnp.float32),
        ),
        in_specs=[any_spec()] + [vmem_spec()] * 6,
        out_specs=(vmem_spec(),) * 4,
        scratch_shapes=[
            pltpu.VMEM((3, NB * BLK, HALF), jnp.float32),
            pltpu.VMEM((2048, 128), jnp.float32),
            pltpu.SemaphoreType.DMA((3,)),
        ],
        compiler_params=pltpu.CompilerParams(vmem_limit_bytes=16 << 20),
        cost_estimate=pl.CostEstimate(
            flops=16 << 20, bytes_accessed=16 << 20, transcendentals=0
        ),
        name="potential",
    )(table, got, even, odd, weights, xc, rho)


def ham_call(order, listed, slots, starts, pieces, scale_mine, scale_beside):
    nbasis = NB * BLK
    return pl.pallas_call(
        ham_body,
        out_shape=jax.ShapeDtypeStruct((64, BLK, BLK), jnp.float32),
        in_specs=[smem_spec()] * 4 + [any_spec()] * (2 * PIECES) + [vmem_spec()] * 2,
        out_specs=any_spec(),
        scratch_shapes=[
            pltpu.VMEM((2, 2, nbasis, 4 * HALF), jnp.bfloat16),
            pltpu.VMEM((64, BLK, BLK), jnp.float32),
            pltpu.VMEM((2, 2, 1, 4 * HALF), jnp.float32),
            pltpu.SemaphoreType.DMA,
            pltpu.SemaphoreType.DMA((4,)),
        ],
        compiler_params=pltpu.CompilerParams(vmem_limit_bytes=40 << 20),
        cost_estimate=pl.CostEstimate(
            flops=2 * 4096 * 1024 * 1024, bytes_accessed=32 << 20, transcendentals=0
        ),
        name="ham",
    )(order, listed, slots, starts, *pieces, scale_mine, scale_beside)


def cast(x):
    return x.astype(jnp.float16)


def wide(x):
    return x.astype(jnp.float32)


def ring_sum(parts, axis_name, send_up, send_down):
    half = parts[2].shape[0] // 2
    from_below = lax.ppermute(cast(parts[2][:half]), axis_name, send_up)
    from_above = lax.ppermute(cast(parts[2][half:]), axis_name, send_down)
    up = jnp.concatenate([cast(parts[1][:half] + wide(from_below)), cast(parts[1][half:])])
    down = jnp.concatenate([cast(parts[3][:half]), cast(parts[3][half:] + wide(from_above))])
    got_below = lax.ppermute(up, axis_name, send_up)
    got_above = lax.ppermute(down, axis_name, send_down)
    return parts[0] + wide(got_below) + wide(got_above)


def direct_sum(parts, axis_name, perms):
    total = parts[0]
    got = [lax.ppermute(cast(parts[d]), axis_name, perms[d]) for d in (2, 1, 3)]
    for g in got:
        total = total + wide(g)
    return total


def per_device(
    basis_values,
    point_coords,
    point_weights,
    xc_kernel,
    gauss_widths,
    atom_coords,
    resp_density,
    tile_list,
    tile_home,
    atom_list,
    atom_home,
):
    groups = lax.axis_size("grid")
    me = lax.axis_index("grid")
    plane = lax.axis_index("pert")
    my_z, my_x, my_c = me // 8, (me // 2) % 4, me % 2
    tile_dev = resp_density.shape[1]
    neighbors = atom_list.shape[1]
    moments = gauss_widths.shape[0]
    natoms = atom_home.shape[0]
    ntiles = tile_home.shape[0]
    slots_here = 2 * neighbors

    own = [basis_values[:HALF].T, basis_values[HALF:].T]
    below0 = lax.ppermute(own[0], "pert", ring(1))
    above1 = lax.ppermute(own[1], "pert", ring(3))
    below1 = lax.ppermute(own[1], "pert", ring(1))
    above0 = lax.ppermute(own[0], "pert", ring(3))
    far0 = lax.ppermute(below0, "pert", ring(1))
    far1 = lax.ppermute(above1, "pert", ring(3))
    pieces = [own[0], own[1], below0, below1, above0, above1, far0, far1]
    beside = [lax.ppermute(piece, "grid", grid_perm(0, 0, 1)) for piece in pieces]
    steps = jnp.array([0, 0, 3, 3, 1, 1, 2, 2], jnp.int32)
    halves = jnp.array([0, 1] * 4, jnp.int32)
    order = ((plane + steps) % 4) * 2 + halves

    tiles = lax.all_gather(resp_density[0], "grid", axis=0, tiled=True)
    wanted = tile_list.reshape(-1)
    tile_match = wanted[:, None] == jnp.arange(ntiles, dtype=jnp.int32)[None, :]
    homes = jnp.sum(jnp.where(tile_match, tile_home[None, :], 0), axis=1)
    homes_beside = lax.ppermute(homes, "grid", grid_perm(0, 0, 1))

    every_home = jnp.concatenate([homes, homes_beside])
    owner, place = every_home // tile_dev, every_home % tile_dev
    off_z = (owner // 8 - my_z) % 4
    off_x = ((owner // 2) % 4 - my_x) % 4
    slot = (off_z * 4 + off_x) * tile_dev + place
    count = 2 * slots_here
    ids = jnp.arange(count, dtype=jnp.int32)
    valid = owner % 2 == my_c
    key = jnp.where(valid, slot, 64) * count + ids
    rank = jnp.sum((key[None, :] < key[:, None]).astype(jnp.int32), axis=1)
    ranked = rank[None, :] == ids[:, None]
    listed = jnp.sum(jnp.where(ranked, ids[None, :], 0), axis=1)
    slots = jnp.sum(jnp.where(ranked & valid[None, :], slot[None, :], 0), axis=1)
    edges = jnp.arange(8, dtype=jnp.int32) * 16
    starts = jnp.sum((valid[None, :] & (slot[None, :] < edges[:, None])).astype(jnp.int32), axis=1)

    atom_match = atom_list[:, :, None] == jnp.arange(natoms, dtype=jnp.int32)
    atom_pos = jnp.sum(jnp.where(atom_match[None], atom_coords[:, None, None, :], 0.0), axis=3)
    atom_homes = jnp.sum(jnp.where(atom_match, atom_home, 0), axis=2).reshape(-1)
    delta = point_coords.reshape(3, 2, 4, 1, HALF) - atom_pos[:, :, None, :, None]
    dist_sq = (jnp.sum(delta * delta, axis=0) + SOFTEN).reshape(PIECES, neighbors, 1, HALF)
    spread = (2.0 * gauss_widths * gauss_widths)[None, None, :, None]
    erf_scale = (ROOT_TWO * gauss_widths)[None, None, :, None]
    gauss = jnp.exp(-dist_sq / spread).reshape(PIECES, neighbors * moments, HALF)
    distance = jnp.sqrt(dist_sq)
    hart = (lax.erf(distance / erf_scale) / distance).reshape(PIECES, neighbors * moments, HALF)
    weights = point_weights.reshape(PIECES, 1, HALF)
    xc = xc_kernel.reshape(PIECES, 1, HALF)

    row = jnp.pad(atom_homes.astype(jnp.float32), (0, 128 - slots_here))
    home_rows = lax.all_to_all(
        jnp.broadcast_to(row[None, None], (groups, 8, 128)), "grid", 0, 0, tiled=True
    )[:, 0, :slots_here]
    wanted_rows = jnp.concatenate(
        [jnp.arange(natoms, dtype=jnp.float32), atom_homes.astype(jnp.float32)]
    )

    def chooser(which):
        held = jnp.pad(
            home_rows.reshape(groups, slots_here // 2, 2)[:, :, which],
            ((0, 0), (0, PAY_ROWS - slots_here // 2)),
            constant_values=-1.0,
        ).reshape(-1)
        return (wanted_rows[:, None] == held[None, :]).astype(jnp.bfloat16)

    even, odd = chooser(0), chooser(1)
    gauss, hart, even, odd, listed, slots, starts = lax.optimization_barrier(
        (gauss, hart, even, odd, listed, slots, starts)
    )

    rho, sent = density_call(order, homes, pieces, tiles, gauss, weights, xc)
    got = lax.all_to_all(sent, "grid", split_axis=0, concat_axis=0, tiled=True)
    all_coeffs, pot, scale, bound = potential_call(
        hart, got.reshape(groups * PAY_ROWS, 128), even, odd, weights, xc, rho, natoms
    )
    atom_dev = natoms // groups
    own_coeffs = lax.dynamic_slice_in_dim(all_coeffs, me * atom_dev, atom_dev, axis=0)
    ham_bound = PHI_MAX_SQ * 2048 * 0.05 * groups * bound[0, 0] * 1.01 + 1e-20

    scale_beside = lax.ppermute(scale, "grid", grid_perm(0, 0, 1))
    dense = ham_call(
        order,
        listed,
        slots,
        starts,
        pieces + beside,
        scale.reshape(2, 1, 4 * HALF),
        scale_beside.reshape(2, 1, 4 * HALF),
    )

    dense = dense.reshape(4, 4, tile_dev, BLK, BLK)
    factor = F16_TOP / ham_bound
    z_up, z_down = grid_perm(1, 0, 0), grid_perm(-1, 0, 0)
    x_up, x_down = grid_perm(0, 1, 0), grid_perm(0, -1, 0)
    half = BLK // 2
    upper = ring_sum([dense[d, :, :, :half] * factor for d in range(4)], "grid", z_up, z_down)
    lower = ring_sum([dense[:, d, :, half:] * factor for d in range(4)], "grid", x_up, x_down)
    z_perms = {d: grid_perm(d, 0, 0) for d in range(1, 4)}
    x_perms = {d: grid_perm(0, d, 0) for d in range(1, 4)}
    upper = direct_sum([upper[d] for d in range(4)], "grid", x_perms)
    lower = direct_sum([lower[d] for d in range(4)], "grid", z_perms)
    hamiltonian = jnp.concatenate([upper, lower], axis=1) * (ham_bound / F16_TOP)
    return (hamiltonian[None], own_coeffs[None], pot.reshape(1, -1))


def solution(mesh):
    placed = (
        P(("grid", "pert"), None),
        P(None, "grid"),
        P("grid"),
        P("grid"),
        P(),
        P(),
        P("pert", "grid", None, None),
        P("grid", None),
        P(),
        P("grid", None),
        P(),
    )
    return jax.shard_map(
        per_device,
        mesh=mesh,
        in_specs=placed,
        out_specs=(P("pert", "grid", None, None), P("pert", "grid", None), P("pert", "grid")),
        check_vma=False,
    )
```

time: 290 us -> 242 us (0.83)
  local copies, waits for them, and re-layouts: 41.2 us -> 10.3 us
  waiting for transfers between devices: 96.9 us -> 73.4 us
  blocking collectives: 0 us -> 18.4 us
  other arithmetic: 52.9 us -> 39.8 us
  Pallas kernels: 35.6 us -> 39.5 us
    convert_element_type x6 -> x9, other arithmetic: 22.4 us -> 2.26 us  [the longest x8 1.13 us: cast(): return x.astype(jnp.float16)]
    all_to_all x0 -> x1, blocking collectives: none -> 18.4 us  [per_device(): got = lax.all_to_all(sent, 'grid', split_axis=0, concat_axis=0, tiled=True)]
    gather x2 -> x0, local copies, waits for them, and re-layouts: 17.9 us -> none  [placed(): jnp.take(tiles_of, index, axis=0)]
    ppermute x1, waiting for transfers between devices: 19.4 us -> 1.9 us  [per_device(): far0 = lax.ppermute(below0, 'pert', ring(1))]
    ppermute x1, waiting for transfers between devices: 18.7 us -> 31.8 us  [per_device(): below0 = lax.ppermute(own[0], 'pert', ring(1))]
    ppermute x4 -> x2, starting transfers between devices: 12.7 us -> 1.87 us  [ring_sum(): got_above = lax.ppermute(down, axis_name, send_down)]
    unnamed x38 -> x49, local copies, waits for them, and re-layouts: 11.6 us -> 2.36 us
    ppermute x9 -> x19, starting transfers between devices: 13.3 us -> 21.9 us  [the longest x6 11.5 us: direct_sum(): got = [lax.ppermute(cast(parts[d]), axis_name, perms[d]) for d in (2, 1, 3)]]
  transfers between devices with their start and end apart: 26 -> 32, of which waited for: 17 -> 12; matrix products, arithmetic and copies ran while one was open for 13% -> 15% of each run, Pallas kernels for 0% -> 9%
where the time goes in v2:
time: 242 us; the launch traced here: 241 us
  waiting for transfers between devices  73.4 us (30%)
  starting transfers between devices  45.2 us (19%)
  other arithmetic  39.8 us (16%)
  Pallas kernels  39.5 us (16%)
  blocking collectives  18.4 us (8%)
  between operations  14.7 us (6%)
  local copies, waits for them, and re-layouts  10.3 us (4%)
    ppermute x1, waiting for transfers between devices, per_device(): below0 = lax.ppermute(own[0], 'pert', ring(1))  31.8 us
    ppermute x2, waiting for transfers between devices, ring_sum(): got_below = lax.ppermute(up, axis_name, send_up)  20.7 us
    pallas_call x1, Pallas kernels, ham_call(): pl.pallas_call(ham_body, out_shape=jax.ShapeDtypeStruct((64, BLK, BLK), j...  18.7 us
    all_to_all x1, blocking collectives, per_device(): got = lax.all_to_all(sent, 'grid', split_axis=0, concat_axis=0, tiled=True)  18.4 us
    pallas_call x1, Pallas kernels, density_call(): pl.pallas_call(density_body, out_shape=(jax.ShapeDtypeStruct((PIECES, 1,...  16.3 us
    ppermute x6, starting transfers between devices, direct_sum(): got = [lax.ppermute(cast(parts[d]), axis_name, perms[d]) for d in (2, 1, 3)]  11.5 us
    exp x1, other arithmetic, per_device(): jnp.exp(-dist_sq / spread).reshape(PIECES, neighbors * moments, HALF)  8.34 us
    all_to_all x1, starting transfers between devices, per_device(): lax.all_to_all(jnp.broadcast_to(row[None, None], (groups, 8, 128)), 'grid...  8.25 us
  transfers between devices with their start and end apart: 32, of which 12 were waited for; matrix products, arithmetic and copies ran while one was open for 15% of the time, Pallas kernels for 9%

profile of v2, /device:TPU:0, one launch (start us, length us, event | category | flops | bytes accessed | tf_op | source)
XLA Modules:
  0.0 241.3 jit_solution(13700160027637470627)
XLA Ops:
  7.2 0.7 all-gather.3.cloned.1.call-update
  7.9 2.7 %fusion.51 = (bf16[512,1024]{1,0:T(8,128)(2,1)S(1)}, bf16[512,1024]{1,0:T(8,128)(2,1)}) fusion(bf16[1024,1024]{1,0:T(8,128)(2,1)} %param.13), kind=kLoop, calls=%fused_computation.130 | loop fusion | bytes 4194304 | tf_op jit(solution)/shard_map/slice | solution.py:351
  11.2 3.2 %collective-permute-start.4 = (bf16[1024,512]{1,0:T(8,128)(2,1)S(1)}, bf16[1024,512]{1,0:T(8,128)(2,1)S(1)}, u32[]{:S(2)}, u32[]{:S(2)}) collective-permute-start(bf16[1024,512]{1,0:T(8,128)(2,1)S(1)} %bitcast.147), channel_id=1, source_target_pairs={{0,3},{1,0},{2,1},{3,2},{4,7},{5,4},{6,5},{7,6},{8,11},{9,8},{10,9... | collective-permute-start | bytes 3145736 | tf_op jit(solution)/shard_map/ppermute | solution.py:353
  14.4 1.5 copy.51
  16.6 2.7 %collective-permute-start.3 = (bf16[1024,512]{1,0:T(8,128)(2,1)S(1)}, bf16[1024,512]{1,0:T(8,128)(2,1)}, u32[]{:S(2)}, u32[]{:S(2)}) collective-permute-start(bf16[1024,512]{1,0:T(8,128)(2,1)S(1)} %bitcast.153), channel_id=1, source_target_pairs={{0,3},{1,0},{2,1},{3,2},{4,7},{5,4},{6,5},{7,6},{8,11},{9,8},{10,9... | collective-permute-start | bytes 3145736 | tf_op jit(solution)/shard_map/ppermute | solution.py:355
  20.6 8.2 %all-to-all-start = ((f32[32,8,128]{2,1,0:T(8,128)}), f32[32,8,128]{2,1,0:T(8,128)S(1)}, u32[]{:S(2)}, u32[]{:S(2)}) async-start(f32[32,8,128]{2,1,0:T(8,128)} %broadcast_in_dim.98), calls=%async_computation | async-start | bytes 262144 | tf_op jit(solution)/shard_map/all_to_all | solution.py:400
  29.8 0.8 add_sqrt_fusion
  31.0 31.8 %collective-permute-done.1.refs_2_ = bf16[1024,512]{1,0:T(8,128)(2,1)} collective-permute-done((bf16[1024,512]{1,0:T(8,128)(2,1)S(1)}, bf16[1024,512]{1,0:T(8,128)(2,1)}, u32[]{:S(2)}, u32[]{:S(2)}) %collective-permute-start.1) | collective-permute-done | bytes 1048608 | tf_op jit(solution)/shard_map/ppermute | solution.py:352
  63.4 1.7 collective-permute-start.5
  66.3 0.7 div.110
  67.6 0.7 div.104
  68.3 8.2 %bitcast_divide_fusion.table = f32[8,1024,512]{2,1,0:T(8,128)} fusion(f32[1024]{0:T(1024)} %div.110, f32[8,16,512]{2,1,0:T(8,128)S(1)} %bitcast.170), kind=kLoop, calls=%fused_computation | loop fusion | flops 8388608 | bytes 17043456 | tf_op jit(solution)/shard_map/div | solution.py:395
  76.5 8.3 %fusion.refs_9_ = f32[8,1024,512]{2,1,0:T(8,128)} fusion(f32[1024]{0:T(1024)S(1)} %copy-done.6, f32[8,16,512]{2,1,0:T(8,128)S(1)} %bitcast.169), kind=kLoop, calls=%fused_computation.3 | loop fusion | flops 4194304 | bytes 17043456 | tf_op jit(solution)/shard_map/exp | solution.py:393
  84.9 0.7 iota_add_fusion
  86.6 1.1 compare_convert_fusion
  88.2 1.9 collective-permute-done.5.refs_6_
  90.8 16.3 %density.1 = (f32[8,1,512]{2,1,0:T(1,128)S(1)}, f32[32,24,128]{2,1,0:T(8,128)S(1)}) custom-call(s32[8]{0:T(128)S(1)} %fusion.38.order, s32[32]{0:T(128)S(1)} %select_reduce_fusion.4.where, bf16[1024,512]{1,0:T(8,128)(2,1)S(1)} %bitcast.155, bf16[1024,512]{1,0:T(8,128)(2,1)S(1)} %bitcast.150, bf16[1024,512]{1,0:T(8,128)(2,1)} %collective-permute-done.1.refs_2_, ...), custom_call_target="tpu_custom_call" | custom-call | flops 8589934592 | bytes 33554432 | tf_op jit(solution)/shard_map/density/pallas_call | solution.py:227
  107.1 18.4 %all_to_all.10 = f32[32,24,128]{2,1,0:T(8,128)S(1)} all-to-all(f32[32,24,128]{2,1,0:T(8,128)S(1)} %get-tuple-element.21), channel_id=1, replica_groups=mesh['grid'=32,'pert'=4] {'grid'}, dimensions={0} | all-to-all | bytes 786432 | tf_op jit(solution)/shard_map/all_to_all | solution.py:421
  125.5 4.6 %potential.1 = (f32[256,64]{1,0:T(8,128)S(1)}, f32[8,1,512]{2,1,0:T(1,128)}, f32[8,1,512]{2,1,0:T(1,128)S(1)}, f32[1,128]{1,0:T(1,128)S(1)}) custom-call(f32[8,1024,512]{2,1,0:T(8,128)S(1)} %bitcast.146, f32[768,128]{1,0:T(8,128)S(1)} %bitcast.157, bf16[288,768]{1,0:T(8,128)(2,1)S(1)} %copy-done.1, bf16[288,768]{1,0:T(8,128)(2,1)S(1)} %copy-done, ...), custom_call_target="tpu_custom_call" | custom-call | flops 16777216 | bytes 16777216 | tf_op jit(solution)/shard_map/potential/pallas_call | solution.py:255
  130.5 0.8 collective-permute-done.15
  131.4 18.7 %ham.1 = f32[64,256,256]{2,1,0:T(8,128)} custom-call(s32[8]{0:T(128)S(1)} %fusion.38.order, s32[64]{0:T(128)S(1)} %get-tuple-element.16.listed, s32[64]{0:T(128)S(1)} %get-tuple-element.17.slots, s32[8]{0:T(128)S(1)} %convert_reduce_fusion.1.starts, bf16[1024,512]{1,0:T(8,128)(2,1)S(1)} %bitcast.156, bf16[1024,512]{1,0:T(8,128)(2,1)S(1)} %bitcast.151, ...), custom_call_target="tpu_custom_call" | custom-call | flops 8589934592 | bytes 33554432 | tf_op jit(solution)/shard_map/ham/pallas_call | solution.py:280
  150.0 3.6 %fusion.4 = (f32[4,1,4,128,256]{4,3,2,0,1:T(8,128)S(1)}, f16[4,1,4,128,256]{4,3,2,0,1:T(8,128)(2,1)S(1)}, f32[4,1,4,128,256]{4,3,2,0,1:T(8,128)S(1)}) fusion(f32[4,4,4,256,256]{4,3,2,1,0:T(8,128)} %bitcast.165, f32[]{:T(128)} %bitcast.17), kind=kLoop, calls=%fused_computation.10 | loop fusion | flops 2097152 | bytes 11534340 | tf_op jit(solution)/shard_map/mul | solution.py:446
  153.6 3.6 %slice_multiply_fusion.2 = (f32[1,4,4,128,256]{4,3,2,1,0:T(8,128)S(1)}, f32[1,4,4,128,256]{4,3,2,1,0:T(8,128)S(1)}, f16[1,4,4,128,256]{4,3,2,1,0:T(8,128)(2,1)S(1)}) fusion(f32[4,4,4,256,256]{4,3,2,1,0:T(8,128)} %bitcast.166, f32[]{:T(128)} %bitcast.17), kind=kLoop, calls=%fused_computation.19 | loop fusion | flops 2097152 | bytes 11534340 | tf_op jit(solution)/shard_map/mul | solution.py:445
  157.6 3.1 %collective-permute-start.23 = (f16[2,4,128,256]{3,2,1,0:T(8,128)(2,1)S(1)}, f16[2,4,128,256]{3,2,1,0:T(8,128)(2,1)S(1)}, u32[]{:S(2)}, u32[]{:S(2)}) collective-permute-start(f16[2,4,128,256]{3,2,1,0:T(8,128)(2,1)S(1)} %get-tuple-element.56), channel_id=1, source_target_pairs={{0,8},{4,12},{8,16},{12,20},{16,24},{20,28},{24,0},{28,4},{32,40},... | collective-permute-start | bytes 1572872 | tf_op jit(solution)/shard_map/ppermute | solution.py:310
  160.8 1.6 collective-permute-start.25
  162.7 1.6 collective-permute-start.16
  164.3 1.7 collective-permute-start.18
  166.2 6.9 %collective-permute-done.23 = f16[2,4,128,256]{3,2,1,0:T(8,128)(2,1)S(1)} collective-permute-done((f16[2,4,128,256]{3,2,1,0:T(8,128)(2,1)S(1)}, f16[2,4,128,256]{3,2,1,0:T(8,128)(2,1)S(1)}, u32[]{:S(2)}, u32[]{:S(2)}) %collective-permute-start.23) | collective-permute-done | bytes 524320 | tf_op jit(solution)/shard_map/ppermute | solution.py:310
  173.3 1.3 pad_maximum_fusion.2
  174.6 2.0 collective-permute-start.24
  176.8 1.3 pad_maximum_fusion.3
  178.1 1.2 collective-permute-start.26
  179.5 1.2 pad_maximum_fusion
  180.7 2.9 %collective-permute-start.17 = (f16[4,4,128,256]{3,2,1,0:T(8,128)(2,1)}, f16[4,4,128,256]{3,2,1,0:T(8,128)(2,1)}, u32[]{:S(2)}, u32[]{:S(2)}) collective-permute-start(f16[4,4,128,256]{3,2,1,0:T(8,128)(2,1)} %pad_maximum_fusion), channel_id=1, source_target_pairs={{0,32},{4,36},{8,40},{12,44},{16,48},{20,52},{24,56},{28,60},{32,6... | collective-permute-start | bytes 3145736 | tf_op jit(solution)/shard_map/ppermute | solution.py:314
  184.8 16.4 %collective-permute-done.24 = f16[4,4,128,256]{3,2,1,0:T(8,128)(2,1)} collective-permute-done((f16[4,4,128,256]{3,2,1,0:T(8,128)(2,1)}, f16[4,4,128,256]{3,2,1,0:T(8,128)(2,1)}, u32[]{:S(2)}, u32[]{:S(2)}) %collective-permute-start.24) | collective-permute-done | bytes 1048608 | tf_op jit(solution)/shard_map/ppermute | solution.py:314
  201.2 2.5 %collective-permute-done.26 = f16[4,4,128,256]{3,2,1,0:T(8,128)(2,1)} collective-permute-done((f16[4,4,128,256]{3,2,1,0:T(8,128)(2,1)}, f16[4,4,128,256]{3,2,1,0:T(8,128)(2,1)}, u32[]{:S(2)}, u32[]{:S(2)}) %collective-permute-start.26) | collective-permute-done | bytes 1048608 | tf_op jit(solution)/shard_map/ppermute | solution.py:315
  203.7 4.2 %collective-permute-done.17 = f16[4,4,128,256]{3,2,1,0:T(8,128)(2,1)} collective-permute-done((f16[4,4,128,256]{3,2,1,0:T(8,128)(2,1)}, f16[4,4,128,256]{3,2,1,0:T(8,128)(2,1)}, u32[]{:S(2)}, u32[]{:S(2)}) %collective-permute-start.17) | collective-permute-done | bytes 1048608 | tf_op jit(solution)/shard_map/ppermute | solution.py:314
  208.4 4.7 %fusion.45 = (f16[4,4,128,256]{3,2,1,0:T(8,128)(2,1)S(1)}, f32[4,4,128,256]{3,2,1,0:T(8,128)S(1)}, f16[4,4,128,256]{3,2,1,0:T(8,128)(2,1)S(1)}, f32[4,4,128,256]{3,2,1,0:T(8,128)S(1)}) fusion(f16[4,4,128,256]{3,2,1,0:T(8,128)(2,1)} %collective-permute-done.19, f16[4,4,128,256]{3,2,1,0:T(8,128)(2,1)} %collective-permute-done.17, f32[]{:T(128)} %bitcast.17, ...), kind=kLoop, calls=%fused_computation.128 | loop fusion | flops 6291456 | bytes 14681088 | tf_op jit(solution)/shard_map/convert.9
  213.7 1.2 collective-permute-start.21
  214.8 2.1 collective-permute-start.22
  217.7 2.2 collective-permute-start.27
  219.9 2.1 collective-permute-start.28
  222.0 2.1 collective-permute-done.20
  224.1 3.6 %collective-permute-start.29 = (f16[4,128,256]{2,1,0:T(8,128)(2,1)S(1)}, f16[4,128,256]{2,1,0:T(8,128)(2,1)S(1)}, u32[]{:S(2)}, u32[]{:S(2)}) collective-permute-start(f16[4,128,256]{2,1,0:T(8,128)(2,1)S(1)} %get-tuple-element.54), channel_id=1, source_target_pairs={{0,96},{4,100},{8,104},{12,108},{16,112},{20,116},{24,120},{28,124... | collective-permute-start | bytes 786440 | tf_op jit(solution)/shard_map/ppermute | solution.py:321
  227.7 0.9 collective-permute-done.21
  228.7 3.7 %collective-permute-done.28 = f16[4,128,256]{2,1,0:T(8,128)(2,1)S(1)} collective-permute-done((f16[4,128,256]{2,1,0:T(8,128)(2,1)S(1)}, f16[4,128,256]{2,1,0:T(8,128)(2,1)S(1)}, u32[]{:S(2)}, u32[]{:S(2)}) %collective-permute-start.28) | collective-permute-done | bytes 262176 | tf_op jit(solution)/shard_map/ppermute | solution.py:321
  232.4 0.9 collective-permute-done.29
  233.4 1.1 maximum_multiply_fusion
  (129 shorter events, 13.4 us)
Async XLA Ops:
  7.2 83.5 %all-gather.3.cloned.1.call-start = ((), (), s32[]{:S(2)}) async-start(), calls=%async_computation.2 | async-start | bytes 17301504 | tf_op jit(solution)/shard_map/all_gather | solution.py:364
  10.6 9.1 %copy-start.7 = (s32[2,16]{1,0:T(2,128)S(1)}, s32[2,16]{1,0:T(2,128)}, u32[]{:S(2)}) copy-start(s32[2,16]{1,0:T(2,128)} %param.22) | copy-start | bytes 388
  10.6 9.1 %copy-start.9 = (s32[256]{0:T(256)S(1)}, s32[256]{0:T(256)}, u32[]{:S(2)}) copy-start(s32[256]{0:T(256)} %param.23) | copy-start | bytes 3076
  10.6 18.3 %copy-start.5 = (f32[3,4096]{1,0:T(4,128)S(1)}, f32[3,4096]{1,0:T(4,128)}, u32[]{:S(2)}) copy-start(f32[3,4096]{1,0:T(4,128)} %param.14) | copy-start | bytes 147460
  10.6 18.4 %copy-start.8 = (f32[3,256]{1,0:T(4,128)S(1)}, f32[3,256]{1,0:T(4,128)}, u32[]{:S(2)}) copy-start(f32[3,256]{1,0:T(4,128)} %param.18) | copy-start | bytes 9220
  10.6 18.7 %copy-start.17 = (f32[64]{0:T(128)S(1)}, f32[64]{0:T(128)}, u32[]{:S(2)}) copy-start(f32[64]{0:T(128)} %param.17) | copy-start | bytes 772
  11.2 19.4 %copy-start.13 = (s32[8]{0:T(128)S(1)}, s32[8]{0:T(128)}, u32[]{:S(2)}) copy-start(s32[8]{0:T(128)} %constant.163.clone) | copy-start | bytes 100
  11.2 19.4 %copy-start.14 = (s32[8]{0:T(128)S(1)}, s32[8]{0:T(128)}, u32[]{:S(2)}) copy-start(s32[8]{0:T(128)} %constant.164.clone) | copy-start | bytes 100
  11.2 51.6 %collective-permute-start.4 = (bf16[1024,512]{1,0:T(8,128)(2,1)S(1)}, bf16[1024,512]{1,0:T(8,128)(2,1)S(1)}, u32[]{:S(2)}, u32[]{:S(2)}) collective-permute-start(bf16[1024,512]{1,0:T(8,128)(2,1)S(1)} %bitcast.147), channel_id=1, source_target_pairs={{0,3},{1,0},{2,1},{3,2},{4,7},{5,4},{6,5},{7,6},{8,11},{9,8},{10,9... | collective-permute-start | bytes 3145736 | tf_op jit(solution)/shard_map/ppermute | solution.py:353
  14.4 48.4 %collective-permute-start.2 = (bf16[1024,512]{1,0:T(8,128)(2,1)S(1)}, bf16[1024,512]{1,0:T(8,128)(2,1)}, u32[]{:S(2)}, u32[]{:S(2)}) collective-permute-start(bf16[1024,512]{1,0:T(8,128)(2,1)S(1)} %bitcast.148), channel_id=1, source_target_pairs={{0,1},{1,2},{2,3},{3,0},{4,5},{5,6},{6,7},{7,4},{8,9},{9,10},{10,1... | collective-permute-start | bytes 3145736 | tf_op jit(solution)/shard_map/ppermute | solution.py:354
  15.9 46.9 %collective-permute-start.1 = (bf16[1024,512]{1,0:T(8,128)(2,1)S(1)}, bf16[1024,512]{1,0:T(8,128)(2,1)}, u32[]{:S(2)}, u32[]{:S(2)}) collective-permute-start(bf16[1024,512]{1,0:T(8,128)(2,1)S(1)} %bitcast.152), channel_id=1, source_target_pairs={{0,1},{1,2},{2,3},{3,0},{4,5},{5,6},{6,7},{7,4},{8,9},{9,10},{10,1... | collective-permute-start | bytes 3145736 | tf_op jit(solution)/shard_map/ppermute | solution.py:352
  16.6 46.9 %collective-permute-start.3 = (bf16[1024,512]{1,0:T(8,128)(2,1)S(1)}, bf16[1024,512]{1,0:T(8,128)(2,1)}, u32[]{:S(2)}, u32[]{:S(2)}) collective-permute-start(bf16[1024,512]{1,0:T(8,128)(2,1)S(1)} %bitcast.153), channel_id=1, source_target_pairs={{0,3},{1,0},{2,1},{3,2},{4,7},{5,4},{6,5},{7,6},{8,11},{9,8},{10,9... | collective-permute-start | bytes 3145736 | tf_op jit(solution)/shard_map/ppermute | solution.py:355
  19.6 11.0 %collective-permute-start = (s32[32]{0:T(128)S(1)}, s32[32]{0:T(128)}, u32[]{:S(2)}, u32[]{:S(2)}) collective-permute-start(s32[32]{0:T(128)S(1)} %select_reduce_fusion.4.where), channel_id=1, source_target_pairs={{0,4},{4,0},{8,12},{12,8},{16,20},{20,16},{24,28},{28,24},{32,36},... | collective-permute-start | bytes 392 | tf_op jit(solution)/shard_map/ppermute | solution.py:368
  20.6 65.5 %all-to-all-start = ((f32[32,8,128]{2,1,0:T(8,128)}), f32[32,8,128]{2,1,0:T(8,128)S(1)}, u32[]{:S(2)}, u32[]{:S(2)}) async-start(f32[32,8,128]{2,1,0:T(8,128)} %broadcast_in_dim.98), calls=%async_computation | async-start | bytes 262144 | tf_op jit(solution)/shard_map/all_to_all | solution.py:400
  30.6 57.1 %collective-permute-start.7 = (bf16[1024,512]{1,0:T(8,128)(2,1)S(1)}, bf16[1024,512]{1,0:T(8,128)(2,1)}, u32[]{:S(2)}, u32[]{:S(2)}) collective-permute-start(bf16[1024,512]{1,0:T(8,128)(2,1)S(1)} %bitcast.154), channel_id=1, source_target_pairs={{0,4},{4,0},{8,12},{12,8},{16,20},{20,16},{24,28},{28,24},{32,36},... | collective-permute-start | bytes 3145736 | tf_op jit(solution)/shard_map/ppermute | solution.py:359
  62.8 24.9 %collective-permute-start.8 = (bf16[1024,512]{1,0:T(8,128)(2,1)S(1)}, bf16[1024,512]{1,0:T(8,128)(2,1)}, u32[]{:S(2)}, u32[]{:S(2)}) collective-permute-start(bf16[1024,512]{1,0:T(8,128)(2,1)S(1)} %bitcast.149), channel_id=1, source_target_pairs={{0,4},{4,0},{8,12},{12,8},{16,20},{20,16},{24,28},{28,24},{32,36},... | collective-permute-start | bytes 3145736 | tf_op jit(solution)/shard_map/ppermute | solution.py:359
  62.8 27.3 %collective-permute-start.6 = (bf16[1024,512]{1,0:T(8,128)(2,1)S(1)}, bf16[1024,512]{1,0:T(8,128)(2,1)}, u32[]{:S(2)}, u32[]{:S(2)}) collective-permute-start(bf16[1024,512]{1,0:T(8,128)(2,1)S(1)} %collective-permute-done.4.refs_5_), channel_id=1, source_target_pairs={{0,3},{1,0},{2,1},{3,2},{4,7},{5,4},{6,5},{7,6},{8,11},{9,8},{10,9... | collective-permute-start | bytes 3145736 | tf_op jit(solution)/shard_map/ppermute | solution.py:357
  62.8 27.8 %collective-permute-start.12 = (bf16[1024,512]{1,0:T(8,128)(2,1)S(1)}, bf16[1024,512]{1,0:T(8,128)(2,1)}, u32[]{:S(2)}, u32[]{:S(2)}) collective-permute-start(bf16[1024,512]{1,0:T(8,128)(2,1)S(1)} %collective-permute-done.4.refs_5_), channel_id=1, source_target_pairs={{0,4},{4,0},{8,12},{12,8},{16,20},{20,16},{24,28},{28,24},{32,36},... | collective-permute-start | bytes 3145736 | tf_op jit(solution)/shard_map/ppermute | solution.py:359
  63.4 26.7 %collective-permute-start.5 = (bf16[1024,512]{1,0:T(8,128)(2,1)}, bf16[1024,512]{1,0:T(8,128)(2,1)}, u32[]{:S(2)}, u32[]{:S(2)}) collective-permute-start(bf16[1024,512]{1,0:T(8,128)(2,1)} %collective-permute-done.1.refs_2_), channel_id=1, source_target_pairs={{0,1},{1,2},{2,3},{3,0},{4,5},{5,6},{6,7},{7,4},{8,9},{9,10},{10,1... | collective-permute-start | bytes 3145736 | tf_op jit(solution)/shard_map/ppermute | solution.py:356
  76.5 9.4 %copy-start.12 = (s32[8]{0:T(128)S(1)}, s32[8]{0:T(128)}, u32[]{:S(2)}) copy-start(s32[8]{0:T(128)} %iota_multiply_fusion) | copy-start | bytes 100
  76.5 14.2 %copy-start.2 = (f32[4096]{0:T(1024)S(1)}, f32[4096]{0:T(1024)}, u32[]{:S(2)}) copy-start(f32[4096]{0:T(1024)} %param.15) | copy-start | bytes 49156
  76.5 14.2 %copy-start.3 = (f32[4096]{0:T(1024)S(1)}, f32[4096]{0:T(1024)}, u32[]{:S(2)}) copy-start(f32[4096]{0:T(1024)} %param.16) | copy-start | bytes 49156
  87.7 42.4 %collective-permute-start.9 = (bf16[1024,512]{1,0:T(8,128)(2,1)}, bf16[1024,512]{1,0:T(8,128)(2,1)}, u32[]{:S(2)}, u32[]{:S(2)}) collective-permute-start(bf16[1024,512]{1,0:T(8,128)(2,1)} %collective-permute-done.1.refs_2_), channel_id=1, source_target_pairs={{0,4},{4,0},{8,12},{12,8},{16,20},{20,16},{24,28},{28,24},{32,36},... | collective-permute-start | bytes 3145736 | tf_op jit(solution)/shard_map/ppermute | solution.py:359
  87.7 42.8 %collective-permute-start.10 = (bf16[1024,512]{1,0:T(8,128)(2,1)}, bf16[1024,512]{1,0:T(8,128)(2,1)}, u32[]{:S(2)}, u32[]{:S(2)}) collective-permute-start(bf16[1024,512]{1,0:T(8,128)(2,1)} %collective-permute-done.2.refs_3_), channel_id=1, source_target_pairs={{0,4},{4,0},{8,12},{12,8},{16,20},{20,16},{24,28},{28,24},{32,36},... | collective-permute-start | bytes 3145736 | tf_op jit(solution)/shard_map/ppermute | solution.py:359
  90.1 40.4 %collective-permute-start.11 = (bf16[1024,512]{1,0:T(8,128)(2,1)}, bf16[1024,512]{1,0:T(8,128)(2,1)}, u32[]{:S(2)}, u32[]{:S(2)}) collective-permute-start(bf16[1024,512]{1,0:T(8,128)(2,1)} %collective-permute-done.3.refs_4_), channel_id=1, source_target_pairs={{0,4},{4,0},{8,12},{12,8},{16,20},{20,16},{24,28},{28,24},{32,36},... | collective-permute-start | bytes 3145736 | tf_op jit(solution)/shard_map/ppermute | solution.py:359
  90.1 40.4 %collective-permute-start.13 = (bf16[1024,512]{1,0:T(8,128)(2,1)}, bf16[1024,512]{1,0:T(8,128)(2,1)}, u32[]{:S(2)}, u32[]{:S(2)}) collective-permute-start(bf16[1024,512]{1,0:T(8,128)(2,1)} %collective-permute-done.5.refs_6_), channel_id=1, source_target_pairs={{0,4},{4,0},{8,12},{12,8},{16,20},{20,16},{24,28},{28,24},{32,36},... | collective-permute-start | bytes 3145736 | tf_op jit(solution)/shard_map/ppermute | solution.py:359
  90.6 39.9 %collective-permute-start.14 = (bf16[1024,512]{1,0:T(8,128)(2,1)}, bf16[1024,512]{1,0:T(8,128)(2,1)}, u32[]{:S(2)}, u32[]{:S(2)}) collective-permute-start(bf16[1024,512]{1,0:T(8,128)(2,1)} %collective-permute-done.6.refs_7_), channel_id=1, source_target_pairs={{0,4},{4,0},{8,12},{12,8},{16,20},{20,16},{24,28},{28,24},{32,36},... | collective-permute-start | bytes 3145736 | tf_op jit(solution)/shard_map/ppermute | solution.py:359
  90.7 34.7 %slice-start = ((s8[16777216]{0:T(1024)(128)(4,1)}), s8[4194304]{0:T(1024)(128)(4,1)S(1)}, s32[]{:S(2)}) async-start(s8[16777216]{0:T(1024)(128)(4,1)} %bitcast.145), calls=%async_computation.3 | async-start | bytes 8388608
  90.7 34.7 %slice-start.1 = ((s8[16777216]{0:T(1024)(128)(4,1)}), s8[4194304]{0:T(1024)(128)(4,1)S(1)}, s32[]{:S(2)}) async-start(s8[16777216]{0:T(1024)(128)(4,1)} %bitcast.145), calls=%async_computation.4 | async-start | bytes 8388608
  90.7 34.7 %slice-start.2 = ((s8[16777216]{0:T(1024)(128)(4,1)}), s8[4194304]{0:T(1024)(128)(4,1)S(1)}, s32[]{:S(2)}) async-start(s8[16777216]{0:T(1024)(128)(4,1)} %bitcast.145), calls=%async_computation.5 | async-start | bytes 8388608
  90.7 34.7 %slice-start.3 = ((s8[16777216]{0:T(1024)(128)(4,1)}), s8[4194304]{0:T(1024)(128)(4,1)S(1)}, s32[]{:S(2)}) async-start(s8[16777216]{0:T(1024)(128)(4,1)} %bitcast.145), calls=%async_computation.6 | async-start | bytes 8388608
  90.7 34.7 %copy-start = (bf16[288,768]{1,0:T(8,128)(2,1)S(1)}, bf16[288,768]{1,0:T(8,128)(2,1)}, u32[]{:S(2)}) copy-start(bf16[288,768]{1,0:T(8,128)(2,1)} %get-tuple-element.23.odd) | copy-start | bytes 1327108
  90.8 34.7 %copy-start.1 = (bf16[288,768]{1,0:T(8,128)(2,1)S(1)}, bf16[288,768]{1,0:T(8,128)(2,1)}, u32[]{:S(2)}) copy-start(bf16[288,768]{1,0:T(8,128)(2,1)} %get-tuple-element.22.even) | copy-start | bytes 1327108
  130.1 1.3 collective-permute-start.15
  157.6 15.5 %collective-permute-start.23 = (f16[2,4,128,256]{3,2,1,0:T(8,128)(2,1)S(1)}, f16[2,4,128,256]{3,2,1,0:T(8,128)(2,1)S(1)}, u32[]{:S(2)}, u32[]{:S(2)}) collective-permute-start(f16[2,4,128,256]{3,2,1,0:T(8,128)(2,1)S(1)} %get-tuple-element.56), channel_id=1, source_target_pairs={{0,8},{4,12},{8,16},{12,20},{16,24},{20,28},{24,0},{28,4},{32,40},... | collective-permute-start | bytes 1572872 | tf_op jit(solution)/shard_map/ppermute | solution.py:310
  160.8 15.8 %collective-permute-start.25 = (f16[2,4,128,256]{3,2,1,0:T(8,128)(2,1)S(1)}, f16[2,4,128,256]{3,2,1,0:T(8,128)(2,1)S(1)}, u32[]{:S(2)}, u32[]{:S(2)}) collective-permute-start(f16[2,4,128,256]{3,2,1,0:T(8,128)(2,1)S(1)} %get-tuple-element.57), channel_id=1, source_target_pairs={{0,24},{4,28},{8,0},{12,4},{16,8},{20,12},{24,16},{28,20},{32,56},... | collective-permute-start | bytes 1572872 | tf_op jit(solution)/shard_map/ppermute | solution.py:311
  162.7 16.6 %collective-permute-start.16 = (f16[2,4,128,256]{3,2,1,0:T(8,128)(2,1)S(1)}, f16[2,4,128,256]{3,2,1,0:T(8,128)(2,1)S(1)}, u32[]{:S(2)}, u32[]{:S(2)}) collective-permute-start(f16[2,4,128,256]{3,2,1,0:T(8,128)(2,1)S(1)} %get-tuple-element.51), channel_id=1, source_target_pairs={{0,32},{4,36},{8,40},{12,44},{16,48},{20,52},{24,56},{28,60},{32,6... | collective-permute-start | bytes 1572872 | tf_op jit(solution)/shard_map/ppermute | solution.py:310
  164.3 19.3 %collective-permute-start.18 = (f16[2,4,128,256]{3,2,1,0:T(8,128)(2,1)S(1)}, f16[2,4,128,256]{3,2,1,0:T(8,128)(2,1)S(1)}, u32[]{:S(2)}, u32[]{:S(2)}) collective-permute-start(f16[2,4,128,256]{3,2,1,0:T(8,128)(2,1)S(1)} %get-tuple-element.52), channel_id=1, source_target_pairs={{0,96},{4,100},{8,104},{12,108},{16,112},{20,116},{24,120},{28,124... | collective-permute-start | bytes 1572872 | tf_op jit(solution)/shard_map/ppermute | solution.py:311
  174.6 26.6 %collective-permute-start.24 = (f16[4,4,128,256]{3,2,1,0:T(8,128)(2,1)}, f16[4,4,128,256]{3,2,1,0:T(8,128)(2,1)}, u32[]{:S(2)}, u32[]{:S(2)}) collective-permute-start(f16[4,4,128,256]{3,2,1,0:T(8,128)(2,1)} %pad_maximum_fusion.2), channel_id=1, source_target_pairs={{0,8},{4,12},{8,16},{12,20},{16,24},{20,28},{24,0},{28,4},{32,40},... | collective-permute-start | bytes 3145736 | tf_op jit(solution)/shard_map/ppermute | solution.py:314
  178.1 25.6 %collective-permute-start.26 = (f16[4,4,128,256]{3,2,1,0:T(8,128)(2,1)}, f16[4,4,128,256]{3,2,1,0:T(8,128)(2,1)}, u32[]{:S(2)}, u32[]{:S(2)}) collective-permute-start(f16[4,4,128,256]{3,2,1,0:T(8,128)(2,1)} %pad_maximum_fusion.3), channel_id=1, source_target_pairs={{0,24},{4,28},{8,0},{12,4},{16,8},{20,12},{24,16},{28,20},{32,56},... | collective-permute-start | bytes 3145736 | tf_op jit(solution)/shard_map/ppermute | solution.py:315
  180.7 27.1 %collective-permute-start.17 = (f16[4,4,128,256]{3,2,1,0:T(8,128)(2,1)}, f16[4,4,128,256]{3,2,1,0:T(8,128)(2,1)}, u32[]{:S(2)}, u32[]{:S(2)}) collective-permute-start(f16[4,4,128,256]{3,2,1,0:T(8,128)(2,1)} %pad_maximum_fusion), channel_id=1, source_target_pairs={{0,32},{4,36},{8,40},{12,44},{16,48},{20,52},{24,56},{28,60},{32,6... | collective-permute-start | bytes 3145736 | tf_op jit(solution)/shard_map/ppermute | solution.py:314
  184.1 24.3 %collective-permute-start.19 = (f16[4,4,128,256]{3,2,1,0:T(8,128)(2,1)S(1)}, f16[4,4,128,256]{3,2,1,0:T(8,128)(2,1)}, u32[]{:S(2)}, u32[]{:S(2)}) collective-permute-start(f16[4,4,128,256]{3,2,1,0:T(8,128)(2,1)S(1)} %pad_maximum_fusion.1), channel_id=1, source_target_pairs={{0,96},{4,100},{8,104},{12,108},{16,112},{20,116},{24,120},{28,124... | collective-permute-start | bytes 3145736 | tf_op jit(solution)/shard_map/ppermute | solution.py:315
  213.2 10.8 %collective-permute-start.20 = (f16[4,128,256]{2,1,0:T(8,128)(2,1)S(1)}, f16[4,128,256]{2,1,0:T(8,128)(2,1)S(1)}, u32[]{:S(2)}, u32[]{:S(2)}) collective-permute-start(f16[4,128,256]{2,1,0:T(8,128)(2,1)S(1)} %get-tuple-element.48), channel_id=1, source_target_pairs={{0,16},{4,20},{8,24},{12,28},{16,0},{20,4},{24,8},{28,12},{32,48},... | collective-permute-start | bytes 786440 | tf_op jit(solution)/shard_map/ppermute | solution.py:321
  213.7 14.9 %collective-permute-start.21 = (f16[4,128,256]{2,1,0:T(8,128)(2,1)S(1)}, f16[4,128,256]{2,1,0:T(8,128)(2,1)S(1)}, u32[]{:S(2)}, u32[]{:S(2)}) collective-permute-start(f16[4,128,256]{2,1,0:T(8,128)(2,1)S(1)} %get-tuple-element.50), channel_id=1, source_target_pairs={{0,8},{4,12},{8,16},{12,20},{16,24},{20,28},{24,0},{28,4},{32,40},... | collective-permute-start | bytes 786440 | tf_op jit(solution)/shard_map/ppermute | solution.py:321
  214.8 13.7 %collective-permute-start.22 = (f16[4,128,256]{2,1,0:T(8,128)(2,1)S(1)}, f16[4,128,256]{2,1,0:T(8,128)(2,1)S(1)}, u32[]{:S(2)}, u32[]{:S(2)}) collective-permute-start(f16[4,128,256]{2,1,0:T(8,128)(2,1)S(1)} %get-tuple-element.49), channel_id=1, source_target_pairs={{0,24},{4,28},{8,0},{12,4},{16,8},{20,12},{24,16},{28,20},{32,56},... | collective-permute-start | bytes 786440 | tf_op jit(solution)/shard_map/ppermute | solution.py:321
  217.7 11.0 %collective-permute-start.27 = (f16[4,128,256]{2,1,0:T(8,128)(2,1)S(1)}, f16[4,128,256]{2,1,0:T(8,128)(2,1)S(1)}, u32[]{:S(2)}, u32[]{:S(2)}) collective-permute-start(f16[4,128,256]{2,1,0:T(8,128)(2,1)S(1)} %get-tuple-element.53), channel_id=1, source_target_pairs={{0,64},{4,68},{8,72},{12,76},{16,80},{20,84},{24,88},{28,92},{32,9... | collective-permute-start | bytes 786440 | tf_op jit(solution)/shard_map/ppermute | solution.py:321
  219.9 12.5 %collective-permute-start.28 = (f16[4,128,256]{2,1,0:T(8,128)(2,1)S(1)}, f16[4,128,256]{2,1,0:T(8,128)(2,1)S(1)}, u32[]{:S(2)}, u32[]{:S(2)}) collective-permute-start(f16[4,128,256]{2,1,0:T(8,128)(2,1)S(1)} %get-tuple-element.55), channel_id=1, source_target_pairs={{0,32},{4,36},{8,40},{12,44},{16,48},{20,52},{24,56},{28,60},{32,6... | collective-permute-start | bytes 786440 | tf_op jit(solution)/shard_map/ppermute | solution.py:321
  224.1 9.3 %collective-permute-start.29 = (f16[4,128,256]{2,1,0:T(8,128)(2,1)S(1)}, f16[4,128,256]{2,1,0:T(8,128)(2,1)S(1)}, u32[]{:S(2)}, u32[]{:S(2)}) collective-permute-start(f16[4,128,256]{2,1,0:T(8,128)(2,1)S(1)} %get-tuple-element.54), channel_id=1, source_target_pairs={{0,96},{4,100},{8,104},{12,108},{16,112},{20,116},{24,120},{28,124... | collective-permute-start | bytes 786440 | tf_op jit(solution)/shard_map/ppermute | solution.py:321
  (6 other events, 51.2 us)
Sparse Core Ops, SparseCore 0:
  10.2 76.2 all-gather.2

commit v3 on v2

--- a/solution.py
+++ b/solution.py
@@ -9,6 +9,7 @@
 ROOT_TWO = 1.4142135623730951
 HALF = 512
 PIECES = 8
+CHUNKS = 5
 BLK = 256
 NB = 4
 PHI_MAX_SQ = 36.0
@@ -33,9 +34,28 @@
     ]
 
 
-def load_pieces(piece_refs, held, sems):
-    for i, ref in enumerate(piece_refs):
-        pltpu.make_async_copy(ref, held.at[i], sems.at[i]).start()
+def core_perm(shift, second):
+    def at(z, x, c):
+        return ((z % 4) * 4 + x % 4) * 2 + c
+
+    pairs = []
+    for z in range(4):
+        for x in range(4):
+            for c in range(2):
+                along_z = (c == 0) != second
+                there = at(z + shift, x, c) if along_z else at(z, x + shift, c)
+                pairs.append((at(z, x, c), there))
+    return pairs
+
+
+def half_views(chunk_refs):
+    views = []
+    for ref in chunk_refs:
+        if ref.shape[-1] == HALF:
+            views.append((ref, None))
+        else:
+            views.extend((ref, h) for h in range(2))
+    return views
 
 
 def split3(x):
@@ -47,9 +67,9 @@
 
 
 def density_body(order, where, *refs):
-    pieces = refs[:PIECES]
+    chunks = refs[:CHUNKS]
     (tiles, table, weights, xc, rho, sent, pacc, block_out, held, dmat, tbuf, psem, dsem, tsem) = (
-        refs[PIECES:]
+        refs[CHUNKS:]
     )
     for b in range(2):
         for t in range(16):
@@ -58,7 +78,9 @@
                 dmat.at[b, pl.ds((t // 4) * BLK, BLK), pl.ds((t % 4) * BLK, BLK)],
                 dsem.at[b],
             ).start()
-    load_pieces(pieces, held, psem)
+    for i, (ref, h) in enumerate(half_views(chunks)):
+        view = ref if h is None else ref.at[:, pl.ds(h * HALF, HALF)]
+        pltpu.make_async_copy(view, held.at[i], psem.at[i]).start()
     pltpu.make_async_copy(table.at[order[0]], tbuf.at[0], tsem.at[0]).start()
     pacc[...] = jnp.zeros_like(pacc)
     block_out[...] = jnp.zeros_like(block_out)
@@ -158,56 +180,51 @@
     lax.fori_loop(0, PIECES, step, 0)
 
 
-def ham_body(order, listed, slots, starts, *refs):
-    pieces = refs[: 2 * PIECES]
-    scale_mine, scale_beside, out, held, dense, rows_of, psem, osem = refs[2 * PIECES :]
-    for i in range(2 * PIECES):
-        pi = order[i % PIECES]
-        pltpu.make_async_copy(
-            pieces[i],
-            held.at[i // PIECES, pi // 4, :, pl.ds(pl.multiple_of((pi % 4) * HALF, HALF), HALF)],
-            psem,
-        ).start()
+def ham_body(order, slots, place, *refs):
+    chunks = refs[: 2 * CHUNKS]
+    scale_mine, scale_beside, dense, held, rows_of, psem = refs[2 * CHUNKS :]
+    core = place[0]
+    for side in range(2):
+        i = 0
+        for ref in chunks[side * CHUNKS : (side + 1) * CHUNKS]:
+            width = ref.shape[-1]
+            pi = order[i]
+            lanes = pl.ds(pl.multiple_of((pi % 4) * HALF, HALF), width)
+            for half in range(2):
+                at = (1 - core) if half else core
+                pltpu.make_async_copy(
+                    ref.at[:, half], held.at[side, pi // 4, at, :, :, lanes], psem
+                ).start()
+            i += width // HALF
     for b in range(2):
         rows_of[0, b] = scale_mine[b]
         rows_of[1, b] = scale_beside[b]
 
     def clear(s, _):
-        dense[s] = jnp.zeros((BLK, BLK), jnp.float32)
+        dense[s] = jnp.zeros(dense.shape[1:], jnp.float32)
         return 0
 
     lax.fori_loop(0, dense.shape[0], clear, 0)
     pltpu.make_async_copy(held, held, psem).wait()
 
-    def product(n, flag):
-        code = listed[n]
-        side, tile = code // 32, code % 32
-        b, row, col = tile // 16, (tile // 4) % 4, tile % 4
-        left = held[side, b, pl.ds(pl.multiple_of(row * BLK, BLK), BLK), :]
-        right = held[side, b, pl.ds(pl.multiple_of(col * BLK, BLK), BLK), :]
-        right = (right.astype(jnp.float32) * (rows_of[side, b] * flag)).astype(jnp.bfloat16)
+    def product(side, b, col):
+        left = held[side, b, 0].reshape(2 * BLK, 4 * HALF)
+        right = jnp.concatenate([held[side, b, core, col], held[side, b, 1 - core, col]], axis=0)
+        right = (right.astype(jnp.float32) * rows_of[side, b]).astype(jnp.bfloat16)
         return lax.dot_general(
             left, right, (((1,), (1,)), ((), ())), preferred_element_type=jnp.float32
         )
 
-    for quarter in range(4):
-        begin, end = starts[quarter], starts[quarter + 1]
-
-        def pair(k, _):
-            n = begin + 2 * k
-            other = jnp.minimum(n + 1, end - 1)
-            one = product(n, 1.0)
-            two = product(other, jnp.where(n + 1 < end, 1.0, 0.0).astype(jnp.float32))
-            dense[slots[n]] += one
-            dense[slots[other]] += two
-            return 0
-
-        lax.fori_loop(0, (end - begin + 1) // 2, pair, 0)
-        part = pl.ds(quarter * 16, 16)
-        pltpu.make_async_copy(dense.at[part], out.at[part], osem.at[quarter]).start()
-    for quarter in range(4):
-        part = pl.ds(quarter * 16, 16)
-        pltpu.make_async_copy(dense.at[part], out.at[part], osem.at[quarter]).wait()
+    def step(n, _):
+        side, b, cols = n // 4, (n // 2) % 2, (n % 2) * 2
+        parts = [product(side, b, cols + k) for k in range(2)]
+        for k in range(2):
+            for row in range(NB):
+                slot = slots[side * 32 + b * 16 + row * NB + cols + k]
+                dense[slot] += parts[k][row * 128 : (row + 1) * 128]
+        return 0
+
+    lax.fori_loop(0, 8, step, 0)
 
 
 def any_spec():
@@ -222,7 +239,7 @@
     return pl.BlockSpec(memory_space=pltpu.SMEM)
 
 
-def density_call(order, where, pieces, tiles, table, weights, xc):
+def density_call(order, where, chunks, tiles, table, weights, xc):
     nbasis = NB * BLK
     return pl.pallas_call(
         density_body,
@@ -230,7 +247,7 @@
             jax.ShapeDtypeStruct((PIECES, 1, HALF), jnp.float32),
             jax.ShapeDtypeStruct((32, PAY_ROWS, 128), jnp.float32),
         ),
-        in_specs=[smem_spec(), smem_spec()] + [any_spec()] * (PIECES + 2) + [vmem_spec()] * 2,
+        in_specs=[smem_spec(), smem_spec()] + [any_spec()] * (CHUNKS + 2) + [vmem_spec()] * 2,
         out_specs=(vmem_spec(), vmem_spec()),
         scratch_shapes=[
             pltpu.VMEM((2, nbasis, 128), jnp.float32),
@@ -247,7 +264,7 @@
             flops=2 * 4096 * 1024 * 1024, bytes_accessed=32 << 20, transcendentals=0
         ),
         name="density",
-    )(order, where, *pieces, tiles, table, weights, xc)
+    )(order, where, *chunks, tiles, table, weights, xc)
 
 
 def potential_call(table, got, even, odd, weights, xc, rho, natoms):
@@ -275,26 +292,31 @@
     )(table, got, even, odd, weights, xc, rho)
 
 
-def ham_call(order, listed, slots, starts, pieces, scale_mine, scale_beside):
+def ham_call(order, slots, place, chunks, scale_mine, scale_beside):
     nbasis = NB * BLK
     return pl.pallas_call(
         ham_body,
-        out_shape=jax.ShapeDtypeStruct((64, BLK, BLK), jnp.float32),
-        in_specs=[smem_spec()] * 4 + [any_spec()] * (2 * PIECES) + [vmem_spec()] * 2,
-        out_specs=any_spec(),
+        out_shape=jax.ShapeDtypeStruct((128, 128, BLK), jnp.float32),
+        in_specs=[smem_spec()] * 3 + [any_spec()] * (2 * CHUNKS) + [vmem_spec()] * 2,
+        out_specs=vmem_spec(),
         scratch_shapes=[
-            pltpu.VMEM((2, 2, nbasis, 4 * HALF), jnp.bfloat16),
-            pltpu.VMEM((64, BLK, BLK), jnp.float32),
+            pltpu.VMEM((2, 2, 2, NB, 128, 4 * HALF), jnp.bfloat16),
             pltpu.VMEM((2, 2, 1, 4 * HALF), jnp.float32),
             pltpu.SemaphoreType.DMA,
-            pltpu.SemaphoreType.DMA((4,)),
         ],
-        compiler_params=pltpu.CompilerParams(vmem_limit_bytes=40 << 20),
+        compiler_params=pltpu.CompilerParams(vmem_limit_bytes=38 << 20),
         cost_estimate=pl.CostEstimate(
             flops=2 * 4096 * 1024 * 1024, bytes_accessed=32 << 20, transcendentals=0
         ),
         name="ham",
-    )(order, listed, slots, starts, *pieces, scale_mine, scale_beside)
+    )(
+        order,
+        slots,
+        place,
+        *[c.reshape(NB, 2, 128, c.shape[-1]) for c in chunks],
+        scale_mine,
+        scale_beside,
+    )
 
 
 def cast(x):
@@ -305,20 +327,20 @@
     return x.astype(jnp.float32)
 
 
-def ring_sum(parts, axis_name, send_up, send_down):
+def ring_sum(parts):
     half = parts[2].shape[0] // 2
-    from_below = lax.ppermute(cast(parts[2][:half]), axis_name, send_up)
-    from_above = lax.ppermute(cast(parts[2][half:]), axis_name, send_down)
+    from_below = lax.ppermute(cast(parts[2][:half]), "grid", core_perm(1, False))
+    from_above = lax.ppermute(cast(parts[2][half:]), "grid", core_perm(-1, False))
     up = jnp.concatenate([cast(parts[1][:half] + wide(from_below)), cast(parts[1][half:])])
     down = jnp.concatenate([cast(parts[3][:half]), cast(parts[3][half:] + wide(from_above))])
-    got_below = lax.ppermute(up, axis_name, send_up)
-    got_above = lax.ppermute(down, axis_name, send_down)
+    got_below = lax.ppermute(up, "grid", core_perm(1, False))
+    got_above = lax.ppermute(down, "grid", core_perm(-1, False))
     return parts[0] + wide(got_below) + wide(got_above)
 
 
-def direct_sum(parts, axis_name, perms):
+def direct_sum(parts):
     total = parts[0]
-    got = [lax.ppermute(cast(parts[d]), axis_name, perms[d]) for d in (2, 1, 3)]
+    got = [lax.ppermute(cast(parts[d]), "grid", core_perm(d, True)) for d in (2, 1, 3)]
     for g in got:
         total = total + wide(g)
     return total
@@ -348,15 +370,13 @@
     ntiles = tile_home.shape[0]
     slots_here = 2 * neighbors
 
-    own = [basis_values[:HALF].T, basis_values[HALF:].T]
-    below0 = lax.ppermute(own[0], "pert", ring(1))
-    above1 = lax.ppermute(own[1], "pert", ring(3))
-    below1 = lax.ppermute(own[1], "pert", ring(1))
-    above0 = lax.ppermute(own[0], "pert", ring(3))
-    far0 = lax.ppermute(below0, "pert", ring(1))
-    far1 = lax.ppermute(above1, "pert", ring(3))
-    pieces = [own[0], own[1], below0, below1, above0, above1, far0, far1]
-    beside = [lax.ppermute(piece, "grid", grid_perm(0, 0, 1)) for piece in pieces]
+    own = basis_values.T
+    below = lax.ppermute(own, "pert", ring(1))
+    above = lax.ppermute(own, "pert", ring(3))
+    far0 = lax.ppermute(below[:, :HALF], "pert", ring(1))
+    far1 = lax.ppermute(above[:, HALF:], "pert", ring(3))
+    chunks = [own, below, above, far0, far1]
+    beside = [lax.ppermute(chunk, "grid", grid_perm(0, 0, 1)) for chunk in chunks]
     steps = jnp.array([0, 0, 3, 3, 1, 1, 2, 2], jnp.int32)
     halves = jnp.array([0, 1] * 4, jnp.int32)
     order = ((plane + steps) % 4) * 2 + halves
@@ -368,20 +388,12 @@
     homes_beside = lax.ppermute(homes, "grid", grid_perm(0, 0, 1))
 
     every_home = jnp.concatenate([homes, homes_beside])
-    owner, place = every_home // tile_dev, every_home % tile_dev
+    owner = every_home // tile_dev
     off_z = (owner // 8 - my_z) % 4
     off_x = ((owner // 2) % 4 - my_x) % 4
-    slot = (off_z * 4 + off_x) * tile_dev + place
-    count = 2 * slots_here
-    ids = jnp.arange(count, dtype=jnp.int32)
-    valid = owner % 2 == my_c
-    key = jnp.where(valid, slot, 64) * count + ids
-    rank = jnp.sum((key[None, :] < key[:, None]).astype(jnp.int32), axis=1)
-    ranked = rank[None, :] == ids[:, None]
-    listed = jnp.sum(jnp.where(ranked, ids[None, :], 0), axis=1)
-    slots = jnp.sum(jnp.where(ranked & valid[None, :], slot[None, :], 0), axis=1)
-    edges = jnp.arange(8, dtype=jnp.int32) * 16
-    starts = jnp.sum((valid[None, :] & (slot[None, :] < edges[:, None])).astype(jnp.int32), axis=1)
+    ahead = jnp.where(my_c == 0, off_z * 4 + off_x, off_x * 4 + off_z)
+    slots = ahead * (2 * tile_dev) + every_home % (2 * tile_dev)
+    core_place = my_c.reshape(1).astype(jnp.int32)
 
     atom_match = atom_list[:, :, None] == jnp.arange(natoms, dtype=jnp.int32)
     atom_pos = jnp.sum(jnp.where(atom_match[None], atom_coords[:, None, None, :], 0.0), axis=3)
@@ -413,11 +425,9 @@
         return (wanted_rows[:, None] == held[None, :]).astype(jnp.bfloat16)
 
     even, odd = chooser(0), chooser(1)
-    gauss, hart, even, odd, listed, slots, starts = lax.optimization_barrier(
-        (gauss, hart, even, odd, listed, slots, starts)
-    )
-
-    rho, sent = density_call(order, homes, pieces, tiles, gauss, weights, xc)
+    gauss, hart, even, odd, slots = lax.optimization_barrier((gauss, hart, even, odd, slots))
+
+    rho, sent = density_call(order, homes, chunks, tiles, gauss, weights, xc)
     got = lax.all_to_all(sent, "grid", split_axis=0, concat_axis=0, tiled=True)
     all_coeffs, pot, scale, bound = potential_call(
         hart, got.reshape(groups * PAY_ROWS, 128), even, odd, weights, xc, rho, natoms
@@ -429,26 +439,24 @@
     scale_beside = lax.ppermute(scale, "grid", grid_perm(0, 0, 1))
     dense = ham_call(
         order,
-        listed,
         slots,
-        starts,
-        pieces + beside,
+        core_place,
+        chunks + beside,
         scale.reshape(2, 1, 4 * HALF),
         scale_beside.reshape(2, 1, 4 * HALF),
     )
 
-    dense = dense.reshape(4, 4, tile_dev, BLK, BLK)
+    dense = dense.reshape(4, 4, 2 * tile_dev, 128, BLK)
     factor = F16_TOP / ham_bound
-    z_up, z_down = grid_perm(1, 0, 0), grid_perm(-1, 0, 0)
-    x_up, x_down = grid_perm(0, 1, 0), grid_perm(0, -1, 0)
-    half = BLK // 2
-    upper = ring_sum([dense[d, :, :, :half] * factor for d in range(4)], "grid", z_up, z_down)
-    lower = ring_sum([dense[:, d, :, half:] * factor for d in range(4)], "grid", x_up, x_down)
-    z_perms = {d: grid_perm(d, 0, 0) for d in range(1, 4)}
-    x_perms = {d: grid_perm(0, d, 0) for d in range(1, 4)}
-    upper = direct_sum([upper[d] for d in range(4)], "grid", x_perms)
-    lower = direct_sum([lower[d] for d in range(4)], "grid", z_perms)
-    hamiltonian = jnp.concatenate([upper, lower], axis=1) * (ham_bound / F16_TOP)
+    chip = direct_sum(list(ring_sum([dense[d] * factor for d in range(4)])))
+    chip = chip.reshape(2, tile_dev, 128, BLK)
+    first_core = my_c == 0
+    keep = jnp.where(first_core, chip[0], chip[1])
+    give = jnp.where(first_core, chip[1], chip[0])
+    came = wide(lax.ppermute(cast(give), "grid", grid_perm(0, 0, 1)))
+    hamiltonian = jnp.concatenate(
+        [jnp.where(first_core, keep, came), jnp.where(first_core, came, keep)], axis=1
+    ) * (ham_bound / F16_TOP)
     return (hamiltonian[None], own_coeffs[None], pot.reshape(1, -1))
 
 

time: 242 us -> 236 us (0.975)
  starting transfers between devices: 45.2 us -> 28.2 us
  waiting for transfers between devices: 73.4 us -> 83.8 us
  other arithmetic: 39.8 us -> 33.2 us
  Pallas kernels: 39.5 us -> 43.3 us
  local copies, waits for them, and re-layouts: 10.3 us -> 13.6 us
    ppermute x28 -> x17, starting transfers between devices: 36.6 us -> 19 us  [the longest x3 4.67 us: direct_sum(): lax.ppermute(cast(parts[d]), 'grid', core_perm(d, True))]
    ppermute x28 -> x17, waiting for transfers between devices: 71.9 us -> 82.3 us  [the longest x1 34.3 us: per_device(): below = lax.ppermute(own, 'pert', ring(1))]
    pallas_call x1, Pallas kernels: 18.7 us -> 22.4 us  [ham_call(): pl.pallas_call(ham_body, out_shape=jax.ShapeDtypeStruct((128, 128, BLK),...]
    slice x1 -> x3, local copies, waits for them, and re-layouts: 2.68 us -> 5.14 us  [the longest x1 2.28 us: per_device(): far1 = lax.ppermute(above[:, HALF:], 'pert', ring(3))]
    mul x4 -> x2, other arithmetic: 8.92 us -> 7.82 us  [the longest x1 6.75 us: per_device(): chip = direct_sum(list(ring_sum([dense[d] * factor for d in range(4)])))]
  transfers between devices with their start and end apart: 32 -> 21, of which waited for: 12 -> 8; matrix products, arithmetic and copies ran while one was open for 15% -> 15% of each run, Pallas kernels for 9% -> 9%
where the time goes in v3:
time: 236 us; the launch traced here: 235 us
  waiting for transfers between devices  83.8 us (36%)
  Pallas kernels  43.3 us (18%)
  other arithmetic  33.2 us (14%)
  starting transfers between devices  28.2 us (12%)
  blocking collectives  18.3 us (8%)
  between operations  14.6 us (6%)
  local copies, waits for them, and re-layouts  13.6 us (6%)
    ppermute x1, waiting for transfers between devices, per_device(): below = lax.ppermute(own, 'pert', ring(1))  34.3 us
    ppermute x1, waiting for transfers between devices, ring_sum(): got_below = lax.ppermute(up, 'grid', core_perm(1, False))  23 us
    pallas_call x1, Pallas kernels, ham_call(): pl.pallas_call(ham_body, out_shape=jax.ShapeDtypeStruct((128, 128, BLK),...  22.4 us
    all_to_all x1, blocking collectives, per_device(): got = lax.all_to_all(sent, 'grid', split_axis=0, concat_axis=0, tiled=True)  18.3 us
    pallas_call x1, Pallas kernels, density_call(): pl.pallas_call(density_body, out_shape=(jax.ShapeDtypeStruct((PIECES, 1,...  16.3 us
    ppermute x1, waiting for transfers between devices, ring_sum(): lax.ppermute(cast(parts[2][:half]), 'grid', core_perm(1, False))  11.7 us
    ppermute x3, waiting for transfers between devices, direct_sum(): lax.ppermute(cast(parts[d]), 'grid', core_perm(d, True))  11.7 us
    all_to_all x1, starting transfers between devices, per_device(): lax.all_to_all(jnp.broadcast_to(row[None, None], (groups, 8, 128)), 'grid...  8.27 us
  transfers between devices with their start and end apart: 21, of which 8 were waited for; matrix products, arithmetic and copies ran while one was open for 15% of the time, Pallas kernels for 9%

profile of v3, /device:TPU:0, one launch (start us, length us, event | category | flops | bytes accessed | tf_op | source)
XLA Modules:
  0.0 234.9 jit_solution(3416219768004784873)
XLA Ops:
  7.2 0.7 all-gather.3.cloned.1.call-update
  8.0 2.9 %copy.28 = bf16[1024,1024]{0,1:T(8,128)(2,1)S(1)} copy(bf16[1024,1024]{1,0:T(8,128)(2,1)} %param.13) | data formatting | bytes 4194304 | tf_op args[0]
  10.9 1.8 collective-permute-start.1
  12.6 1.5 collective-permute-start.2
  14.5 0.6 collective-permute-start
  15.3 0.7 broadcast_in_dim.66
  16.0 8.3 %all-to-all-start = ((f32[32,8,128]{2,1,0:T(8,128)}), f32[32,8,128]{2,1,0:T(8,128)S(1)}, u32[]{:S(2)}, u32[]{:S(2)}) async-start(f32[32,8,128]{2,1,0:T(8,128)} %broadcast_in_dim.66), calls=%async_computation | async-start | bytes 262144 | tf_op jit(solution)/shard_map/all_to_all | solution.py:412
  24.7 0.8 add_sqrt_fusion
  25.5 34.3 %collective-permute-done.1.refs_1_ = bf16[1024,1024]{1,0:T(8,128)(2,1)} collective-permute-done((bf16[1024,1024]{1,0:T(8,128)(2,1)S(1)}, bf16[1024,1024]{1,0:T(8,128)(2,1)}, u32[]{:S(2)}, u32[]{:S(2)}) %collective-permute-start.1) | collective-permute-done | bytes 2097184 | tf_op jit(solution)/shard_map/ppermute | solution.py:374
  59.8 2.3 slice.99
  62.4 2.3 slice.100
  64.7 2.9 %collective-permute-start.4 = (bf16[1024,512]{1,0:T(8,128)(2,1)}, bf16[1024,512]{1,0:T(8,128)(2,1)}, u32[]{:S(2)}, u32[]{:S(2)}) collective-permute-start(bf16[1024,512]{1,0:T(8,128)(2,1)} %slice.100), channel_id=1, source_target_pairs={{0,3},{1,0},{2,1},{3,2},{4,7},{5,4},{6,5},{7,6},{8,11},{9,8},{10,9... | collective-permute-start | bytes 3145736 | tf_op jit(solution)/shard_map/ppermute | solution.py:377
  67.6 0.5 broadcast_multiply_fusion
  68.1 0.5 copy-done.11
  69.2 0.7 fusion.10.order
  69.8 0.6 pad_maximum_fusion.2
  70.4 0.7 div.109
  71.1 0.7 div.110
  71.7 0.7 div.103
  72.4 0.7 div.104
  73.1 8.2 %bitcast_divide_fusion.table = f32[8,1024,512]{2,1,0:T(8,128)} fusion(f32[1024]{0:T(1024)} %div.110, f32[8,16,512]{2,1,0:T(8,128)S(1)} %bitcast.88), kind=kLoop, calls=%fused_computation | loop fusion | flops 8388608 | bytes 17043456 | tf_op jit(solution)/shard_map/div | solution.py:407
  81.3 8.1 %fusion.refs_6_ = f32[8,1024,512]{2,1,0:T(8,128)} fusion(f32[1024]{0:T(1024)S(1)} %copy-done.6, f32[8,16,512]{2,1,0:T(8,128)S(1)} %bitcast.87), kind=kLoop, calls=%fused_computation.3 | loop fusion | flops 4194304 | bytes 17043456 | tf_op jit(solution)/shard_map/exp | solution.py:405
  90.0 1.1 compare_convert_fusion
  91.7 16.3 %density.1 = (f32[8,1,512]{2,1,0:T(1,128)S(1)}, f32[32,24,128]{2,1,0:T(8,128)S(1)}) custom-call(s32[8]{0:T(128)S(1)} %fusion.10.order, s32[32]{0:T(128)S(1)} %select_reduce_fusion.2.where, bf16[1024,1024]{1,0:T(8,128)(2,1)S(1)} %bitcast.70, bf16[1024,1024]{1,0:T(8,128)(2,1)} %collective-permute-done.1.refs_1_, ...), custom_call_target="tpu_custom_call" | custom-call | flops 8589934592 | bytes 33554432 | tf_op jit(solution)/shard_map/density/pallas_call | solution.py:244
  108.0 18.3 %all_to_all.10 = f32[32,24,128]{2,1,0:T(8,128)S(1)} all-to-all(f32[32,24,128]{2,1,0:T(8,128)S(1)} %get-tuple-element.17), channel_id=1, replica_groups=mesh['grid'=32,'pert'=4] {'grid'}, dimensions={0} | all-to-all | bytes 786432 | tf_op jit(solution)/shard_map/all_to_all | solution.py:431
  126.3 4.6 %potential.1 = (f32[256,64]{1,0:T(8,128)S(1)}, f32[8,1,512]{2,1,0:T(1,128)}, f32[8,1,512]{2,1,0:T(1,128)S(1)}, f32[1,128]{1,0:T(1,128)S(1)}) custom-call(f32[8,1024,512]{2,1,0:T(8,128)S(1)} %bitcast.66, f32[768,128]{1,0:T(8,128)S(1)} %bitcast.73, bf16[288,768]{1,0:T(8,128)(2,1)S(1)} %copy-done.1, bf16[288,768]{1,0:T(8,128)(2,1)S(1)} %copy-done, ...), custom_call_target="tpu_custom_call" | custom-call | flops 16777216 | bytes 16777216 | tf_op jit(solution)/shard_map/potential/pallas_call | solution.py:272
  131.3 0.8 collective-permute-done.10
  132.2 22.4 %ham.1 = f32[128,128,256]{2,1,0:T(8,128)} custom-call(s32[8]{0:T(128)S(1)} %fusion.10.order, s32[64]{0:T(128)S(1)} %fusion.7.slots, s32[1]{0:T(128)} %bitcast.7.place, bf16[4,2,128,1024]{3,2,1,0:T(8,128)(2,1)S(1)} %bitcast.71, bf16[4,2,128,1024]{3,2,1,0:T(8,128)(2,1)} %bitcast.10.refs_1_, bf16[4,2,128,1024]{3,2,1,0:T(8,128)(2,1)} %bitcast.11.refs_2_, ...), custom_call_target="tpu_custom_call" | custom-call | flops 8589934592 | bytes 33554432 | tf_op jit(solution)/shard_map/ham/pallas_call | solution.py:297
  154.6 6.8 %slice_multiply_fusion.2 = (f32[32,128,256]{2,1,0:T(8,128)S(1)}, f32[32,128,256]{2,1,0:T(8,128)S(1)}, f16[32,128,256]{2,1,0:T(8,128)(2,1)S(1)}, f32[32,128,256]{2,1,0:T(8,128)S(1)}) fusion(f32[128,128,256]{2,1,0:T(8,128)} %ham.1, f32[]{:T(128)} %bitcast.26), kind=kLoop, calls=%fused_computation.7 | loop fusion | flops 5242880 | bytes 31457284 | tf_op jit(solution)/shard_map/mul | solution.py:451
  161.4 0.6 fusion.18
  161.9 0.6 collective-permute-start.11
  162.5 2.7 %collective-permute-start.13 = (f16[2,8,128,256]{3,2,1,0:T(8,128)(2,1)S(1)}, f16[2,8,128,256]{3,2,1,0:T(8,128)(2,1)S(1)}, u32[]{:S(2)}, u32[]{:S(2)}) collective-permute-start(f16[2,8,128,256]{3,2,1,0:T(8,128)(2,1)S(1)} %bitcast.89), channel_id=1, source_target_pairs={{0,96},{4,28},{8,104},{12,4},{16,112},{20,12},{24,120},{28,20},{32... | collective-permute-start | bytes 3145736 | tf_op jit(solution)/shard_map/ppermute | solution.py:333
  165.3 1.0 slice_convert_fusion
  166.3 11.7 %collective-permute-done.11 = f16[2,8,128,256]{3,2,1,0:T(8,128)(2,1)S(1)} collective-permute-done((f16[2,8,128,256]{3,2,1,0:T(8,128)(2,1)S(1)}, f16[2,8,128,256]{3,2,1,0:T(8,128)(2,1)S(1)}, u32[]{:S(2)}, u32[]{:S(2)}) %collective-permute-start.11) | collective-permute-done | bytes 1048608 | tf_op jit(solution)/shard_map/ppermute | solution.py:332
  178.4 0.6 pad_maximum_fusion
  179.4 0.6 pad_maximum_fusion.1
  180.0 3.3 %collective-permute-start.14 = (f16[4,8,128,256]{3,2,1,0:T(8,128)(2,1)S(1)}, f16[4,8,128,256]{3,2,1,0:T(8,128)(2,1)S(1)}, u32[]{:S(2)}, u32[]{:S(2)}) collective-permute-start(f16[4,8,128,256]{3,2,1,0:T(8,128)(2,1)S(1)} %pad_maximum_fusion.1), channel_id=1, source_target_pairs={{0,96},{4,28},{8,104},{12,4},{16,112},{20,12},{24,120},{28,20},{32... | collective-permute-start | bytes 6291464 | tf_op jit(solution)/shard_map/ppermute | solution.py:337
  183.3 23.0 %collective-permute-done.12 = f16[4,8,128,256]{3,2,1,0:T(8,128)(2,1)S(1)} collective-permute-done((f16[4,8,128,256]{3,2,1,0:T(8,128)(2,1)S(1)}, f16[4,8,128,256]{3,2,1,0:T(8,128)(2,1)S(1)}, u32[]{:S(2)}, u32[]{:S(2)}) %collective-permute-start.12) | collective-permute-done | bytes 2097184 | tf_op jit(solution)/shard_map/ppermute | solution.py:336
  206.3 0.6 collective-permute-done.14
  206.9 1.3 fusion.16
  208.5 1.4 collective-permute-start.15
  210.0 0.9 collective-permute-start.16
  210.9 2.3 collective-permute-start.17
  213.2 6.2 %collective-permute-done.15 = f16[8,128,256]{2,1,0:T(8,128)(2,1)S(1)} collective-permute-done((f16[8,128,256]{2,1,0:T(8,128)(2,1)S(1)}, f16[8,128,256]{2,1,0:T(8,128)(2,1)S(1)}, u32[]{:S(2)}, u32[]{:S(2)}) %collective-permute-start.15) | collective-permute-done | bytes 524320 | tf_op jit(solution)/shard_map/ppermute | solution.py:343
  219.4 5.5 %collective-permute-done.16 = f16[8,128,256]{2,1,0:T(8,128)(2,1)S(1)} collective-permute-done((f16[8,128,256]{2,1,0:T(8,128)(2,1)S(1)}, f16[8,128,256]{2,1,0:T(8,128)(2,1)S(1)}, u32[]{:S(2)}, u32[]{:S(2)}) %collective-permute-start.16) | collective-permute-done | bytes 524320 | tf_op jit(solution)/shard_map/ppermute | solution.py:343
  225.3 0.6 dynamic-slice_bitcast_fusion
  225.9 0.9 collective-permute-done.18
  227.0 1.1 maximum_multiply_fusion
  (92 shorter events, 4.9 us)
Async XLA Ops:
  7.2 84.5 %all-gather.3.cloned.1.call-start = ((), (), s32[]{:S(2)}) async-start(), calls=%async_computation.2 | async-start | bytes 17301504 | tf_op jit(solution)/shard_map/all_gather | solution.py:384
  7.9 6.3 %copy-start.14 = (s32[2,16]{1,0:T(2,128)S(1)}, s32[2,16]{1,0:T(2,128)}, u32[]{:S(2)}) copy-start(s32[2,16]{1,0:T(2,128)} %param.20) | copy-start | bytes 388
  7.9 6.4 %copy-start.15 = (s32[128]{0:T(128)S(1)}, s32[128]{0:T(128)}, u32[]{:S(2)}) copy-start(s32[128]{0:T(128)} %param.21) | copy-start | bytes 1540
  7.9 7.1 %copy-start.8 = (s32[2,16]{1,0:T(2,128)S(1)}, s32[2,16]{1,0:T(2,128)}, u32[]{:S(2)}) copy-start(s32[2,16]{1,0:T(2,128)} %param.22) | copy-start | bytes 388
  7.9 7.1 %copy-start.10 = (s32[256]{0:T(256)S(1)}, s32[256]{0:T(256)}, u32[]{:S(2)}) copy-start(s32[256]{0:T(256)} %param.23) | copy-start | bytes 3076
  7.9 16.3 %copy-start.5 = (f32[3,4096]{1,0:T(4,128)S(1)}, f32[3,4096]{1,0:T(4,128)}, u32[]{:S(2)}) copy-start(f32[3,4096]{1,0:T(4,128)} %param.14) | copy-start | bytes 147460
  8.0 16.5 %copy-start.9 = (f32[3,256]{1,0:T(4,128)S(1)}, f32[3,256]{1,0:T(4,128)}, u32[]{:S(2)}) copy-start(f32[3,256]{1,0:T(4,128)} %param.18) | copy-start | bytes 9220
  10.9 48.9 %collective-permute-start.1 = (bf16[1024,1024]{1,0:T(8,128)(2,1)S(1)}, bf16[1024,1024]{1,0:T(8,128)(2,1)}, u32[]{:S(2)}, u32[]{:S(2)}) collective-permute-start(bf16[1024,1024]{1,0:T(8,128)(2,1)S(1)} %bitcast.67), channel_id=1, source_target_pairs={{0,1},{1,2},{2,3},{3,0},{4,5},{5,6},{6,7},{7,4},{8,9},{9,10},{10,1... | collective-permute-start | bytes 6291464 | tf_op jit(solution)/shard_map/ppermute | solution.py:374
  12.6 49.8 %collective-permute-start.2 = (bf16[1024,1024]{1,0:T(8,128)(2,1)S(1)}, bf16[1024,1024]{1,0:T(8,128)(2,1)}, u32[]{:S(2)}, u32[]{:S(2)}) collective-permute-start(bf16[1024,1024]{1,0:T(8,128)(2,1)S(1)} %bitcast.68), channel_id=1, source_target_pairs={{0,3},{1,0},{2,1},{3,2},{4,7},{5,4},{6,5},{7,6},{8,11},{9,8},{10,9... | collective-permute-start | bytes 6291464 | tf_op jit(solution)/shard_map/ppermute | solution.py:375
  14.2 116.7 %collective-permute-start.5 = (bf16[1024,1024]{1,0:T(8,128)(2,1)S(1)}, bf16[1024,1024]{1,0:T(8,128)(2,1)}, u32[]{:S(2)}, u32[]{:S(2)}) collective-permute-start(bf16[1024,1024]{1,0:T(8,128)(2,1)S(1)} %bitcast.69), channel_id=1, source_target_pairs={{0,4},{4,0},{8,12},{12,8},{16,20},{20,16},{24,28},{28,24},{32,36},... | collective-permute-start | bytes 6291464 | tf_op jit(solution)/shard_map/ppermute | solution.py:379
  14.5 53.7 %collective-permute-start = (s32[32]{0:T(128)S(1)}, s32[32]{0:T(128)S(1)}, u32[]{:S(2)}, u32[]{:S(2)}) collective-permute-start(s32[32]{0:T(128)S(1)} %select_reduce_fusion.2.where), channel_id=1, source_target_pairs={{0,4},{4,0},{8,12},{12,8},{16,20},{20,16},{24,28},{28,24},{32,36},... | collective-permute-start | bytes 392 | tf_op jit(solution)/shard_map/ppermute | solution.py:388
  16.0 73.5 %all-to-all-start = ((f32[32,8,128]{2,1,0:T(8,128)}), f32[32,8,128]{2,1,0:T(8,128)S(1)}, u32[]{:S(2)}, u32[]{:S(2)}) async-start(f32[32,8,128]{2,1,0:T(8,128)} %broadcast_in_dim.66), calls=%async_computation | async-start | bytes 262144 | tf_op jit(solution)/shard_map/all_to_all | solution.py:412
  25.5 42.1 %copy-start.16 = (f32[64]{0:T(128)S(1)}, f32[64]{0:T(128)}, u32[]{:S(2)}) copy-start(f32[64]{0:T(128)} %param.17) | copy-start | bytes 772
  25.5 43.7 %copy-start.13 = (s32[8]{0:T(128)S(1)}, s32[8]{0:T(128)}, u32[]{:S(2)}) copy-start(s32[8]{0:T(128)} %constant.147.clone) | copy-start | bytes 100
  62.1 29.1 %collective-permute-start.3 = (bf16[1024,512]{1,0:T(8,128)(2,1)}, bf16[1024,512]{1,0:T(8,128)(2,1)S(1)}, u32[]{:S(2)}, u32[]{:S(2)}) collective-permute-start(bf16[1024,512]{1,0:T(8,128)(2,1)} %slice.99), channel_id=1, source_target_pairs={{0,1},{1,2},{2,3},{3,0},{4,5},{5,6},{6,7},{7,4},{8,9},{9,10},{10,1... | collective-permute-start | bytes 3145736 | tf_op jit(solution)/shard_map/ppermute | solution.py:376
  64.7 26.5 %collective-permute-start.4 = (bf16[1024,512]{1,0:T(8,128)(2,1)}, bf16[1024,512]{1,0:T(8,128)(2,1)}, u32[]{:S(2)}, u32[]{:S(2)}) collective-permute-start(bf16[1024,512]{1,0:T(8,128)(2,1)} %slice.100), channel_id=1, source_target_pairs={{0,3},{1,0},{2,1},{3,2},{4,7},{5,4},{6,5},{7,6},{8,11},{9,8},{10,9... | collective-permute-start | bytes 3145736 | tf_op jit(solution)/shard_map/ppermute | solution.py:377
  68.1 63.2 %collective-permute-start.6 = (bf16[1024,1024]{1,0:T(8,128)(2,1)}, bf16[1024,1024]{1,0:T(8,128)(2,1)}, u32[]{:S(2)}, u32[]{:S(2)}) collective-permute-start(bf16[1024,1024]{1,0:T(8,128)(2,1)} %collective-permute-done.1.refs_1_), channel_id=1, source_target_pairs={{0,4},{4,0},{8,12},{12,8},{16,20},{20,16},{24,28},{28,24},{32,36},... | collective-permute-start | bytes 6291464 | tf_op jit(solution)/shard_map/ppermute | solution.py:379
  68.1 0.5 copy-start.11
  68.7 62.7 %collective-permute-start.7 = (bf16[1024,1024]{1,0:T(8,128)(2,1)}, bf16[1024,1024]{1,0:T(8,128)(2,1)}, u32[]{:S(2)}, u32[]{:S(2)}) collective-permute-start(bf16[1024,1024]{1,0:T(8,128)(2,1)} %collective-permute-done.2.refs_2_), channel_id=1, source_target_pairs={{0,4},{4,0},{8,12},{12,8},{16,20},{20,16},{24,28},{28,24},{32,36},... | collective-permute-start | bytes 6291464 | tf_op jit(solution)/shard_map/ppermute | solution.py:379
  73.1 8.2 %copy-start.4 = (f32[2,4,16,512]{3,2,1,0:T(8,128)S(1)}, f32[2,4,16,512]{3,2,1,0:T(8,128)}, u32[]{:S(2)}) copy-start(f32[2,4,16,512]{3,2,1,0:T(8,128)} %get-tuple-element.43) | copy-start | bytes 786436
  73.1 8.2 %copy-start.6 = (f32[1024]{0:T(1024)S(1)}, f32[1024]{0:T(1024)}, u32[]{:S(2)}) copy-start(f32[1024]{0:T(1024)} %div.104) | copy-start | bytes 12292
  81.3 8.1 %copy-start.12 = (s32[32]{0:T(128)S(1)}, s32[32]{0:T(128)}, u32[]{:S(2)}) copy-start(s32[32]{0:T(128)} %copy-done.11) | copy-start | bytes 388
  81.3 8.7 %copy-start.7 = (f32[288]{0:T(512)S(1)}, f32[288]{0:T(512)}, u32[]{:S(2)}) copy-start(f32[288]{0:T(512)} %pad_maximum_fusion.2) | copy-start | bytes 3460
  81.3 10.4 %copy-start.2 = (f32[4096]{0:T(1024)S(1)}, f32[4096]{0:T(1024)}, u32[]{:S(2)}) copy-start(f32[4096]{0:T(1024)} %param.15) | copy-start | bytes 49156
  81.3 10.4 %copy-start.3 = (f32[4096]{0:T(1024)S(1)}, f32[4096]{0:T(1024)}, u32[]{:S(2)}) copy-start(f32[4096]{0:T(1024)} %param.16) | copy-start | bytes 49156
  91.1 40.2 %collective-permute-start.8 = (bf16[1024,512]{1,0:T(8,128)(2,1)S(1)}, bf16[1024,512]{1,0:T(8,128)(2,1)}, u32[]{:S(2)}, u32[]{:S(2)}) collective-permute-start(bf16[1024,512]{1,0:T(8,128)(2,1)S(1)} %collective-permute-done.3.refs_3_), channel_id=1, source_target_pairs={{0,4},{4,0},{8,12},{12,8},{16,20},{20,16},{24,28},{28,24},{32,36},... | collective-permute-start | bytes 3145736 | tf_op jit(solution)/shard_map/ppermute | solution.py:379
  91.1 40.2 %collective-permute-start.9 = (bf16[1024,512]{1,0:T(8,128)(2,1)}, bf16[1024,512]{1,0:T(8,128)(2,1)}, u32[]{:S(2)}, u32[]{:S(2)}) collective-permute-start(bf16[1024,512]{1,0:T(8,128)(2,1)} %collective-permute-done.4.refs_4_), channel_id=1, source_target_pairs={{0,4},{4,0},{8,12},{12,8},{16,20},{20,16},{24,28},{28,24},{32,36},... | collective-permute-start | bytes 3145736 | tf_op jit(solution)/shard_map/ppermute | solution.py:379
  91.6 34.6 %slice-start = ((s8[16777216]{0:T(1024)(128)(4,1)}), s8[4194304]{0:T(1024)(128)(4,1)S(1)}, s32[]{:S(2)}) async-start(s8[16777216]{0:T(1024)(128)(4,1)} %bitcast.65), calls=%async_computation.3 | async-start | bytes 8388608
  91.7 34.6 %slice-start.1 = ((s8[16777216]{0:T(1024)(128)(4,1)}), s8[4194304]{0:T(1024)(128)(4,1)S(1)}, s32[]{:S(2)}) async-start(s8[16777216]{0:T(1024)(128)(4,1)} %bitcast.65), calls=%async_computation.4 | async-start | bytes 8388608
  91.7 34.6 %slice-start.2 = ((s8[16777216]{0:T(1024)(128)(4,1)}), s8[4194304]{0:T(1024)(128)(4,1)S(1)}, s32[]{:S(2)}) async-start(s8[16777216]{0:T(1024)(128)(4,1)} %bitcast.65), calls=%async_computation.5 | async-start | bytes 8388608
  91.7 34.6 %slice-start.3 = ((s8[16777216]{0:T(1024)(128)(4,1)}), s8[4194304]{0:T(1024)(128)(4,1)S(1)}, s32[]{:S(2)}) async-start(s8[16777216]{0:T(1024)(128)(4,1)} %bitcast.65), calls=%async_computation.6 | async-start | bytes 8388608
  91.7 34.6 %copy-start = (bf16[288,768]{1,0:T(8,128)(2,1)S(1)}, bf16[288,768]{1,0:T(8,128)(2,1)}, u32[]{:S(2)}) copy-start(bf16[288,768]{1,0:T(8,128)(2,1)} %get-tuple-element.19.odd) | copy-start | bytes 1327108
  91.7 34.6 %copy-start.1 = (bf16[288,768]{1,0:T(8,128)(2,1)S(1)}, bf16[288,768]{1,0:T(8,128)(2,1)}, u32[]{:S(2)}) copy-start(bf16[288,768]{1,0:T(8,128)(2,1)} %get-tuple-element.18.even) | copy-start | bytes 1327108
  130.9 1.3 collective-permute-start.10
  161.9 16.1 %collective-permute-start.11 = (f16[2,8,128,256]{3,2,1,0:T(8,128)(2,1)S(1)}, f16[2,8,128,256]{3,2,1,0:T(8,128)(2,1)S(1)}, u32[]{:S(2)}, u32[]{:S(2)}) collective-permute-start(f16[2,8,128,256]{3,2,1,0:T(8,128)(2,1)S(1)} %bitcast.90), channel_id=1, source_target_pairs={{0,32},{4,12},{8,40},{12,20},{16,48},{20,28},{24,56},{28,4},{32,64... | collective-permute-start | bytes 3145736 | tf_op jit(solution)/shard_map/ppermute | solution.py:332
  162.5 16.5 %collective-permute-start.13 = (f16[2,8,128,256]{3,2,1,0:T(8,128)(2,1)S(1)}, f16[2,8,128,256]{3,2,1,0:T(8,128)(2,1)S(1)}, u32[]{:S(2)}, u32[]{:S(2)}) collective-permute-start(f16[2,8,128,256]{3,2,1,0:T(8,128)(2,1)S(1)} %bitcast.89), channel_id=1, source_target_pairs={{0,96},{4,28},{8,104},{12,4},{16,112},{20,12},{24,120},{28,20},{32... | collective-permute-start | bytes 3145736 | tf_op jit(solution)/shard_map/ppermute | solution.py:333
  179.0 27.3 %collective-permute-start.12 = (f16[4,8,128,256]{3,2,1,0:T(8,128)(2,1)S(1)}, f16[4,8,128,256]{3,2,1,0:T(8,128)(2,1)S(1)}, u32[]{:S(2)}, u32[]{:S(2)}) collective-permute-start(f16[4,8,128,256]{3,2,1,0:T(8,128)(2,1)S(1)} %pad_maximum_fusion), channel_id=1, source_target_pairs={{0,32},{4,12},{8,40},{12,20},{16,48},{20,28},{24,56},{28,4},{32,64... | collective-permute-start | bytes 6291464 | tf_op jit(solution)/shard_map/ppermute | solution.py:336
  180.0 26.8 %collective-permute-start.14 = (f16[4,8,128,256]{3,2,1,0:T(8,128)(2,1)S(1)}, f16[4,8,128,256]{3,2,1,0:T(8,128)(2,1)S(1)}, u32[]{:S(2)}, u32[]{:S(2)}) collective-permute-start(f16[4,8,128,256]{3,2,1,0:T(8,128)(2,1)S(1)} %pad_maximum_fusion.1), channel_id=1, source_target_pairs={{0,96},{4,28},{8,104},{12,4},{16,112},{20,12},{24,120},{28,20},{32... | collective-permute-start | bytes 6291464 | tf_op jit(solution)/shard_map/ppermute | solution.py:337
  208.5 10.9 %collective-permute-start.15 = (f16[8,128,256]{2,1,0:T(8,128)(2,1)S(1)}, f16[8,128,256]{2,1,0:T(8,128)(2,1)S(1)}, u32[]{:S(2)}, u32[]{:S(2)}) collective-permute-start(f16[8,128,256]{2,1,0:T(8,128)(2,1)S(1)} %get-tuple-element.35), channel_id=1, source_target_pairs={{0,16},{4,68},{8,24},{12,76},{16,0},{20,84},{24,8},{28,92},{32,48}... | collective-permute-start | bytes 1572872 | tf_op jit(solution)/shard_map/ppermute | solution.py:343
  210.0 14.9 %collective-permute-start.16 = (f16[8,128,256]{2,1,0:T(8,128)(2,1)S(1)}, f16[8,128,256]{2,1,0:T(8,128)(2,1)S(1)}, u32[]{:S(2)}, u32[]{:S(2)}) collective-permute-start(f16[8,128,256]{2,1,0:T(8,128)(2,1)S(1)} %get-tuple-element.37), channel_id=1, source_target_pairs={{0,8},{4,36},{8,16},{12,44},{16,24},{20,52},{24,0},{28,60},{32,40}... | collective-permute-start | bytes 1572872 | tf_op jit(solution)/shard_map/ppermute | solution.py:343
  210.9 14.0 %collective-permute-start.17 = (f16[8,128,256]{2,1,0:T(8,128)(2,1)S(1)}, f16[8,128,256]{2,1,0:T(8,128)(2,1)S(1)}, u32[]{:S(2)}, u32[]{:S(2)}) collective-permute-start(f16[8,128,256]{2,1,0:T(8,128)(2,1)S(1)} %get-tuple-element.36), channel_id=1, source_target_pairs={{0,24},{4,100},{8,0},{12,108},{16,8},{20,116},{24,16},{28,124},{32... | collective-permute-start | bytes 1572872 | tf_op jit(solution)/shard_map/ppermute | solution.py:343
  225.2 1.6 collective-permute-start.18
Sparse Core Ops, SparseCore 0:
  10.2 76.5 all-gather.2

commit v4 on v3

--- a/solution.py
+++ b/solution.py
@@ -9,7 +9,9 @@
 ROOT_TWO = 1.4142135623730951
 HALF = 512
 PIECES = 8
-CHUNKS = 5
+CHUNKS = 8
+SOURCES = 5
+EARLY = 6
 BLK = 256
 NB = 4
 PHI_MAX_SQ = 36.0
@@ -48,16 +50,6 @@
     return pairs
 
 
-def half_views(chunk_refs):
-    views = []
-    for ref in chunk_refs:
-        if ref.shape[-1] == HALF:
-            views.append((ref, None))
-        else:
-            views.extend((ref, h) for h in range(2))
-    return views
-
-
 def split3(x):
     first = x.astype(jnp.bfloat16)
     rest = x - first.astype(jnp.float32)
@@ -66,37 +58,50 @@
     return first, second, third
 
 
-def density_body(order, where, *refs):
-    chunks = refs[:CHUNKS]
-    (tiles, table, weights, xc, rho, sent, pacc, block_out, held, dmat, tbuf, psem, dsem, tsem) = (
-        refs[CHUNKS:]
-    )
-    for b in range(2):
-        for t in range(16):
-            pltpu.make_async_copy(
-                tiles.at[where[b * 16 + t]],
-                dmat.at[b, pl.ds((t // 4) * BLK, BLK), pl.ds((t % 4) * BLK, BLK)],
-                dsem.at[b],
-            ).start()
-    for i, (ref, h) in enumerate(half_views(chunks)):
-        view = ref if h is None else ref.at[:, pl.ds(h * HALF, HALF)]
-        pltpu.make_async_copy(view, held.at[i], psem.at[i]).start()
-    pltpu.make_async_copy(table.at[order[0]], tbuf.at[0], tsem.at[0]).start()
-    pacc[...] = jnp.zeros_like(pacc)
-    block_out[...] = jnp.zeros_like(block_out)
-    for b in range(2):
-        pltpu.make_async_copy(dmat.at[b], dmat.at[b], dsem.at[b]).wait()
+def assemble_body(place, which, where, *refs):
+    sources = [refs[:SOURCES], refs[SOURCES : 2 * SOURCES]]
+    dmat, sem = refs[2 * SOURCES :]
+    core = place[0]
+    for side in range(2):
+        half = (1 - core) if side else core
+
+        def fetch(n, _, side=side, half=half):
+            b, row, col = n // 16, (n // 4) % 4, n % 4
+            target = dmat.at[
+                b,
+                pl.ds(pl.multiple_of(row * BLK + half * 128, 128), 128),
+                pl.ds(pl.multiple_of(col * BLK, BLK), BLK),
+            ]
+            for k in range(SOURCES):
+
+                @pl.when(which[side * 32 + n] == k)
+                def _(k=k):
+                    pltpu.make_async_copy(
+                        sources[side][k].at[where[side * 32 + n]], target, sem
+                    ).start()
+
+            return 0
+
+        lax.fori_loop(0, 32, fetch, 0)
+    pltpu.make_async_copy(dmat, dmat, sem).wait()
+
+
+def density_steps(order, first, count, chunks, dmat, table, weights, xc, rho, pacc, bufs, top):
+    held, tbuf, psem, tsem = bufs
+    for i in range(count):
+        pltpu.make_async_copy(chunks[i], held.at[i], psem.at[i]).start()
+    pltpu.make_async_copy(table.at[order[first]], tbuf.at[0], tsem.at[0]).start()
 
     def step(i, top):
         slot = lax.rem(i, 2)
 
-        @pl.when(i + 1 < PIECES)
+        @pl.when(i + 1 < count)
         def _():
             pltpu.make_async_copy(
-                table.at[order[i + 1]], tbuf.at[1 - slot], tsem.at[1 - slot]
+                table.at[order[first + i + 1]], tbuf.at[1 - slot], tsem.at[1 - slot]
             ).start()
 
-        pi = order[i]
+        pi = order[first + i]
         b = pi // 4
         pltpu.make_async_copy(held.at[i], held.at[i], psem.at[i]).wait()
         piece = held[i]
@@ -119,7 +124,32 @@
             pacc[b, rows, :] = part
         return jnp.maximum(top, jnp.abs(xc[pi] * total))
 
-    top = lax.fori_loop(0, PIECES, step, jnp.zeros((1, HALF), jnp.float32))
+    return lax.fori_loop(0, count, step, top)
+
+
+def density_first_body(order, *refs):
+    chunks = refs[:EARLY]
+    table, dmat, weights, xc, rho, pacc, top, *bufs = refs[EARLY:]
+    pacc[...] = jnp.zeros_like(pacc)
+    rho[...] = jnp.zeros_like(rho)
+    top[...] = density_steps(
+        order, 0, EARLY, chunks, dmat, table, weights, xc, rho, pacc, bufs,
+        jnp.zeros((1, HALF), jnp.float32),
+    )
+
+
+def density_last_body(order, *refs):
+    count = PIECES - EARLY
+    chunks = refs[:count]
+    (table, dmat, weights, xc, rho_in, pacc_in, top_in, rho, sent, pacc, block_out, *bufs) = (
+        refs[count:]
+    )
+    pacc[...] = pacc_in[...]
+    rho[...] = rho_in[...]
+    block_out[...] = jnp.zeros_like(block_out)
+    top = density_steps(
+        order, EARLY, count, chunks, dmat, table, weights, xc, rho, pacc, bufs, top_in[...]
+    )
     ones = jnp.ones((8, 128), jnp.bfloat16)
     for b in range(2):
         total = jnp.zeros((8, NB * BLK), jnp.float32)
@@ -182,7 +212,8 @@
 
 def ham_body(order, slots, place, *refs):
     chunks = refs[: 2 * CHUNKS]
-    scale_mine, scale_beside, dense, held, rows_of, psem = refs[2 * CHUNKS :]
+    scale_mine, scale_beside, *rest = refs[2 * CHUNKS :]
+    outs, (dense, held, rows_of, psem, osem) = rest[:4], rest[4:]
     core = place[0]
     for side in range(2):
         i = 0
@@ -225,6 +256,10 @@
         return 0
 
     lax.fori_loop(0, 8, step, 0)
+    for d in range(4):
+        pltpu.make_async_copy(dense.at[pl.ds(d * 32, 32)], outs[d], osem.at[d]).start()
+    for d in range(4):
+        pltpu.make_async_copy(dense.at[pl.ds(d * 32, 32)], outs[d], osem.at[d]).wait()
 
 
 def any_spec():
@@ -239,32 +274,72 @@
     return pl.BlockSpec(memory_space=pltpu.SMEM)
 
 
-def density_call(order, where, chunks, tiles, table, weights, xc):
+def assemble_call(place, which, where, sources):
     nbasis = NB * BLK
     return pl.pallas_call(
-        density_body,
+        assemble_body,
+        out_shape=jax.ShapeDtypeStruct((2, nbasis, nbasis), jnp.bfloat16),
+        in_specs=[smem_spec()] * 3 + [any_spec()] * (2 * SOURCES),
+        out_specs=vmem_spec(),
+        scratch_shapes=[pltpu.SemaphoreType.DMA],
+        compiler_params=pltpu.CompilerParams(vmem_limit_bytes=8 << 20),
+        cost_estimate=pl.CostEstimate(flops=0, bytes_accessed=8 << 20, transcendentals=0),
+        name="assemble",
+    )(place, which, where, *sources)
+
+
+def density_buffers(count):
+    nbasis = NB * BLK
+    return [
+        pltpu.VMEM((count, nbasis, HALF), jnp.bfloat16),
+        pltpu.VMEM((2, nbasis, HALF), jnp.float32),
+        pltpu.SemaphoreType.DMA((count,)),
+        pltpu.SemaphoreType.DMA((2,)),
+    ]
+
+
+def density_cost(count):
+    return pl.CostEstimate(
+        flops=2 * count * HALF * 1024 * 1024, bytes_accessed=count * (3 << 20), transcendentals=0
+    )
+
+
+def density_first(order, chunks, table, dmat, weights, xc):
+    return pl.pallas_call(
+        density_first_body,
+        out_shape=(
+            jax.ShapeDtypeStruct((PIECES, 1, HALF), jnp.float32),
+            jax.ShapeDtypeStruct((2, NB * BLK, 128), jnp.float32),
+            jax.ShapeDtypeStruct((1, HALF), jnp.float32),
+        ),
+        in_specs=[smem_spec()] + [any_spec()] * (EARLY + 1) + [vmem_spec()] * 3,
+        out_specs=(vmem_spec(),) * 3,
+        scratch_shapes=density_buffers(EARLY),
+        compiler_params=pltpu.CompilerParams(vmem_limit_bytes=30 << 20),
+        cost_estimate=density_cost(EARLY),
+        name="density_first",
+    )(order, *chunks, table, dmat, weights, xc)
+
+
+def density_last(order, chunks, table, dmat, weights, xc, rho, pacc, top):
+    count = PIECES - EARLY
+    return pl.pallas_call(
+        density_last_body,
         out_shape=(
             jax.ShapeDtypeStruct((PIECES, 1, HALF), jnp.float32),
             jax.ShapeDtypeStruct((32, PAY_ROWS, 128), jnp.float32),
         ),
-        in_specs=[smem_spec(), smem_spec()] + [any_spec()] * (CHUNKS + 2) + [vmem_spec()] * 2,
-        out_specs=(vmem_spec(), vmem_spec()),
+        in_specs=[smem_spec()] + [any_spec()] * (count + 1) + [vmem_spec()] * 6,
+        out_specs=(vmem_spec(),) * 2,
         scratch_shapes=[
-            pltpu.VMEM((2, nbasis, 128), jnp.float32),
+            pltpu.VMEM((2, NB * BLK, 128), jnp.float32),
             pltpu.VMEM((PAY_ROWS, 128), jnp.float32),
-            pltpu.VMEM((PIECES, nbasis, HALF), jnp.bfloat16),
-            pltpu.VMEM((2, nbasis, nbasis), jnp.bfloat16),
-            pltpu.VMEM((2, nbasis, HALF), jnp.float32),
-            pltpu.SemaphoreType.DMA((PIECES,)),
-            pltpu.SemaphoreType.DMA((2,)),
-            pltpu.SemaphoreType.DMA((2,)),
-        ],
-        compiler_params=pltpu.CompilerParams(vmem_limit_bytes=36 << 20),
-        cost_estimate=pl.CostEstimate(
-            flops=2 * 4096 * 1024 * 1024, bytes_accessed=32 << 20, transcendentals=0
-        ),
-        name="density",
-    )(order, where, *chunks, tiles, table, weights, xc)
+        ]
+        + density_buffers(count),
+        compiler_params=pltpu.CompilerParams(vmem_limit_bytes=24 << 20),
+        cost_estimate=density_cost(count),
+        name="density_last",
+    )(order, *chunks, table, dmat, weights, xc, rho, pacc, top)
 
 
 def potential_call(table, got, even, odd, weights, xc, rho, natoms):
@@ -296,13 +371,15 @@
     nbasis = NB * BLK
     return pl.pallas_call(
         ham_body,
-        out_shape=jax.ShapeDtypeStruct((128, 128, BLK), jnp.float32),
+        out_shape=(jax.ShapeDtypeStruct((32, 128, BLK), jnp.float32),) * 4,
         in_specs=[smem_spec()] * 3 + [any_spec()] * (2 * CHUNKS) + [vmem_spec()] * 2,
-        out_specs=vmem_spec(),
+        out_specs=(any_spec(),) * 4,
         scratch_shapes=[
+            pltpu.VMEM((128, 128, BLK), jnp.float32),
             pltpu.VMEM((2, 2, 2, NB, 128, 4 * HALF), jnp.bfloat16),
             pltpu.VMEM((2, 2, 1, 4 * HALF), jnp.float32),
             pltpu.SemaphoreType.DMA,
+            pltpu.SemaphoreType.DMA((4,)),
         ],
         compiler_params=pltpu.CompilerParams(vmem_limit_bytes=38 << 20),
         cost_estimate=pl.CostEstimate(
@@ -327,15 +404,16 @@
     return x.astype(jnp.float32)
 
 
-def ring_sum(parts):
+def ring_sum(parts, factor):
     half = parts[2].shape[0] // 2
-    from_below = lax.ppermute(cast(parts[2][:half]), "grid", core_perm(1, False))
-    from_above = lax.ppermute(cast(parts[2][half:]), "grid", core_perm(-1, False))
-    up = jnp.concatenate([cast(parts[1][:half] + wide(from_below)), cast(parts[1][half:])])
-    down = jnp.concatenate([cast(parts[3][:half]), cast(parts[3][half:] + wide(from_above))])
+    from_below = lax.ppermute(cast(parts[2][:half] * factor), "grid", core_perm(1, False))
+    from_above = lax.ppermute(cast(parts[2][half:] * factor), "grid", core_perm(-1, False))
+    zero = jnp.zeros_like(from_below)
+    up = cast(parts[1] * factor + wide(jnp.concatenate([from_below, zero])))
+    down = cast(parts[3] * factor + wide(jnp.concatenate([zero, from_above])))
     got_below = lax.ppermute(up, "grid", core_perm(1, False))
     got_above = lax.ppermute(down, "grid", core_perm(-1, False))
-    return parts[0] + wide(got_below) + wide(got_above)
+    return parts[0] * factor + wide(got_below) + wide(got_above)
 
 
 def direct_sum(parts):
@@ -370,18 +448,25 @@
     ntiles = tile_home.shape[0]
     slots_here = 2 * neighbors
 
-    own = basis_values.T
-    below = lax.ppermute(own, "pert", ring(1))
-    above = lax.ppermute(own, "pert", ring(3))
-    far0 = lax.ppermute(below[:, :HALF], "pert", ring(1))
-    far1 = lax.ppermute(above[:, HALF:], "pert", ring(3))
-    chunks = [own, below, above, far0, far1]
-    beside = [lax.ppermute(chunk, "grid", grid_perm(0, 0, 1)) for chunk in chunks]
+    own0, own1 = basis_values[:HALF].T, basis_values[HALF:].T
+    below0 = lax.ppermute(own0, "pert", ring(1))
+    above1 = lax.ppermute(own1, "pert", ring(3))
+    below1 = lax.ppermute(own1, "pert", ring(1))
+    above0 = lax.ppermute(own0, "pert", ring(3))
     steps = jnp.array([0, 0, 3, 3, 1, 1, 2, 2], jnp.int32)
     halves = jnp.array([0, 1] * 4, jnp.int32)
     order = ((plane + steps) % 4) * 2 + halves
 
-    tiles = lax.all_gather(resp_density[0], "grid", axis=0, tiled=True)
+    swap = grid_perm(0, 0, 1)
+    first_core = my_c == 0
+    top_half, low_half = resp_density[0, :, :128], resp_density[0, :, 128:]
+    kept = jnp.where(first_core, top_half, low_half)
+    came = lax.ppermute(jnp.where(first_core, low_half, top_half), "grid", swap)
+    base = jnp.concatenate(
+        [jnp.where(first_core, kept, came), jnp.where(first_core, came, kept)], axis=0
+    )
+    ring_tiles = [lax.ppermute(base, "grid", core_perm(-d, False)) for d in (1, 2, 3)]
+
     wanted = tile_list.reshape(-1)
     tile_match = wanted[:, None] == jnp.arange(ntiles, dtype=jnp.int32)[None, :]
     homes = jnp.sum(jnp.where(tile_match, tile_home[None, :], 0), axis=1)
@@ -394,6 +479,22 @@
     ahead = jnp.where(my_c == 0, off_z * 4 + off_x, off_x * 4 + off_z)
     slots = ahead * (2 * tile_dev) + every_home % (2 * tile_dev)
     core_place = my_c.reshape(1).astype(jnp.int32)
+
+    my_owner = homes // tile_dev
+    to_z = (my_owner // 8 - my_z) % 4
+    to_x = ((my_owner // 2) % 4 - my_x) % 4
+    in_chip = homes % (2 * tile_dev)
+
+    def found(one, two):
+        source = jnp.where(two == 2, 2 + one // 2, jnp.where(two == 3, 4, two))
+        return source, jnp.where(two == 2, one % 2, one) * (2 * tile_dev) + in_chip
+
+    own_first = jnp.where(first_core, to_z, to_x)
+    own_second = jnp.where(first_core, to_x, to_z)
+    which_own, where_own = found(own_first, own_second)
+    which_other, where_other = found(own_second, own_first)
+    which = jnp.concatenate([which_own, which_other])
+    where = jnp.concatenate([where_own, where_other])
 
     atom_match = atom_list[:, :, None] == jnp.arange(natoms, dtype=jnp.int32)
     atom_pos = jnp.sum(jnp.where(atom_match[None], atom_coords[:, None, None, :], 0.0), axis=3)
@@ -408,6 +509,11 @@
     weights = point_weights.reshape(PIECES, 1, HALF)
     xc = xc_kernel.reshape(PIECES, 1, HALF)
 
+    ring_tiles, gauss = lax.optimization_barrier((ring_tiles, gauss))
+    stored = jnp.concatenate([base] + ring_tiles, axis=0)
+    ahead_tiles = lax.ppermute(stored, "grid", core_perm(-1, True))
+    behind_tiles = lax.ppermute(stored, "grid", core_perm(1, True))
+
     row = jnp.pad(atom_homes.astype(jnp.float32), (0, 128 - slots_here))
     home_rows = lax.all_to_all(
         jnp.broadcast_to(row[None, None], (groups, 8, 128)), "grid", 0, 0, tiled=True
@@ -425,9 +531,24 @@
         return (wanted_rows[:, None] == held[None, :]).astype(jnp.bfloat16)
 
     even, odd = chooser(0), chooser(1)
-    gauss, hart, even, odd, slots = lax.optimization_barrier((gauss, hart, even, odd, slots))
-
-    rho, sent = density_call(order, homes, chunks, tiles, gauss, weights, xc)
+    below0, above1, hart = lax.optimization_barrier((below0, above1, hart))
+    far0 = lax.ppermute(below0, "pert", ring(1))
+    far1 = lax.ppermute(above1, "pert", ring(3))
+    chunks = [own0, own1, below0, below1, above0, above1, far0, far1]
+    beside = [lax.ppermute(chunk, "grid", swap) for chunk in chunks]
+
+    ahead_tiles, behind_tiles, even, odd, slots = lax.optimization_barrier(
+        (ahead_tiles, behind_tiles, even, odd, slots)
+    )
+    rows2 = 4 * tile_dev
+    far_tiles0 = lax.ppermute(ahead_tiles[:rows2], "grid", core_perm(-1, True))
+    far_tiles1 = lax.ppermute(behind_tiles[rows2:], "grid", core_perm(1, True))
+    sources = [stored, ahead_tiles, far_tiles0, far_tiles1, behind_tiles]
+    sources = sources + [lax.ppermute(s, "grid", swap) for s in sources]
+    dmat = assemble_call(core_place, which, where, sources)
+
+    rho, pacc, top = density_first(order, chunks[:EARLY], gauss, dmat, weights, xc)
+    rho, sent = density_last(order, chunks[EARLY:], gauss, dmat, weights, xc, rho, pacc, top)
     got = lax.all_to_all(sent, "grid", split_axis=0, concat_axis=0, tiled=True)
     all_coeffs, pot, scale, bound = potential_call(
         hart, got.reshape(groups * PAY_ROWS, 128), even, odd, weights, xc, rho, natoms
@@ -436,7 +557,7 @@
     own_coeffs = lax.dynamic_slice_in_dim(all_coeffs, me * atom_dev, atom_dev, axis=0)
     ham_bound = PHI_MAX_SQ * 2048 * 0.05 * groups * bound[0, 0] * 1.01 + 1e-20
 
-    scale_beside = lax.ppermute(scale, "grid", grid_perm(0, 0, 1))
+    scale_beside = lax.ppermute(scale, "grid", swap)
     dense = ham_call(
         order,
         slots,
@@ -446,14 +567,13 @@
         scale_beside.reshape(2, 1, 4 * HALF),
     )
 
-    dense = dense.reshape(4, 4, 2 * tile_dev, 128, BLK)
     factor = F16_TOP / ham_bound
-    chip = direct_sum(list(ring_sum([dense[d] * factor for d in range(4)])))
+    dense = [d.reshape(4, 2 * tile_dev, 128, BLK) for d in dense]
+    chip = direct_sum(list(ring_sum(dense, factor)))
     chip = chip.reshape(2, tile_dev, 128, BLK)
-    first_core = my_c == 0
     keep = jnp.where(first_core, chip[0], chip[1])
     give = jnp.where(first_core, chip[1], chip[0])
-    came = wide(lax.ppermute(cast(give), "grid", grid_perm(0, 0, 1)))
+    came = wide(lax.ppermute(cast(give), "grid", swap))
     hamiltonian = jnp.concatenate(
         [jnp.where(first_core, keep, came), jnp.where(first_core, came, keep)], axis=1
     ) * (ham_bound / F16_TOP)

time: 236 us -> 276 us (1.17)
  waiting for transfers between devices: 83.8 us -> 104 us
  starting transfers between devices: 28.2 us -> 44.8 us
  local copies, waits for them, and re-layouts: 13.6 us -> 29.5 us
  between operations: 14.6 us -> 1.3 us
  blocking collectives: 18.3 us -> 13.2 us
  Pallas kernels: 43.3 us -> 47.7 us
    unnamed x46 -> x77, local copies, waits for them, and re-layouts: 3.73 us -> 22.9 us
    ppermute x13 -> x31, waiting for transfers between devices: 47.8 us -> 63.3 us  [the longest x1 18.5 us: per_device(): far0 = lax.ppermute(below0, 'pert', ring(1))]
    ppermute x13 -> x31, starting transfers between devices: 11.3 us -> 26.5 us  [the longest x3 5.48 us: per_device(): lax.ppermute(base, 'grid', core_perm(-d, False))]
    all_to_all x1, waiting for transfers between devices: 0.01 us -> 6.32 us  [per_device(): lax.all_to_all(jnp.broadcast_to(row[None, None], (groups, 8, 128)), 'grid...]
    mul x1 -> x3, other arithmetic: 6.75 us -> 1.13 us  [the longest x1 0.43 us: ring_sum(): up = cast(parts[1] * factor + wide(jnp.concatenate([from_below, zero])))]
    all_to_all x1, blocking collectives: 18.3 us -> 13.2 us  [per_device(): got = lax.all_to_all(sent, 'grid', split_axis=0, concat_axis=0, tiled=True)]
    ppermute x3, starting transfers between devices: 4.67 us -> 9.27 us  [direct_sum(): lax.ppermute(cast(parts[d]), 'grid', core_perm(d, True))]
    pallas_call x2 -> x4, Pallas kernels: 38.7 us -> 43.1 us  [the longest x1 21.8 us: ham_call(): pl.pallas_call(ham_body, out_shape=(jax.ShapeDtypeStruct((32, 128, BLK),...]
  transfers between devices with their start and end apart: 21 -> 38, of which waited for: 8 -> 18; matrix products, arithmetic and copies ran while one was open for 15% -> 12% of each run, Pallas kernels for 9% -> 9%
where the time goes in v4:
time: 276 us; the launch traced here: 273 us
  waiting for transfers between devices  104 us (38%)
  Pallas kernels  47.7 us (17%)
  starting transfers between devices  44.8 us (16%)
  other arithmetic  32.8 us (12%)
  local copies, waits for them, and re-layouts  29.5 us (11%)
  blocking collectives  13.2 us (5%)
    ppermute x1, waiting for transfers between devices, ring_sum(): got_below = lax.ppermute(up, 'grid', core_perm(1, False))  22.9 us
    unnamed x77, local copies, waits for them, and re-layouts  22.9 us
    pallas_call x1, Pallas kernels, ham_call(): pl.pallas_call(ham_body, out_shape=(jax.ShapeDtypeStruct((32, 128, BLK),...  21.8 us
    ppermute x1, waiting for transfers between devices, per_device(): far0 = lax.ppermute(below0, 'pert', ring(1))  18.5 us
    all_to_all x1, blocking collectives, per_device(): got = lax.all_to_all(sent, 'grid', split_axis=0, concat_axis=0, tiled=True)  13.2 us
    ppermute x1, waiting for transfers between devices, per_device(): ahead_tiles = lax.ppermute(stored, 'grid', core_perm(-1, True))  11.9 us
    pallas_call x1, Pallas kernels, density_first(): pl.pallas_call(density_first_body, out_shape=(jax.ShapeDtypeStruct((PIECE...  11.7 us
    ppermute x1, waiting for transfers between devices, ring_sum(): lax.ppermute(cast(parts[2][:half] * factor), 'grid', core_perm(1, False))  10.1 us
  transfers between devices with their start and end apart: 38, of which 18 were waited for; matrix products, arithmetic and copies ran while one was open for 12% of the time, Pallas kernels for 9%

profile of v4, /device:TPU:0, one launch (start us, length us, event | category | flops | bytes accessed | tf_op | source)
XLA Modules:
  0.0 273.4 jit_solution(10707236939436459374)
XLA Ops:
  3.4 1.8 constant_dynamic-update-slice_fusion.4
  5.2 1.8 constant_dynamic-update-slice_fusion.3
  7.1 4.2 %collective-permute-start.1 = (bf16[8,128,256]{2,1,0:T(8,128)(2,1)S(1)}, bf16[8,128,256]{2,1,0:T(8,128)(2,1)S(1)}, u32[]{:S(2)}, u32[]{:S(2)}) collective-permute-start(bf16[8,128,256]{2,1,0:T(8,128)(2,1)S(1)} %pad_maximum_fusion), channel_id=1, source_target_pairs={{0,96},{4,28},{8,104},{12,4},{16,112},{20,12},{24,120},{28,20},{32... | collective-permute-start | bytes 1572872 | tf_op jit(solution)/shard_map/ppermute | solution.py:468
  11.3 1.3 collective-permute-start.3
  13.1 8.2 %fusion.refs_6_.refs_2_ = f32[8,1024,512]{2,1,0:T(8,128)} fusion(f32[1024]{0:T(1024)S(1)} %div.148, f32[8,16,512]{2,1,0:T(8,128)S(1)} %bitcast.101), kind=kLoop, calls=%fused_computation.3 | loop fusion | flops 4194304 | bytes 17043456 | tf_op jit(solution)/shard_map/exp | solution.py:506
  21.2 2.4 collective-permute-done.1
  23.6 3.7 %collective-permute-done.3 = bf16[8,128,256]{2,1,0:T(8,128)(2,1)S(1)} collective-permute-done((bf16[8,128,256]{2,1,0:T(8,128)(2,1)S(1)}, bf16[8,128,256]{2,1,0:T(8,128)(2,1)S(1)}, u32[]{:S(2)}, u32[]{:S(2)}) %collective-permute-start.3) | collective-permute-done | bytes 524320 | tf_op jit(solution)/shard_map/ppermute | solution.py:468
  29.8 2.8 %collective-permute-start.4 = (bf16[32,128,256]{2,1,0:T(8,128)(2,1)}, bf16[32,128,256]{2,1,0:T(8,128)(2,1)S(1)}, u32[]{:S(2)}, u32[]{:S(2)}) collective-permute-start(bf16[32,128,256]{2,1,0:T(8,128)(2,1)} %constant_dynamic-update-slice_fusion.refs_0_), channel_id=1, source_target_pairs={{0,24},{4,100},{8,0},{12,108},{16,8},{20,116},{24,16},{28,124},{32... | collective-permute-start | bytes 6291464 | tf_op jit(solution)/shard_map/ppermute | solution.py:514
  32.7 1.5 fusion.20
  34.2 1.5 copy.33
  35.7 1.6 collective-permute-start.7
  37.4 2.3 copy.34
  39.6 1.7 collective-permute-start.8
  42.9 1.7 collective-permute-start.10
  44.6 11.9 %collective-permute-done.4.refs_1_ = bf16[32,128,256]{2,1,0:T(8,128)(2,1)S(1)} collective-permute-done((bf16[32,128,256]{2,1,0:T(8,128)(2,1)}, bf16[32,128,256]{2,1,0:T(8,128)(2,1)S(1)}, u32[]{:S(2)}, u32[]{:S(2)}) %collective-permute-start.4) | collective-permute-done | bytes 2097184 | tf_op jit(solution)/shard_map/ppermute | solution.py:514
  56.5 1.6 collective-permute-start.9
  59.1 5.6 %all-to-all-start = ((f32[32,8,128]{2,1,0:T(8,128)}), f32[32,8,128]{2,1,0:T(8,128)S(1)}, u32[]{:S(2)}, u32[]{:S(2)}) async-start(f32[32,8,128]{2,1,0:T(8,128)} %broadcast_in_dim.70), calls=%async_computation | async-start | bytes 262144 | tf_op jit(solution)/shard_map/all_to_all | solution.py:518
  66.1 6.3 %all-to-all-done = f32[32,8,128]{2,1,0:T(8,128)S(1)} async-done(((f32[32,8,128]{2,1,0:T(8,128)}), f32[32,8,128]{2,1,0:T(8,128)S(1)}, u32[]{:S(2)}, u32[]{:S(2)}) %all-to-all-start) | async-done | bytes 131104 | tf_op jit(solution)/shard_map/all_to_all | solution.py:518
  75.5 1.3 slice.56
  76.8 1.4 collective-permute-start.21
  78.9 7.0 %collective-permute-done.10.refs_4_ = bf16[1024,512]{1,0:T(8,128)(2,1)} collective-permute-done((bf16[1024,512]{1,0:T(8,128)(2,1)S(1)}, bf16[1024,512]{1,0:T(8,128)(2,1)}, u32[]{:S(2)}, u32[]{:S(2)}) %collective-permute-start.10) | collective-permute-done | bytes 1048608 | tf_op jit(solution)/shard_map/ppermute | solution.py:455
  86.5 5.4 %collective-permute-done.21.refs_2_ = bf16[16,128,256]{2,1,0:T(8,128)(2,1)} collective-permute-done((bf16[16,128,256]{2,1,0:T(8,128)(2,1)S(1)}, bf16[16,128,256]{2,1,0:T(8,128)(2,1)}, u32[]{:S(2)}, u32[]{:S(2)}) %collective-permute-start.21) | collective-permute-done | bytes 1048608 | tf_op jit(solution)/shard_map/ppermute | solution.py:544
  91.8 2.5 collective-permute-done.22.refs_3_
  94.4 7.4 %bitcast_divide_fusion.table = f32[8,1024,512]{2,1,0:T(8,128)} fusion(f32[1024]{0:T(1024)S(1)} %div.170, f32[8,16,512]{2,1,0:T(8,128)S(1)} %bitcast.100), kind=kLoop, calls=%fused_computation | loop fusion | flops 8388608 | bytes 17043456 | tf_op jit(solution)/shard_map/div | solution.py:508
  102.5 1.6 collective-permute-start.11
  104.0 1.7 collective-permute-start.12
  105.9 4.3 %assemble.1.refs_7_.refs_3_ = bf16[2,1024,1024]{2,1,0:T(8,128)(2,1)S(1)} custom-call(s32[1]{0:T(128)} %bitcast.7.place, s32[64]{0:T(128)S(1)} %get-tuple-element.85.which, s32[64]{0:T(128)S(1)} %get-tuple-element.86.where, bf16[32,128,256]{2,1,0:T(8,128)(2,1)} %constant_dynamic-update-slice_fusion.refs_0_, ...), custom_call_target="tpu_custom_call" | custom-call | bytes 8388608 | tf_op jit(solution)/shard_map/assemble/pallas_call | solution.py:279
  111.0 18.5 %collective-permute-done.11.refs_0_ = bf16[1024,512]{1,0:T(8,128)(2,1)} collective-permute-done((bf16[1024,512]{1,0:T(8,128)(2,1)}, bf16[1024,512]{1,0:T(8,128)(2,1)}, u32[]{:S(2)}, u32[]{:S(2)}) %collective-permute-start.11) | collective-permute-done | bytes 1048608 | tf_op jit(solution)/shard_map/ppermute | solution.py:535
  130.1 11.7 %density_first.1 = (f32[8,1,512]{2,1,0:T(1,128)S(1)}, f32[2,1024,128]{2,1,0:T(8,128)S(1)}, f32[1,512]{1,0:T(1,128)S(1)}) custom-call(s32[8]{0:T(128)S(1)} %fusion.9.order, bf16[1024,512]{1,0:T(8,128)(2,1)S(1)} %bitcast.81, bf16[1024,512]{1,0:T(8,128)(2,1)} %bitcast.10.refs_1_, bf16[1024,512]{1,0:T(8,128)(2,1)} %collective-permute-done.7.refs_2_, ...), custom_call_target="tpu_custom_call" | custom-call | flops 6442450944 | bytes 18874368 | tf_op jit(solution)/shard_map/density_first/pallas_call | solution.py:308
  141.9 5.3 %density_last.1 = (f32[8,1,512]{2,1,0:T(1,128)S(1)}, f32[32,24,128]{2,1,0:T(8,128)S(1)}) custom-call(s32[8]{0:T(128)S(1)} %fusion.9.order, bf16[1024,512]{1,0:T(8,128)(2,1)} %collective-permute-done.11.refs_0_, bf16[1024,512]{1,0:T(8,128)(2,1)} %collective-permute-done.12.refs_1_, f32[8,1024,512]{2,1,0:T(8,128)S(1)} %bitcast.77, ...), custom_call_target="tpu_custom_call" | custom-call | flops 2147483648 | bytes 6291456 | tf_op jit(solution)/shard_map/density_last/pallas_call | solution.py:326
  147.2 13.2 %all_to_all.10 = f32[32,24,128]{2,1,0:T(8,128)S(1)} all-to-all(f32[32,24,128]{2,1,0:T(8,128)S(1)} %get-tuple-element.41), channel_id=1, replica_groups=mesh['grid'=32,'pert'=4] {'grid'}, dimensions={0} | all-to-all | bytes 786432 | tf_op jit(solution)/shard_map/all_to_all | solution.py:552
  160.4 5.8 %copy-done = f32[8,1024,512]{2,1,0:T(8,128)S(1)} copy-done((f32[8,1024,512]{2,1,0:T(8,128)S(1)}, f32[8,1024,512]{2,1,0:T(8,128)}, u32[]{:S(2)}) %copy-start) | copy-done | bytes 16777240
  166.1 4.6 %potential.1 = (f32[256,64]{1,0:T(8,128)S(1)}, f32[8,1,512]{2,1,0:T(1,128)}, f32[8,1,512]{2,1,0:T(1,128)S(1)}, f32[1,128]{1,0:T(1,128)S(1)}) custom-call(f32[8,1024,512]{2,1,0:T(8,128)S(1)} %copy-done, f32[768,128]{1,0:T(8,128)S(1)} %bitcast.83, bf16[288,768]{1,0:T(8,128)(2,1)S(1)} %copy-done.5, bf16[288,768]{1,0:T(8,128)(2,1)S(1)} %copy-done.4, ...), custom_call_target="tpu_custom_call" | custom-call | flops 16777216 | bytes 16777216 | tf_op jit(solution)/shard_map/potential/pallas_call | solution.py:347
  176.3 1.2 copy-done.11
  178.7 1.2 copy-done.15
  180.0 21.8 %ham.1 = (f32[32,128,256]{2,1,0:T(8,128)}, f32[32,128,256]{2,1,0:T(8,128)}, f32[32,128,256]{2,1,0:T(8,128)}, f32[32,128,256]{2,1,0:T(8,128)}) custom-call(s32[8]{0:T(128)S(1)} %fusion.9.order, s32[64]{0:T(128)S(1)} %fusion.6.slots, s32[1]{0:T(128)} %bitcast.7.place, bf16[4,2,128,512]{3,2,1,0:T(8,128)(2,1)S(1)} %bitcast.82, ...), custom_call_target="tpu_custom_call" | custom-call | flops 8589934592 | bytes 33554432 | tf_op jit(solution)/shard_map/ham/pallas_call | solution.py:372
  201.8 3.0 %multiply_convert_fusion.1 = (f16[16,128,256]{2,1,0:T(8,128)(2,1)S(1)}, f16[16,128,256]{2,1,0:T(8,128)(2,1)S(1)}) fusion(f32[32,128,256]{2,1,0:T(8,128)} %get-tuple-element.49, f32[]{:T(128)} %bitcast.33), kind=kLoop, calls=%fused_computation.8 | loop fusion | flops 2097152 | bytes 6291460 | tf_op jit(solution)/shard_map/convert_element_type | solution.py:400
  205.5 2.6 collective-permute-start.31
  208.5 1.8 copy-done.17
  210.7 10.1 %collective-permute-done.29 = f16[2,8,128,256]{3,2,1,0:T(8,128)(2,1)S(1)} collective-permute-done((f16[2,8,128,256]{3,2,1,0:T(8,128)(2,1)S(1)}, f16[2,8,128,256]{3,2,1,0:T(8,128)(2,1)S(1)}, u32[]{:S(2)}, u32[]{:S(2)}) %collective-permute-start.29) | collective-permute-done | bytes 1048608 | tf_op jit(solution)/shard_map/ppermute | solution.py:409
  222.4 3.3 %collective-permute-start.32 = (f16[4,8,128,256]{3,2,1,0:T(8,128)(2,1)S(1)}, f16[4,8,128,256]{3,2,1,0:T(8,128)(2,1)S(1)}, u32[]{:S(2)}, u32[]{:S(2)}) collective-permute-start(f16[4,8,128,256]{3,2,1,0:T(8,128)(2,1)S(1)} %add_convert_fusion), channel_id=1, source_target_pairs={{0,96},{4,28},{8,104},{12,4},{16,112},{20,12},{24,120},{28,20},{32... | collective-permute-start | bytes 6291464 | tf_op jit(solution)/shard_map/ppermute | solution.py:415
  225.9 22.9 %collective-permute-done.30 = f16[4,8,128,256]{3,2,1,0:T(8,128)(2,1)S(1)} collective-permute-done((f16[4,8,128,256]{3,2,1,0:T(8,128)(2,1)S(1)}, f16[4,8,128,256]{3,2,1,0:T(8,128)(2,1)S(1)}, u32[]{:S(2)}, u32[]{:S(2)}) %collective-permute-start.30) | collective-permute-done | bytes 2097184 | tf_op jit(solution)/shard_map/ppermute | solution.py:414
  249.2 1.3 fusion.19
  252.1 5.5 %collective-permute-start.34 = (f16[8,128,256]{2,1,0:T(8,128)(2,1)S(1)}, f16[8,128,256]{2,1,0:T(8,128)(2,1)S(1)}, u32[]{:S(2)}, u32[]{:S(2)}) collective-permute-start(f16[8,128,256]{2,1,0:T(8,128)(2,1)S(1)} %get-tuple-element.69), channel_id=1, source_target_pairs={{0,8},{4,36},{8,16},{12,44},{16,24},{20,52},{24,0},{28,60},{32,40}... | collective-permute-start | bytes 1572872 | tf_op jit(solution)/shard_map/ppermute | solution.py:421
  257.6 2.6 collective-permute-start.35
  260.1 1.5 collective-permute-done.33
  261.6 5.7 %collective-permute-done.34 = f16[8,128,256]{2,1,0:T(8,128)(2,1)S(1)} collective-permute-done((f16[8,128,256]{2,1,0:T(8,128)(2,1)S(1)}, f16[8,128,256]{2,1,0:T(8,128)(2,1)S(1)}, u32[]{:S(2)}, u32[]{:S(2)}) %collective-permute-start.34) | collective-permute-done | bytes 524320 | tf_op jit(solution)/shard_map/ppermute | solution.py:421
  267.3 3.0 %collective-permute-done.35 = f16[8,128,256]{2,1,0:T(8,128)(2,1)S(1)} collective-permute-done((f16[8,128,256]{2,1,0:T(8,128)(2,1)S(1)}, f16[8,128,256]{2,1,0:T(8,128)(2,1)S(1)}, u32[]{:S(2)}, u32[]{:S(2)}) %collective-permute-start.35) | collective-permute-done | bytes 524320 | tf_op jit(solution)/shard_map/ppermute | solution.py:421
  (167 shorter events, 31.1 us)
Async XLA Ops:
  1.8 1.6 collective-permute-start
  7.1 16.5 %collective-permute-start.1 = (bf16[8,128,256]{2,1,0:T(8,128)(2,1)S(1)}, bf16[8,128,256]{2,1,0:T(8,128)(2,1)S(1)}, u32[]{:S(2)}, u32[]{:S(2)}) collective-permute-start(bf16[8,128,256]{2,1,0:T(8,128)(2,1)S(1)} %pad_maximum_fusion), channel_id=1, source_target_pairs={{0,96},{4,28},{8,104},{12,4},{16,112},{20,12},{24,120},{28,20},{32... | collective-permute-start | bytes 1572872 | tf_op jit(solution)/shard_map/ppermute | solution.py:468
  11.3 12.3 %collective-permute-start.2 = (bf16[8,128,256]{2,1,0:T(8,128)(2,1)S(1)}, bf16[8,128,256]{2,1,0:T(8,128)(2,1)S(1)}, u32[]{:S(2)}, u32[]{:S(2)}) collective-permute-start(bf16[8,128,256]{2,1,0:T(8,128)(2,1)S(1)} %pad_maximum_fusion), channel_id=1, source_target_pairs={{0,64},{4,20},{8,72},{12,28},{16,80},{20,4},{24,88},{28,12},{32,96... | collective-permute-start | bytes 1572872 | tf_op jit(solution)/shard_map/ppermute | solution.py:468
  11.3 16.0 %collective-permute-start.3 = (bf16[8,128,256]{2,1,0:T(8,128)(2,1)S(1)}, bf16[8,128,256]{2,1,0:T(8,128)(2,1)S(1)}, u32[]{:S(2)}, u32[]{:S(2)}) collective-permute-start(bf16[8,128,256]{2,1,0:T(8,128)(2,1)S(1)} %pad_maximum_fusion), channel_id=1, source_target_pairs={{0,32},{4,12},{8,40},{12,20},{16,48},{20,28},{24,56},{28,4},{32,64... | collective-permute-start | bytes 1572872 | tf_op jit(solution)/shard_map/ppermute | solution.py:468
  29.8 28.3 %copy-start.21 = (s32[2,16]{1,0:T(2,128)S(1)}, s32[2,16]{1,0:T(2,128)}, u32[]{:S(2)}) copy-start(s32[2,16]{1,0:T(2,128)} %param.22) | copy-start | bytes 388
  29.8 28.3 %copy-start.23 = (s32[256]{0:T(256)S(1)}, s32[256]{0:T(256)}, u32[]{:S(2)}) copy-start(s32[256]{0:T(256)} %param.23) | copy-start | bytes 3076
  29.8 26.7 %collective-permute-start.4 = (bf16[32,128,256]{2,1,0:T(8,128)(2,1)}, bf16[32,128,256]{2,1,0:T(8,128)(2,1)S(1)}, u32[]{:S(2)}, u32[]{:S(2)}) collective-permute-start(bf16[32,128,256]{2,1,0:T(8,128)(2,1)} %constant_dynamic-update-slice_fusion.refs_0_), channel_id=1, source_target_pairs={{0,24},{4,100},{8,0},{12,108},{16,8},{20,116},{24,16},{28,124},{32... | collective-permute-start | bytes 6291464 | tf_op jit(solution)/shard_map/ppermute | solution.py:514
  32.7 42.7 %collective-permute-start.5 = (bf16[32,128,256]{2,1,0:T(8,128)(2,1)}, bf16[32,128,256]{2,1,0:T(8,128)(2,1)}, u32[]{:S(2)}, u32[]{:S(2)}) collective-permute-start(bf16[32,128,256]{2,1,0:T(8,128)(2,1)} %constant_dynamic-update-slice_fusion.refs_0_), channel_id=1, source_target_pairs={{0,8},{4,36},{8,16},{12,44},{16,24},{20,52},{24,0},{28,60},{32,40}... | collective-permute-start | bytes 6291464 | tf_op jit(solution)/shard_map/ppermute | solution.py:515
  35.7 66.1 %copy-start.1 = (bf16[512,1024]{0,1:T(8,128)(2,1)}, bf16[512,1024]{0,1:T(8,128)(2,1)S(1)}, u32[]{:S(2)}) copy-start(bf16[512,1024]{0,1:T(8,128)(2,1)S(1)} %copy.33) | copy-start | bytes 3145732
  35.7 41.1 %collective-permute-start.7 = (bf16[1024,512]{1,0:T(8,128)(2,1)S(1)}, bf16[1024,512]{1,0:T(8,128)(2,1)}, u32[]{:S(2)}, u32[]{:S(2)}) collective-permute-start(bf16[1024,512]{1,0:T(8,128)(2,1)S(1)} %bitcast.78), channel_id=1, source_target_pairs={{0,1},{1,2},{2,3},{3,0},{4,5},{5,6},{6,7},{7,4},{8,9},{9,10},{10,1... | collective-permute-start | bytes 3145736 | tf_op jit(solution)/shard_map/ppermute | solution.py:452
  39.6 38.6 %collective-permute-start.8 = (bf16[1024,512]{1,0:T(8,128)(2,1)}, bf16[1024,512]{1,0:T(8,128)(2,1)}, u32[]{:S(2)}, u32[]{:S(2)}) collective-permute-start(bf16[1024,512]{1,0:T(8,128)(2,1)} %bitcast.10.refs_1_), channel_id=1, source_target_pairs={{0,3},{1,0},{2,1},{3,2},{4,7},{5,4},{6,5},{7,6},{8,11},{9,8},{10,9... | collective-permute-start | bytes 3145736 | tf_op jit(solution)/shard_map/ppermute | solution.py:453
  41.6 1.2 collective-permute-start.6
  42.9 43.1 %collective-permute-start.10 = (bf16[1024,512]{1,0:T(8,128)(2,1)S(1)}, bf16[1024,512]{1,0:T(8,128)(2,1)}, u32[]{:S(2)}, u32[]{:S(2)}) collective-permute-start(bf16[1024,512]{1,0:T(8,128)(2,1)S(1)} %bitcast.79), channel_id=1, source_target_pairs={{0,3},{1,0},{2,1},{3,2},{4,7},{5,4},{6,5},{7,6},{8,11},{9,8},{10,9... | collective-permute-start | bytes 3145736 | tf_op jit(solution)/shard_map/ppermute | solution.py:455
  56.5 29.4 %collective-permute-start.9 = (bf16[1024,512]{1,0:T(8,128)(2,1)}, bf16[1024,512]{1,0:T(8,128)(2,1)}, u32[]{:S(2)}, u32[]{:S(2)}) collective-permute-start(bf16[1024,512]{1,0:T(8,128)(2,1)} %bitcast.10.refs_1_), channel_id=1, source_target_pairs={{0,1},{1,2},{2,3},{3,0},{4,5},{5,6},{6,7},{7,4},{8,9},{9,10},{10,1... | collective-permute-start | bytes 3145736 | tf_op jit(solution)/shard_map/ppermute | solution.py:454
  59.1 13.4 %all-to-all-start = ((f32[32,8,128]{2,1,0:T(8,128)}), f32[32,8,128]{2,1,0:T(8,128)S(1)}, u32[]{:S(2)}, u32[]{:S(2)}) async-start(f32[32,8,128]{2,1,0:T(8,128)} %broadcast_in_dim.70), calls=%async_computation | async-start | bytes 262144 | tf_op jit(solution)/shard_map/all_to_all | solution.py:518
  75.3 26.5 %collective-permute-start.23 = (bf16[32,128,256]{2,1,0:T(8,128)(2,1)}, bf16[32,128,256]{2,1,0:T(8,128)(2,1)}, u32[]{:S(2)}, u32[]{:S(2)}) collective-permute-start(bf16[32,128,256]{2,1,0:T(8,128)(2,1)} %constant_dynamic-update-slice_fusion.refs_0_), channel_id=1, source_target_pairs={{0,4},{4,0},{8,12},{12,8},{16,20},{20,16},{24,28},{28,24},{32,36},... | collective-permute-start | bytes 6291464 | tf_op jit(solution)/shard_map/ppermute | solution.py:547
  76.8 15.0 %collective-permute-start.21 = (bf16[16,128,256]{2,1,0:T(8,128)(2,1)S(1)}, bf16[16,128,256]{2,1,0:T(8,128)(2,1)}, u32[]{:S(2)}, u32[]{:S(2)}) collective-permute-start(bf16[16,128,256]{2,1,0:T(8,128)(2,1)S(1)} %slice.55), channel_id=1, source_target_pairs={{0,24},{4,100},{8,0},{12,108},{16,8},{20,116},{24,16},{28,124},{32... | collective-permute-start | bytes 3145736 | tf_op jit(solution)/shard_map/ppermute | solution.py:544
  78.2 16.1 %collective-permute-start.22 = (bf16[16,128,256]{2,1,0:T(8,128)(2,1)S(1)}, bf16[16,128,256]{2,1,0:T(8,128)(2,1)}, u32[]{:S(2)}, u32[]{:S(2)}) collective-permute-start(bf16[16,128,256]{2,1,0:T(8,128)(2,1)S(1)} %slice.56), channel_id=1, source_target_pairs={{0,8},{4,36},{8,16},{12,44},{16,24},{20,52},{24,0},{28,60},{32,40}... | collective-permute-start | bytes 3145736 | tf_op jit(solution)/shard_map/ppermute | solution.py:545
  85.9 18.1 %collective-permute-start.24 = (bf16[32,128,256]{2,1,0:T(8,128)(2,1)S(1)}, bf16[32,128,256]{2,1,0:T(8,128)(2,1)}, u32[]{:S(2)}, u32[]{:S(2)}) collective-permute-start(bf16[32,128,256]{2,1,0:T(8,128)(2,1)S(1)} %collective-permute-done.4.refs_1_), channel_id=1, source_target_pairs={{0,4},{4,0},{8,12},{12,8},{16,20},{20,16},{24,28},{28,24},{32,36},... | collective-permute-start | bytes 6291464 | tf_op jit(solution)/shard_map/ppermute | solution.py:547
  85.9 19.8 %collective-permute-start.27 = (bf16[32,128,256]{2,1,0:T(8,128)(2,1)}, bf16[32,128,256]{2,1,0:T(8,128)(2,1)}, u32[]{:S(2)}, u32[]{:S(2)}) collective-permute-start(bf16[32,128,256]{2,1,0:T(8,128)(2,1)} %collective-permute-done.5.refs_4_), channel_id=1, source_target_pairs={{0,4},{4,0},{8,12},{12,8},{16,20},{20,16},{24,28},{28,24},{32,36},... | collective-permute-start | bytes 6291464 | tf_op jit(solution)/shard_map/ppermute | solution.py:547
  91.8 10.5 %collective-permute-start.25 = (bf16[16,128,256]{2,1,0:T(8,128)(2,1)}, bf16[16,128,256]{2,1,0:T(8,128)(2,1)}, u32[]{:S(2)}, u32[]{:S(2)}) collective-permute-start(bf16[16,128,256]{2,1,0:T(8,128)(2,1)} %collective-permute-done.21.refs_2_), channel_id=1, source_target_pairs={{0,4},{4,0},{8,12},{12,8},{16,20},{20,16},{24,28},{28,24},{32,36},... | collective-permute-start | bytes 3145736 | tf_op jit(solution)/shard_map/ppermute | solution.py:547
  94.3 8.1 %collective-permute-start.26 = (bf16[16,128,256]{2,1,0:T(8,128)(2,1)}, bf16[16,128,256]{2,1,0:T(8,128)(2,1)}, u32[]{:S(2)}, u32[]{:S(2)}) collective-permute-start(bf16[16,128,256]{2,1,0:T(8,128)(2,1)} %collective-permute-done.22.refs_3_), channel_id=1, source_target_pairs={{0,4},{4,0},{8,12},{12,8},{16,20},{20,16},{24,28},{28,24},{32,36},... | collective-permute-start | bytes 3145736 | tf_op jit(solution)/shard_map/ppermute | solution.py:547
  101.9 8.4 %collective-permute-start.13 = (bf16[1024,512]{1,0:T(8,128)(2,1)S(1)}, bf16[1024,512]{1,0:T(8,128)(2,1)}, u32[]{:S(2)}, u32[]{:S(2)}) collective-permute-start(bf16[1024,512]{1,0:T(8,128)(2,1)S(1)} %bitcast.80), channel_id=1, source_target_pairs={{0,4},{4,0},{8,12},{12,8},{16,20},{20,16},{24,28},{28,24},{32,36},... | collective-permute-start | bytes 3145736 | tf_op jit(solution)/shard_map/ppermute | solution.py:538
  102.4 8.5 %collective-permute-start.14 = (bf16[1024,512]{1,0:T(8,128)(2,1)}, bf16[1024,512]{1,0:T(8,128)(2,1)}, u32[]{:S(2)}, u32[]{:S(2)}) collective-permute-start(bf16[1024,512]{1,0:T(8,128)(2,1)} %bitcast.10.refs_1_), channel_id=1, source_target_pairs={{0,4},{4,0},{8,12},{12,8},{16,20},{20,16},{24,28},{28,24},{32,36},... | collective-permute-start | bytes 3145736 | tf_op jit(solution)/shard_map/ppermute | solution.py:538
  102.5 27.0 %collective-permute-start.11 = (bf16[1024,512]{1,0:T(8,128)(2,1)}, bf16[1024,512]{1,0:T(8,128)(2,1)}, u32[]{:S(2)}, u32[]{:S(2)}) collective-permute-start(bf16[1024,512]{1,0:T(8,128)(2,1)} %collective-permute-done.7.refs_2_), channel_id=1, source_target_pairs={{0,1},{1,2},{2,3},{3,0},{4,5},{5,6},{6,7},{7,4},{8,9},{9,10},{10,1... | collective-permute-start | bytes 3145736 | tf_op jit(solution)/shard_map/ppermute | solution.py:535
  104.0 25.5 %collective-permute-start.12 = (bf16[1024,512]{1,0:T(8,128)(2,1)}, bf16[1024,512]{1,0:T(8,128)(2,1)}, u32[]{:S(2)}, u32[]{:S(2)}) collective-permute-start(bf16[1024,512]{1,0:T(8,128)(2,1)} %collective-permute-done.8.refs_5_), channel_id=1, source_target_pairs={{0,3},{1,0},{2,1},{3,2},{4,7},{5,4},{6,5},{7,6},{8,11},{9,8},{10,9... | collective-permute-start | bytes 3145736 | tf_op jit(solution)/shard_map/ppermute | solution.py:536
  105.7 24.3 %collective-permute-start.15 = (bf16[1024,512]{1,0:T(8,128)(2,1)}, bf16[1024,512]{1,0:T(8,128)(2,1)}, u32[]{:S(2)}, u32[]{:S(2)}) collective-permute-start(bf16[1024,512]{1,0:T(8,128)(2,1)} %collective-permute-done.7.refs_2_), channel_id=1, source_target_pairs={{0,4},{4,0},{8,12},{12,8},{16,20},{20,16},{24,28},{28,24},{32,36},... | collective-permute-start | bytes 3145736 | tf_op jit(solution)/shard_map/ppermute | solution.py:538
  105.9 24.2 %copy-start.2 = (bf16[512,1024]{0,1:T(8,128)(2,1)S(1)}, bf16[512,1024]{0,1:T(8,128)(2,1)}, u32[]{:S(2)}) copy-start(bf16[512,1024]{0,1:T(8,128)(2,1)} %copy-done.1) | copy-start | bytes 3145732
  105.9 24.2 %copy-start.6 = (f32[4096]{0:T(1024)S(1)}, f32[4096]{0:T(1024)}, u32[]{:S(2)}) copy-start(f32[4096]{0:T(1024)} %param.15) | copy-start | bytes 49156
  105.9 24.2 %copy-start.7 = (f32[4096]{0:T(1024)S(1)}, f32[4096]{0:T(1024)}, u32[]{:S(2)}) copy-start(f32[4096]{0:T(1024)} %param.16) | copy-start | bytes 49156
  105.9 35.9 %slice-start = ((s8[16777216]{0:T(1024)(128)(4,1)}), s8[4194304]{0:T(1024)(128)(4,1)S(1)}, s32[]{:S(2)}) async-start(s8[16777216]{0:T(1024)(128)(4,1)} %bitcast.76), calls=%async_computation.2 | async-start | bytes 8388608
  105.9 35.9 %slice-start.1 = ((s8[16777216]{0:T(1024)(128)(4,1)}), s8[4194304]{0:T(1024)(128)(4,1)S(1)}, s32[]{:S(2)}) async-start(s8[16777216]{0:T(1024)(128)(4,1)} %bitcast.76), calls=%async_computation.3 | async-start | bytes 8388608
  110.3 60.4 %collective-permute-start.18 = (bf16[1024,512]{1,0:T(8,128)(2,1)}, bf16[1024,512]{1,0:T(8,128)(2,1)S(1)}, u32[]{:S(2)}, u32[]{:S(2)}) collective-permute-start(bf16[1024,512]{1,0:T(8,128)(2,1)} %collective-permute-done.8.refs_5_), channel_id=1, source_target_pairs={{0,4},{4,0},{8,12},{12,8},{16,20},{20,16},{24,28},{28,24},{32,36},... | collective-permute-start | bytes 3145736 | tf_op jit(solution)/shard_map/ppermute | solution.py:538
  110.9 61.1 %collective-permute-start.16 = (bf16[1024,512]{1,0:T(8,128)(2,1)}, bf16[1024,512]{1,0:T(8,128)(2,1)S(1)}, u32[]{:S(2)}, u32[]{:S(2)}) collective-permute-start(bf16[1024,512]{1,0:T(8,128)(2,1)} %collective-permute-done.9.refs_3_), channel_id=1, source_target_pairs={{0,4},{4,0},{8,12},{12,8},{16,20},{20,16},{24,28},{28,24},{32,36},... | collective-permute-start | bytes 3145736 | tf_op jit(solution)/shard_map/ppermute | solution.py:538
  129.5 43.5 %collective-permute-start.17 = (bf16[1024,512]{1,0:T(8,128)(2,1)}, bf16[1024,512]{1,0:T(8,128)(2,1)S(1)}, u32[]{:S(2)}, u32[]{:S(2)}) collective-permute-start(bf16[1024,512]{1,0:T(8,128)(2,1)} %collective-permute-done.10.refs_4_), channel_id=1, source_target_pairs={{0,4},{4,0},{8,12},{12,8},{16,20},{20,16},{24,28},{28,24},{32,36},... | collective-permute-start | bytes 3145736 | tf_op jit(solution)/shard_map/ppermute | solution.py:538
  129.6 44.5 %collective-permute-start.19 = (bf16[1024,512]{1,0:T(8,128)(2,1)}, bf16[1024,512]{1,0:T(8,128)(2,1)S(1)}, u32[]{:S(2)}, u32[]{:S(2)}) collective-permute-start(bf16[1024,512]{1,0:T(8,128)(2,1)} %collective-permute-done.11.refs_0_), channel_id=1, source_target_pairs={{0,4},{4,0},{8,12},{12,8},{16,20},{20,16},{24,28},{28,24},{32,36},... | collective-permute-start | bytes 3145736 | tf_op jit(solution)/shard_map/ppermute | solution.py:538
  130.0 45.1 %collective-permute-start.20 = (bf16[1024,512]{1,0:T(8,128)(2,1)}, bf16[1024,512]{1,0:T(8,128)(2,1)}, u32[]{:S(2)}, u32[]{:S(2)}) collective-permute-start(bf16[1024,512]{1,0:T(8,128)(2,1)} %collective-permute-done.12.refs_1_), channel_id=1, source_target_pairs={{0,4},{4,0},{8,12},{12,8},{16,20},{20,16},{24,28},{28,24},{32,36},... | collective-permute-start | bytes 3145736 | tf_op jit(solution)/shard_map/ppermute | solution.py:538
  141.8 18.5 %copy-start.4 = (bf16[288,768]{1,0:T(8,128)(2,1)S(1)}, bf16[288,768]{1,0:T(8,128)(2,1)}, u32[]{:S(2)}) copy-start(bf16[288,768]{1,0:T(8,128)(2,1)} %get-tuple-element.43.odd) | copy-start | bytes 1327108
  141.9 18.5 %copy-start.5 = (bf16[288,768]{1,0:T(8,128)(2,1)S(1)}, bf16[288,768]{1,0:T(8,128)(2,1)}, u32[]{:S(2)}) copy-start(bf16[288,768]{1,0:T(8,128)(2,1)} %get-tuple-element.42.even) | copy-start | bytes 1327108
  171.7 3.3 %collective-permute-start.28 = (f32[8,1,512]{2,1,0:T(1,128)S(1)}, f32[8,1,512]{2,1,0:T(1,128)S(1)}, u32[]{:S(2)}, u32[]{:S(2)}) collective-permute-start(f32[8,1,512]{2,1,0:T(1,128)S(1)} %get-tuple-element.45), channel_id=1, source_target_pairs={{0,4},{4,0},{8,12},{12,8},{16,20},{20,16},{24,28},{28,24},{32,36},... | collective-permute-start | bytes 49160 | tf_op jit(solution)/shard_map/ppermute | solution.py:560
  204.8 16.1 %collective-permute-start.29 = (f16[2,8,128,256]{3,2,1,0:T(8,128)(2,1)S(1)}, f16[2,8,128,256]{3,2,1,0:T(8,128)(2,1)S(1)}, u32[]{:S(2)}, u32[]{:S(2)}) collective-permute-start(f16[2,8,128,256]{3,2,1,0:T(8,128)(2,1)S(1)} %bitcast.103), channel_id=1, source_target_pairs={{0,32},{4,12},{8,40},{12,20},{16,48},{20,28},{24,56},{28,4},{32,64... | collective-permute-start | bytes 3145736 | tf_op jit(solution)/shard_map/ppermute | solution.py:409
  205.5 16.2 %collective-permute-start.31 = (f16[2,8,128,256]{3,2,1,0:T(8,128)(2,1)S(1)}, f16[2,8,128,256]{3,2,1,0:T(8,128)(2,1)S(1)}, u32[]{:S(2)}, u32[]{:S(2)}) collective-permute-start(f16[2,8,128,256]{3,2,1,0:T(8,128)(2,1)S(1)} %bitcast.102), channel_id=1, source_target_pairs={{0,96},{4,28},{8,104},{12,4},{16,112},{20,12},{24,120},{28,20},{32... | collective-permute-start | bytes 3145736 | tf_op jit(solution)/shard_map/ppermute | solution.py:410
  221.6 27.3 %collective-permute-start.30 = (f16[4,8,128,256]{3,2,1,0:T(8,128)(2,1)S(1)}, f16[4,8,128,256]{3,2,1,0:T(8,128)(2,1)S(1)}, u32[]{:S(2)}, u32[]{:S(2)}) collective-permute-start(f16[4,8,128,256]{3,2,1,0:T(8,128)(2,1)S(1)} %add_convert_fusion.1), channel_id=1, source_target_pairs={{0,32},{4,12},{8,40},{12,20},{16,48},{20,28},{24,56},{28,4},{32,64... | collective-permute-start | bytes 6291464 | tf_op jit(solution)/shard_map/ppermute | solution.py:414
  222.4 26.8 %collective-permute-start.32 = (f16[4,8,128,256]{3,2,1,0:T(8,128)(2,1)S(1)}, f16[4,8,128,256]{3,2,1,0:T(8,128)(2,1)S(1)}, u32[]{:S(2)}, u32[]{:S(2)}) collective-permute-start(f16[4,8,128,256]{3,2,1,0:T(8,128)(2,1)S(1)} %add_convert_fusion), channel_id=1, source_target_pairs={{0,96},{4,28},{8,104},{12,4},{16,112},{20,12},{24,120},{28,20},{32... | collective-permute-start | bytes 6291464 | tf_op jit(solution)/shard_map/ppermute | solution.py:415
  250.9 10.8 %collective-permute-start.33 = (f16[8,128,256]{2,1,0:T(8,128)(2,1)S(1)}, f16[8,128,256]{2,1,0:T(8,128)(2,1)S(1)}, u32[]{:S(2)}, u32[]{:S(2)}) collective-permute-start(f16[8,128,256]{2,1,0:T(8,128)(2,1)S(1)} %get-tuple-element.67), channel_id=1, source_target_pairs={{0,16},{4,68},{8,24},{12,76},{16,0},{20,84},{24,8},{28,92},{32,48}... | collective-permute-start | bytes 1572872 | tf_op jit(solution)/shard_map/ppermute | solution.py:421
  252.1 15.2 %collective-permute-start.34 = (f16[8,128,256]{2,1,0:T(8,128)(2,1)S(1)}, f16[8,128,256]{2,1,0:T(8,128)(2,1)S(1)}, u32[]{:S(2)}, u32[]{:S(2)}) collective-permute-start(f16[8,128,256]{2,1,0:T(8,128)(2,1)S(1)} %get-tuple-element.69), channel_id=1, source_target_pairs={{0,8},{4,36},{8,16},{12,44},{16,24},{20,52},{24,0},{28,60},{32,40}... | collective-permute-start | bytes 1572872 | tf_op jit(solution)/shard_map/ppermute | solution.py:421
  257.6 12.7 %collective-permute-start.35 = (f16[8,128,256]{2,1,0:T(8,128)(2,1)S(1)}, f16[8,128,256]{2,1,0:T(8,128)(2,1)S(1)}, u32[]{:S(2)}, u32[]{:S(2)}) collective-permute-start(f16[8,128,256]{2,1,0:T(8,128)(2,1)S(1)} %get-tuple-element.68), channel_id=1, source_target_pairs={{0,24},{4,100},{8,0},{12,108},{16,8},{20,116},{24,16},{28,124},{32... | collective-permute-start | bytes 1572872 | tf_op jit(solution)/shard_map/ppermute | solution.py:421
  270.6 1.6 collective-permute-start.36
  (25 other events, 173.1 us)

commit v5 on v4

--- a/solution.py
+++ b/solution.py
@@ -4,6 +4,7 @@
 from jax.experimental import pallas as pl
 from jax.experimental.pallas import tpu as pltpu
 from jax.sharding import PartitionSpec as P
+
 
 SOFTEN = 0.25
 ROOT_TWO = 1.4142135623730951
@@ -58,10 +59,7 @@
     return first, second, third
 
 
-def assemble_body(place, which, where, *refs):
-    sources = [refs[:SOURCES], refs[SOURCES : 2 * SOURCES]]
-    dmat, sem = refs[2 * SOURCES :]
-    core = place[0]
+def fetch_tiles(core, which, where, sources, dmat, sem):
     for side in range(2):
         half = (1 - core) if side else core
 
@@ -77,13 +75,12 @@
                 @pl.when(which[side * 32 + n] == k)
                 def _(k=k):
                     pltpu.make_async_copy(
-                        sources[side][k].at[where[side * 32 + n]], target, sem
+                        sources[side * SOURCES + k].at[where[side * 32 + n]], target, sem
                     ).start()
 
             return 0
 
         lax.fori_loop(0, 32, fetch, 0)
-    pltpu.make_async_copy(dmat, dmat, sem).wait()
 
 
 def density_steps(order, first, count, chunks, dmat, table, weights, xc, rho, pacc, bufs, top):
@@ -127,11 +124,14 @@
     return lax.fori_loop(0, count, step, top)
 
 
-def density_first_body(order, *refs):
+def density_first_body(order, place, which, where, *refs):
     chunks = refs[:EARLY]
-    table, dmat, weights, xc, rho, pacc, top, *bufs = refs[EARLY:]
+    sources = refs[EARLY : EARLY + 2 * SOURCES]
+    table, weights, xc, rho, pacc, top, dmat, sem, *bufs = refs[EARLY + 2 * SOURCES :]
+    fetch_tiles(place[0], which, where, sources, dmat, sem)
     pacc[...] = jnp.zeros_like(pacc)
     rho[...] = jnp.zeros_like(rho)
+    pltpu.make_async_copy(dmat, dmat, sem).wait()
     top[...] = density_steps(
         order, 0, EARLY, chunks, dmat, table, weights, xc, rho, pacc, bufs,
         jnp.zeros((1, HALF), jnp.float32),
@@ -263,7 +263,7 @@
 
 
 def any_spec():
-    return pl.BlockSpec(memory_space=pl.ANY)
+    return pl.BlockSpec(memory_space=pltpu.HBM)
 
 
 def vmem_spec():
@@ -272,20 +272,6 @@
 
 def smem_spec():
     return pl.BlockSpec(memory_space=pltpu.SMEM)
-
-
-def assemble_call(place, which, where, sources):
-    nbasis = NB * BLK
-    return pl.pallas_call(
-        assemble_body,
-        out_shape=jax.ShapeDtypeStruct((2, nbasis, nbasis), jnp.bfloat16),
-        in_specs=[smem_spec()] * 3 + [any_spec()] * (2 * SOURCES),
-        out_specs=vmem_spec(),
-        scratch_shapes=[pltpu.SemaphoreType.DMA],
-        compiler_params=pltpu.CompilerParams(vmem_limit_bytes=8 << 20),
-        cost_estimate=pl.CostEstimate(flops=0, bytes_accessed=8 << 20, transcendentals=0),
-        name="assemble",
-    )(place, which, where, *sources)
 
 
 def density_buffers(count):
@@ -304,21 +290,25 @@
     )
 
 
-def density_first(order, chunks, table, dmat, weights, xc):
+def density_first(order, place, which, where, chunks, sources, table, weights, xc):
+    nbasis = NB * BLK
     return pl.pallas_call(
         density_first_body,
         out_shape=(
             jax.ShapeDtypeStruct((PIECES, 1, HALF), jnp.float32),
-            jax.ShapeDtypeStruct((2, NB * BLK, 128), jnp.float32),
+            jax.ShapeDtypeStruct((2, nbasis, 128), jnp.float32),
             jax.ShapeDtypeStruct((1, HALF), jnp.float32),
+            jax.ShapeDtypeStruct((2, nbasis, nbasis), jnp.bfloat16),
         ),
-        in_specs=[smem_spec()] + [any_spec()] * (EARLY + 1) + [vmem_spec()] * 3,
-        out_specs=(vmem_spec(),) * 3,
-        scratch_shapes=density_buffers(EARLY),
+        in_specs=[smem_spec()] * 4
+        + [any_spec()] * (EARLY + 2 * SOURCES + 1)
+        + [vmem_spec()] * 2,
+        out_specs=(vmem_spec(),) * 4,
+        scratch_shapes=[pltpu.SemaphoreType.DMA] + density_buffers(EARLY),
         compiler_params=pltpu.CompilerParams(vmem_limit_bytes=30 << 20),
         cost_estimate=density_cost(EARLY),
         name="density_first",
-    )(order, *chunks, table, dmat, weights, xc)
+    )(order, place, which, where, *chunks, *sources, table, weights, xc)
 
 
 def density_last(order, chunks, table, dmat, weights, xc, rho, pacc, top):
@@ -368,7 +358,6 @@
 
 
 def ham_call(order, slots, place, chunks, scale_mine, scale_beside):
-    nbasis = NB * BLK
     return pl.pallas_call(
         ham_body,
         out_shape=(jax.ShapeDtypeStruct((32, 128, BLK), jnp.float32),) * 4,
@@ -424,7 +413,7 @@
     return total
 
 
-def per_device(
+def one_device(
     basis_values,
     point_coords,
     point_weights,
@@ -505,7 +494,9 @@
     erf_scale = (ROOT_TWO * gauss_widths)[None, None, :, None]
     gauss = jnp.exp(-dist_sq / spread).reshape(PIECES, neighbors * moments, HALF)
     distance = jnp.sqrt(dist_sq)
-    hart = (lax.erf(distance / erf_scale) / distance).reshape(PIECES, neighbors * moments, HALF)
+    hart = (lax.erf(distance / erf_scale) / distance).reshape(
+        PIECES, neighbors * moments, HALF
+    )
     weights = point_weights.reshape(PIECES, 1, HALF)
     xc = xc_kernel.reshape(PIECES, 1, HALF)
 
@@ -545,9 +536,9 @@
     far_tiles1 = lax.ppermute(behind_tiles[rows2:], "grid", core_perm(1, True))
     sources = [stored, ahead_tiles, far_tiles0, far_tiles1, behind_tiles]
     sources = sources + [lax.ppermute(s, "grid", swap) for s in sources]
-    dmat = assemble_call(core_place, which, where, sources)
-
-    rho, pacc, top = density_first(order, chunks[:EARLY], gauss, dmat, weights, xc)
+    rho, pacc, top, dmat = density_first(
+        order, core_place, which, where, chunks[:EARLY], sources, gauss, weights, xc
+    )
     rho, sent = density_last(order, chunks[EARLY:], gauss, dmat, weights, xc, rho, pacc, top)
     got = lax.all_to_all(sent, "grid", split_axis=0, concat_axis=0, tiled=True)
     all_coeffs, pot, scale, bound = potential_call(
@@ -595,7 +586,7 @@
         P(),
     )
     return jax.shard_map(
-        per_device,
+        one_device,
         mesh=mesh,
         in_specs=placed,
         out_specs=(P("pert", "grid", None, None), P("pert", "grid", None), P("pert", "grid")),

time: 276 us -> 282 us (1.022)
  waiting for transfers between devices: 104 us -> 120 us
  starting transfers between devices: 44.8 us -> 37.2 us
  other arithmetic: 32.8 us -> 28.6 us
    ppermute x30, waiting for transfers between devices: 54.3 us -> 66.7 us  [the longest x1 19.4 us: one_device(): above0 = lax.ppermute(own0, 'pert', ring(3))]
    pallas_call x1, Pallas kernels: 11.7 us -> 16.6 us  [density_first(): pl.pallas_call(density_first_body, out_shape=(jax.ShapeDtypeStruct((PIECE...]
    ppermute x3, starting transfers between devices: 9.27 us -> 4.52 us  [direct_sum(): lax.ppermute(cast(parts[d]), 'grid', core_perm(d, True))]
    pallas_call x1 -> x0, Pallas kernels: 4.34 us -> none  [assemble_call(): pl.pallas_call(assemble_body, out_shape=jax.ShapeDtypeStruct((2, nbasis,...]
    unnamed x77 -> x49, local copies, waits for them, and re-layouts: 22.9 us -> 20.6 us
  transfers between devices with their start and end apart: 38 -> 38, of which waited for: 18 -> 17; matrix products, arithmetic and copies ran while one was open for 12% -> 12% of each run, Pallas kernels for 9% -> 10%
where the time goes in v5:
time: 282 us; the launch traced here: 277 us
  waiting for transfers between devices  120 us (43%)
  Pallas kernels  48.3 us (17%)
  starting transfers between devices  37.2 us (13%)
  other arithmetic  28.6 us (10%)
  local copies, waits for them, and re-layouts  27.7 us (10%)
  blocking collectives  14.2 us (5%)
    ppermute x1, waiting for transfers between devices, ring_sum(): got_below = lax.ppermute(up, 'grid', core_perm(1, False))  22.9 us
    pallas_call x1, Pallas kernels, ham_call(): pl.pallas_call(ham_body, out_shape=(jax.ShapeDtypeStruct((32, 128, BLK),...  21.8 us
    unnamed x49, local copies, waits for them, and re-layouts  20.6 us
    ppermute x1, waiting for transfers between devices, one_device(): above0 = lax.ppermute(own0, 'pert', ring(3))  19.4 us
    pallas_call x1, Pallas kernels, density_first(): pl.pallas_call(density_first_body, out_shape=(jax.ShapeDtypeStruct((PIECE...  16.6 us
    ppermute x1, waiting for transfers between devices, one_device(): above1 = lax.ppermute(own1, 'pert', ring(3))  14.9 us
    all_to_all x1, blocking collectives, one_device(): got = lax.all_to_all(sent, 'grid', split_axis=0, concat_axis=0, tiled=True)  14.2 us
    ppermute x3, waiting for transfers between devices, direct_sum(): lax.ppermute(cast(parts[d]), 'grid', core_perm(d, True))  11.9 us
  transfers between devices with their start and end apart: 38, of which 17 were waited for; matrix products, arithmetic and copies ran while one was open for 12% of the time, Pallas kernels for 10%

profile of v5, /device:TPU:0, one launch (start us, length us, event | category | flops | bytes accessed | tf_op | source)
XLA Modules:
  0.0 276.8 jit_solution(4283614990692869748)
XLA Ops:
  0.7 1.1 select_bitcast_fusion
  1.9 2.7 fusion.20
  5.1 1.8 collective-permute-start.7
  8.6 4.1 %collective-permute-start.1 = (bf16[8,128,256]{2,1,0:T(8,128)(2,1)S(1)}, bf16[8,128,256]{2,1,0:T(8,128)(2,1)S(1)}, u32[]{:S(2)}, u32[]{:S(2)}) collective-permute-start(bf16[8,128,256]{2,1,0:T(8,128)(2,1)S(1)} %pad_maximum_fusion), channel_id=1, source_target_pairs={{0,96},{4,28},{8,104},{12,4},{16,112},{20,12},{24,120},{28,20},{32... | collective-permute-start | bytes 1572872 | tf_op jit(solution)/shard_map/ppermute | solution.py:457
  12.8 1.3 collective-permute-start.3
  14.5 8.1 %fusion.refs_16_.refs_2_ = f32[8,1024,512]{2,1,0:T(8,128)} fusion(f32[1024]{0:T(1024)S(1)} %div.148, f32[8,16,512]{2,1,0:T(8,128)S(1)} %bitcast.99), kind=kLoop, calls=%fused_computation.3 | loop fusion | flops 4194304 | bytes 17043456 | tf_op jit(solution)/shard_map/exp | solution.py:495
  22.7 2.4 collective-permute-done.1
  25.1 3.7 %collective-permute-done.3 = bf16[8,128,256]{2,1,0:T(8,128)(2,1)S(1)} collective-permute-done((bf16[8,128,256]{2,1,0:T(8,128)(2,1)S(1)}, bf16[8,128,256]{2,1,0:T(8,128)(2,1)S(1)}, u32[]{:S(2)}, u32[]{:S(2)}) %collective-permute-start.3) | collective-permute-done | bytes 524320 | tf_op jit(solution)/shard_map/ppermute | solution.py:457
  31.3 2.8 collective-permute-start.4
  34.1 2.3 copy.34
  36.3 1.7 collective-permute-start.8
  38.0 1.8 collective-permute-start.10
  40.2 7.4 %bitcast_divide_fusion.table = f32[8,1024,512]{2,1,0:T(8,128)} fusion(f32[1024]{0:T(1024)S(1)} %div.170, f32[8,16,512]{2,1,0:T(8,128)S(1)} %bitcast.98), kind=kLoop, calls=%fused_computation | loop fusion | flops 8388608 | bytes 17043456 | tf_op jit(solution)/shard_map/div | solution.py:497
  47.8 14.9 %collective-permute-done.8.refs_5_ = bf16[1024,512]{1,0:T(8,128)(2,1)} collective-permute-done((bf16[1024,512]{1,0:T(8,128)(2,1)}, bf16[1024,512]{1,0:T(8,128)(2,1)}, u32[]{:S(2)}, u32[]{:S(2)}) %collective-permute-start.8) | collective-permute-done | bytes 1048608 | tf_op jit(solution)/shard_map/ppermute | solution.py:442
  62.7 1.2 collective-permute-done.6
  64.0 19.4 %collective-permute-done.10.refs_4_ = bf16[1024,512]{1,0:T(8,128)(2,1)} collective-permute-done((bf16[1024,512]{1,0:T(8,128)(2,1)S(1)}, bf16[1024,512]{1,0:T(8,128)(2,1)}, u32[]{:S(2)}, u32[]{:S(2)}) %collective-permute-start.10) | collective-permute-done | bytes 1048608 | tf_op jit(solution)/shard_map/ppermute | solution.py:444
  83.4 1.2 collective-permute-start.11
  84.6 2.1 collective-permute-start.12
  87.6 5.0 %all-to-all-start = ((f32[32,8,128]{2,1,0:T(8,128)}), f32[32,8,128]{2,1,0:T(8,128)S(1)}, u32[]{:S(2)}, u32[]{:S(2)}) async-start(f32[32,8,128]{2,1,0:T(8,128)} %broadcast_in_dim.70), calls=%async_computation | async-start | bytes 262144 | tf_op jit(solution)/shard_map/all_to_all | solution.py:509
  92.8 7.6 %all-to-all-done = f32[32,8,128]{2,1,0:T(8,128)S(1)} async-done(((f32[32,8,128]{2,1,0:T(8,128)}), f32[32,8,128]{2,1,0:T(8,128)S(1)}, u32[]{:S(2)}, u32[]{:S(2)}) %all-to-all-start) | async-done | bytes 131104 | tf_op jit(solution)/shard_map/all_to_all | solution.py:509
  100.8 1.1 compare_convert_fusion
  102.0 1.3 slice.56
  103.5 1.3 collective-permute-start.21
  104.8 5.7 %collective-permute-done.11.refs_0_ = bf16[1024,512]{1,0:T(8,128)(2,1)} collective-permute-done((bf16[1024,512]{1,0:T(8,128)(2,1)}, bf16[1024,512]{1,0:T(8,128)(2,1)}, u32[]{:S(2)}, u32[]{:S(2)}) %collective-permute-start.11) | collective-permute-done | bytes 1048608 | tf_op jit(solution)/shard_map/ppermute | solution.py:526
  111.0 7.4 %collective-permute-done.21.refs_8_ = bf16[16,128,256]{2,1,0:T(8,128)(2,1)} collective-permute-done((bf16[16,128,256]{2,1,0:T(8,128)(2,1)S(1)}, bf16[16,128,256]{2,1,0:T(8,128)(2,1)}, u32[]{:S(2)}, u32[]{:S(2)}) %collective-permute-start.21) | collective-permute-done | bytes 1048608 | tf_op jit(solution)/shard_map/ppermute | solution.py:535
  118.4 8.2 %collective-permute-done.22.refs_9_ = bf16[16,128,256]{2,1,0:T(8,128)(2,1)} collective-permute-done((bf16[16,128,256]{2,1,0:T(8,128)(2,1)S(1)}, bf16[16,128,256]{2,1,0:T(8,128)(2,1)}, u32[]{:S(2)}, u32[]{:S(2)}) %collective-permute-start.22) | collective-permute-done | bytes 1048608 | tf_op jit(solution)/shard_map/ppermute | solution.py:536
  127.5 2.1 collective-permute-done.26.refs_14_
  130.3 16.6 %density_first.1 = (f32[8,1,512]{2,1,0:T(1,128)S(1)}, f32[2,1024,128]{2,1,0:T(8,128)S(1)}, f32[1,512]{1,0:T(1,128)S(1)}, bf16[2,1024,1024]{2,1,0:T(8,128)(2,1)}) custom-call(s32[8]{0:T(128)S(1)} %fusion.9.order, s32[1]{0:T(128)} %bitcast.7.place, s32[64]{0:T(128)S(1)} %get-tuple-element.87.which, s32[64]{0:T(128)S(1)} %get-tuple-element.88.where, ...), custom_call_target="tpu_custom_call" | custom-call | flops 6442450944 | bytes 18874368 | tf_op jit(solution)/shard_map/density_first/pallas_call | solution.py:295
  146.9 5.8 %copy-done = f32[8,1024,512]{2,1,0:T(8,128)S(1)} copy-done((f32[8,1024,512]{2,1,0:T(8,128)S(1)}, f32[8,1024,512]{2,1,0:T(8,128)}, u32[]{:S(2)}) %copy-start) | copy-done | bytes 16777240
  152.7 2.2 copy-done.2
  154.9 5.3 %density_last.1 = (f32[8,1,512]{2,1,0:T(1,128)S(1)}, f32[32,24,128]{2,1,0:T(8,128)S(1)}) custom-call(s32[8]{0:T(128)S(1)} %fusion.9.order, bf16[1024,512]{1,0:T(8,128)(2,1)} %collective-permute-done.11.refs_0_, bf16[1024,512]{1,0:T(8,128)(2,1)} %collective-permute-done.12.refs_1_, f32[8,1024,512]{2,1,0:T(8,128)S(1)} %copy-done, ...), custom_call_target="tpu_custom_call" | custom-call | flops 2147483648 | bytes 6291456 | tf_op jit(solution)/shard_map/density_last/pallas_call | solution.py:316
  160.2 14.2 %all_to_all.10 = f32[32,24,128]{2,1,0:T(8,128)S(1)} all-to-all(f32[32,24,128]{2,1,0:T(8,128)S(1)} %get-tuple-element.43), channel_id=1, replica_groups=mesh['grid'=32,'pert'=4] {'grid'}, dimensions={0} | all-to-all | bytes 786432 | tf_op jit(solution)/shard_map/all_to_all | solution.py:543
  174.4 5.8 %copy-done.1 = f32[8,1024,512]{2,1,0:T(8,128)S(1)} copy-done((f32[8,1024,512]{2,1,0:T(8,128)S(1)}, f32[8,1024,512]{2,1,0:T(8,128)}, u32[]{:S(2)}) %copy-start.1) | copy-done | bytes 16777240
  180.2 4.6 %potential.1 = (f32[256,64]{1,0:T(8,128)S(1)}, f32[8,1,512]{2,1,0:T(1,128)}, f32[8,1,512]{2,1,0:T(1,128)S(1)}, f32[1,128]{1,0:T(1,128)S(1)}) custom-call(f32[8,1024,512]{2,1,0:T(8,128)S(1)} %copy-done.1, f32[768,128]{1,0:T(8,128)S(1)} %bitcast.81, bf16[288,768]{1,0:T(8,128)(2,1)S(1)} %copy-done.4, bf16[288,768]{1,0:T(8,128)(2,1)S(1)} %copy-done.3, ...), custom_call_target="tpu_custom_call" | custom-call | flops 16777216 | bytes 16777216 | tf_op jit(solution)/shard_map/potential/pallas_call | solution.py:337
  186.2 21.8 %ham.1 = (f32[32,128,256]{2,1,0:T(8,128)}, f32[32,128,256]{2,1,0:T(8,128)}, f32[32,128,256]{2,1,0:T(8,128)}, f32[32,128,256]{2,1,0:T(8,128)}) custom-call(s32[8]{0:T(128)S(1)} %fusion.9.order, s32[64]{0:T(128)S(1)} %fusion.6.slots, s32[1]{0:T(128)} %bitcast.7.place, bf16[4,2,128,512]{3,2,1,0:T(8,128)(2,1)S(1)} %bitcast.80, ...), custom_call_target="tpu_custom_call" | custom-call | flops 8589934592 | bytes 33554432 | tf_op jit(solution)/shard_map/ham/pallas_call | solution.py:361
  208.0 3.0 %multiply_convert_fusion.1 = (f16[16,128,256]{2,1,0:T(8,128)(2,1)S(1)}, f16[16,128,256]{2,1,0:T(8,128)(2,1)S(1)}) fusion(f32[32,128,256]{2,1,0:T(8,128)} %get-tuple-element.51, f32[]{:T(128)} %bitcast.33), kind=kLoop, calls=%fused_computation.8 | loop fusion | flops 2097152 | bytes 6291460 | tf_op jit(solution)/shard_map/convert_element_type | solution.py:389
  211.7 2.6 collective-permute-start.31
  214.6 1.9 copy-done.9
  217.0 10.1 %collective-permute-done.29 = f16[2,8,128,256]{3,2,1,0:T(8,128)(2,1)S(1)} collective-permute-done((f16[2,8,128,256]{3,2,1,0:T(8,128)(2,1)S(1)}, f16[2,8,128,256]{3,2,1,0:T(8,128)(2,1)S(1)}, u32[]{:S(2)}, u32[]{:S(2)}) %collective-permute-start.29) | collective-permute-done | bytes 1048608 | tf_op jit(solution)/shard_map/ppermute | solution.py:398
  228.8 3.3 %collective-permute-start.32 = (f16[4,8,128,256]{3,2,1,0:T(8,128)(2,1)S(1)}, f16[4,8,128,256]{3,2,1,0:T(8,128)(2,1)S(1)}, u32[]{:S(2)}, u32[]{:S(2)}) collective-permute-start(f16[4,8,128,256]{3,2,1,0:T(8,128)(2,1)S(1)} %add_convert_fusion), channel_id=1, source_target_pairs={{0,96},{4,28},{8,104},{12,4},{16,112},{20,12},{24,120},{28,20},{32... | collective-permute-start | bytes 6291464 | tf_op jit(solution)/shard_map/ppermute | solution.py:404
  232.4 22.9 %collective-permute-done.30 = f16[4,8,128,256]{3,2,1,0:T(8,128)(2,1)S(1)} collective-permute-done((f16[4,8,128,256]{3,2,1,0:T(8,128)(2,1)S(1)}, f16[4,8,128,256]{3,2,1,0:T(8,128)(2,1)S(1)}, u32[]{:S(2)}, u32[]{:S(2)}) %collective-permute-start.30) | collective-permute-done | bytes 2097184 | tf_op jit(solution)/shard_map/ppermute | solution.py:403
  255.7 1.3 fusion.19
  257.3 1.3 collective-permute-start.33
  258.6 1.2 collective-permute-start.34
  259.8 2.0 collective-permute-start.35
  261.8 6.3 %collective-permute-done.33 = f16[8,128,256]{2,1,0:T(8,128)(2,1)S(1)} collective-permute-done((f16[8,128,256]{2,1,0:T(8,128)(2,1)S(1)}, f16[8,128,256]{2,1,0:T(8,128)(2,1)S(1)}, u32[]{:S(2)}, u32[]{:S(2)}) %collective-permute-start.33) | collective-permute-done | bytes 524320 | tf_op jit(solution)/shard_map/ppermute | solution.py:410
  268.2 5.5 %collective-permute-done.34 = f16[8,128,256]{2,1,0:T(8,128)(2,1)S(1)} collective-permute-done((f16[8,128,256]{2,1,0:T(8,128)(2,1)S(1)}, f16[8,128,256]{2,1,0:T(8,128)(2,1)S(1)}, u32[]{:S(2)}, u32[]{:S(2)}) %collective-permute-start.34) | collective-permute-done | bytes 524320 | tf_op jit(solution)/shard_map/ppermute | solution.py:410
  275.8 1.1 maximum_multiply_fusion
  (137 shorter events, 17.3 us)
Async XLA Ops:
  1.8 12.2 %copy-start.19 = (f32[64]{0:T(128)S(1)}, f32[64]{0:T(128)}, u32[]{:S(2)}) copy-start(f32[64]{0:T(128)} %param.17) | copy-start | bytes 772
  1.8 12.3 %copy-start.13 = (f32[3,256]{1,0:T(4,128)S(1)}, f32[3,256]{1,0:T(4,128)}, u32[]{:S(2)}) copy-start(f32[3,256]{1,0:T(4,128)} %param.18) | copy-start | bytes 9220
  1.8 5.2 %collective-permute-start = (bf16[4,128,256]{2,1,0:T(8,128)(2,1)S(1)}, bf16[4,128,256]{2,1,0:T(8,128)(2,1)S(1)}, u32[]{:S(2)}, u32[]{:S(2)}) collective-permute-start(bf16[4,128,256]{2,1,0:T(8,128)(2,1)S(1)} %select_bitcast_fusion), channel_id=1, source_target_pairs={{0,4},{4,0},{8,12},{12,8},{16,20},{20,16},{24,28},{28,24},{32,36},... | collective-permute-start | bytes 786440 | tf_op jit(solution)/shard_map/ppermute | solution.py:453
  5.1 34.7 %collective-permute-start.7 = (bf16[1024,512]{1,0:T(8,128)(2,1)S(1)}, bf16[1024,512]{1,0:T(8,128)(2,1)}, u32[]{:S(2)}, u32[]{:S(2)}) collective-permute-start(bf16[1024,512]{1,0:T(8,128)(2,1)S(1)} %bitcast.76), channel_id=1, source_target_pairs={{0,1},{1,2},{2,3},{3,0},{4,5},{5,6},{6,7},{7,4},{8,9},{9,10},{10,1... | collective-permute-start | bytes 3145736 | tf_op jit(solution)/shard_map/ppermute | solution.py:441
  8.6 16.4 %collective-permute-start.1 = (bf16[8,128,256]{2,1,0:T(8,128)(2,1)S(1)}, bf16[8,128,256]{2,1,0:T(8,128)(2,1)S(1)}, u32[]{:S(2)}, u32[]{:S(2)}) collective-permute-start(bf16[8,128,256]{2,1,0:T(8,128)(2,1)S(1)} %pad_maximum_fusion), channel_id=1, source_target_pairs={{0,96},{4,28},{8,104},{12,4},{16,112},{20,12},{24,120},{28,20},{32... | collective-permute-start | bytes 1572872 | tf_op jit(solution)/shard_map/ppermute | solution.py:457
  12.7 12.3 %collective-permute-start.2 = (bf16[8,128,256]{2,1,0:T(8,128)(2,1)S(1)}, bf16[8,128,256]{2,1,0:T(8,128)(2,1)S(1)}, u32[]{:S(2)}, u32[]{:S(2)}) collective-permute-start(bf16[8,128,256]{2,1,0:T(8,128)(2,1)S(1)} %pad_maximum_fusion), channel_id=1, source_target_pairs={{0,64},{4,20},{8,72},{12,28},{16,80},{20,4},{24,88},{28,12},{32,96... | collective-permute-start | bytes 1572872 | tf_op jit(solution)/shard_map/ppermute | solution.py:457
  12.8 16.0 %collective-permute-start.3 = (bf16[8,128,256]{2,1,0:T(8,128)(2,1)S(1)}, bf16[8,128,256]{2,1,0:T(8,128)(2,1)S(1)}, u32[]{:S(2)}, u32[]{:S(2)}) collective-permute-start(bf16[8,128,256]{2,1,0:T(8,128)(2,1)S(1)} %pad_maximum_fusion), channel_id=1, source_target_pairs={{0,32},{4,12},{8,40},{12,20},{16,48},{20,28},{24,56},{28,4},{32,64... | collective-permute-start | bytes 1572872 | tf_op jit(solution)/shard_map/ppermute | solution.py:457
  22.6 17.4 %copy-start.18 = (s32[2,16]{1,0:T(2,128)S(1)}, s32[2,16]{1,0:T(2,128)}, u32[]{:S(2)}) copy-start(s32[2,16]{1,0:T(2,128)} %param.20) | copy-start | bytes 388
  31.3 53.3 %collective-permute-start.4 = (bf16[32,128,256]{2,1,0:T(8,128)(2,1)}, bf16[32,128,256]{2,1,0:T(8,128)(2,1)S(1)}, u32[]{:S(2)}, u32[]{:S(2)}) collective-permute-start(bf16[32,128,256]{2,1,0:T(8,128)(2,1)} %constant_dynamic-update-slice_fusion.refs_6_), channel_id=1, source_target_pairs={{0,24},{4,100},{8,0},{12,108},{16,8},{20,116},{24,16},{28,124},{32... | collective-permute-start | bytes 6291464 | tf_op jit(solution)/shard_map/ppermute | solution.py:505
  34.1 52.6 %collective-permute-start.5 = (bf16[32,128,256]{2,1,0:T(8,128)(2,1)}, bf16[32,128,256]{2,1,0:T(8,128)(2,1)}, u32[]{:S(2)}, u32[]{:S(2)}) collective-permute-start(bf16[32,128,256]{2,1,0:T(8,128)(2,1)} %constant_dynamic-update-slice_fusion.refs_6_), channel_id=1, source_target_pairs={{0,8},{4,36},{8,16},{12,44},{16,24},{20,52},{24,0},{28,60},{32,40}... | collective-permute-start | bytes 6291464 | tf_op jit(solution)/shard_map/ppermute | solution.py:506
  36.3 26.3 %collective-permute-start.8 = (bf16[1024,512]{1,0:T(8,128)(2,1)}, bf16[1024,512]{1,0:T(8,128)(2,1)}, u32[]{:S(2)}, u32[]{:S(2)}) collective-permute-start(bf16[1024,512]{1,0:T(8,128)(2,1)} %bitcast.10.refs_1_), channel_id=1, source_target_pairs={{0,3},{1,0},{2,1},{3,2},{4,7},{5,4},{6,5},{7,6},{8,11},{9,8},{10,9... | collective-permute-start | bytes 3145736 | tf_op jit(solution)/shard_map/ppermute | solution.py:442
  38.0 45.4 %collective-permute-start.10 = (bf16[1024,512]{1,0:T(8,128)(2,1)S(1)}, bf16[1024,512]{1,0:T(8,128)(2,1)}, u32[]{:S(2)}, u32[]{:S(2)}) collective-permute-start(bf16[1024,512]{1,0:T(8,128)(2,1)S(1)} %bitcast.77), channel_id=1, source_target_pairs={{0,3},{1,0},{2,1},{3,2},{4,7},{5,4},{6,5},{7,6},{8,11},{9,8},{10,9... | collective-permute-start | bytes 3145736 | tf_op jit(solution)/shard_map/ppermute | solution.py:444
  39.8 43.6 %collective-permute-start.9 = (bf16[1024,512]{1,0:T(8,128)(2,1)}, bf16[1024,512]{1,0:T(8,128)(2,1)}, u32[]{:S(2)}, u32[]{:S(2)}) collective-permute-start(bf16[1024,512]{1,0:T(8,128)(2,1)} %bitcast.10.refs_1_), channel_id=1, source_target_pairs={{0,1},{1,2},{2,3},{3,0},{4,5},{5,6},{6,7},{7,4},{8,9},{9,10},{10,1... | collective-permute-start | bytes 3145736 | tf_op jit(solution)/shard_map/ppermute | solution.py:443
  40.2 46.4 %copy-start.14 = (s32[256]{0:T(256)S(1)}, s32[256]{0:T(256)}, u32[]{:S(2)}) copy-start(s32[256]{0:T(256)} %param.23) | copy-start | bytes 3076
  47.6 79.2 %copy-start.15 = (s32[8]{0:T(128)S(1)}, s32[8]{0:T(128)}, u32[]{:S(2)}) copy-start(s32[8]{0:T(128)} %constant.222.clone) | copy-start | bytes 100
  47.6 79.2 %copy-start.16 = (s32[8]{0:T(128)S(1)}, s32[8]{0:T(128)}, u32[]{:S(2)}) copy-start(s32[8]{0:T(128)} %constant.223.clone) | copy-start | bytes 100
  47.6 82.7 %copy-start.5 = (f32[4096]{0:T(1024)S(1)}, f32[4096]{0:T(1024)}, u32[]{:S(2)}) copy-start(f32[4096]{0:T(1024)} %param.15) | copy-start | bytes 49156
  47.6 82.7 %copy-start.6 = (f32[4096]{0:T(1024)S(1)}, f32[4096]{0:T(1024)}, u32[]{:S(2)}) copy-start(f32[4096]{0:T(1024)} %param.16) | copy-start | bytes 49156
  62.7 1.2 collective-permute-start.6
  63.9 39.5 %collective-permute-start.13 = (bf16[1024,512]{1,0:T(8,128)(2,1)S(1)}, bf16[1024,512]{1,0:T(8,128)(2,1)}, u32[]{:S(2)}, u32[]{:S(2)}) collective-permute-start(bf16[1024,512]{1,0:T(8,128)(2,1)S(1)} %bitcast.78), channel_id=1, source_target_pairs={{0,4},{4,0},{8,12},{12,8},{16,20},{20,16},{24,28},{28,24},{32,36},... | collective-permute-start | bytes 3145736 | tf_op jit(solution)/shard_map/ppermute | solution.py:529
  83.4 20.1 %collective-permute-start.14 = (bf16[1024,512]{1,0:T(8,128)(2,1)}, bf16[1024,512]{1,0:T(8,128)(2,1)}, u32[]{:S(2)}, u32[]{:S(2)}) collective-permute-start(bf16[1024,512]{1,0:T(8,128)(2,1)} %bitcast.10.refs_1_), channel_id=1, source_target_pairs={{0,4},{4,0},{8,12},{12,8},{16,20},{20,16},{24,28},{28,24},{32,36},... | collective-permute-start | bytes 3145736 | tf_op jit(solution)/shard_map/ppermute | solution.py:529
  83.4 27.1 %collective-permute-start.11 = (bf16[1024,512]{1,0:T(8,128)(2,1)}, bf16[1024,512]{1,0:T(8,128)(2,1)}, u32[]{:S(2)}, u32[]{:S(2)}) collective-permute-start(bf16[1024,512]{1,0:T(8,128)(2,1)} %collective-permute-done.7.refs_2_), channel_id=1, source_target_pairs={{0,1},{1,2},{2,3},{3,0},{4,5},{5,6},{6,7},{7,4},{8,9},{9,10},{10,1... | collective-permute-start | bytes 3145736 | tf_op jit(solution)/shard_map/ppermute | solution.py:526
  84.6 25.9 %collective-permute-start.12 = (bf16[1024,512]{1,0:T(8,128)(2,1)}, bf16[1024,512]{1,0:T(8,128)(2,1)}, u32[]{:S(2)}, u32[]{:S(2)}) collective-permute-start(bf16[1024,512]{1,0:T(8,128)(2,1)} %collective-permute-done.8.refs_5_), channel_id=1, source_target_pairs={{0,3},{1,0},{2,1},{3,2},{4,7},{5,4},{6,5},{7,6},{8,11},{9,8},{10,9... | collective-permute-start | bytes 3145736 | tf_op jit(solution)/shard_map/ppermute | solution.py:527
  86.6 23.9 %collective-permute-start.15 = (bf16[1024,512]{1,0:T(8,128)(2,1)}, bf16[1024,512]{1,0:T(8,128)(2,1)}, u32[]{:S(2)}, u32[]{:S(2)}) collective-permute-start(bf16[1024,512]{1,0:T(8,128)(2,1)} %collective-permute-done.7.refs_2_), channel_id=1, source_target_pairs={{0,4},{4,0},{8,12},{12,8},{16,20},{20,16},{24,28},{28,24},{32,36},... | collective-permute-start | bytes 3145736 | tf_op jit(solution)/shard_map/ppermute | solution.py:529
  87.6 12.7 %all-to-all-start = ((f32[32,8,128]{2,1,0:T(8,128)}), f32[32,8,128]{2,1,0:T(8,128)S(1)}, u32[]{:S(2)}, u32[]{:S(2)}) async-start(f32[32,8,128]{2,1,0:T(8,128)} %broadcast_in_dim.70), calls=%async_computation | async-start | bytes 262144 | tf_op jit(solution)/shard_map/all_to_all | solution.py:509
  103.3 23.5 %collective-permute-start.23 = (bf16[32,128,256]{2,1,0:T(8,128)(2,1)}, bf16[32,128,256]{2,1,0:T(8,128)(2,1)}, u32[]{:S(2)}, u32[]{:S(2)}) collective-permute-start(bf16[32,128,256]{2,1,0:T(8,128)(2,1)} %constant_dynamic-update-slice_fusion.refs_6_), channel_id=1, source_target_pairs={{0,4},{4,0},{8,12},{12,8},{16,20},{20,16},{24,28},{28,24},{32,36},... | collective-permute-start | bytes 6291464 | tf_op jit(solution)/shard_map/ppermute | solution.py:538
  103.5 14.9 %collective-permute-start.21 = (bf16[16,128,256]{2,1,0:T(8,128)(2,1)S(1)}, bf16[16,128,256]{2,1,0:T(8,128)(2,1)}, u32[]{:S(2)}, u32[]{:S(2)}) collective-permute-start(bf16[16,128,256]{2,1,0:T(8,128)(2,1)S(1)} %slice.55), channel_id=1, source_target_pairs={{0,24},{4,100},{8,0},{12,108},{16,8},{20,116},{24,16},{28,124},{32... | collective-permute-start | bytes 3145736 | tf_op jit(solution)/shard_map/ppermute | solution.py:535
  110.5 16.1 %collective-permute-start.22 = (bf16[16,128,256]{2,1,0:T(8,128)(2,1)S(1)}, bf16[16,128,256]{2,1,0:T(8,128)(2,1)}, u32[]{:S(2)}, u32[]{:S(2)}) collective-permute-start(bf16[16,128,256]{2,1,0:T(8,128)(2,1)S(1)} %slice.56), channel_id=1, source_target_pairs={{0,8},{4,36},{8,16},{12,44},{16,24},{20,52},{24,0},{28,60},{32,40}... | collective-permute-start | bytes 3145736 | tf_op jit(solution)/shard_map/ppermute | solution.py:536
  110.5 19.3 %collective-permute-start.24 = (bf16[32,128,256]{2,1,0:T(8,128)(2,1)S(1)}, bf16[32,128,256]{2,1,0:T(8,128)(2,1)}, u32[]{:S(2)}, u32[]{:S(2)}) collective-permute-start(bf16[32,128,256]{2,1,0:T(8,128)(2,1)S(1)} %collective-permute-done.4.refs_7_), channel_id=1, source_target_pairs={{0,4},{4,0},{8,12},{12,8},{16,20},{20,16},{24,28},{28,24},{32,36},... | collective-permute-start | bytes 6291464 | tf_op jit(solution)/shard_map/ppermute | solution.py:538
  110.5 19.6 %collective-permute-start.27 = (bf16[32,128,256]{2,1,0:T(8,128)(2,1)}, bf16[32,128,256]{2,1,0:T(8,128)(2,1)}, u32[]{:S(2)}, u32[]{:S(2)}) collective-permute-start(bf16[32,128,256]{2,1,0:T(8,128)(2,1)} %collective-permute-done.5.refs_10_), channel_id=1, source_target_pairs={{0,4},{4,0},{8,12},{12,8},{16,20},{20,16},{24,28},{28,24},{32,36},... | collective-permute-start | bytes 6291464 | tf_op jit(solution)/shard_map/ppermute | solution.py:538
  118.4 9.0 %collective-permute-start.25 = (bf16[16,128,256]{2,1,0:T(8,128)(2,1)}, bf16[16,128,256]{2,1,0:T(8,128)(2,1)}, u32[]{:S(2)}, u32[]{:S(2)}) collective-permute-start(bf16[16,128,256]{2,1,0:T(8,128)(2,1)} %collective-permute-done.21.refs_8_), channel_id=1, source_target_pairs={{0,4},{4,0},{8,12},{12,8},{16,20},{20,16},{24,28},{28,24},{32,36},... | collective-permute-start | bytes 3145736 | tf_op jit(solution)/shard_map/ppermute | solution.py:538
  126.6 3.0 %collective-permute-start.26 = (bf16[16,128,256]{2,1,0:T(8,128)(2,1)}, bf16[16,128,256]{2,1,0:T(8,128)(2,1)}, u32[]{:S(2)}, u32[]{:S(2)}) collective-permute-start(bf16[16,128,256]{2,1,0:T(8,128)(2,1)} %collective-permute-done.22.refs_9_), channel_id=1, source_target_pairs={{0,4},{4,0},{8,12},{12,8},{16,20},{20,16},{24,28},{28,24},{32,36},... | collective-permute-start | bytes 3145736 | tf_op jit(solution)/shard_map/ppermute | solution.py:538
  126.8 58.0 %collective-permute-start.18 = (bf16[1024,512]{1,0:T(8,128)(2,1)}, bf16[1024,512]{1,0:T(8,128)(2,1)S(1)}, u32[]{:S(2)}, u32[]{:S(2)}) collective-permute-start(bf16[1024,512]{1,0:T(8,128)(2,1)} %collective-permute-done.8.refs_5_), channel_id=1, source_target_pairs={{0,4},{4,0},{8,12},{12,8},{16,20},{20,16},{24,28},{28,24},{32,36},... | collective-permute-start | bytes 3145736 | tf_op jit(solution)/shard_map/ppermute | solution.py:529
  127.4 57.8 %collective-permute-start.16 = (bf16[1024,512]{1,0:T(8,128)(2,1)}, bf16[1024,512]{1,0:T(8,128)(2,1)S(1)}, u32[]{:S(2)}, u32[]{:S(2)}) collective-permute-start(bf16[1024,512]{1,0:T(8,128)(2,1)} %collective-permute-done.9.refs_3_), channel_id=1, source_target_pairs={{0,4},{4,0},{8,12},{12,8},{16,20},{20,16},{24,28},{28,24},{32,36},... | collective-permute-start | bytes 3145736 | tf_op jit(solution)/shard_map/ppermute | solution.py:529
  129.6 55.6 %collective-permute-start.17 = (bf16[1024,512]{1,0:T(8,128)(2,1)}, bf16[1024,512]{1,0:T(8,128)(2,1)S(1)}, u32[]{:S(2)}, u32[]{:S(2)}) collective-permute-start(bf16[1024,512]{1,0:T(8,128)(2,1)} %collective-permute-done.10.refs_4_), channel_id=1, source_target_pairs={{0,4},{4,0},{8,12},{12,8},{16,20},{20,16},{24,28},{28,24},{32,36},... | collective-permute-start | bytes 3145736 | tf_op jit(solution)/shard_map/ppermute | solution.py:529
  129.8 55.5 %collective-permute-start.19 = (bf16[1024,512]{1,0:T(8,128)(2,1)}, bf16[1024,512]{1,0:T(8,128)(2,1)S(1)}, u32[]{:S(2)}, u32[]{:S(2)}) collective-permute-start(bf16[1024,512]{1,0:T(8,128)(2,1)} %collective-permute-done.11.refs_0_), channel_id=1, source_target_pairs={{0,4},{4,0},{8,12},{12,8},{16,20},{20,16},{24,28},{28,24},{32,36},... | collective-permute-start | bytes 3145736 | tf_op jit(solution)/shard_map/ppermute | solution.py:529
  130.1 55.1 %collective-permute-start.20 = (bf16[1024,512]{1,0:T(8,128)(2,1)}, bf16[1024,512]{1,0:T(8,128)(2,1)S(1)}, u32[]{:S(2)}, u32[]{:S(2)}) collective-permute-start(bf16[1024,512]{1,0:T(8,128)(2,1)} %collective-permute-done.12.refs_1_), channel_id=1, source_target_pairs={{0,4},{4,0},{8,12},{12,8},{16,20},{20,16},{24,28},{28,24},{32,36},... | collective-permute-start | bytes 3145736 | tf_op jit(solution)/shard_map/ppermute | solution.py:529
  154.9 19.5 %copy-start.3 = (bf16[288,768]{1,0:T(8,128)(2,1)S(1)}, bf16[288,768]{1,0:T(8,128)(2,1)}, u32[]{:S(2)}) copy-start(bf16[288,768]{1,0:T(8,128)(2,1)} %get-tuple-element.45.odd) | copy-start | bytes 1327108
  154.9 19.5 %copy-start.4 = (bf16[288,768]{1,0:T(8,128)(2,1)S(1)}, bf16[288,768]{1,0:T(8,128)(2,1)}, u32[]{:S(2)}) copy-start(bf16[288,768]{1,0:T(8,128)(2,1)} %get-tuple-element.44.even) | copy-start | bytes 1327108
  184.8 1.3 collective-permute-start.28
  211.0 16.1 %collective-permute-start.29 = (f16[2,8,128,256]{3,2,1,0:T(8,128)(2,1)S(1)}, f16[2,8,128,256]{3,2,1,0:T(8,128)(2,1)S(1)}, u32[]{:S(2)}, u32[]{:S(2)}) collective-permute-start(f16[2,8,128,256]{3,2,1,0:T(8,128)(2,1)S(1)} %bitcast.101), channel_id=1, source_target_pairs={{0,32},{4,12},{8,40},{12,20},{16,48},{20,28},{24,56},{28,4},{32,64... | collective-permute-start | bytes 3145736 | tf_op jit(solution)/shard_map/ppermute | solution.py:398
  211.7 16.4 %collective-permute-start.31 = (f16[2,8,128,256]{3,2,1,0:T(8,128)(2,1)S(1)}, f16[2,8,128,256]{3,2,1,0:T(8,128)(2,1)S(1)}, u32[]{:S(2)}, u32[]{:S(2)}) collective-permute-start(f16[2,8,128,256]{3,2,1,0:T(8,128)(2,1)S(1)} %bitcast.100), channel_id=1, source_target_pairs={{0,96},{4,28},{8,104},{12,4},{16,112},{20,12},{24,120},{28,20},{32... | collective-permute-start | bytes 3145736 | tf_op jit(solution)/shard_map/ppermute | solution.py:399
  227.8 27.5 %collective-permute-start.30 = (f16[4,8,128,256]{3,2,1,0:T(8,128)(2,1)S(1)}, f16[4,8,128,256]{3,2,1,0:T(8,128)(2,1)S(1)}, u32[]{:S(2)}, u32[]{:S(2)}) collective-permute-start(f16[4,8,128,256]{3,2,1,0:T(8,128)(2,1)S(1)} %add_convert_fusion.1), channel_id=1, source_target_pairs={{0,32},{4,12},{8,40},{12,20},{16,48},{20,28},{24,56},{28,4},{32,64... | collective-permute-start | bytes 6291464 | tf_op jit(solution)/shard_map/ppermute | solution.py:403
  228.8 26.8 %collective-permute-start.32 = (f16[4,8,128,256]{3,2,1,0:T(8,128)(2,1)S(1)}, f16[4,8,128,256]{3,2,1,0:T(8,128)(2,1)S(1)}, u32[]{:S(2)}, u32[]{:S(2)}) collective-permute-start(f16[4,8,128,256]{3,2,1,0:T(8,128)(2,1)S(1)} %add_convert_fusion), channel_id=1, source_target_pairs={{0,96},{4,28},{8,104},{12,4},{16,112},{20,12},{24,120},{28,20},{32... | collective-permute-start | bytes 6291464 | tf_op jit(solution)/shard_map/ppermute | solution.py:404
  257.3 10.9 %collective-permute-start.33 = (f16[8,128,256]{2,1,0:T(8,128)(2,1)S(1)}, f16[8,128,256]{2,1,0:T(8,128)(2,1)S(1)}, u32[]{:S(2)}, u32[]{:S(2)}) collective-permute-start(f16[8,128,256]{2,1,0:T(8,128)(2,1)S(1)} %get-tuple-element.69), channel_id=1, source_target_pairs={{0,16},{4,68},{8,24},{12,76},{16,0},{20,84},{24,8},{28,92},{32,48}... | collective-permute-start | bytes 1572872 | tf_op jit(solution)/shard_map/ppermute | solution.py:410
  258.6 15.1 %collective-permute-start.34 = (f16[8,128,256]{2,1,0:T(8,128)(2,1)S(1)}, f16[8,128,256]{2,1,0:T(8,128)(2,1)S(1)}, u32[]{:S(2)}, u32[]{:S(2)}) collective-permute-start(f16[8,128,256]{2,1,0:T(8,128)(2,1)S(1)} %get-tuple-element.71), channel_id=1, source_target_pairs={{0,8},{4,36},{8,16},{12,44},{16,24},{20,52},{24,0},{28,60},{32,40}... | collective-permute-start | bytes 1572872 | tf_op jit(solution)/shard_map/ppermute | solution.py:410
  259.8 13.9 %collective-permute-start.35 = (f16[8,128,256]{2,1,0:T(8,128)(2,1)S(1)}, f16[8,128,256]{2,1,0:T(8,128)(2,1)S(1)}, u32[]{:S(2)}, u32[]{:S(2)}) collective-permute-start(f16[8,128,256]{2,1,0:T(8,128)(2,1)S(1)} %get-tuple-element.70), channel_id=1, source_target_pairs={{0,24},{4,100},{8,0},{12,108},{16,8},{20,116},{24,16},{28,124},{32... | collective-permute-start | bytes 1572872 | tf_op jit(solution)/shard_map/ppermute | solution.py:410
  274.0 1.6 collective-permute-start.36
  (11 other events, 59.7 us)

commit v6 on v5

--- a/solution.py
+++ b/solution.py
@@ -1,3 +1,5 @@
+import functools
+
 import jax
 import jax.numpy as jnp
 from jax import lax
@@ -141,12 +143,16 @@
 def density_last_body(order, *refs):
     count = PIECES - EARLY
     chunks = refs[:count]
-    (table, dmat, weights, xc, rho_in, pacc_in, top_in, rho, sent, pacc, block_out, *bufs) = (
-        refs[count:]
-    )
-    pacc[...] = pacc_in[...]
+    (table, dmat_in, pacc_in, weights, xc, home_rows, rho_in, top_in, rho, sent, *rest) = refs[count:]
+    pacc, dmat, block_out, lsem, *bufs = rest
+    batch = order[EARLY] // 4
+    pltpu.make_async_copy(dmat_in.at[pl.ds(batch, 1)], dmat.at[pl.ds(batch, 1)], lsem.at[0]).start()
+    pltpu.make_async_copy(pacc_in, pacc, lsem.at[1]).start()
     rho[...] = rho_in[...]
     block_out[...] = jnp.zeros_like(block_out)
+    block_out[pl.ds(17, 2), :] = home_rows[...]
+    pltpu.make_async_copy(dmat_in.at[pl.ds(batch, 1)], dmat.at[pl.ds(batch, 1)], lsem.at[0]).wait()
+    pltpu.make_async_copy(pacc_in, pacc, lsem.at[1]).wait()
     top = density_steps(
         order, EARLY, count, chunks, dmat, table, weights, xc, rho, pacc, bufs, top_in[...]
     )
@@ -164,17 +170,35 @@
         sent[dest] = block_out[...]
 
 
-def potential_body(table, got, even, odd, weights, xc, rho, coeffs, pot, scale, bound, *scratch):
-    tbuf, column, tsem = scratch
+def potential_body(table, got, mine, weights, xc, rho, coeffs, pot, scale, bound, *scratch):
+    tbuf, column, data, tsem = scratch
     for i in range(2):
         pltpu.make_async_copy(table.at[i], tbuf.at[i], tsem.at[i]).start()
-    first = jnp.zeros((even.shape[0], 128), jnp.float32)
-    second = jnp.zeros((even.shape[0], 128), jnp.float32)
-    for term in split3(got[...]):
-        first = first + jnp.dot(even[...], term, preferred_element_type=jnp.float32)
-        second = second + jnp.dot(odd[...], term, preferred_element_type=jnp.float32)
+    natoms = coeffs.shape[0]
+    homes = []
+    for which in range(2):
+        segments = []
+        for group in range(4):
+            row = jnp.zeros((1, 128), jnp.float32)
+            for k in range(8):
+                row = row + got[pl.ds((group * 8 + k) * PAY_ROWS + 17 + which, 1), :]
+            segments.append(row)
+        homes.append(jnp.concatenate(segments, axis=1))
+    for k in range(32):
+        data[pl.ds(k * 16, 16), :] = got[pl.ds(k * PAY_ROWS, 16), :]
+    stored = lax.broadcasted_iota(jnp.int32, (natoms, 128), 0).astype(jnp.float32)
+    wanted = jnp.concatenate([stored, mine[...]], axis=0)
+    wanted = jnp.concatenate([wanted] * 4, axis=1)
+    even, odd = [
+        jnp.where(wanted == row, 1.0, 0.0).astype(jnp.bfloat16)
+        for row in homes
+    ]
+    first = jnp.zeros((natoms + 32, 128), jnp.float32)
+    second = jnp.zeros((natoms + 32, 128), jnp.float32)
+    for term in split3(data[...]):
+        first = first + jnp.dot(even, term, preferred_element_type=jnp.float32)
+        second = second + jnp.dot(odd, term, preferred_element_type=jnp.float32)
     summed = first[:, :64] + second[:, 64:]
-    natoms = coeffs.shape[0]
     coeffs[...] = summed[:natoms]
     turned = summed[natoms:].T
     for k in range(32):
@@ -210,7 +234,7 @@
     lax.fori_loop(0, PIECES, step, 0)
 
 
-def ham_body(order, slots, place, *refs):
+def ham_body(quarter, order, slots, place, *refs):
     chunks = refs[: 2 * CHUNKS]
     scale_mine, scale_beside, *rest = refs[2 * CHUNKS :]
     outs, (dense, held, rows_of, psem, osem) = rest[:4], rest[4:]
@@ -239,7 +263,7 @@
     pltpu.make_async_copy(held, held, psem).wait()
 
     def product(side, b, col):
-        left = held[side, b, 0].reshape(2 * BLK, 4 * HALF)
+        left = held[side, b, 0, :, quarter * 64 : (quarter + 1) * 64].reshape(BLK, 4 * HALF)
         right = jnp.concatenate([held[side, b, core, col], held[side, b, 1 - core, col]], axis=0)
         right = (right.astype(jnp.float32) * rows_of[side, b]).astype(jnp.bfloat16)
         return lax.dot_general(
@@ -252,7 +276,7 @@
         for k in range(2):
             for row in range(NB):
                 slot = slots[side * 32 + b * 16 + row * NB + cols + k]
-                dense[slot] += parts[k][row * 128 : (row + 1) * 128]
+                dense[slot] += parts[k][row * 64 : (row + 1) * 64]
         return 0
 
     lax.fori_loop(0, 8, step, 0)
@@ -311,28 +335,31 @@
     )(order, place, which, where, *chunks, *sources, table, weights, xc)
 
 
-def density_last(order, chunks, table, dmat, weights, xc, rho, pacc, top):
+def density_last(order, chunks, table, dmat, pacc, weights, xc, home_rows, rho, top):
     count = PIECES - EARLY
+    nbasis = NB * BLK
     return pl.pallas_call(
         density_last_body,
         out_shape=(
             jax.ShapeDtypeStruct((PIECES, 1, HALF), jnp.float32),
             jax.ShapeDtypeStruct((32, PAY_ROWS, 128), jnp.float32),
         ),
-        in_specs=[smem_spec()] + [any_spec()] * (count + 1) + [vmem_spec()] * 6,
+        in_specs=[smem_spec()] + [any_spec()] * (count + 3) + [vmem_spec()] * 5,
         out_specs=(vmem_spec(),) * 2,
         scratch_shapes=[
-            pltpu.VMEM((2, NB * BLK, 128), jnp.float32),
+            pltpu.VMEM((2, nbasis, 128), jnp.float32),
+            pltpu.VMEM((2, nbasis, nbasis), jnp.bfloat16),
             pltpu.VMEM((PAY_ROWS, 128), jnp.float32),
+            pltpu.SemaphoreType.DMA((2,)),
         ]
         + density_buffers(count),
         compiler_params=pltpu.CompilerParams(vmem_limit_bytes=24 << 20),
         cost_estimate=density_cost(count),
         name="density_last",
-    )(order, *chunks, table, dmat, weights, xc, rho, pacc, top)
-
-
-def potential_call(table, got, even, odd, weights, xc, rho, natoms):
+    )(order, *chunks, table, dmat, pacc, weights, xc, home_rows, rho, top)
+
+
+def potential_call(table, got, mine, weights, xc, rho, natoms):
     row = jax.ShapeDtypeStruct((PIECES, 1, HALF), jnp.float32)
     return pl.pallas_call(
         potential_body,
@@ -342,11 +369,12 @@
             row,
             jax.ShapeDtypeStruct((1, 128), jnp.float32),
         ),
-        in_specs=[any_spec()] + [vmem_spec()] * 6,
+        in_specs=[any_spec()] + [vmem_spec()] * 5,
         out_specs=(vmem_spec(),) * 4,
         scratch_shapes=[
             pltpu.VMEM((3, NB * BLK, HALF), jnp.float32),
             pltpu.VMEM((2048, 128), jnp.float32),
+            pltpu.VMEM((512, 128), jnp.float32),
             pltpu.SemaphoreType.DMA((3,)),
         ],
         compiler_params=pltpu.CompilerParams(vmem_limit_bytes=16 << 20),
@@ -354,17 +382,17 @@
             flops=16 << 20, bytes_accessed=16 << 20, transcendentals=0
         ),
         name="potential",
-    )(table, got, even, odd, weights, xc, rho)
-
-
-def ham_call(order, slots, place, chunks, scale_mine, scale_beside):
+    )(table, got, mine, weights, xc, rho)
+
+
+def ham_call(quarter, order, slots, place, chunks, scale_mine, scale_beside):
     return pl.pallas_call(
-        ham_body,
-        out_shape=(jax.ShapeDtypeStruct((32, 128, BLK), jnp.float32),) * 4,
+        functools.partial(ham_body, quarter),
+        out_shape=(jax.ShapeDtypeStruct((32, 64, BLK), jnp.float32),) * 4,
         in_specs=[smem_spec()] * 3 + [any_spec()] * (2 * CHUNKS) + [vmem_spec()] * 2,
         out_specs=(any_spec(),) * 4,
         scratch_shapes=[
-            pltpu.VMEM((128, 128, BLK), jnp.float32),
+            pltpu.VMEM((128, 64, BLK), jnp.float32),
             pltpu.VMEM((2, 2, 2, NB, 128, 4 * HALF), jnp.bfloat16),
             pltpu.VMEM((2, 2, 1, 4 * HALF), jnp.float32),
             pltpu.SemaphoreType.DMA,
@@ -372,7 +400,7 @@
         ],
         compiler_params=pltpu.CompilerParams(vmem_limit_bytes=38 << 20),
         cost_estimate=pl.CostEstimate(
-            flops=2 * 4096 * 1024 * 1024, bytes_accessed=32 << 20, transcendentals=0
+            flops=4096 * 1024 * 1024, bytes_accessed=24 << 20, transcendentals=0
         ),
         name="ham",
     )(
@@ -505,31 +533,19 @@
     ahead_tiles = lax.ppermute(stored, "grid", core_perm(-1, True))
     behind_tiles = lax.ppermute(stored, "grid", core_perm(1, True))
 
-    row = jnp.pad(atom_homes.astype(jnp.float32), (0, 128 - slots_here))
-    home_rows = lax.all_to_all(
-        jnp.broadcast_to(row[None, None], (groups, 8, 128)), "grid", 0, 0, tiled=True
-    )[:, 0, :slots_here]
-    wanted_rows = jnp.concatenate(
-        [jnp.arange(natoms, dtype=jnp.float32), atom_homes.astype(jnp.float32)]
-    )
-
-    def chooser(which):
-        held = jnp.pad(
-            home_rows.reshape(groups, slots_here // 2, 2)[:, :, which],
-            ((0, 0), (0, PAY_ROWS - slots_here // 2)),
-            constant_values=-1.0,
-        ).reshape(-1)
-        return (wanted_rows[:, None] == held[None, :]).astype(jnp.bfloat16)
-
-    even, odd = chooser(0), chooser(1)
+    lane = jnp.arange(128, dtype=jnp.int32)
+    here = (lane // 16) == (me % 8)
+    home_floats = atom_homes.astype(jnp.float32)
+    home_rows = jnp.where(here[None, :], jnp.tile(home_floats.reshape(16, 2).T, (1, 8)), 0.0)
+    my_homes = jnp.broadcast_to(home_floats[:, None], (slots_here, 128))
     below0, above1, hart = lax.optimization_barrier((below0, above1, hart))
     far0 = lax.ppermute(below0, "pert", ring(1))
     far1 = lax.ppermute(above1, "pert", ring(3))
     chunks = [own0, own1, below0, below1, above0, above1, far0, far1]
     beside = [lax.ppermute(chunk, "grid", swap) for chunk in chunks]
 
-    ahead_tiles, behind_tiles, even, odd, slots = lax.optimization_barrier(
-        (ahead_tiles, behind_tiles, even, odd, slots)
+    ahead_tiles, behind_tiles, slots, home_rows, my_homes = lax.optimization_barrier(
+        (ahead_tiles, behind_tiles, slots, home_rows, my_homes)
     )
     rows2 = 4 * tile_dev
     far_tiles0 = lax.ppermute(ahead_tiles[:rows2], "grid", core_perm(-1, True))
@@ -539,34 +555,39 @@
     rho, pacc, top, dmat = density_first(
         order, core_place, which, where, chunks[:EARLY], sources, gauss, weights, xc
     )
-    rho, sent = density_last(order, chunks[EARLY:], gauss, dmat, weights, xc, rho, pacc, top)
+    rho, sent = density_last(
+        order, chunks[EARLY:], gauss, dmat, pacc, weights, xc, home_rows, rho, top
+    )
     got = lax.all_to_all(sent, "grid", split_axis=0, concat_axis=0, tiled=True)
     all_coeffs, pot, scale, bound = potential_call(
-        hart, got.reshape(groups * PAY_ROWS, 128), even, odd, weights, xc, rho, natoms
+        hart, got.reshape(groups * PAY_ROWS, 128), my_homes, weights, xc, rho, natoms
     )
     atom_dev = natoms // groups
     own_coeffs = lax.dynamic_slice_in_dim(all_coeffs, me * atom_dev, atom_dev, axis=0)
     ham_bound = PHI_MAX_SQ * 2048 * 0.05 * groups * bound[0, 0] * 1.01 + 1e-20
 
     scale_beside = lax.ppermute(scale, "grid", swap)
-    dense = ham_call(
-        order,
-        slots,
-        core_place,
-        chunks + beside,
-        scale.reshape(2, 1, 4 * HALF),
-        scale_beside.reshape(2, 1, 4 * HALF),
-    )
-
     factor = F16_TOP / ham_bound
-    dense = [d.reshape(4, 2 * tile_dev, 128, BLK) for d in dense]
-    chip = direct_sum(list(ring_sum(dense, factor)))
-    chip = chip.reshape(2, tile_dev, 128, BLK)
-    keep = jnp.where(first_core, chip[0], chip[1])
-    give = jnp.where(first_core, chip[1], chip[0])
-    came = wide(lax.ppermute(cast(give), "grid", swap))
+    sums = []
+    for quarter in range(2):
+        dense = ham_call(
+            quarter,
+            order,
+            slots,
+            core_place,
+            chunks + beside,
+            scale.reshape(2, 1, 4 * HALF),
+            scale_beside.reshape(2, 1, 4 * HALF),
+        )
+        dense = [d.reshape(4, 2 * tile_dev, 64, BLK) for d in dense]
+        chip = direct_sum(list(ring_sum(dense, factor)))
+        chip = chip.reshape(2, tile_dev, 64, BLK)
+        keep = jnp.where(first_core, chip[0], chip[1])
+        give = jnp.where(first_core, chip[1], chip[0])
+        came = wide(lax.ppermute(cast(give), "grid", swap))
+        sums.append((jnp.where(first_core, keep, came), jnp.where(first_core, came, keep)))
     hamiltonian = jnp.concatenate(
-        [jnp.where(first_core, keep, came), jnp.where(first_core, came, keep)], axis=1
+        [sums[0][0], sums[1][0], sums[0][1], sums[1][1]], axis=1
     ) * (ham_bound / F16_TOP)
     return (hamiltonian[None], own_coeffs[None], pot.reshape(1, -1))
 

time: 282 us -> 284 us (level); the launches traced: 277 us -> 282 us
  blocking collectives: 14.2 us -> 0 us
  starting transfers between devices: 37.2 us -> 48.3 us
  local copies, waits for them, and re-layouts: 27.7 us -> 37.1 us
  Pallas kernels: 48.3 us -> 57 us
  waiting for transfers between devices: 120 us -> 112 us
    all_to_all x1 -> x0, blocking collectives: 14.2 us -> none  [one_device(): got = lax.all_to_all(sent, 'grid', split_axis=0, concat_axis=0, tiled=True)]
    ppermute x1, waiting for transfers between devices: 5.68 us -> 17.8 us  [one_device(): far0 = lax.ppermute(below0, 'pert', ring(1))]
    pallas_call x1 -> x2, Pallas kernels: 21.8 us -> 31.2 us  [ham_call(): pl.pallas_call(functools.partial(ham_body, quarter), out_shape=(jax.Shape...]
    ppermute x1 -> x2, waiting for transfers between devices: 10.1 us -> 1.59 us  [ring_sum(): lax.ppermute(cast(parts[2][:half] * factor), 'grid', core_perm(1, False))]
    ppermute x1, waiting for transfers between devices: 7.41 us -> 0.01 us  [one_device(): far_tiles0 = lax.ppermute(ahead_tiles[:rows2], 'grid', core_perm(-1, True))]
    ppermute x1, waiting for transfers between devices: 8.17 us -> 15.3 us  [one_device(): far_tiles1 = lax.ppermute(behind_tiles[rows2:], 'grid', core_perm(1, True))]
    unnamed x49 -> x66, local copies, waits for them, and re-layouts: 20.6 us -> 27.6 us
    ppermute x1 -> x2, waiting for transfers between devices: 22.9 us -> 16.6 us  [ring_sum(): got_below = lax.ppermute(up, 'grid', core_perm(1, False))]
  transfers between devices with their start and end apart: 38 -> 46, of which waited for: 17 -> 17; matrix products, arithmetic and copies ran while one was open for 12% -> 13% of each run, Pallas kernels for 10% -> 9%
where the time goes in v6:
time: 284 us; the launch traced here: 282 us
  waiting for transfers between devices  112 us (39%)
  Pallas kernels  57 us (20%)
  starting transfers between devices  48.3 us (17%)
  local copies, waits for them, and re-layouts  37.1 us (13%)
  other arithmetic  26 us (9%)
    pallas_call x2, Pallas kernels, ham_call(): pl.pallas_call(functools.partial(ham_body, quarter), out_shape=(jax.Shape...  31.2 us
    unnamed x66, local copies, waits for them, and re-layouts  27.6 us
    ppermute x1, waiting for transfers between devices, one_device(): above0 = lax.ppermute(own0, 'pert', ring(3))  19.2 us
    ppermute x1, waiting for transfers between devices, one_device(): far0 = lax.ppermute(below0, 'pert', ring(1))  17.8 us
    ppermute x2, waiting for transfers between devices, ring_sum(): got_below = lax.ppermute(up, 'grid', core_perm(1, False))  16.6 us
    pallas_call x1, Pallas kernels, density_first(): pl.pallas_call(density_first_body, out_shape=(jax.ShapeDtypeStruct((PIECE...  15.9 us
    ppermute x1, waiting for transfers between devices, one_device(): far_tiles1 = lax.ppermute(behind_tiles[rows2:], 'grid', core_perm(1, True))  15.3 us
    ppermute x1, waiting for transfers between devices, one_device(): above1 = lax.ppermute(own1, 'pert', ring(3))  14.6 us
  transfers between devices with their start and end apart: 46, of which 17 were waited for; matrix products, arithmetic and copies ran while one was open for 13% of the time, Pallas kernels for 9%

profile of v6, /device:TPU:0, one launch (start us, length us, event | category | flops | bytes accessed | tf_op | source)
XLA Modules:
  0.0 281.8 jit_solution(5788874554790948627)
XLA Ops:
  1.8 2.7 fusion.27
  5.1 1.8 collective-permute-start.7
  8.6 4.1 %collective-permute-start.1 = (bf16[8,128,256]{2,1,0:T(8,128)(2,1)S(1)}, bf16[8,128,256]{2,1,0:T(8,128)(2,1)S(1)}, u32[]{:S(2)}, u32[]{:S(2)}) collective-permute-start(bf16[8,128,256]{2,1,0:T(8,128)(2,1)S(1)} %pad_maximum_fusion), channel_id=1, source_target_pairs={{0,96},{4,28},{8,104},{12,4},{16,112},{20,12},{24,120},{28,20},{32... | collective-permute-start | bytes 1572872 | tf_op jit(solution)/shard_map/ppermute | solution.py:485
  14.5 8.2 %fusion.refs_16_.refs_2_ = f32[8,1024,512]{2,1,0:T(8,128)} fusion(f32[1024]{0:T(1024)S(1)} %div.156, f32[8,16,512]{2,1,0:T(8,128)S(1)} %bitcast.130), kind=kLoop, calls=%fused_computation.3 | loop fusion | flops 4194304 | bytes 17043456 | tf_op jit(solution)/shard_map/exp | solution.py:523
  22.7 2.4 collective-permute-done.1
  25.1 3.8 %collective-permute-done.3 = bf16[8,128,256]{2,1,0:T(8,128)(2,1)} collective-permute-done((bf16[8,128,256]{2,1,0:T(8,128)(2,1)S(1)}, bf16[8,128,256]{2,1,0:T(8,128)(2,1)}, u32[]{:S(2)}, u32[]{:S(2)}) %collective-permute-start.3) | collective-permute-done | bytes 524320 | tf_op jit(solution)/shard_map/ppermute | solution.py:485
  29.7 1.9 constant_dynamic-update-slice_fusion.1
  31.6 1.9 constant_dynamic-update-slice_fusion.refs_6_
  33.5 2.8 collective-permute-start.4
  36.2 1.5 copy.26
  37.7 1.8 collective-permute-start.8
  39.5 1.7 collective-permute-start.10
  41.7 7.5 %bitcast_divide_fusion.table = f32[8,1024,512]{2,1,0:T(8,128)} fusion(f32[1024]{0:T(1024)S(1)} %div.180, f32[8,16,512]{2,1,0:T(8,128)S(1)} %bitcast.129), kind=kLoop, calls=%fused_computation | loop fusion | flops 8388608 | bytes 17043456 | tf_op jit(solution)/shard_map/div | solution.py:525
  49.4 14.6 %collective-permute-done.8.refs_5_ = bf16[1024,512]{1,0:T(8,128)(2,1)} collective-permute-done((bf16[1024,512]{1,0:T(8,128)(2,1)S(1)}, bf16[1024,512]{1,0:T(8,128)(2,1)}, u32[]{:S(2)}, u32[]{:S(2)}) %collective-permute-start.8) | collective-permute-done | bytes 1048608 | tf_op jit(solution)/shard_map/ppermute | solution.py:470
  65.3 19.2 %collective-permute-done.10.refs_4_ = bf16[1024,512]{1,0:T(8,128)(2,1)} collective-permute-done((bf16[1024,512]{1,0:T(8,128)(2,1)S(1)}, bf16[1024,512]{1,0:T(8,128)(2,1)}, u32[]{:S(2)}, u32[]{:S(2)}) %collective-permute-start.10) | collective-permute-done | bytes 1048608 | tf_op jit(solution)/shard_map/ppermute | solution.py:472
  84.4 1.4 collective-permute-start.11
  85.8 1.9 collective-permute-start.12
  89.7 1.3 slice.61
  93.6 17.8 %collective-permute-done.11.refs_0_ = bf16[1024,512]{1,0:T(8,128)(2,1)} collective-permute-done((bf16[1024,512]{1,0:T(8,128)(2,1)S(1)}, bf16[1024,512]{1,0:T(8,128)(2,1)}, u32[]{:S(2)}, u32[]{:S(2)}) %collective-permute-start.11) | collective-permute-done | bytes 1048608 | tf_op jit(solution)/shard_map/ppermute | solution.py:542
  112.2 15.3 %collective-permute-done.22.refs_9_ = bf16[16,128,256]{2,1,0:T(8,128)(2,1)} collective-permute-done((bf16[16,128,256]{2,1,0:T(8,128)(2,1)S(1)}, bf16[16,128,256]{2,1,0:T(8,128)(2,1)}, u32[]{:S(2)}, u32[]{:S(2)}) %collective-permute-start.22) | collective-permute-done | bytes 1048608 | tf_op jit(solution)/shard_map/ppermute | solution.py:552
  128.4 2.1 collective-permute-done.26.refs_14_
  131.2 15.9 %density_first.1 = (f32[8,1,512]{2,1,0:T(1,128)S(1)}, f32[2,1024,128]{2,1,0:T(8,128)S(1)}, f32[1,512]{1,0:T(1,128)S(1)}, bf16[2,1024,1024]{2,1,0:T(8,128)(2,1)}) custom-call(s32[8]{0:T(128)S(1)} %fusion.14.order, s32[1]{0:T(128)} %bitcast.5.place, s32[64]{0:T(128)S(1)} %get-tuple-element.100.which, s32[64]{0:T(128)S(1)} %get-tuple-element.101.where, ...), custom_call_target="tpu_custom_call" | custom-call | flops 6442450944 | bytes 18874368 | tf_op jit(solution)/shard_map/density_first/pallas_call | solution.py:319
  147.1 5.8 %copy-done = f32[8,1024,512]{2,1,0:T(8,128)S(1)} copy-done((f32[8,1024,512]{2,1,0:T(8,128)S(1)}, f32[8,1024,512]{2,1,0:T(8,128)}, u32[]{:S(2)}) %copy-start) | copy-done | bytes 16777240
  152.8 2.2 copy-done.2
  155.0 5.5 %density_last.1 = (f32[8,1,512]{2,1,0:T(1,128)S(1)}, f32[32,24,128]{2,1,0:T(8,128)S(1)}) custom-call(s32[8]{0:T(128)S(1)} %fusion.14.order, bf16[1024,512]{1,0:T(8,128)(2,1)} %collective-permute-done.11.refs_0_, bf16[1024,512]{1,0:T(8,128)(2,1)} %collective-permute-done.12.refs_1_, f32[8,1024,512]{2,1,0:T(8,128)S(1)} %copy-done, ...), custom_call_target="tpu_custom_call" | custom-call | flops 2147483648 | bytes 6291456 | tf_op jit(solution)/shard_map/density_last/pallas_call | solution.py:341
  161.9 4.4 %all-to-all-start = ((f32[32,24,128]{2,1,0:T(8,128)}), f32[32,24,128]{2,1,0:T(8,128)S(1)}, u32[]{:S(2)}, u32[]{:S(2)}) async-start(f32[32,24,128]{2,1,0:T(8,128)} %copy-done.3), calls=%async_computation | async-start | bytes 786432 | tf_op jit(solution)/shard_map/all_to_all | solution.py:561
  166.3 10.2 %all-to-all-done = f32[32,24,128]{2,1,0:T(8,128)S(1)} async-done(((f32[32,24,128]{2,1,0:T(8,128)}), f32[32,24,128]{2,1,0:T(8,128)S(1)}, u32[]{:S(2)}, u32[]{:S(2)}) %all-to-all-start) | async-done | bytes 393248 | tf_op jit(solution)/shard_map/all_to_all | solution.py:561
  176.5 5.8 %copy-done.1 = f32[8,1024,512]{2,1,0:T(8,128)S(1)} copy-done((f32[8,1024,512]{2,1,0:T(8,128)S(1)}, f32[8,1024,512]{2,1,0:T(8,128)}, u32[]{:S(2)}) %copy-start.1) | copy-done | bytes 16777240
  184.4 4.4 %potential.1 = (f32[256,64]{1,0:T(8,128)S(1)}, f32[8,1,512]{2,1,0:T(1,128)}, f32[8,1,512]{2,1,0:T(1,128)S(1)}, f32[1,128]{1,0:T(1,128)S(1)}) custom-call(f32[8,1024,512]{2,1,0:T(8,128)S(1)} %copy-done.1, f32[768,128]{1,0:T(8,128)S(1)} %bitcast.111, f32[32,128]{1,0:T(8,128)S(1)} %copy-done.7, f32[8,1,512]{2,1,0:T(1,128)S(1)} %bitcast.114, ...), custom_call_target="tpu_custom_call" | custom-call | flops 16777216 | bytes 16777216 | tf_op jit(solution)/shard_map/potential/pallas_call | solution.py:364
  190.1 15.6 %ham.2 = (f32[32,64,256]{2,1,0:T(8,128)}, f32[32,64,256]{2,1,0:T(8,128)}, f32[32,64,256]{2,1,0:T(8,128)}, f32[32,64,256]{2,1,0:T(8,128)}) custom-call(s32[8]{0:T(128)S(1)} %copy-done.11, s32[64]{0:T(128)S(1)} %copy-done.12, s32[1]{0:T(128)} %bitcast.5.place, bf16[4,2,128,512]{3,2,1,0:T(8,128)(2,1)S(1)} %bitcast.101, bf16[4,2,128,512]{3,2,1,0:T(8,128)(2,1)S(1)} %bitcast.107, ...), custom_call_target="tpu_custom_call" | custom-call | flops 4294967296 | bytes 25165824 | tf_op jit(solution)/shard_map/ham/pallas_call | solution.py:389
  205.7 15.6 %ham.3 = (f32[32,64,256]{2,1,0:T(8,128)}, f32[32,64,256]{2,1,0:T(8,128)}, f32[32,64,256]{2,1,0:T(8,128)}, f32[32,64,256]{2,1,0:T(8,128)}) custom-call(s32[8]{0:T(128)S(1)} %copy-done.11, s32[64]{0:T(128)S(1)} %copy-done.12, s32[1]{0:T(128)} %bitcast.5.place, bf16[4,2,128,512]{3,2,1,0:T(8,128)(2,1)S(1)} %bitcast.102, bf16[4,2,128,512]{3,2,1,0:T(8,128)(2,1)S(1)} %bitcast.108, ...), custom_call_target="tpu_custom_call" | custom-call | flops 4294967296 | bytes 25165824 | tf_op jit(solution)/shard_map/ham/pallas_call | solution.py:389
  221.5 1.4 copy-done.20
  223.8 2.7 collective-permute-start.31
  226.7 1.4 copy-done.18
  228.5 3.2 %collective-permute-start.39 = (f16[2,8,64,256]{3,2,1,0:T(8,128)(2,1)S(1)}, f16[2,8,64,256]{3,2,1,0:T(8,128)(2,1)S(1)}, u32[]{:S(2)}, u32[]{:S(2)}) collective-permute-start(f16[2,8,64,256]{3,2,1,0:T(8,128)(2,1)S(1)} %bitcast.131), channel_id=1, source_target_pairs={{0,96},{4,28},{8,104},{12,4},{16,112},{20,12},{24,120},{28,20},{32... | collective-permute-start | bytes 1572872 | tf_op jit(solution)/shard_map/ppermute | solution.py:427
  231.9 1.4 copy-done.16
  234.5 3.3 %collective-permute-start.32 = (f16[4,8,64,256]{3,2,1,0:T(8,128)(2,1)S(1)}, f16[4,8,64,256]{3,2,1,0:T(8,128)(2,1)S(1)}, u32[]{:S(2)}, u32[]{:S(2)}) collective-permute-start(f16[4,8,64,256]{3,2,1,0:T(8,128)(2,1)S(1)} %add_convert_fusion.2), channel_id=1, source_target_pairs={{0,96},{4,28},{8,104},{12,4},{16,112},{20,12},{24,120},{28,20},{32... | collective-permute-start | bytes 3145736 | tf_op jit(solution)/shard_map/ppermute | solution.py:432
  237.8 1.5 collective-permute-done.37
  240.2 3.3 %collective-permute-start.40 = (f16[4,8,64,256]{3,2,1,0:T(8,128)(2,1)S(1)}, f16[4,8,64,256]{3,2,1,0:T(8,128)(2,1)S(1)}, u32[]{:S(2)}, u32[]{:S(2)}) collective-permute-start(f16[4,8,64,256]{3,2,1,0:T(8,128)(2,1)S(1)} %add_convert_fusion), channel_id=1, source_target_pairs={{0,96},{4,28},{8,104},{12,4},{16,112},{20,12},{24,120},{28,20},{32... | collective-permute-start | bytes 3145736 | tf_op jit(solution)/shard_map/ppermute | solution.py:432
  243.6 1.4 copy-done.15
  245.2 5.3 %collective-permute-done.30 = f16[4,8,64,256]{3,2,1,0:T(8,128)(2,1)S(1)} collective-permute-done((f16[4,8,64,256]{3,2,1,0:T(8,128)(2,1)S(1)}, f16[4,8,64,256]{3,2,1,0:T(8,128)(2,1)S(1)}, u32[]{:S(2)}, u32[]{:S(2)}) %collective-permute-start.30) | collective-permute-done | bytes 1048608 | tf_op jit(solution)/shard_map/ppermute | solution.py:431
  251.4 1.5 collective-permute-start.33
  253.7 2.3 collective-permute-start.35
  256.1 11.3 %collective-permute-done.38 = f16[4,8,64,256]{3,2,1,0:T(8,128)(2,1)S(1)} collective-permute-done((f16[4,8,64,256]{3,2,1,0:T(8,128)(2,1)S(1)}, f16[4,8,64,256]{3,2,1,0:T(8,128)(2,1)S(1)}, u32[]{:S(2)}, u32[]{:S(2)}) %collective-permute-start.38) | collective-permute-done | bytes 1048608 | tf_op jit(solution)/shard_map/ppermute | solution.py:431
  268.3 1.5 collective-permute-start.41
  270.6 2.3 collective-permute-start.43
  273.2 3.1 %collective-permute-done.41 = f16[8,64,256]{2,1,0:T(8,128)(2,1)S(1)} collective-permute-done((f16[8,64,256]{2,1,0:T(8,128)(2,1)S(1)}, f16[8,64,256]{2,1,0:T(8,128)(2,1)S(1)}, u32[]{:S(2)}, u32[]{:S(2)}) %collective-permute-start.41) | collective-permute-done | bytes 262176 | tf_op jit(solution)/shard_map/ppermute | solution.py:438
  276.3 2.7 collective-permute-done.42
  (177 shorter events, 30.2 us)
Async XLA Ops:
  1.7 5.2 %collective-permute-start = (bf16[4,128,256]{2,1,0:T(8,128)(2,1)S(1)}, bf16[4,128,256]{2,1,0:T(8,128)(2,1)S(1)}, u32[]{:S(2)}, u32[]{:S(2)}) collective-permute-start(bf16[4,128,256]{2,1,0:T(8,128)(2,1)S(1)} %select_bitcast_fusion), channel_id=1, source_target_pairs={{0,4},{4,0},{8,12},{12,8},{16,20},{20,16},{24,28},{28,24},{32,36},... | collective-permute-start | bytes 786440 | tf_op jit(solution)/shard_map/ppermute | solution.py:481
  5.1 36.2 %collective-permute-start.7 = (bf16[1024,512]{1,0:T(8,128)(2,1)S(1)}, bf16[1024,512]{1,0:T(8,128)(2,1)S(1)}, u32[]{:S(2)}, u32[]{:S(2)}) collective-permute-start(bf16[1024,512]{1,0:T(8,128)(2,1)S(1)} %bitcast.97), channel_id=1, source_target_pairs={{0,1},{1,2},{2,3},{3,0},{4,5},{5,6},{6,7},{7,4},{8,9},{9,10},{10,1... | collective-permute-start | bytes 3145736 | tf_op jit(solution)/shard_map/ppermute | solution.py:469
  8.6 16.4 %collective-permute-start.1 = (bf16[8,128,256]{2,1,0:T(8,128)(2,1)S(1)}, bf16[8,128,256]{2,1,0:T(8,128)(2,1)S(1)}, u32[]{:S(2)}, u32[]{:S(2)}) collective-permute-start(bf16[8,128,256]{2,1,0:T(8,128)(2,1)S(1)} %pad_maximum_fusion), channel_id=1, source_target_pairs={{0,96},{4,28},{8,104},{12,4},{16,112},{20,12},{24,120},{28,20},{32... | collective-permute-start | bytes 1572872 | tf_op jit(solution)/shard_map/ppermute | solution.py:485
  12.7 12.3 %collective-permute-start.2 = (bf16[8,128,256]{2,1,0:T(8,128)(2,1)S(1)}, bf16[8,128,256]{2,1,0:T(8,128)(2,1)}, u32[]{:S(2)}, u32[]{:S(2)}) collective-permute-start(bf16[8,128,256]{2,1,0:T(8,128)(2,1)S(1)} %pad_maximum_fusion), channel_id=1, source_target_pairs={{0,64},{4,20},{8,72},{12,28},{16,80},{20,4},{24,88},{28,12},{32,96... | collective-permute-start | bytes 1572872 | tf_op jit(solution)/shard_map/ppermute | solution.py:485
  12.7 16.1 %collective-permute-start.3 = (bf16[8,128,256]{2,1,0:T(8,128)(2,1)S(1)}, bf16[8,128,256]{2,1,0:T(8,128)(2,1)}, u32[]{:S(2)}, u32[]{:S(2)}) collective-permute-start(bf16[8,128,256]{2,1,0:T(8,128)(2,1)S(1)} %pad_maximum_fusion), channel_id=1, source_target_pairs={{0,32},{4,12},{8,40},{12,20},{16,48},{20,28},{24,56},{28,4},{32,64... | collective-permute-start | bytes 1572872 | tf_op jit(solution)/shard_map/ppermute | solution.py:485
  33.5 52.4 %collective-permute-start.4 = (bf16[32,128,256]{2,1,0:T(8,128)(2,1)}, bf16[32,128,256]{2,1,0:T(8,128)(2,1)}, u32[]{:S(2)}, u32[]{:S(2)}) collective-permute-start(bf16[32,128,256]{2,1,0:T(8,128)(2,1)} %constant_dynamic-update-slice_fusion.refs_6_), channel_id=1, source_target_pairs={{0,24},{4,100},{8,0},{12,108},{16,8},{20,116},{24,16},{28,124},{32... | collective-permute-start | bytes 6291464 | tf_op jit(solution)/shard_map/ppermute | solution.py:533
  36.2 51.4 %collective-permute-start.5 = (bf16[32,128,256]{2,1,0:T(8,128)(2,1)}, bf16[32,128,256]{2,1,0:T(8,128)(2,1)}, u32[]{:S(2)}, u32[]{:S(2)}) collective-permute-start(bf16[32,128,256]{2,1,0:T(8,128)(2,1)} %constant_dynamic-update-slice_fusion.refs_6_), channel_id=1, source_target_pairs={{0,8},{4,36},{8,16},{12,44},{16,24},{20,52},{24,0},{28,60},{32,40}... | collective-permute-start | bytes 6291464 | tf_op jit(solution)/shard_map/ppermute | solution.py:534
  37.7 26.2 %collective-permute-start.8 = (bf16[1024,512]{1,0:T(8,128)(2,1)S(1)}, bf16[1024,512]{1,0:T(8,128)(2,1)}, u32[]{:S(2)}, u32[]{:S(2)}) collective-permute-start(bf16[1024,512]{1,0:T(8,128)(2,1)S(1)} %bitcast.103), channel_id=1, source_target_pairs={{0,3},{1,0},{2,1},{3,2},{4,7},{5,4},{6,5},{7,6},{8,11},{9,8},{10,9... | collective-permute-start | bytes 3145736 | tf_op jit(solution)/shard_map/ppermute | solution.py:470
  39.5 44.9 %collective-permute-start.10 = (bf16[1024,512]{1,0:T(8,128)(2,1)S(1)}, bf16[1024,512]{1,0:T(8,128)(2,1)}, u32[]{:S(2)}, u32[]{:S(2)}) collective-permute-start(bf16[1024,512]{1,0:T(8,128)(2,1)S(1)} %bitcast.98), channel_id=1, source_target_pairs={{0,3},{1,0},{2,1},{3,2},{4,7},{5,4},{6,5},{7,6},{8,11},{9,8},{10,9... | collective-permute-start | bytes 3145736 | tf_op jit(solution)/shard_map/ppermute | solution.py:472
  41.3 43.2 %collective-permute-start.9 = (bf16[1024,512]{1,0:T(8,128)(2,1)S(1)}, bf16[1024,512]{1,0:T(8,128)(2,1)}, u32[]{:S(2)}, u32[]{:S(2)}) collective-permute-start(bf16[1024,512]{1,0:T(8,128)(2,1)S(1)} %bitcast.104), channel_id=1, source_target_pairs={{0,1},{1,2},{2,3},{3,0},{4,5},{5,6},{6,7},{7,4},{8,9},{9,10},{10,1... | collective-permute-start | bytes 3145736 | tf_op jit(solution)/shard_map/ppermute | solution.py:471
  41.7 46.1 %copy-start.25 = (s32[256]{0:T(256)S(1)}, s32[256]{0:T(256)}, u32[]{:S(2)}) copy-start(s32[256]{0:T(256)} %param.23) | copy-start | bytes 3076
  63.9 1.2 collective-permute-start.6
  65.1 27.2 %collective-permute-start.13 = (bf16[1024,512]{1,0:T(8,128)(2,1)S(1)}, bf16[1024,512]{1,0:T(8,128)(2,1)}, u32[]{:S(2)}, u32[]{:S(2)}) collective-permute-start(bf16[1024,512]{1,0:T(8,128)(2,1)S(1)} %bitcast.99), channel_id=1, source_target_pairs={{0,4},{4,0},{8,12},{12,8},{16,20},{20,16},{24,28},{28,24},{32,36},... | collective-permute-start | bytes 3145736 | tf_op jit(solution)/shard_map/ppermute | solution.py:545
  84.4 8.4 %collective-permute-start.14 = (bf16[1024,512]{1,0:T(8,128)(2,1)S(1)}, bf16[1024,512]{1,0:T(8,128)(2,1)}, u32[]{:S(2)}, u32[]{:S(2)}) collective-permute-start(bf16[1024,512]{1,0:T(8,128)(2,1)S(1)} %bitcast.105), channel_id=1, source_target_pairs={{0,4},{4,0},{8,12},{12,8},{16,20},{20,16},{24,28},{28,24},{32,36},... | collective-permute-start | bytes 3145736 | tf_op jit(solution)/shard_map/ppermute | solution.py:545
  84.4 27.0 %collective-permute-start.11 = (bf16[1024,512]{1,0:T(8,128)(2,1)S(1)}, bf16[1024,512]{1,0:T(8,128)(2,1)}, u32[]{:S(2)}, u32[]{:S(2)}) collective-permute-start(bf16[1024,512]{1,0:T(8,128)(2,1)S(1)} %collective-permute-done.7.refs_2_), channel_id=1, source_target_pairs={{0,1},{1,2},{2,3},{3,0},{4,5},{5,6},{6,7},{7,4},{8,9},{9,10},{10,1... | collective-permute-start | bytes 3145736 | tf_op jit(solution)/shard_map/ppermute | solution.py:542
  85.8 25.6 %collective-permute-start.12 = (bf16[1024,512]{1,0:T(8,128)(2,1)}, bf16[1024,512]{1,0:T(8,128)(2,1)}, u32[]{:S(2)}, u32[]{:S(2)}) collective-permute-start(bf16[1024,512]{1,0:T(8,128)(2,1)} %collective-permute-done.8.refs_5_), channel_id=1, source_target_pairs={{0,3},{1,0},{2,1},{3,2},{4,7},{5,4},{6,5},{7,6},{8,11},{9,8},{10,9... | collective-permute-start | bytes 3145736 | tf_op jit(solution)/shard_map/ppermute | solution.py:543
  87.7 23.8 %collective-permute-start.15 = (bf16[1024,512]{1,0:T(8,128)(2,1)S(1)}, bf16[1024,512]{1,0:T(8,128)(2,1)}, u32[]{:S(2)}, u32[]{:S(2)}) collective-permute-start(bf16[1024,512]{1,0:T(8,128)(2,1)S(1)} %collective-permute-done.7.refs_2_), channel_id=1, source_target_pairs={{0,4},{4,0},{8,12},{12,8},{16,20},{20,16},{24,28},{28,24},{32,36},... | collective-permute-start | bytes 3145736 | tf_op jit(solution)/shard_map/ppermute | solution.py:545
  89.7 41.5 %copy-start.5 = (f32[4096]{0:T(1024)S(1)}, f32[4096]{0:T(1024)}, u32[]{:S(2)}) copy-start(f32[4096]{0:T(1024)} %param.16) | copy-start | bytes 49156
  92.3 35.4 %collective-permute-start.23 = (bf16[32,128,256]{2,1,0:T(8,128)(2,1)}, bf16[32,128,256]{2,1,0:T(8,128)(2,1)}, u32[]{:S(2)}, u32[]{:S(2)}) collective-permute-start(bf16[32,128,256]{2,1,0:T(8,128)(2,1)} %constant_dynamic-update-slice_fusion.refs_6_), channel_id=1, source_target_pairs={{0,4},{4,0},{8,12},{12,8},{16,20},{20,16},{24,28},{28,24},{32,36},... | collective-permute-start | bytes 6291464 | tf_op jit(solution)/shard_map/ppermute | solution.py:554
  92.8 19.1 %collective-permute-start.21 = (bf16[16,128,256]{2,1,0:T(8,128)(2,1)S(1)}, bf16[16,128,256]{2,1,0:T(8,128)(2,1)}, u32[]{:S(2)}, u32[]{:S(2)}) collective-permute-start(bf16[16,128,256]{2,1,0:T(8,128)(2,1)S(1)} %slice.61), channel_id=1, source_target_pairs={{0,24},{4,100},{8,0},{12,108},{16,8},{20,116},{24,16},{28,124},{32... | collective-permute-start | bytes 3145736 | tf_op jit(solution)/shard_map/ppermute | solution.py:551
  111.4 16.1 %collective-permute-start.22 = (bf16[16,128,256]{2,1,0:T(8,128)(2,1)S(1)}, bf16[16,128,256]{2,1,0:T(8,128)(2,1)}, u32[]{:S(2)}, u32[]{:S(2)}) collective-permute-start(bf16[16,128,256]{2,1,0:T(8,128)(2,1)S(1)} %slice.62), channel_id=1, source_target_pairs={{0,8},{4,36},{8,16},{12,44},{16,24},{20,52},{24,0},{28,60},{32,40}... | collective-permute-start | bytes 3145736 | tf_op jit(solution)/shard_map/ppermute | solution.py:552
  111.4 19.2 %collective-permute-start.24 = (bf16[32,128,256]{2,1,0:T(8,128)(2,1)}, bf16[32,128,256]{2,1,0:T(8,128)(2,1)}, u32[]{:S(2)}, u32[]{:S(2)}) collective-permute-start(bf16[32,128,256]{2,1,0:T(8,128)(2,1)} %collective-permute-done.4.refs_7_), channel_id=1, source_target_pairs={{0,4},{4,0},{8,12},{12,8},{16,20},{20,16},{24,28},{28,24},{32,36},... | collective-permute-start | bytes 6291464 | tf_op jit(solution)/shard_map/ppermute | solution.py:554
  111.4 19.6 %collective-permute-start.27 = (bf16[32,128,256]{2,1,0:T(8,128)(2,1)}, bf16[32,128,256]{2,1,0:T(8,128)(2,1)}, u32[]{:S(2)}, u32[]{:S(2)}) collective-permute-start(bf16[32,128,256]{2,1,0:T(8,128)(2,1)} %collective-permute-done.5.refs_10_), channel_id=1, source_target_pairs={{0,4},{4,0},{8,12},{12,8},{16,20},{20,16},{24,28},{28,24},{32,36},... | collective-permute-start | bytes 6291464 | tf_op jit(solution)/shard_map/ppermute | solution.py:554
  111.9 16.4 %collective-permute-start.25 = (bf16[16,128,256]{2,1,0:T(8,128)(2,1)}, bf16[16,128,256]{2,1,0:T(8,128)(2,1)}, u32[]{:S(2)}, u32[]{:S(2)}) collective-permute-start(bf16[16,128,256]{2,1,0:T(8,128)(2,1)} %collective-permute-done.21.refs_8_), channel_id=1, source_target_pairs={{0,4},{4,0},{8,12},{12,8},{16,20},{20,16},{24,28},{28,24},{32,36},... | collective-permute-start | bytes 3145736 | tf_op jit(solution)/shard_map/ppermute | solution.py:554
  127.5 3.0 %collective-permute-start.26 = (bf16[16,128,256]{2,1,0:T(8,128)(2,1)}, bf16[16,128,256]{2,1,0:T(8,128)(2,1)}, u32[]{:S(2)}, u32[]{:S(2)}) collective-permute-start(bf16[16,128,256]{2,1,0:T(8,128)(2,1)} %collective-permute-done.22.refs_9_), channel_id=1, source_target_pairs={{0,4},{4,0},{8,12},{12,8},{16,20},{20,16},{24,28},{28,24},{32,36},... | collective-permute-start | bytes 3145736 | tf_op jit(solution)/shard_map/ppermute | solution.py:554
  127.7 61.1 %collective-permute-start.18 = (bf16[1024,512]{1,0:T(8,128)(2,1)}, bf16[1024,512]{1,0:T(8,128)(2,1)}, u32[]{:S(2)}, u32[]{:S(2)}) collective-permute-start(bf16[1024,512]{1,0:T(8,128)(2,1)} %collective-permute-done.8.refs_5_), channel_id=1, source_target_pairs={{0,4},{4,0},{8,12},{12,8},{16,20},{20,16},{24,28},{28,24},{32,36},... | collective-permute-start | bytes 3145736 | tf_op jit(solution)/shard_map/ppermute | solution.py:545
  128.3 61.5 %collective-permute-start.16 = (bf16[1024,512]{1,0:T(8,128)(2,1)}, bf16[1024,512]{1,0:T(8,128)(2,1)}, u32[]{:S(2)}, u32[]{:S(2)}) collective-permute-start(bf16[1024,512]{1,0:T(8,128)(2,1)} %collective-permute-done.9.refs_3_), channel_id=1, source_target_pairs={{0,4},{4,0},{8,12},{12,8},{16,20},{20,16},{24,28},{28,24},{32,36},... | collective-permute-start | bytes 3145736 | tf_op jit(solution)/shard_map/ppermute | solution.py:545
  130.5 59.3 %collective-permute-start.17 = (bf16[1024,512]{1,0:T(8,128)(2,1)}, bf16[1024,512]{1,0:T(8,128)(2,1)}, u32[]{:S(2)}, u32[]{:S(2)}) collective-permute-start(bf16[1024,512]{1,0:T(8,128)(2,1)} %collective-permute-done.10.refs_4_), channel_id=1, source_target_pairs={{0,4},{4,0},{8,12},{12,8},{16,20},{20,16},{24,28},{28,24},{32,36},... | collective-permute-start | bytes 3145736 | tf_op jit(solution)/shard_map/ppermute | solution.py:545
  130.7 59.2 %collective-permute-start.19 = (bf16[1024,512]{1,0:T(8,128)(2,1)}, bf16[1024,512]{1,0:T(8,128)(2,1)}, u32[]{:S(2)}, u32[]{:S(2)}) collective-permute-start(bf16[1024,512]{1,0:T(8,128)(2,1)} %collective-permute-done.11.refs_0_), channel_id=1, source_target_pairs={{0,4},{4,0},{8,12},{12,8},{16,20},{20,16},{24,28},{28,24},{32,36},... | collective-permute-start | bytes 3145736 | tf_op jit(solution)/shard_map/ppermute | solution.py:545
  131.0 58.8 %collective-permute-start.20 = (bf16[1024,512]{1,0:T(8,128)(2,1)}, bf16[1024,512]{1,0:T(8,128)(2,1)}, u32[]{:S(2)}, u32[]{:S(2)}) collective-permute-start(bf16[1024,512]{1,0:T(8,128)(2,1)} %collective-permute-done.12.refs_1_), channel_id=1, source_target_pairs={{0,4},{4,0},{8,12},{12,8},{16,20},{20,16},{24,28},{28,24},{32,36},... | collective-permute-start | bytes 3145736 | tf_op jit(solution)/shard_map/ppermute | solution.py:545
  161.9 14.6 %all-to-all-start = ((f32[32,24,128]{2,1,0:T(8,128)}), f32[32,24,128]{2,1,0:T(8,128)S(1)}, u32[]{:S(2)}, u32[]{:S(2)}) async-start(f32[32,24,128]{2,1,0:T(8,128)} %copy-done.3), calls=%async_computation | async-start | bytes 786432 | tf_op jit(solution)/shard_map/all_to_all | solution.py:561
  188.8 1.3 collective-permute-start.28
  223.2 10.5 %collective-permute-start.29 = (f16[2,8,64,256]{3,2,1,0:T(8,128)(2,1)S(1)}, f16[2,8,64,256]{3,2,1,0:T(8,128)(2,1)S(1)}, u32[]{:S(2)}, u32[]{:S(2)}) collective-permute-start(f16[2,8,64,256]{3,2,1,0:T(8,128)(2,1)S(1)} %bitcast.134), channel_id=1, source_target_pairs={{0,32},{4,12},{8,40},{12,20},{16,48},{20,28},{24,56},{28,4},{32,64... | collective-permute-start | bytes 1572872 | tf_op jit(solution)/shard_map/ppermute | solution.py:426
  223.8 10.3 %collective-permute-start.31 = (f16[2,8,64,256]{3,2,1,0:T(8,128)(2,1)S(1)}, f16[2,8,64,256]{3,2,1,0:T(8,128)(2,1)S(1)}, u32[]{:S(2)}, u32[]{:S(2)}) collective-permute-start(f16[2,8,64,256]{3,2,1,0:T(8,128)(2,1)S(1)} %bitcast.132), channel_id=1, source_target_pairs={{0,96},{4,28},{8,104},{12,4},{16,112},{20,12},{24,120},{28,20},{32... | collective-permute-start | bytes 1572872 | tf_op jit(solution)/shard_map/ppermute | solution.py:427
  228.4 10.9 %collective-permute-start.37 = (f16[2,8,64,256]{3,2,1,0:T(8,128)(2,1)S(1)}, f16[2,8,64,256]{3,2,1,0:T(8,128)(2,1)S(1)}, u32[]{:S(2)}, u32[]{:S(2)}) collective-permute-start(f16[2,8,64,256]{3,2,1,0:T(8,128)(2,1)S(1)} %bitcast.133), channel_id=1, source_target_pairs={{0,32},{4,12},{8,40},{12,20},{16,48},{20,28},{24,56},{28,4},{32,64... | collective-permute-start | bytes 1572872 | tf_op jit(solution)/shard_map/ppermute | solution.py:426
  228.5 11.3 %collective-permute-start.39 = (f16[2,8,64,256]{3,2,1,0:T(8,128)(2,1)S(1)}, f16[2,8,64,256]{3,2,1,0:T(8,128)(2,1)S(1)}, u32[]{:S(2)}, u32[]{:S(2)}) collective-permute-start(f16[2,8,64,256]{3,2,1,0:T(8,128)(2,1)S(1)} %bitcast.131), channel_id=1, source_target_pairs={{0,96},{4,28},{8,104},{12,4},{16,112},{20,12},{24,120},{28,20},{32... | collective-permute-start | bytes 1572872 | tf_op jit(solution)/shard_map/ppermute | solution.py:427
  234.0 16.5 %collective-permute-start.30 = (f16[4,8,64,256]{3,2,1,0:T(8,128)(2,1)S(1)}, f16[4,8,64,256]{3,2,1,0:T(8,128)(2,1)S(1)}, u32[]{:S(2)}, u32[]{:S(2)}) collective-permute-start(f16[4,8,64,256]{3,2,1,0:T(8,128)(2,1)S(1)} %add_convert_fusion.3), channel_id=1, source_target_pairs={{0,32},{4,12},{8,40},{12,20},{16,48},{20,28},{24,56},{28,4},{32,64... | collective-permute-start | bytes 3145736 | tf_op jit(solution)/shard_map/ppermute | solution.py:431
  234.5 16.0 %collective-permute-start.32 = (f16[4,8,64,256]{3,2,1,0:T(8,128)(2,1)S(1)}, f16[4,8,64,256]{3,2,1,0:T(8,128)(2,1)S(1)}, u32[]{:S(2)}, u32[]{:S(2)}) collective-permute-start(f16[4,8,64,256]{3,2,1,0:T(8,128)(2,1)S(1)} %add_convert_fusion.2), channel_id=1, source_target_pairs={{0,96},{4,28},{8,104},{12,4},{16,112},{20,12},{24,120},{28,20},{32... | collective-permute-start | bytes 3145736 | tf_op jit(solution)/shard_map/ppermute | solution.py:432
  239.7 27.7 %collective-permute-start.38 = (f16[4,8,64,256]{3,2,1,0:T(8,128)(2,1)S(1)}, f16[4,8,64,256]{3,2,1,0:T(8,128)(2,1)S(1)}, u32[]{:S(2)}, u32[]{:S(2)}) collective-permute-start(f16[4,8,64,256]{3,2,1,0:T(8,128)(2,1)S(1)} %add_convert_fusion.1), channel_id=1, source_target_pairs={{0,32},{4,12},{8,40},{12,20},{16,48},{20,28},{24,56},{28,4},{32,64... | collective-permute-start | bytes 3145736 | tf_op jit(solution)/shard_map/ppermute | solution.py:431
  240.2 27.2 %collective-permute-start.40 = (f16[4,8,64,256]{3,2,1,0:T(8,128)(2,1)S(1)}, f16[4,8,64,256]{3,2,1,0:T(8,128)(2,1)S(1)}, u32[]{:S(2)}, u32[]{:S(2)}) collective-permute-start(f16[4,8,64,256]{3,2,1,0:T(8,128)(2,1)S(1)} %add_convert_fusion), channel_id=1, source_target_pairs={{0,96},{4,28},{8,104},{12,4},{16,112},{20,12},{24,120},{28,20},{32... | collective-permute-start | bytes 3145736 | tf_op jit(solution)/shard_map/ppermute | solution.py:432
  251.4 19.3 %collective-permute-start.33 = (f16[8,64,256]{2,1,0:T(8,128)(2,1)S(1)}, f16[8,64,256]{2,1,0:T(8,128)(2,1)S(1)}, u32[]{:S(2)}, u32[]{:S(2)}) collective-permute-start(f16[8,64,256]{2,1,0:T(8,128)(2,1)S(1)} %get-tuple-element.83), channel_id=1, source_target_pairs={{0,16},{4,68},{8,24},{12,76},{16,0},{20,84},{24,8},{28,92},{32,48}... | collective-permute-start | bytes 786440 | tf_op jit(solution)/shard_map/ppermute | solution.py:438
  252.8 20.1 %collective-permute-start.34 = (f16[8,64,256]{2,1,0:T(8,128)(2,1)S(1)}, f16[8,64,256]{2,1,0:T(8,128)(2,1)S(1)}, u32[]{:S(2)}, u32[]{:S(2)}) collective-permute-start(f16[8,64,256]{2,1,0:T(8,128)(2,1)S(1)} %get-tuple-element.85), channel_id=1, source_target_pairs={{0,8},{4,36},{8,16},{12,44},{16,24},{20,52},{24,0},{28,60},{32,40}... | collective-permute-start | bytes 786440 | tf_op jit(solution)/shard_map/ppermute | solution.py:438
  253.7 19.2 %collective-permute-start.35 = (f16[8,64,256]{2,1,0:T(8,128)(2,1)S(1)}, f16[8,64,256]{2,1,0:T(8,128)(2,1)S(1)}, u32[]{:S(2)}, u32[]{:S(2)}) collective-permute-start(f16[8,64,256]{2,1,0:T(8,128)(2,1)S(1)} %get-tuple-element.84), channel_id=1, source_target_pairs={{0,24},{4,100},{8,0},{12,108},{16,8},{20,116},{24,16},{28,124},{32... | collective-permute-start | bytes 786440 | tf_op jit(solution)/shard_map/ppermute | solution.py:438
  268.3 8.1 %collective-permute-start.41 = (f16[8,64,256]{2,1,0:T(8,128)(2,1)S(1)}, f16[8,64,256]{2,1,0:T(8,128)(2,1)S(1)}, u32[]{:S(2)}, u32[]{:S(2)}) collective-permute-start(f16[8,64,256]{2,1,0:T(8,128)(2,1)S(1)} %get-tuple-element.86), channel_id=1, source_target_pairs={{0,16},{4,68},{8,24},{12,76},{16,0},{20,84},{24,8},{28,92},{32,48}... | collective-permute-start | bytes 786440 | tf_op jit(solution)/shard_map/ppermute | solution.py:438
  269.7 9.3 %collective-permute-start.42 = (f16[8,64,256]{2,1,0:T(8,128)(2,1)S(1)}, f16[8,64,256]{2,1,0:T(8,128)(2,1)S(1)}, u32[]{:S(2)}, u32[]{:S(2)}) collective-permute-start(f16[8,64,256]{2,1,0:T(8,128)(2,1)S(1)} %get-tuple-element.88), channel_id=1, source_target_pairs={{0,8},{4,36},{8,16},{12,44},{16,24},{20,52},{24,0},{28,60},{32,40}... | collective-permute-start | bytes 786440 | tf_op jit(solution)/shard_map/ppermute | solution.py:438
  270.6 8.4 %collective-permute-start.43 = (f16[8,64,256]{2,1,0:T(8,128)(2,1)S(1)}, f16[8,64,256]{2,1,0:T(8,128)(2,1)S(1)}, u32[]{:S(2)}, u32[]{:S(2)}) collective-permute-start(f16[8,64,256]{2,1,0:T(8,128)(2,1)S(1)} %get-tuple-element.87), channel_id=1, source_target_pairs={{0,24},{4,100},{8,0},{12,108},{16,8},{20,116},{24,16},{28,124},{32... | collective-permute-start | bytes 786440 | tf_op jit(solution)/shard_map/ppermute | solution.py:438
  273.1 6.2 %collective-permute-start.36 = (f16[4,64,256]{2,1,0:T(8,128)(2,1)S(1)}, f16[4,64,256]{2,1,0:T(8,128)(2,1)S(1)}, u32[]{:S(2)}, u32[]{:S(2)}) collective-permute-start(f16[4,64,256]{2,1,0:T(8,128)(2,1)S(1)} %select_convert_fusion.1), channel_id=1, source_target_pairs={{0,4},{4,0},{8,12},{12,8},{16,20},{20,16},{24,28},{28,24},{32,36},... | collective-permute-start | bytes 393224 | tf_op jit(solution)/shard_map/ppermute | solution.py:587
  279.2 1.4 collective-permute-start.44
  (29 other events, 252.4 us)

commit v7 on v6

--- a/solution.py
+++ b/solution.py
@@ -1,5 +1,3 @@
-import functools
-
 import jax
 import jax.numpy as jnp
 from jax import lax
@@ -13,6 +11,7 @@
 HALF = 512
 PIECES = 8
 CHUNKS = 8
+VMEM_GRANT = 60 << 20
 SOURCES = 5
 EARLY = 6
 BLK = 256
@@ -234,7 +233,7 @@
     lax.fori_loop(0, PIECES, step, 0)
 
 
-def ham_body(quarter, order, slots, place, *refs):
+def ham_body(order, slots, place, *refs):
     chunks = refs[: 2 * CHUNKS]
     scale_mine, scale_beside, *rest = refs[2 * CHUNKS :]
     outs, (dense, held, rows_of, psem, osem) = rest[:4], rest[4:]
@@ -263,7 +262,7 @@
     pltpu.make_async_copy(held, held, psem).wait()
 
     def product(side, b, col):
-        left = held[side, b, 0, :, quarter * 64 : (quarter + 1) * 64].reshape(BLK, 4 * HALF)
+        left = held[side, b, 0].reshape(2 * BLK, 4 * HALF)
         right = jnp.concatenate([held[side, b, core, col], held[side, b, 1 - core, col]], axis=0)
         right = (right.astype(jnp.float32) * rows_of[side, b]).astype(jnp.bfloat16)
         return lax.dot_general(
@@ -276,7 +275,7 @@
         for k in range(2):
             for row in range(NB):
                 slot = slots[side * 32 + b * 16 + row * NB + cols + k]
-                dense[slot] += parts[k][row * 64 : (row + 1) * 64]
+                dense[slot] += parts[k][row * 128 : (row + 1) * 128]
         return 0
 
     lax.fori_loop(0, 8, step, 0)
@@ -329,7 +328,7 @@
         + [vmem_spec()] * 2,
         out_specs=(vmem_spec(),) * 4,
         scratch_shapes=[pltpu.SemaphoreType.DMA] + density_buffers(EARLY),
-        compiler_params=pltpu.CompilerParams(vmem_limit_bytes=30 << 20),
+        compiler_params=pltpu.CompilerParams(vmem_limit_bytes=VMEM_GRANT),
         cost_estimate=density_cost(EARLY),
         name="density_first",
     )(order, place, which, where, *chunks, *sources, table, weights, xc)
@@ -353,7 +352,7 @@
             pltpu.SemaphoreType.DMA((2,)),
         ]
         + density_buffers(count),
-        compiler_params=pltpu.CompilerParams(vmem_limit_bytes=24 << 20),
+        compiler_params=pltpu.CompilerParams(vmem_limit_bytes=VMEM_GRANT),
         cost_estimate=density_cost(count),
         name="density_last",
     )(order, *chunks, table, dmat, pacc, weights, xc, home_rows, rho, top)
@@ -377,7 +376,7 @@
             pltpu.VMEM((512, 128), jnp.float32),
             pltpu.SemaphoreType.DMA((3,)),
         ],
-        compiler_params=pltpu.CompilerParams(vmem_limit_bytes=16 << 20),
+        compiler_params=pltpu.CompilerParams(vmem_limit_bytes=VMEM_GRANT),
         cost_estimate=pl.CostEstimate(
             flops=16 << 20, bytes_accessed=16 << 20, transcendentals=0
         ),
@@ -385,20 +384,20 @@
     )(table, got, mine, weights, xc, rho)
 
 
-def ham_call(quarter, order, slots, place, chunks, scale_mine, scale_beside):
+def ham_call(order, slots, place, chunks, scale_mine, scale_beside):
     return pl.pallas_call(
-        functools.partial(ham_body, quarter),
-        out_shape=(jax.ShapeDtypeStruct((32, 64, BLK), jnp.float32),) * 4,
+        ham_body,
+        out_shape=(jax.ShapeDtypeStruct((32, 128, BLK), jnp.float32),) * 4,
         in_specs=[smem_spec()] * 3 + [any_spec()] * (2 * CHUNKS) + [vmem_spec()] * 2,
         out_specs=(any_spec(),) * 4,
         scratch_shapes=[
-            pltpu.VMEM((128, 64, BLK), jnp.float32),
+            pltpu.VMEM((128, 128, BLK), jnp.float32),
             pltpu.VMEM((2, 2, 2, NB, 128, 4 * HALF), jnp.bfloat16),
             pltpu.VMEM((2, 2, 1, 4 * HALF), jnp.float32),
             pltpu.SemaphoreType.DMA,
             pltpu.SemaphoreType.DMA((4,)),
         ],
-        compiler_params=pltpu.CompilerParams(vmem_limit_bytes=38 << 20),
+        compiler_params=pltpu.CompilerParams(vmem_limit_bytes=VMEM_GRANT),
         cost_estimate=pl.CostEstimate(
             flops=4096 * 1024 * 1024, bytes_accessed=24 << 20, transcendentals=0
         ),
@@ -423,14 +422,16 @@
 
 def ring_sum(parts, factor):
     half = parts[2].shape[0] // 2
-    from_below = lax.ppermute(cast(parts[2][:half] * factor), "grid", core_perm(1, False))
-    from_above = lax.ppermute(cast(parts[2][half:] * factor), "grid", core_perm(-1, False))
-    zero = jnp.zeros_like(from_below)
-    up = cast(parts[1] * factor + wide(jnp.concatenate([from_below, zero])))
-    down = cast(parts[3] * factor + wide(jnp.concatenate([zero, from_above])))
-    got_below = lax.ppermute(up, "grid", core_perm(1, False))
-    got_above = lax.ppermute(down, "grid", core_perm(-1, False))
-    return parts[0] * factor + wide(got_below) + wide(got_above)
+    up, down = core_perm(1, False), core_perm(-1, False)
+    from_below = lax.ppermute(cast(parts[2][:half] * factor), "grid", up)
+    from_above = lax.ppermute(cast(parts[2][half:] * factor), "grid", down)
+    below_high = lax.ppermute(cast(parts[1][half:] * factor), "grid", up)
+    above_low = lax.ppermute(cast(parts[3][:half] * factor), "grid", down)
+    below_low = lax.ppermute(cast(parts[1][:half] * factor + wide(from_below)), "grid", up)
+    above_high = lax.ppermute(cast(parts[3][half:] * factor + wide(from_above)), "grid", down)
+    low = parts[0][:half] * factor + wide(below_low) + wide(above_low)
+    high = parts[0][half:] * factor + wide(below_high) + wide(above_high)
+    return [low[0], low[1], high[0], high[1]]
 
 
 def direct_sum(parts):
@@ -568,26 +569,22 @@
 
     scale_beside = lax.ppermute(scale, "grid", swap)
     factor = F16_TOP / ham_bound
-    sums = []
-    for quarter in range(2):
-        dense = ham_call(
-            quarter,
-            order,
-            slots,
-            core_place,
-            chunks + beside,
-            scale.reshape(2, 1, 4 * HALF),
-            scale_beside.reshape(2, 1, 4 * HALF),
-        )
-        dense = [d.reshape(4, 2 * tile_dev, 64, BLK) for d in dense]
-        chip = direct_sum(list(ring_sum(dense, factor)))
-        chip = chip.reshape(2, tile_dev, 64, BLK)
-        keep = jnp.where(first_core, chip[0], chip[1])
-        give = jnp.where(first_core, chip[1], chip[0])
-        came = wide(lax.ppermute(cast(give), "grid", swap))
-        sums.append((jnp.where(first_core, keep, came), jnp.where(first_core, came, keep)))
+    dense = ham_call(
+        order,
+        slots,
+        core_place,
+        chunks + beside,
+        scale.reshape(2, 1, 4 * HALF),
+        scale_beside.reshape(2, 1, 4 * HALF),
+    )
+    dense = [d.reshape(4, 2 * tile_dev, 128, BLK) for d in dense]
+    chip = direct_sum(ring_sum(dense, factor))
+    chip = chip.reshape(2, tile_dev, 128, BLK)
+    keep = jnp.where(first_core, chip[0], chip[1])
+    give = jnp.where(first_core, chip[1], chip[0])
+    came = wide(lax.ppermute(cast(give), "grid", swap))
     hamiltonian = jnp.concatenate(
-        [sums[0][0], sums[1][0], sums[0][1], sums[1][1]], axis=1
+        [jnp.where(first_core, keep, came), jnp.where(first_core, came, keep)], axis=1
     ) * (ham_bound / F16_TOP)
     return (hamiltonian[None], own_coeffs[None], pot.reshape(1, -1))
 

time: 284 us -> 278 us (0.979)
  local copies, waits for them, and re-layouts: 37.1 us -> 17.3 us
  starting transfers between devices: 48.3 us -> 32.4 us
  blocking collectives: 0 us -> 14.8 us
  waiting for transfers between devices: 112 us -> 123 us
  other arithmetic: 26 us -> 30.5 us
    unnamed x66 -> x42, local copies, waits for them, and re-layouts: 27.6 us -> 7.29 us
    ppermute x8 -> x6, waiting for transfers between devices: 18.2 us -> 37.5 us  [the longest x1 17.8 us: ring_sum(): above_low = lax.ppermute(cast(parts[3][:half] * factor), 'grid', down)]
    all_to_all x0 -> x1, blocking collectives: none -> 14.8 us  [one_device(): got = lax.all_to_all(sent, 'grid', split_axis=0, concat_axis=0, tiled=True)]
    all_to_all x1 -> x0, waiting for transfers between devices: 10.2 us -> none  [one_device(): got = lax.all_to_all(sent, 'grid', split_axis=0, concat_axis=0, tiled=True)]
    pallas_call x2 -> x1, Pallas kernels: 31.2 us -> 23.3 us  [ham_call(): pl.pallas_call(ham_body, out_shape=(jax.ShapeDtypeStruct((32, 128, BLK),...]
    ppermute x8 -> x6, starting transfers between devices: 13.3 us -> 7.04 us  [the longest x1 2.28 us: ring_sum(): lax.ppermute(cast(parts[3][half:] * factor + wide(from_above)), 'grid', d...]
    ppermute x6 -> x3, starting transfers between devices: 9.38 us -> 4.39 us  [direct_sum(): lax.ppermute(cast(parts[d]), 'grid', core_perm(d, True))]
    all_to_all x1 -> x0, starting transfers between devices: 4.39 us -> none  [one_device(): got = lax.all_to_all(sent, 'grid', split_axis=0, concat_axis=0, tiled=True)]
  transfers between devices with their start and end apart: 46 -> 39, of which waited for: 17 -> 15; matrix products, arithmetic and copies ran while one was open for 13% -> 14% of each run, Pallas kernels for 9% -> 12%
where the time goes in v7:
time: 278 us; the launch traced here: 276 us
  waiting for transfers between devices  123 us (44%)
  Pallas kernels  56.8 us (20%)
  starting transfers between devices  32.4 us (12%)
  other arithmetic  30.5 us (11%)
  local copies, waits for them, and re-layouts  17.3 us (6%)
  blocking collectives  14.8 us (5%)
    pallas_call x1, Pallas kernels, ham_call(): pl.pallas_call(ham_body, out_shape=(jax.ShapeDtypeStruct((32, 128, BLK),...  23.3 us
    ppermute x1, waiting for transfers between devices, one_device(): above0 = lax.ppermute(own0, 'pert', ring(3))  19.2 us
    ppermute x1, waiting for transfers between devices, ring_sum(): above_low = lax.ppermute(cast(parts[3][:half] * factor), 'grid', down)  17.8 us
    ppermute x1, waiting for transfers between devices, one_device(): far0 = lax.ppermute(below0, 'pert', ring(1))  17.2 us
    pallas_call x1, Pallas kernels, density_first(): pl.pallas_call(density_first_body, out_shape=(jax.ShapeDtypeStruct((PIECE...  17.2 us
    ppermute x1, waiting for transfers between devices, one_device(): far_tiles1 = lax.ppermute(behind_tiles[rows2:], 'grid', core_perm(1, True))  15.3 us
    all_to_all x1, blocking collectives, one_device(): got = lax.all_to_all(sent, 'grid', split_axis=0, concat_axis=0, tiled=True)  14.8 us
    ppermute x1, waiting for transfers between devices, one_device(): above1 = lax.ppermute(own1, 'pert', ring(3))  14.6 us
  transfers between devices with their start and end apart: 39, of which 15 were waited for; matrix products, arithmetic and copies ran while one was open for 14% of the time, Pallas kernels for 12%

profile of v7, /device:TPU:0, one launch (start us, length us, event | category | flops | bytes accessed | tf_op | source)
XLA Modules:
  0.0 276.2 jit_solution(16906763986463156803)
XLA Ops:
  0.6 1.1 select_bitcast_fusion
  1.8 2.7 fusion.21
  5.1 1.8 collective-permute-start.7
  8.6 0.8 pad_maximum_fusion
  9.4 4.0 %collective-permute-start.1 = (bf16[8,128,256]{2,1,0:T(8,128)(2,1)}, bf16[8,128,256]{2,1,0:T(8,128)(2,1)S(1)}, u32[]{:S(2)}, u32[]{:S(2)}) collective-permute-start(bf16[8,128,256]{2,1,0:T(8,128)(2,1)} %pad_maximum_fusion), channel_id=1, source_target_pairs={{0,96},{4,28},{8,104},{12,4},{16,112},{20,12},{24,120},{28,20},{32... | collective-permute-start | bytes 1572872 | tf_op jit(solution)/shard_map/ppermute | solution.py:486
  13.4 1.3 collective-permute-start.3
  15.2 8.2 %fusion.refs_16_.refs_2_ = f32[8,1024,512]{2,1,0:T(8,128)} fusion(f32[1024]{0:T(1024)S(1)} %div.156, f32[8,16,512]{2,1,0:T(8,128)S(1)} %bitcast.94), kind=kLoop, calls=%fused_computation.3 | loop fusion | flops 4194304 | bytes 17043456 | tf_op jit(solution)/shard_map/exp | solution.py:524
  23.4 2.7 collective-permute-done.1
  26.1 3.7 %collective-permute-done.3 = bf16[8,128,256]{2,1,0:T(8,128)(2,1)} collective-permute-done((bf16[8,128,256]{2,1,0:T(8,128)(2,1)}, bf16[8,128,256]{2,1,0:T(8,128)(2,1)}, u32[]{:S(2)}, u32[]{:S(2)}) %collective-permute-start.3) | collective-permute-done | bytes 524320 | tf_op jit(solution)/shard_map/ppermute | solution.py:486
  29.8 0.8 constant_dynamic-update-slice_fusion.2
  30.6 1.9 constant_dynamic-update-slice_fusion.1
  32.5 1.9 constant_dynamic-update-slice_fusion.refs_6_
  34.4 2.8 collective-permute-start.4
  37.1 1.5 copy.26
  38.6 1.8 collective-permute-start.8
  40.5 1.7 collective-permute-start.10
  42.6 7.4 %bitcast_divide_fusion.table = f32[8,1024,512]{2,1,0:T(8,128)} fusion(f32[1024]{0:T(1024)S(1)} %div.180, f32[8,16,512]{2,1,0:T(8,128)S(1)} %bitcast.93), kind=kLoop, calls=%fused_computation | loop fusion | flops 8388608 | bytes 17043456 | tf_op jit(solution)/shard_map/div | solution.py:526
  50.3 14.6 %collective-permute-done.8.refs_5_ = bf16[1024,512]{1,0:T(8,128)(2,1)} collective-permute-done((bf16[1024,512]{1,0:T(8,128)(2,1)S(1)}, bf16[1024,512]{1,0:T(8,128)(2,1)}, u32[]{:S(2)}, u32[]{:S(2)}) %collective-permute-start.8) | collective-permute-done | bytes 1048608 | tf_op jit(solution)/shard_map/ppermute | solution.py:471
  64.9 1.2 collective-permute-done.6
  66.2 19.2 %collective-permute-done.10.refs_4_ = bf16[1024,512]{1,0:T(8,128)(2,1)} collective-permute-done((bf16[1024,512]{1,0:T(8,128)(2,1)S(1)}, bf16[1024,512]{1,0:T(8,128)(2,1)}, u32[]{:S(2)}, u32[]{:S(2)}) %collective-permute-start.10) | collective-permute-done | bytes 1048608 | tf_op jit(solution)/shard_map/ppermute | solution.py:473
  85.3 1.5 collective-permute-start.11
  86.8 1.9 collective-permute-start.12
  91.1 1.3 slice.82
  92.5 1.3 slice.83
  95.1 17.2 %collective-permute-done.11.refs_0_ = bf16[1024,512]{1,0:T(8,128)(2,1)} collective-permute-done((bf16[1024,512]{1,0:T(8,128)(2,1)S(1)}, bf16[1024,512]{1,0:T(8,128)(2,1)}, u32[]{:S(2)}, u32[]{:S(2)}) %collective-permute-start.11) | collective-permute-done | bytes 1048608 | tf_op jit(solution)/shard_map/ppermute | solution.py:543
  113.1 15.3 %collective-permute-done.22.refs_9_ = bf16[16,128,256]{2,1,0:T(8,128)(2,1)} collective-permute-done((bf16[16,128,256]{2,1,0:T(8,128)(2,1)S(1)}, bf16[16,128,256]{2,1,0:T(8,128)(2,1)}, u32[]{:S(2)}, u32[]{:S(2)}) %collective-permute-start.22) | collective-permute-done | bytes 1048608 | tf_op jit(solution)/shard_map/ppermute | solution.py:553
  130.3 1.1 collective-permute-done.26.refs_14_
  132.9 17.2 %density_first.1 = (f32[8,1,512]{2,1,0:T(1,128)}, f32[2,1024,128]{2,1,0:T(8,128)}, f32[1,512]{1,0:T(1,128)}, bf16[2,1024,1024]{2,1,0:T(8,128)(2,1)}) custom-call(s32[8]{0:T(128)} %fusion.10.order, s32[1]{0:T(128)} %bitcast.5.place, s32[64]{0:T(128)} %get-tuple-element.86.which, s32[64]{0:T(128)} %get-tuple-element.87.where, bf16[1024,512]{1,0:T(8,128)(2,1)} %bitcast.80, ...), custom_call_target="tpu_custom_call" | custom-call | flops 6442450944 | bytes 18874368 | tf_op jit(solution)/shard_map/density_first/pallas_call | solution.py:318
  150.1 8.2 %density_last.1 = (f32[8,1,512]{2,1,0:T(1,128)}, f32[32,24,128]{2,1,0:T(8,128)}) custom-call(s32[8]{0:T(128)} %fusion.10.order, bf16[1024,512]{1,0:T(8,128)(2,1)} %collective-permute-done.11.refs_0_, bf16[1024,512]{1,0:T(8,128)(2,1)} %collective-permute-done.12.refs_1_, f32[8,1024,512]{2,1,0:T(8,128)} %fusion.refs_16_.refs_2_, ...), custom_call_target="tpu_custom_call" | custom-call | flops 2147483648 | bytes 6291456 | tf_op jit(solution)/shard_map/density_last/pallas_call | solution.py:340
  158.3 14.8 %all_to_all.5 = f32[32,24,128]{2,1,0:T(8,128)} all-to-all(f32[32,24,128]{2,1,0:T(8,128)} %get-tuple-element.44), channel_id=1, replica_groups=mesh['grid'=32,'pert'=4] {'grid'}, dimensions={0} | all-to-all | bytes 786432 | tf_op jit(solution)/shard_map/all_to_all | solution.py:562
  173.1 8.2 %potential.1 = (f32[256,64]{1,0:T(8,128)}, f32[8,1,512]{2,1,0:T(1,128)}, f32[8,1,512]{2,1,0:T(1,128)}, f32[1,128]{1,0:T(1,128)}) custom-call(f32[8,1024,512]{2,1,0:T(8,128)} %bitcast_divide_fusion.table, f32[768,128]{1,0:T(8,128)} %bitcast.92, f32[32,128]{1,0:T(8,128)} %broadcast_in_dim.84.mine, f32[8,1,512]{2,1,0:T(1,128)} %bitcast.102, ...), custom_call_target="tpu_custom_call" | custom-call | flops 16777216 | bytes 16777216 | tf_op jit(solution)/shard_map/potential/pallas_call | solution.py:363
  183.3 23.3 %ham.1 = (f32[32,128,256]{2,1,0:T(8,128)}, f32[32,128,256]{2,1,0:T(8,128)}, f32[32,128,256]{2,1,0:T(8,128)}, f32[32,128,256]{2,1,0:T(8,128)}) custom-call(s32[8]{0:T(128)} %fusion.10.order, s32[64]{0:T(128)} %fusion.7.slots, s32[1]{0:T(128)} %bitcast.5.place, bf16[4,2,128,512]{3,2,1,0:T(8,128)(2,1)} %bitcast.81, bf16[4,2,128,512]{3,2,1,0:T(8,128)(2,1)} %bitcast.86, ...), custom_call_target="tpu_custom_call" | custom-call | flops 4294967296 | bytes 25165824 | tf_op jit(solution)/shard_map/ham/pallas_call | solution.py:388
  206.7 3.0 %multiply_convert_fusion = (f16[16,128,256]{2,1,0:T(8,128)(2,1)S(1)}, f16[16,128,256]{2,1,0:T(8,128)(2,1)S(1)}) fusion(f32[32,128,256]{2,1,0:T(8,128)} %get-tuple-element.51, f32[]{:T(128)} %bitcast.31), kind=kLoop, calls=%fused_computation.6 | loop fusion | flops 2097152 | bytes 6291460 | tf_op jit(solution)/shard_map/convert_element_type | solution.py:416
  209.6 1.1 collective-permute-start.33
  210.7 1.0 collective-permute-start.29
  212.9 1.1 copy-done.5
  214.5 10.0 %collective-permute-done.33 = f16[2,8,128,256]{3,2,1,0:T(8,128)(2,1)S(1)} collective-permute-done((f16[2,8,128,256]{3,2,1,0:T(8,128)(2,1)S(1)}, f16[2,8,128,256]{3,2,1,0:T(8,128)(2,1)S(1)}, u32[]{:S(2)}, u32[]{:S(2)}) %collective-permute-start.33) | collective-permute-done | bytes 1048608 | tf_op jit(solution)/shard_map/ppermute | solution.py:427
  224.9 2.3 collective-permute-start.34
  227.9 1.8 collective-permute-start.30
  230.1 7.8 %collective-permute-done.32 = f16[2,8,128,256]{3,2,1,0:T(8,128)(2,1)S(1)} collective-permute-done((f16[2,8,128,256]{3,2,1,0:T(8,128)(2,1)S(1)}, f16[2,8,128,256]{3,2,1,0:T(8,128)(2,1)S(1)}, u32[]{:S(2)}, u32[]{:S(2)}) %collective-permute-start.32) | collective-permute-done | bytes 1048608 | tf_op jit(solution)/shard_map/ppermute | solution.py:428
  237.9 1.8 collective-permute-done.34
  240.7 1.4 collective-permute-start.35
  242.1 2.1 collective-permute-start.37
  244.2 17.8 %collective-permute-done.31 = f16[2,8,128,256]{3,2,1,0:T(8,128)(2,1)S(1)} collective-permute-done((f16[2,8,128,256]{3,2,1,0:T(8,128)(2,1)S(1)}, f16[2,8,128,256]{3,2,1,0:T(8,128)(2,1)S(1)}, u32[]{:S(2)}, u32[]{:S(2)}) %collective-permute-start.31) | collective-permute-done | bytes 1048608 | tf_op jit(solution)/shard_map/ppermute | solution.py:429
  262.5 0.9 collective-permute-start.36
  263.5 9.5 %collective-permute-done.36 = f16[8,128,256]{2,1,0:T(8,128)(2,1)S(1)} collective-permute-done((f16[8,128,256]{2,1,0:T(8,128)(2,1)S(1)}, f16[8,128,256]{2,1,0:T(8,128)(2,1)S(1)}, u32[]{:S(2)}, u32[]{:S(2)}) %collective-permute-start.36) | collective-permute-done | bytes 524320 | tf_op jit(solution)/shard_map/ppermute | solution.py:439
  273.5 1.3 dynamic-slice_bitcast_fusion
  275.1 1.1 maximum_multiply_fusion
  (130 shorter events, 18.4 us)
Async XLA Ops:
  1.7 5.2 %collective-permute-start = (bf16[4,128,256]{2,1,0:T(8,128)(2,1)S(1)}, bf16[4,128,256]{2,1,0:T(8,128)(2,1)S(1)}, u32[]{:S(2)}, u32[]{:S(2)}) collective-permute-start(bf16[4,128,256]{2,1,0:T(8,128)(2,1)S(1)} %select_bitcast_fusion), channel_id=1, source_target_pairs={{0,4},{4,0},{8,12},{12,8},{16,20},{20,16},{24,28},{28,24},{32,36},... | collective-permute-start | bytes 786440 | tf_op jit(solution)/shard_map/ppermute | solution.py:482
  5.0 61.0 %copy-start = (bf16[512,1024]{0,1:T(8,128)(2,1)}, bf16[512,1024]{0,1:T(8,128)(2,1)S(1)}, u32[]{:S(2)}) copy-start(bf16[512,1024]{0,1:T(8,128)(2,1)S(1)} %copy.25) | copy-start | bytes 3145732
  5.0 9.6 %copy-start.17 = (f32[64]{0:T(128)S(1)}, f32[64]{0:T(128)}, u32[]{:S(2)}) copy-start(f32[64]{0:T(128)} %param.17) | copy-start | bytes 772
  5.1 9.8 %copy-start.12 = (f32[3,256]{1,0:T(4,128)S(1)}, f32[3,256]{1,0:T(4,128)}, u32[]{:S(2)}) copy-start(f32[3,256]{1,0:T(4,128)} %param.18) | copy-start | bytes 9220
  5.1 37.1 %collective-permute-start.7 = (bf16[1024,512]{1,0:T(8,128)(2,1)S(1)}, bf16[1024,512]{1,0:T(8,128)(2,1)S(1)}, u32[]{:S(2)}, u32[]{:S(2)}) collective-permute-start(bf16[1024,512]{1,0:T(8,128)(2,1)S(1)} %bitcast.77), channel_id=1, source_target_pairs={{0,1},{1,2},{2,3},{3,0},{4,5},{5,6},{6,7},{7,4},{8,9},{9,10},{10,1... | collective-permute-start | bytes 3145736 | tf_op jit(solution)/shard_map/ppermute | solution.py:470
  9.4 16.7 %collective-permute-start.1 = (bf16[8,128,256]{2,1,0:T(8,128)(2,1)}, bf16[8,128,256]{2,1,0:T(8,128)(2,1)S(1)}, u32[]{:S(2)}, u32[]{:S(2)}) collective-permute-start(bf16[8,128,256]{2,1,0:T(8,128)(2,1)} %pad_maximum_fusion), channel_id=1, source_target_pairs={{0,96},{4,28},{8,104},{12,4},{16,112},{20,12},{24,120},{28,20},{32... | collective-permute-start | bytes 1572872 | tf_op jit(solution)/shard_map/ppermute | solution.py:486
  13.4 12.6 %collective-permute-start.2 = (bf16[8,128,256]{2,1,0:T(8,128)(2,1)}, bf16[8,128,256]{2,1,0:T(8,128)(2,1)}, u32[]{:S(2)}, u32[]{:S(2)}) collective-permute-start(bf16[8,128,256]{2,1,0:T(8,128)(2,1)} %pad_maximum_fusion), channel_id=1, source_target_pairs={{0,64},{4,20},{8,72},{12,28},{16,80},{20,4},{24,88},{28,12},{32,96... | collective-permute-start | bytes 1572872 | tf_op jit(solution)/shard_map/ppermute | solution.py:486
  13.4 16.3 %collective-permute-start.3 = (bf16[8,128,256]{2,1,0:T(8,128)(2,1)}, bf16[8,128,256]{2,1,0:T(8,128)(2,1)}, u32[]{:S(2)}, u32[]{:S(2)}) collective-permute-start(bf16[8,128,256]{2,1,0:T(8,128)(2,1)} %pad_maximum_fusion), channel_id=1, source_target_pairs={{0,32},{4,12},{8,40},{12,20},{16,48},{20,28},{24,56},{28,4},{32,64... | collective-permute-start | bytes 1572872 | tf_op jit(solution)/shard_map/ppermute | solution.py:486
  30.6 11.9 %copy-start.16 = (s32[2,16]{1,0:T(2,128)S(1)}, s32[2,16]{1,0:T(2,128)}, u32[]{:S(2)}) copy-start(s32[2,16]{1,0:T(2,128)} %param.20) | copy-start | bytes 388
  34.4 52.4 %collective-permute-start.4 = (bf16[32,128,256]{2,1,0:T(8,128)(2,1)}, bf16[32,128,256]{2,1,0:T(8,128)(2,1)}, u32[]{:S(2)}, u32[]{:S(2)}) collective-permute-start(bf16[32,128,256]{2,1,0:T(8,128)(2,1)} %constant_dynamic-update-slice_fusion.refs_6_), channel_id=1, source_target_pairs={{0,24},{4,100},{8,0},{12,108},{16,8},{20,116},{24,16},{28,124},{32... | collective-permute-start | bytes 6291464 | tf_op jit(solution)/shard_map/ppermute | solution.py:534
  37.1 51.5 %collective-permute-start.5 = (bf16[32,128,256]{2,1,0:T(8,128)(2,1)}, bf16[32,128,256]{2,1,0:T(8,128)(2,1)}, u32[]{:S(2)}, u32[]{:S(2)}) collective-permute-start(bf16[32,128,256]{2,1,0:T(8,128)(2,1)} %constant_dynamic-update-slice_fusion.refs_6_), channel_id=1, source_target_pairs={{0,8},{4,36},{8,16},{12,44},{16,24},{20,52},{24,0},{28,60},{32,40}... | collective-permute-start | bytes 6291464 | tf_op jit(solution)/shard_map/ppermute | solution.py:535
  38.6 46.7 %copy-start.1 = (bf16[512,1024]{0,1:T(8,128)(2,1)}, bf16[512,1024]{0,1:T(8,128)(2,1)S(1)}, u32[]{:S(2)}) copy-start(bf16[512,1024]{0,1:T(8,128)(2,1)S(1)} %copy.26) | copy-start | bytes 3145732
  38.6 26.2 %collective-permute-start.8 = (bf16[1024,512]{1,0:T(8,128)(2,1)S(1)}, bf16[1024,512]{1,0:T(8,128)(2,1)}, u32[]{:S(2)}, u32[]{:S(2)}) collective-permute-start(bf16[1024,512]{1,0:T(8,128)(2,1)S(1)} %bitcast.82), channel_id=1, source_target_pairs={{0,3},{1,0},{2,1},{3,2},{4,7},{5,4},{6,5},{7,6},{8,11},{9,8},{10,9... | collective-permute-start | bytes 3145736 | tf_op jit(solution)/shard_map/ppermute | solution.py:471
  40.5 44.9 %collective-permute-start.10 = (bf16[1024,512]{1,0:T(8,128)(2,1)S(1)}, bf16[1024,512]{1,0:T(8,128)(2,1)}, u32[]{:S(2)}, u32[]{:S(2)}) collective-permute-start(bf16[1024,512]{1,0:T(8,128)(2,1)S(1)} %bitcast.78), channel_id=1, source_target_pairs={{0,3},{1,0},{2,1},{3,2},{4,7},{5,4},{6,5},{7,6},{8,11},{9,8},{10,9... | collective-permute-start | bytes 3145736 | tf_op jit(solution)/shard_map/ppermute | solution.py:473
  42.2 46.5 %copy-start.3 = (bf16[1024,512]{1,0:T(8,128)(2,1)}, bf16[1024,512]{1,0:T(8,128)(2,1)S(1)}, u32[]{:S(2)}) copy-start(bf16[1024,512]{1,0:T(8,128)(2,1)S(1)} %collective-permute-done.7.refs_2_) | copy-start | bytes 3145732
  42.2 43.2 %collective-permute-start.9 = (bf16[1024,512]{1,0:T(8,128)(2,1)S(1)}, bf16[1024,512]{1,0:T(8,128)(2,1)}, u32[]{:S(2)}, u32[]{:S(2)}) collective-permute-start(bf16[1024,512]{1,0:T(8,128)(2,1)S(1)} %bitcast.83), channel_id=1, source_target_pairs={{0,1},{1,2},{2,3},{3,0},{4,5},{5,6},{6,7},{7,4},{8,9},{9,10},{10,1... | collective-permute-start | bytes 3145736 | tf_op jit(solution)/shard_map/ppermute | solution.py:472
  42.6 46.1 %copy-start.13 = (s32[256]{0:T(256)S(1)}, s32[256]{0:T(256)}, u32[]{:S(2)}) copy-start(s32[256]{0:T(256)} %param.23) | copy-start | bytes 3076
  64.9 1.2 collective-permute-start.6
  66.0 27.8 %collective-permute-start.13 = (bf16[1024,512]{1,0:T(8,128)(2,1)S(1)}, bf16[1024,512]{1,0:T(8,128)(2,1)}, u32[]{:S(2)}, u32[]{:S(2)}) collective-permute-start(bf16[1024,512]{1,0:T(8,128)(2,1)S(1)} %bitcast.79), channel_id=1, source_target_pairs={{0,4},{4,0},{8,12},{12,8},{16,20},{20,16},{24,28},{28,24},{32,36},... | collective-permute-start | bytes 3145736 | tf_op jit(solution)/shard_map/ppermute | solution.py:546
  85.3 9.0 %collective-permute-start.14 = (bf16[1024,512]{1,0:T(8,128)(2,1)S(1)}, bf16[1024,512]{1,0:T(8,128)(2,1)}, u32[]{:S(2)}, u32[]{:S(2)}) collective-permute-start(bf16[1024,512]{1,0:T(8,128)(2,1)S(1)} %bitcast.84), channel_id=1, source_target_pairs={{0,4},{4,0},{8,12},{12,8},{16,20},{20,16},{24,28},{28,24},{32,36},... | collective-permute-start | bytes 3145736 | tf_op jit(solution)/shard_map/ppermute | solution.py:546
  85.3 27.0 %collective-permute-start.11 = (bf16[1024,512]{1,0:T(8,128)(2,1)S(1)}, bf16[1024,512]{1,0:T(8,128)(2,1)}, u32[]{:S(2)}, u32[]{:S(2)}) collective-permute-start(bf16[1024,512]{1,0:T(8,128)(2,1)S(1)} %collective-permute-done.7.refs_2_), channel_id=1, source_target_pairs={{0,1},{1,2},{2,3},{3,0},{4,5},{5,6},{6,7},{7,4},{8,9},{9,10},{10,1... | collective-permute-start | bytes 3145736 | tf_op jit(solution)/shard_map/ppermute | solution.py:543
  86.8 25.5 %collective-permute-start.12 = (bf16[1024,512]{1,0:T(8,128)(2,1)}, bf16[1024,512]{1,0:T(8,128)(2,1)}, u32[]{:S(2)}, u32[]{:S(2)}) collective-permute-start(bf16[1024,512]{1,0:T(8,128)(2,1)} %collective-permute-done.8.refs_5_), channel_id=1, source_target_pairs={{0,3},{1,0},{2,1},{3,2},{4,7},{5,4},{6,5},{7,6},{8,11},{9,8},{10,9... | collective-permute-start | bytes 3145736 | tf_op jit(solution)/shard_map/ppermute | solution.py:544
  88.7 23.7 %collective-permute-start.15 = (bf16[1024,512]{1,0:T(8,128)(2,1)S(1)}, bf16[1024,512]{1,0:T(8,128)(2,1)}, u32[]{:S(2)}, u32[]{:S(2)}) collective-permute-start(bf16[1024,512]{1,0:T(8,128)(2,1)S(1)} %collective-permute-done.7.refs_2_), channel_id=1, source_target_pairs={{0,4},{4,0},{8,12},{12,8},{16,20},{20,16},{24,28},{28,24},{32,36},... | collective-permute-start | bytes 3145736 | tf_op jit(solution)/shard_map/ppermute | solution.py:546
  91.1 38.0 %copy-start.14 = (s32[8]{0:T(128)S(1)}, s32[8]{0:T(128)}, u32[]{:S(2)}) copy-start(s32[8]{0:T(128)} %constant.235.clone) | copy-start | bytes 100
  91.1 38.0 %copy-start.15 = (s32[8]{0:T(128)S(1)}, s32[8]{0:T(128)}, u32[]{:S(2)}) copy-start(s32[8]{0:T(128)} %constant.236.clone) | copy-start | bytes 100
  93.8 36.0 %collective-permute-start.23 = (bf16[32,128,256]{2,1,0:T(8,128)(2,1)}, bf16[32,128,256]{2,1,0:T(8,128)(2,1)}, u32[]{:S(2)}, u32[]{:S(2)}) collective-permute-start(bf16[32,128,256]{2,1,0:T(8,128)(2,1)} %constant_dynamic-update-slice_fusion.refs_6_), channel_id=1, source_target_pairs={{0,4},{4,0},{8,12},{12,8},{16,20},{20,16},{24,28},{28,24},{32,36},... | collective-permute-start | bytes 6291464 | tf_op jit(solution)/shard_map/ppermute | solution.py:555
  94.3 18.5 %collective-permute-start.21 = (bf16[16,128,256]{2,1,0:T(8,128)(2,1)S(1)}, bf16[16,128,256]{2,1,0:T(8,128)(2,1)}, u32[]{:S(2)}, u32[]{:S(2)}) collective-permute-start(bf16[16,128,256]{2,1,0:T(8,128)(2,1)S(1)} %slice.82), channel_id=1, source_target_pairs={{0,24},{4,100},{8,0},{12,108},{16,8},{20,116},{24,16},{28,124},{32... | collective-permute-start | bytes 3145736 | tf_op jit(solution)/shard_map/ppermute | solution.py:552
  112.3 16.1 %collective-permute-start.22 = (bf16[16,128,256]{2,1,0:T(8,128)(2,1)S(1)}, bf16[16,128,256]{2,1,0:T(8,128)(2,1)}, u32[]{:S(2)}, u32[]{:S(2)}) collective-permute-start(bf16[16,128,256]{2,1,0:T(8,128)(2,1)S(1)} %slice.83), channel_id=1, source_target_pairs={{0,8},{4,36},{8,16},{12,44},{16,24},{20,52},{24,0},{28,60},{32,40}... | collective-permute-start | bytes 3145736 | tf_op jit(solution)/shard_map/ppermute | solution.py:553
  112.3 19.2 %collective-permute-start.24 = (bf16[32,128,256]{2,1,0:T(8,128)(2,1)}, bf16[32,128,256]{2,1,0:T(8,128)(2,1)S(1)}, u32[]{:S(2)}, u32[]{:S(2)}) collective-permute-start(bf16[32,128,256]{2,1,0:T(8,128)(2,1)} %collective-permute-done.4.refs_7_), channel_id=1, source_target_pairs={{0,4},{4,0},{8,12},{12,8},{16,20},{20,16},{24,28},{28,24},{32,36},... | collective-permute-start | bytes 6291464 | tf_op jit(solution)/shard_map/ppermute | solution.py:555
  112.4 19.6 %collective-permute-start.27 = (bf16[32,128,256]{2,1,0:T(8,128)(2,1)}, bf16[32,128,256]{2,1,0:T(8,128)(2,1)}, u32[]{:S(2)}, u32[]{:S(2)}) collective-permute-start(bf16[32,128,256]{2,1,0:T(8,128)(2,1)} %collective-permute-done.5.refs_10_), channel_id=1, source_target_pairs={{0,4},{4,0},{8,12},{12,8},{16,20},{20,16},{24,28},{28,24},{32,36},... | collective-permute-start | bytes 6291464 | tf_op jit(solution)/shard_map/ppermute | solution.py:555
  112.9 17.4 %collective-permute-start.25 = (bf16[16,128,256]{2,1,0:T(8,128)(2,1)}, bf16[16,128,256]{2,1,0:T(8,128)(2,1)}, u32[]{:S(2)}, u32[]{:S(2)}) collective-permute-start(bf16[16,128,256]{2,1,0:T(8,128)(2,1)} %collective-permute-done.21.refs_8_), channel_id=1, source_target_pairs={{0,4},{4,0},{8,12},{12,8},{16,20},{20,16},{24,28},{28,24},{32,36},... | collective-permute-start | bytes 3145736 | tf_op jit(solution)/shard_map/ppermute | solution.py:555
  128.4 3.0 %collective-permute-start.26 = (bf16[16,128,256]{2,1,0:T(8,128)(2,1)}, bf16[16,128,256]{2,1,0:T(8,128)(2,1)}, u32[]{:S(2)}, u32[]{:S(2)}) collective-permute-start(bf16[16,128,256]{2,1,0:T(8,128)(2,1)} %collective-permute-done.22.refs_9_), channel_id=1, source_target_pairs={{0,4},{4,0},{8,12},{12,8},{16,20},{20,16},{24,28},{28,24},{32,36},... | collective-permute-start | bytes 3145736 | tf_op jit(solution)/shard_map/ppermute | solution.py:555
  129.7 51.5 %collective-permute-start.18 = (bf16[1024,512]{1,0:T(8,128)(2,1)}, bf16[1024,512]{1,0:T(8,128)(2,1)S(1)}, u32[]{:S(2)}, u32[]{:S(2)}) collective-permute-start(bf16[1024,512]{1,0:T(8,128)(2,1)} %collective-permute-done.8.refs_5_), channel_id=1, source_target_pairs={{0,4},{4,0},{8,12},{12,8},{16,20},{20,16},{24,28},{28,24},{32,36},... | collective-permute-start | bytes 3145736 | tf_op jit(solution)/shard_map/ppermute | solution.py:546
  130.2 52.0 %collective-permute-start.16 = (bf16[1024,512]{1,0:T(8,128)(2,1)}, bf16[1024,512]{1,0:T(8,128)(2,1)}, u32[]{:S(2)}, u32[]{:S(2)}) collective-permute-start(bf16[1024,512]{1,0:T(8,128)(2,1)} %collective-permute-done.9.refs_3_), channel_id=1, source_target_pairs={{0,4},{4,0},{8,12},{12,8},{16,20},{20,16},{24,28},{28,24},{32,36},... | collective-permute-start | bytes 3145736 | tf_op jit(solution)/shard_map/ppermute | solution.py:546
  131.4 50.9 %collective-permute-start.17 = (bf16[1024,512]{1,0:T(8,128)(2,1)}, bf16[1024,512]{1,0:T(8,128)(2,1)}, u32[]{:S(2)}, u32[]{:S(2)}) collective-permute-start(bf16[1024,512]{1,0:T(8,128)(2,1)} %collective-permute-done.10.refs_4_), channel_id=1, source_target_pairs={{0,4},{4,0},{8,12},{12,8},{16,20},{20,16},{24,28},{28,24},{32,36},... | collective-permute-start | bytes 3145736 | tf_op jit(solution)/shard_map/ppermute | solution.py:546
  131.6 50.7 %collective-permute-start.19 = (bf16[1024,512]{1,0:T(8,128)(2,1)}, bf16[1024,512]{1,0:T(8,128)(2,1)}, u32[]{:S(2)}, u32[]{:S(2)}) collective-permute-start(bf16[1024,512]{1,0:T(8,128)(2,1)} %collective-permute-done.11.refs_0_), channel_id=1, source_target_pairs={{0,4},{4,0},{8,12},{12,8},{16,20},{20,16},{24,28},{28,24},{32,36},... | collective-permute-start | bytes 3145736 | tf_op jit(solution)/shard_map/ppermute | solution.py:546
  132.0 50.4 %collective-permute-start.20 = (bf16[1024,512]{1,0:T(8,128)(2,1)}, bf16[1024,512]{1,0:T(8,128)(2,1)}, u32[]{:S(2)}, u32[]{:S(2)}) collective-permute-start(bf16[1024,512]{1,0:T(8,128)(2,1)} %collective-permute-done.12.refs_1_), channel_id=1, source_target_pairs={{0,4},{4,0},{8,12},{12,8},{16,20},{20,16},{24,28},{28,24},{32,36},... | collective-permute-start | bytes 3145736 | tf_op jit(solution)/shard_map/ppermute | solution.py:546
  181.3 1.5 collective-permute-start.28
  209.6 14.9 %collective-permute-start.33 = (f16[2,8,128,256]{3,2,1,0:T(8,128)(2,1)S(1)}, f16[2,8,128,256]{3,2,1,0:T(8,128)(2,1)S(1)}, u32[]{:S(2)}, u32[]{:S(2)}) collective-permute-start(f16[2,8,128,256]{3,2,1,0:T(8,128)(2,1)S(1)} %bitcast.97), channel_id=1, source_target_pairs={{0,96},{4,28},{8,104},{12,4},{16,112},{20,12},{24,120},{28,20},{32... | collective-permute-start | bytes 3145736 | tf_op jit(solution)/shard_map/ppermute | solution.py:427
  210.7 16.8 %collective-permute-start.29 = (f16[2,8,128,256]{3,2,1,0:T(8,128)(2,1)S(1)}, f16[2,8,128,256]{3,2,1,0:T(8,128)(2,1)S(1)}, u32[]{:S(2)}, u32[]{:S(2)}) collective-permute-start(f16[2,8,128,256]{3,2,1,0:T(8,128)(2,1)S(1)} %bitcast.96), channel_id=1, source_target_pairs={{0,32},{4,12},{8,40},{12,20},{16,48},{20,28},{24,56},{28,4},{32,64... | collective-permute-start | bytes 3145736 | tf_op jit(solution)/shard_map/ppermute | solution.py:426
  212.3 25.7 %collective-permute-start.32 = (f16[2,8,128,256]{3,2,1,0:T(8,128)(2,1)S(1)}, f16[2,8,128,256]{3,2,1,0:T(8,128)(2,1)S(1)}, u32[]{:S(2)}, u32[]{:S(2)}) collective-permute-start(f16[2,8,128,256]{3,2,1,0:T(8,128)(2,1)S(1)} %bitcast.99), channel_id=1, source_target_pairs={{0,32},{4,12},{8,40},{12,20},{16,48},{20,28},{24,56},{28,4},{32,64... | collective-permute-start | bytes 3145736 | tf_op jit(solution)/shard_map/ppermute | solution.py:428
  224.9 14.9 %collective-permute-start.34 = (f16[2,8,128,256]{3,2,1,0:T(8,128)(2,1)S(1)}, f16[2,8,128,256]{3,2,1,0:T(8,128)(2,1)S(1)}, u32[]{:S(2)}, u32[]{:S(2)}) collective-permute-start(f16[2,8,128,256]{3,2,1,0:T(8,128)(2,1)S(1)} %add_convert_fusion.1), channel_id=1, source_target_pairs={{0,96},{4,28},{8,104},{12,4},{16,112},{20,12},{24,120},{28,20},{32... | collective-permute-start | bytes 3145736 | tf_op jit(solution)/shard_map/ppermute | solution.py:431
  227.2 34.8 %collective-permute-start.31 = (f16[2,8,128,256]{3,2,1,0:T(8,128)(2,1)S(1)}, f16[2,8,128,256]{3,2,1,0:T(8,128)(2,1)S(1)}, u32[]{:S(2)}, u32[]{:S(2)}) collective-permute-start(f16[2,8,128,256]{3,2,1,0:T(8,128)(2,1)S(1)} %bitcast.98), channel_id=1, source_target_pairs={{0,96},{4,28},{8,104},{12,4},{16,112},{20,12},{24,120},{28,20},{32... | collective-permute-start | bytes 3145736 | tf_op jit(solution)/shard_map/ppermute | solution.py:429
  227.9 34.1 %collective-permute-start.30 = (f16[2,8,128,256]{3,2,1,0:T(8,128)(2,1)S(1)}, f16[2,8,128,256]{3,2,1,0:T(8,128)(2,1)S(1)}, u32[]{:S(2)}, u32[]{:S(2)}) collective-permute-start(f16[2,8,128,256]{3,2,1,0:T(8,128)(2,1)S(1)} %add_convert_fusion.2), channel_id=1, source_target_pairs={{0,32},{4,12},{8,40},{12,20},{16,48},{20,28},{24,56},{28,4},{32,64... | collective-permute-start | bytes 3145736 | tf_op jit(solution)/shard_map/ppermute | solution.py:430
  240.7 22.7 %collective-permute-start.35 = (f16[8,128,256]{2,1,0:T(8,128)(2,1)S(1)}, f16[8,128,256]{2,1,0:T(8,128)(2,1)S(1)}, u32[]{:S(2)}, u32[]{:S(2)}) collective-permute-start(f16[8,128,256]{2,1,0:T(8,128)(2,1)S(1)} %get-tuple-element.77), channel_id=1, source_target_pairs={{0,16},{4,68},{8,24},{12,76},{16,0},{20,84},{24,8},{28,92},{32,48}... | collective-permute-start | bytes 1572872 | tf_op jit(solution)/shard_map/ppermute | solution.py:439
  242.1 21.3 %collective-permute-start.37 = (f16[8,128,256]{2,1,0:T(8,128)(2,1)S(1)}, f16[8,128,256]{2,1,0:T(8,128)(2,1)S(1)}, u32[]{:S(2)}, u32[]{:S(2)}) collective-permute-start(f16[8,128,256]{2,1,0:T(8,128)(2,1)S(1)} %get-tuple-element.78), channel_id=1, source_target_pairs={{0,24},{4,100},{8,0},{12,108},{16,8},{20,116},{24,16},{28,124},{32... | collective-permute-start | bytes 1572872 | tf_op jit(solution)/shard_map/ppermute | solution.py:439
  262.5 10.5 %collective-permute-start.36 = (f16[8,128,256]{2,1,0:T(8,128)(2,1)S(1)}, f16[8,128,256]{2,1,0:T(8,128)(2,1)S(1)}, u32[]{:S(2)}, u32[]{:S(2)}) collective-permute-start(f16[8,128,256]{2,1,0:T(8,128)(2,1)S(1)} %fusion.6), channel_id=1, source_target_pairs={{0,8},{4,36},{8,16},{12,44},{16,24},{20,52},{24,0},{28,60},{32,40}... | collective-permute-start | bytes 1572872 | tf_op jit(solution)/shard_map/ppermute | solution.py:439
  273.4 1.6 collective-permute-start.38
  (10 other events, 34.8 us)

commit v8 on v7

--- a/solution.py
+++ b/solution.py
@@ -12,8 +12,7 @@
 PIECES = 8
 CHUNKS = 8
 VMEM_GRANT = 60 << 20
-SOURCES = 5
-EARLY = 6
+SOURCES = 8
 BLK = 256
 NB = 4
 PHI_MAX_SQ = 36.0
@@ -71,35 +70,41 @@
                 pl.ds(pl.multiple_of(row * BLK + half * 128, 128), 128),
                 pl.ds(pl.multiple_of(col * BLK, BLK), BLK),
             ]
-            for k in range(SOURCES):
-
-                @pl.when(which[side * 32 + n] == k)
-                def _(k=k):
+            at = side * 32 + n
+
+            def pick(low, high):
+                if high - low == 1:
                     pltpu.make_async_copy(
-                        sources[side * SOURCES + k].at[where[side * 32 + n]], target, sem
+                        sources[side * SOURCES + low].at[where[at]], target, sem
                     ).start()
-
+                    return
+                middle = (low + high) // 2
+                pl.when(which[at] < middle)(lambda: pick(low, middle))
+                pl.when(which[at] >= middle)(lambda: pick(middle, high))
+
+            pick(0, SOURCES)
             return 0
 
         lax.fori_loop(0, 32, fetch, 0)
 
 
-def density_steps(order, first, count, chunks, dmat, table, weights, xc, rho, pacc, bufs, top):
+def density_steps(order, chunks, dmat, sem, table, weights, xc, rho, pacc, bufs, top):
     held, tbuf, psem, tsem = bufs
-    for i in range(count):
+    for i in range(CHUNKS):
         pltpu.make_async_copy(chunks[i], held.at[i], psem.at[i]).start()
-    pltpu.make_async_copy(table.at[order[first]], tbuf.at[0], tsem.at[0]).start()
+    pltpu.make_async_copy(table.at[order[0]], tbuf.at[0], tsem.at[0]).start()
+    pltpu.make_async_copy(dmat, dmat, sem).wait()
 
     def step(i, top):
         slot = lax.rem(i, 2)
 
-        @pl.when(i + 1 < count)
+        @pl.when(i + 1 < CHUNKS)
         def _():
             pltpu.make_async_copy(
-                table.at[order[first + i + 1]], tbuf.at[1 - slot], tsem.at[1 - slot]
+                table.at[order[i + 1]], tbuf.at[1 - slot], tsem.at[1 - slot]
             ).start()
 
-        pi = order[first + i]
+        pi = order[i]
         b = pi // 4
         pltpu.make_async_copy(held.at[i], held.at[i], psem.at[i]).wait()
         piece = held[i]
@@ -122,38 +127,21 @@
             pacc[b, rows, :] = part
         return jnp.maximum(top, jnp.abs(xc[pi] * total))
 
-    return lax.fori_loop(0, count, step, top)
-
-
-def density_first_body(order, place, which, where, *refs):
-    chunks = refs[:EARLY]
-    sources = refs[EARLY : EARLY + 2 * SOURCES]
-    table, weights, xc, rho, pacc, top, dmat, sem, *bufs = refs[EARLY + 2 * SOURCES :]
+    return lax.fori_loop(0, CHUNKS, step, top)
+
+
+def density_body(order, place, which, where, *refs):
+    chunks = refs[:CHUNKS]
+    sources = refs[CHUNKS : CHUNKS + 2 * SOURCES]
+    table, weights, xc, home_rows, rho, sent, *rest = refs[CHUNKS + 2 * SOURCES :]
+    pacc, dmat, block_out, sem, *bufs = rest
     fetch_tiles(place[0], which, where, sources, dmat, sem)
     pacc[...] = jnp.zeros_like(pacc)
-    rho[...] = jnp.zeros_like(rho)
-    pltpu.make_async_copy(dmat, dmat, sem).wait()
-    top[...] = density_steps(
-        order, 0, EARLY, chunks, dmat, table, weights, xc, rho, pacc, bufs,
-        jnp.zeros((1, HALF), jnp.float32),
-    )
-
-
-def density_last_body(order, *refs):
-    count = PIECES - EARLY
-    chunks = refs[:count]
-    (table, dmat_in, pacc_in, weights, xc, home_rows, rho_in, top_in, rho, sent, *rest) = refs[count:]
-    pacc, dmat, block_out, lsem, *bufs = rest
-    batch = order[EARLY] // 4
-    pltpu.make_async_copy(dmat_in.at[pl.ds(batch, 1)], dmat.at[pl.ds(batch, 1)], lsem.at[0]).start()
-    pltpu.make_async_copy(pacc_in, pacc, lsem.at[1]).start()
-    rho[...] = rho_in[...]
     block_out[...] = jnp.zeros_like(block_out)
     block_out[pl.ds(17, 2), :] = home_rows[...]
-    pltpu.make_async_copy(dmat_in.at[pl.ds(batch, 1)], dmat.at[pl.ds(batch, 1)], lsem.at[0]).wait()
-    pltpu.make_async_copy(pacc_in, pacc, lsem.at[1]).wait()
     top = density_steps(
-        order, EARLY, count, chunks, dmat, table, weights, xc, rho, pacc, bufs, top_in[...]
+        order, chunks, dmat, sem, table, weights, xc, rho, pacc, bufs,
+        jnp.zeros((1, HALF), jnp.float32),
     )
     ones = jnp.ones((8, 128), jnp.bfloat16)
     for b in range(2):
@@ -297,65 +285,34 @@
     return pl.BlockSpec(memory_space=pltpu.SMEM)
 
 
-def density_buffers(count):
-    nbasis = NB * BLK
-    return [
-        pltpu.VMEM((count, nbasis, HALF), jnp.bfloat16),
-        pltpu.VMEM((2, nbasis, HALF), jnp.float32),
-        pltpu.SemaphoreType.DMA((count,)),
-        pltpu.SemaphoreType.DMA((2,)),
-    ]
-
-
-def density_cost(count):
-    return pl.CostEstimate(
-        flops=2 * count * HALF * 1024 * 1024, bytes_accessed=count * (3 << 20), transcendentals=0
-    )
-
-
-def density_first(order, place, which, where, chunks, sources, table, weights, xc):
+def density_call(order, place, which, where, chunks, sources, table, weights, xc, home_rows):
     nbasis = NB * BLK
     return pl.pallas_call(
-        density_first_body,
-        out_shape=(
-            jax.ShapeDtypeStruct((PIECES, 1, HALF), jnp.float32),
-            jax.ShapeDtypeStruct((2, nbasis, 128), jnp.float32),
-            jax.ShapeDtypeStruct((1, HALF), jnp.float32),
-            jax.ShapeDtypeStruct((2, nbasis, nbasis), jnp.bfloat16),
-        ),
-        in_specs=[smem_spec()] * 4
-        + [any_spec()] * (EARLY + 2 * SOURCES + 1)
-        + [vmem_spec()] * 2,
-        out_specs=(vmem_spec(),) * 4,
-        scratch_shapes=[pltpu.SemaphoreType.DMA] + density_buffers(EARLY),
-        compiler_params=pltpu.CompilerParams(vmem_limit_bytes=VMEM_GRANT),
-        cost_estimate=density_cost(EARLY),
-        name="density_first",
-    )(order, place, which, where, *chunks, *sources, table, weights, xc)
-
-
-def density_last(order, chunks, table, dmat, pacc, weights, xc, home_rows, rho, top):
-    count = PIECES - EARLY
-    nbasis = NB * BLK
-    return pl.pallas_call(
-        density_last_body,
+        density_body,
         out_shape=(
             jax.ShapeDtypeStruct((PIECES, 1, HALF), jnp.float32),
             jax.ShapeDtypeStruct((32, PAY_ROWS, 128), jnp.float32),
         ),
-        in_specs=[smem_spec()] + [any_spec()] * (count + 3) + [vmem_spec()] * 5,
+        in_specs=[smem_spec()] * 4
+        + [any_spec()] * (CHUNKS + 2 * SOURCES + 1)
+        + [vmem_spec()] * 3,
         out_specs=(vmem_spec(),) * 2,
         scratch_shapes=[
             pltpu.VMEM((2, nbasis, 128), jnp.float32),
             pltpu.VMEM((2, nbasis, nbasis), jnp.bfloat16),
             pltpu.VMEM((PAY_ROWS, 128), jnp.float32),
+            pltpu.SemaphoreType.DMA,
+            pltpu.VMEM((CHUNKS, nbasis, HALF), jnp.bfloat16),
+            pltpu.VMEM((2, nbasis, HALF), jnp.float32),
+            pltpu.SemaphoreType.DMA((CHUNKS,)),
             pltpu.SemaphoreType.DMA((2,)),
-        ]
-        + density_buffers(count),
+        ],
         compiler_params=pltpu.CompilerParams(vmem_limit_bytes=VMEM_GRANT),
-        cost_estimate=density_cost(count),
-        name="density_last",
-    )(order, *chunks, table, dmat, pacc, weights, xc, home_rows, rho, top)
+        cost_estimate=pl.CostEstimate(
+            flops=2 * 4096 * 1024 * 1024, bytes_accessed=32 << 20, transcendentals=0
+        ),
+        name="density",
+    )(order, place, which, where, *chunks, *sources, table, weights, xc, home_rows)
 
 
 def potential_call(table, got, mine, weights, xc, rho, natoms):
@@ -504,8 +461,7 @@
     in_chip = homes % (2 * tile_dev)
 
     def found(one, two):
-        source = jnp.where(two == 2, 2 + one // 2, jnp.where(two == 3, 4, two))
-        return source, jnp.where(two == 2, one % 2, one) * (2 * tile_dev) + in_chip
+        return two * 2 + one // 2, (one % 2) * (2 * tile_dev) + in_chip
 
     own_first = jnp.where(first_core, to_z, to_x)
     own_second = jnp.where(first_core, to_x, to_z)
@@ -529,35 +485,36 @@
     weights = point_weights.reshape(PIECES, 1, HALF)
     xc = xc_kernel.reshape(PIECES, 1, HALF)
 
-    ring_tiles, gauss = lax.optimization_barrier((ring_tiles, gauss))
-    stored = jnp.concatenate([base] + ring_tiles, axis=0)
-    ahead_tiles = lax.ppermute(stored, "grid", core_perm(-1, True))
-    behind_tiles = lax.ppermute(stored, "grid", core_perm(1, True))
-
     lane = jnp.arange(128, dtype=jnp.int32)
     here = (lane // 16) == (me % 8)
     home_floats = atom_homes.astype(jnp.float32)
     home_rows = jnp.where(here[None, :], jnp.tile(home_floats.reshape(16, 2).T, (1, 8)), 0.0)
     my_homes = jnp.broadcast_to(home_floats[:, None], (slots_here, 128))
-    below0, above1, hart = lax.optimization_barrier((below0, above1, hart))
+
+    back, forth = core_perm(-1, True), core_perm(1, True)
+    near = jnp.concatenate([base, ring_tiles[0]], axis=0)
+    other = jnp.concatenate([ring_tiles[1], ring_tiles[2]], axis=0)
+    near_ahead = lax.ppermute(near, "grid", back)
+    other_behind = lax.ppermute(other, "grid", forth)
+    near_behind = lax.ppermute(near, "grid", forth)
+    other_ahead = lax.ppermute(other, "grid", back)
+    near_ahead, slots, home_rows, my_homes, which, where = lax.optimization_barrier(
+        (near_ahead, slots, home_rows, my_homes, which, where)
+    )
+    near_far = lax.ppermute(near_ahead, "grid", back)
+    other_far = lax.ppermute(other_behind, "grid", forth)
+    sources = [
+        near, other, near_ahead, other_ahead, near_far, other_far, near_behind, other_behind,
+    ]
+    sources = sources + [lax.ppermute(s, "grid", swap) for s in sources]
+
     far0 = lax.ppermute(below0, "pert", ring(1))
     far1 = lax.ppermute(above1, "pert", ring(3))
     chunks = [own0, own1, below0, below1, above0, above1, far0, far1]
     beside = [lax.ppermute(chunk, "grid", swap) for chunk in chunks]
 
-    ahead_tiles, behind_tiles, slots, home_rows, my_homes = lax.optimization_barrier(
-        (ahead_tiles, behind_tiles, slots, home_rows, my_homes)
-    )
-    rows2 = 4 * tile_dev
-    far_tiles0 = lax.ppermute(ahead_tiles[:rows2], "grid", core_perm(-1, True))
-    far_tiles1 = lax.ppermute(behind_tiles[rows2:], "grid", core_perm(1, True))
-    sources = [stored, ahead_tiles, far_tiles0, far_tiles1, behind_tiles]
-    sources = sources + [lax.ppermute(s, "grid", swap) for s in sources]
-    rho, pacc, top, dmat = density_first(
-        order, core_place, which, where, chunks[:EARLY], sources, gauss, weights, xc
-    )
-    rho, sent = density_last(
-        order, chunks[EARLY:], gauss, dmat, pacc, weights, xc, home_rows, rho, top
+    rho, sent = density_call(
+        order, core_place, which, where, chunks, sources, gauss, weights, xc, home_rows
     )
     got = lax.all_to_all(sent, "grid", split_axis=0, concat_axis=0, tiled=True)
     all_coeffs, pot, scale, bound = potential_call(

time: 278 us -> 272 us (0.978)
  starting transfers between devices: 32.4 us -> 50.1 us
  blocking collectives: 14.8 us -> 0 us
  local copies, waits for them, and re-layouts: 17.3 us -> 12.1 us
  Pallas kernels: 56.8 us -> 53.4 us
    ppermute x1, waiting for transfers between devices: 19.2 us -> 0.42 us  [one_device(): above0 = lax.ppermute(own0, 'pert', ring(3))]
    ppermute x1, waiting for transfers between devices: 0.01 us -> 17.1 us  [one_device(): below1 = lax.ppermute(own1, 'pert', ring(1))]
    all_to_all x1 -> x0, blocking collectives: 14.8 us -> none  [one_device(): got = lax.all_to_all(sent, 'grid', split_axis=0, concat_axis=0, tiled=True)]
    ppermute x1, waiting for transfers between devices: 14.6 us -> 2.04 us  [one_device(): above1 = lax.ppermute(own1, 'pert', ring(3))]
    all_to_all x0 -> x1, starting transfers between devices: none -> 8.5 us  [one_device(): got = lax.all_to_all(sent, 'grid', split_axis=0, concat_axis=0, tiled=True)]
    ppermute x1, waiting for transfers between devices: 0.02 us -> 7.53 us  [one_device(): far1 = lax.ppermute(above1, 'pert', ring(3))]
    ppermute x1, waiting for transfers between devices: 17.2 us -> 10.2 us  [one_device(): far0 = lax.ppermute(below0, 'pert', ring(1))]
    ppermute x4 -> x6, waiting for transfers between devices: 15.3 us -> 21.2 us  [the longest x1 9.39 us: one_device(): near_ahead = lax.ppermute(near, 'grid', back)]
  transfers between devices with their start and end apart: 39 -> 45, of which waited for: 15 -> 19; matrix products, arithmetic and copies ran while one was open for 14% -> 13% of each run, Pallas kernels for 12% -> 11%
where the time goes in v8:
time: 272 us; the launch traced here: 270 us
  waiting for transfers between devices  121 us (44%)
  Pallas kernels  53.4 us (20%)
  starting transfers between devices  50.1 us (18%)
  other arithmetic  32 us (12%)
  local copies, waits for them, and re-layouts  12.1 us (4%)
    pallas_call x1, Pallas kernels, ham_call(): pl.pallas_call(ham_body, out_shape=(jax.ShapeDtypeStruct((32, 128, BLK),...  23.3 us
    pallas_call x1, Pallas kernels, density_call(): pl.pallas_call(density_body, out_shape=(jax.ShapeDtypeStruct((PIECES, 1,...  21.9 us
    ppermute x1, waiting for transfers between devices, ring_sum(): above_low = lax.ppermute(cast(parts[3][:half] * factor), 'grid', down)  18 us
    ppermute x1, waiting for transfers between devices, one_device(): below1 = lax.ppermute(own1, 'pert', ring(1))  17.1 us
    ppermute x1, waiting for transfers between devices, one_device(): far0 = lax.ppermute(below0, 'pert', ring(1))  10.2 us
    ppermute x1, waiting for transfers between devices, ring_sum(): from_above = lax.ppermute(cast(parts[2][half:] * factor), 'grid', down)  10 us
    ppermute x3, waiting for transfers between devices, direct_sum(): lax.ppermute(cast(parts[d]), 'grid', core_perm(d, True))  9.56 us
    ppermute x1, waiting for transfers between devices, one_device(): near_ahead = lax.ppermute(near, 'grid', back)  9.39 us
  transfers between devices with their start and end apart: 45, of which 19 were waited for; matrix products, arithmetic and copies ran while one was open for 13% of the time, Pallas kernels for 11%

profile of v8, /device:TPU:0, one launch (start us, length us, event | category | flops | bytes accessed | tf_op | source)
XLA Modules:
  0.0 270.1 jit_solution(10051228814591749944)
XLA Ops:
  0.7 1.2 select_bitcast_fusion
  2.0 1.5 collective-permute-done
  5.5 4.0 %collective-permute-start.18 = (bf16[8,128,256]{2,1,0:T(8,128)(2,1)}, bf16[8,128,256]{2,1,0:T(8,128)(2,1)}, u32[]{:S(2)}, u32[]{:S(2)}) collective-permute-start(bf16[8,128,256]{2,1,0:T(8,128)(2,1)} %pad_maximum_fusion.1), channel_id=1, source_target_pairs={{0,64},{4,20},{8,72},{12,28},{16,80},{20,4},{24,88},{28,12},{32,96... | collective-permute-start | bytes 1572872 | tf_op jit(solution)/shard_map/ppermute | solution.py:443
  9.5 1.1 fusion.25
  11.2 1.6 collective-permute-start.4
  12.8 1.5 copy.26
  14.3 1.8 collective-permute-start.7
  17.1 1.4 collective-permute-start.19
  18.8 1.9 constant_dynamic-update-slice_fusion.1
  20.8 5.1 %collective-permute-done.1 = bf16[8,128,256]{2,1,0:T(8,128)(2,1)} collective-permute-done((bf16[8,128,256]{2,1,0:T(8,128)(2,1)}, bf16[8,128,256]{2,1,0:T(8,128)(2,1)}, u32[]{:S(2)}, u32[]{:S(2)}) %collective-permute-start.1) | collective-permute-done | bytes 524320 | tf_op jit(solution)/shard_map/ppermute | solution.py:443
  25.9 2.9 %collective-permute-start.6 = (bf16[1024,512]{1,0:T(8,128)(2,1)S(1)}, bf16[1024,512]{1,0:T(8,128)(2,1)}, u32[]{:S(2)}, u32[]{:S(2)}) collective-permute-start(bf16[1024,512]{1,0:T(8,128)(2,1)S(1)} %bitcast.76), channel_id=1, source_target_pairs={{0,3},{1,0},{2,1},{3,2},{4,7},{5,4},{6,5},{7,6},{8,11},{9,8},{10,9... | collective-permute-start | bytes 3145736 | tf_op jit(solution)/shard_map/ppermute | solution.py:430
  28.9 2.2 pad_maximum_fusion.refs_8_
  31.1 1.9 constant_dynamic-update-slice_fusion.refs_9_
  33.4 5.0 %collective-permute-done.4.refs_2_ = bf16[1024,512]{1,0:T(8,128)(2,1)S(1)} collective-permute-done((bf16[1024,512]{1,0:T(8,128)(2,1)S(1)}, bf16[1024,512]{1,0:T(8,128)(2,1)S(1)}, u32[]{:S(2)}, u32[]{:S(2)}) %collective-permute-start.4) | collective-permute-done | bytes 1048608 | tf_op jit(solution)/shard_map/ppermute | solution.py:427
  38.5 2.0 collective-permute-done.7.refs_5_
  40.5 1.5 collective-permute-start.22
  42.0 17.1 %collective-permute-done.5.refs_3_ = bf16[1024,512]{1,0:T(8,128)(2,1)} collective-permute-done((bf16[1024,512]{1,0:T(8,128)(2,1)S(1)}, bf16[1024,512]{1,0:T(8,128)(2,1)}, u32[]{:S(2)}, u32[]{:S(2)}) %collective-permute-start.5) | collective-permute-done | bytes 1048608 | tf_op jit(solution)/shard_map/ppermute | solution.py:429
  59.2 1.1 collective-permute-start.2
  60.8 1.1 collective-permute-start.20
  61.9 1.4 collective-permute-start.26
  63.3 1.6 collective-permute-start.24
  64.9 9.4 %collective-permute-done.2.refs_10_ = bf16[16,128,256]{2,1,0:T(8,128)(2,1)} collective-permute-done((bf16[16,128,256]{2,1,0:T(8,128)(2,1)}, bf16[16,128,256]{2,1,0:T(8,128)(2,1)}, u32[]{:S(2)}, u32[]{:S(2)}) %collective-permute-start.2) | collective-permute-done | bytes 1048608 | tf_op jit(solution)/shard_map/ppermute | solution.py:497
  77.7 7.8 %collective-permute-done.20.refs_11_ = bf16[16,128,256]{2,1,0:T(8,128)(2,1)} collective-permute-done((bf16[16,128,256]{2,1,0:T(8,128)(2,1)}, bf16[16,128,256]{2,1,0:T(8,128)(2,1)}, u32[]{:S(2)}, u32[]{:S(2)}) %collective-permute-start.20) | collective-permute-done | bytes 1048608 | tf_op jit(solution)/shard_map/ppermute | solution.py:500
  85.5 1.7 collective-permute-start.9
  87.9 1.5 collective-permute-start.28
  89.4 10.2 %collective-permute-done.8.refs_6_ = bf16[1024,512]{1,0:T(8,128)(2,1)S(1)} collective-permute-done((bf16[1024,512]{1,0:T(8,128)(2,1)S(1)}, bf16[1024,512]{1,0:T(8,128)(2,1)S(1)}, u32[]{:S(2)}, u32[]{:S(2)}) %collective-permute-start.8) | collective-permute-done | bytes 1048608 | tf_op jit(solution)/shard_map/ppermute | solution.py:511
  99.6 2.7 collective-permute-start.21
  102.4 7.5 %collective-permute-done.9.refs_7_ = bf16[1024,512]{1,0:T(8,128)(2,1)S(1)} collective-permute-done((bf16[1024,512]{1,0:T(8,128)(2,1)}, bf16[1024,512]{1,0:T(8,128)(2,1)S(1)}, u32[]{:S(2)}, u32[]{:S(2)}) %collective-permute-start.9) | collective-permute-done | bytes 1048608 | tf_op jit(solution)/shard_map/ppermute | solution.py:512
  110.9 4.0 %collective-permute-done.21.refs_12_ = bf16[16,128,256]{2,1,0:T(8,128)(2,1)} collective-permute-done((bf16[16,128,256]{2,1,0:T(8,128)(2,1)}, bf16[16,128,256]{2,1,0:T(8,128)(2,1)}, u32[]{:S(2)}, u32[]{:S(2)}) %collective-permute-start.21) | collective-permute-done | bytes 1048608 | tf_op jit(solution)/shard_map/ppermute | solution.py:504
  115.5 8.1 %fusion.refs_24_ = f32[8,1024,512]{2,1,0:T(8,128)} fusion(f32[1024]{0:T(1024)S(1)} %div.197, f32[8,16,512]{2,1,0:T(8,128)S(1)} %bitcast.94), kind=kLoop, calls=%fused_computation.3 | loop fusion | flops 4194304 | bytes 17043456 | tf_op jit(solution)/shard_map/exp | solution.py:480
  125.8 21.9 %density.1 = (f32[8,1,512]{2,1,0:T(1,128)}, f32[32,24,128]{2,1,0:T(8,128)}) custom-call(s32[8]{0:T(128)} %fusion.10.order, s32[1]{0:T(128)} %bitcast.3.place, s32[64]{0:T(128)} %get-tuple-element.20.which, s32[64]{0:T(128)} %get-tuple-element.21.where, bf16[1024,512]{1,0:T(8,128)(2,1)} %bitcast.78, bf16[1024,512]{1,0:T(8,128)(2,1)} %bitcast.83, ...), custom_call_target="tpu_custom_call" | custom-call | flops 8589934592 | bytes 33554432 | tf_op jit(solution)/shard_map/density/pallas_call | solution.py:290
  147.7 8.5 %all-to-all-start = ((f32[32,24,128]{2,1,0:T(8,128)}), f32[32,24,128]{2,1,0:T(8,128)S(1)}, u32[]{:S(2)}, u32[]{:S(2)}) async-start(f32[32,24,128]{2,1,0:T(8,128)} %get-tuple-element.24), calls=%async_computation | async-start | bytes 786432 | tf_op jit(solution)/shard_map/all_to_all | solution.py:519
  156.3 7.4 %bitcast_divide_fusion.table = f32[8,1024,512]{2,1,0:T(8,128)} fusion(f32[1024]{0:T(1024)S(1)} %div.190, f32[8,16,512]{2,1,0:T(8,128)S(1)} %bitcast.93), kind=kLoop, calls=%fused_computation | loop fusion | flops 8388608 | bytes 17043456 | tf_op jit(solution)/shard_map/div | solution.py:482
  163.7 2.7 all-to-all-done
  167.1 8.2 %potential.1 = (f32[256,64]{1,0:T(8,128)}, f32[8,1,512]{2,1,0:T(1,128)}, f32[8,1,512]{2,1,0:T(1,128)}, f32[1,128]{1,0:T(1,128)}) custom-call(f32[8,1024,512]{2,1,0:T(8,128)} %bitcast_divide_fusion.table, f32[768,128]{1,0:T(8,128)} %bitcast.92, f32[32,128]{1,0:T(8,128)} %broadcast_in_dim.78.mine, f32[8,1,512]{2,1,0:T(1,128)} %bitcast.100, ...), custom_call_target="tpu_custom_call" | custom-call | flops 16777216 | bytes 16777216 | tf_op jit(solution)/shard_map/potential/pallas_call | solution.py:320
  177.4 23.3 %ham.1 = (f32[32,128,256]{2,1,0:T(8,128)}, f32[32,128,256]{2,1,0:T(8,128)}, f32[32,128,256]{2,1,0:T(8,128)}, f32[32,128,256]{2,1,0:T(8,128)}) custom-call(s32[8]{0:T(128)} %fusion.10.order, s32[64]{0:T(128)} %fusion.7.slots, s32[1]{0:T(128)} %bitcast.3.place, bf16[4,2,128,512]{3,2,1,0:T(8,128)(2,1)} %bitcast.79, bf16[4,2,128,512]{3,2,1,0:T(8,128)(2,1)} %bitcast.84, ...), custom_call_target="tpu_custom_call" | custom-call | flops 4294967296 | bytes 25165824 | tf_op jit(solution)/shard_map/ham/pallas_call | solution.py:345
  200.7 2.9 %multiply_convert_fusion = (f16[16,128,256]{2,1,0:T(8,128)(2,1)S(1)}, f16[16,128,256]{2,1,0:T(8,128)(2,1)S(1)}) fusion(f32[32,128,256]{2,1,0:T(8,128)} %get-tuple-element.31, f32[]{:T(128)} %bitcast.31), kind=kLoop, calls=%fused_computation.6 | loop fusion | flops 2097152 | bytes 6291460 | tf_op jit(solution)/shard_map/convert_element_type | solution.py:373
  203.6 1.1 collective-permute-start.38
  208.4 10.0 %collective-permute-done.38 = f16[2,8,128,256]{3,2,1,0:T(8,128)(2,1)S(1)} collective-permute-done((f16[2,8,128,256]{3,2,1,0:T(8,128)(2,1)S(1)}, f16[2,8,128,256]{3,2,1,0:T(8,128)(2,1)S(1)}, u32[]{:S(2)}, u32[]{:S(2)}) %collective-permute-start.38) | collective-permute-done | bytes 1048608 | tf_op jit(solution)/shard_map/ppermute | solution.py:384
  218.9 2.3 collective-permute-start.39
  221.6 2.0 collective-permute-start.35
  224.1 7.9 %collective-permute-done.37 = f16[2,8,128,256]{3,2,1,0:T(8,128)(2,1)S(1)} collective-permute-done((f16[2,8,128,256]{3,2,1,0:T(8,128)(2,1)S(1)}, f16[2,8,128,256]{3,2,1,0:T(8,128)(2,1)S(1)}, u32[]{:S(2)}, u32[]{:S(2)}) %collective-permute-start.37) | collective-permute-done | bytes 1048608 | tf_op jit(solution)/shard_map/ppermute | solution.py:385
  232.0 1.8 collective-permute-done.39
  234.5 2.2 collective-permute-start.40
  236.7 1.3 collective-permute-start.42
  238.0 18.0 %collective-permute-done.36 = f16[2,8,128,256]{3,2,1,0:T(8,128)(2,1)S(1)} collective-permute-done((f16[2,8,128,256]{3,2,1,0:T(8,128)(2,1)S(1)}, f16[2,8,128,256]{3,2,1,0:T(8,128)(2,1)S(1)}, u32[]{:S(2)}, u32[]{:S(2)}) %collective-permute-start.36) | collective-permute-done | bytes 1048608 | tf_op jit(solution)/shard_map/ppermute | solution.py:386
  257.4 9.6 %collective-permute-done.41 = f16[8,128,256]{2,1,0:T(8,128)(2,1)S(1)} collective-permute-done((f16[8,128,256]{2,1,0:T(8,128)(2,1)S(1)}, f16[8,128,256]{2,1,0:T(8,128)(2,1)S(1)}, u32[]{:S(2)}, u32[]{:S(2)}) %collective-permute-start.41) | collective-permute-done | bytes 524320 | tf_op jit(solution)/shard_map/ppermute | solution.py:396
  267.4 1.3 dynamic-slice_bitcast_fusion
  (141 shorter events, 23.9 us)
Async XLA Ops:
  1.9 1.6 collective-permute-start
  5.5 11.7 %collective-permute-start.18 = (bf16[8,128,256]{2,1,0:T(8,128)(2,1)}, bf16[8,128,256]{2,1,0:T(8,128)(2,1)}, u32[]{:S(2)}, u32[]{:S(2)}) collective-permute-start(bf16[8,128,256]{2,1,0:T(8,128)(2,1)} %pad_maximum_fusion.1), channel_id=1, source_target_pairs={{0,64},{4,20},{8,72},{12,28},{16,80},{20,4},{24,88},{28,12},{32,96... | collective-permute-start | bytes 1572872 | tf_op jit(solution)/shard_map/ppermute | solution.py:443
  11.2 27.3 %collective-permute-start.4 = (bf16[1024,512]{1,0:T(8,128)(2,1)S(1)}, bf16[1024,512]{1,0:T(8,128)(2,1)S(1)}, u32[]{:S(2)}, u32[]{:S(2)}) collective-permute-start(bf16[1024,512]{1,0:T(8,128)(2,1)S(1)} %bitcast.75), channel_id=1, source_target_pairs={{0,1},{1,2},{2,3},{3,0},{4,5},{5,6},{6,7},{7,4},{8,9},{9,10},{10,1... | collective-permute-start | bytes 3145736 | tf_op jit(solution)/shard_map/ppermute | solution.py:427
  14.3 26.2 %collective-permute-start.7 = (bf16[1024,512]{1,0:T(8,128)(2,1)S(1)}, bf16[1024,512]{1,0:T(8,128)(2,1)}, u32[]{:S(2)}, u32[]{:S(2)}) collective-permute-start(bf16[1024,512]{1,0:T(8,128)(2,1)S(1)} %bitcast.80), channel_id=1, source_target_pairs={{0,3},{1,0},{2,1},{3,2},{4,7},{5,4},{6,5},{7,6},{8,11},{9,8},{10,9... | collective-permute-start | bytes 3145736 | tf_op jit(solution)/shard_map/ppermute | solution.py:428
  16.1 43.0 %collective-permute-start.5 = (bf16[1024,512]{1,0:T(8,128)(2,1)S(1)}, bf16[1024,512]{1,0:T(8,128)(2,1)}, u32[]{:S(2)}, u32[]{:S(2)}) collective-permute-start(bf16[1024,512]{1,0:T(8,128)(2,1)S(1)} %bitcast.81), channel_id=1, source_target_pairs={{0,1},{1,2},{2,3},{3,0},{4,5},{5,6},{6,7},{7,4},{8,9},{9,10},{10,1... | collective-permute-start | bytes 3145736 | tf_op jit(solution)/shard_map/ppermute | solution.py:429
  16.4 9.5 %collective-permute-start.1 = (bf16[8,128,256]{2,1,0:T(8,128)(2,1)}, bf16[8,128,256]{2,1,0:T(8,128)(2,1)}, u32[]{:S(2)}, u32[]{:S(2)}) collective-permute-start(bf16[8,128,256]{2,1,0:T(8,128)(2,1)} %pad_maximum_fusion.1), channel_id=1, source_target_pairs={{0,96},{4,28},{8,104},{12,4},{16,112},{20,12},{24,120},{28,20},{32... | collective-permute-start | bytes 1572872 | tf_op jit(solution)/shard_map/ppermute | solution.py:443
  17.1 13.9 %collective-permute-start.19 = (bf16[8,128,256]{2,1,0:T(8,128)(2,1)}, bf16[8,128,256]{2,1,0:T(8,128)(2,1)}, u32[]{:S(2)}, u32[]{:S(2)}) collective-permute-start(bf16[8,128,256]{2,1,0:T(8,128)(2,1)} %pad_maximum_fusion.1), channel_id=1, source_target_pairs={{0,32},{4,12},{8,40},{12,20},{16,48},{20,28},{24,56},{28,4},{32,64... | collective-permute-start | bytes 1572872 | tf_op jit(solution)/shard_map/ppermute | solution.py:443
  18.8 96.1 %copy-start.20 = (f32[64]{0:T(128)S(1)}, f32[64]{0:T(128)}, u32[]{:S(2)}) copy-start(f32[64]{0:T(128)} %param.17) | copy-start | bytes 772
  18.8 96.3 %copy-start.14 = (f32[3,256]{1,0:T(4,128)S(1)}, f32[3,256]{1,0:T(4,128)}, u32[]{:S(2)}) copy-start(f32[3,256]{1,0:T(4,128)} %param.18) | copy-start | bytes 9220
  25.9 34.8 %collective-permute-start.6 = (bf16[1024,512]{1,0:T(8,128)(2,1)S(1)}, bf16[1024,512]{1,0:T(8,128)(2,1)}, u32[]{:S(2)}, u32[]{:S(2)}) collective-permute-start(bf16[1024,512]{1,0:T(8,128)(2,1)S(1)} %bitcast.76), channel_id=1, source_target_pairs={{0,3},{1,0},{2,1},{3,2},{4,7},{5,4},{6,5},{7,6},{8,11},{9,8},{10,9... | collective-permute-start | bytes 3145736 | tf_op jit(solution)/shard_map/ppermute | solution.py:430
  31.1 1.9 collective-permute-start.3
  32.9 29.0 %collective-permute-start.10 = (bf16[1024,512]{1,0:T(8,128)(2,1)S(1)}, bf16[1024,512]{1,0:T(8,128)(2,1)}, u32[]{:S(2)}, u32[]{:S(2)}) collective-permute-start(bf16[1024,512]{1,0:T(8,128)(2,1)S(1)} %bitcast.77), channel_id=1, source_target_pairs={{0,4},{4,0},{8,12},{12,8},{16,20},{20,16},{24,28},{28,24},{32,36},... | collective-permute-start | bytes 3145736 | tf_op jit(solution)/shard_map/ppermute | solution.py:514
  38.5 85.1 %copy-start.2 = (bf16[1024,512]{1,0:T(8,128)(2,1)}, bf16[1024,512]{1,0:T(8,128)(2,1)S(1)}, u32[]{:S(2)}) copy-start(bf16[1024,512]{1,0:T(8,128)(2,1)S(1)} %collective-permute-done.4.refs_2_) | copy-start | bytes 3145732
  38.5 24.8 %collective-permute-start.11 = (bf16[1024,512]{1,0:T(8,128)(2,1)S(1)}, bf16[1024,512]{1,0:T(8,128)(2,1)}, u32[]{:S(2)}, u32[]{:S(2)}) collective-permute-start(bf16[1024,512]{1,0:T(8,128)(2,1)S(1)} %bitcast.82), channel_id=1, source_target_pairs={{0,4},{4,0},{8,12},{12,8},{16,20},{20,16},{24,28},{28,24},{32,36},... | collective-permute-start | bytes 3145736 | tf_op jit(solution)/shard_map/ppermute | solution.py:514
  40.5 24.3 %collective-permute-start.22 = (bf16[16,128,256]{2,1,0:T(8,128)(2,1)}, bf16[16,128,256]{2,1,0:T(8,128)(2,1)}, u32[]{:S(2)}, u32[]{:S(2)}) collective-permute-start(bf16[16,128,256]{2,1,0:T(8,128)(2,1)} %constant_dynamic-update-slice_fusion.refs_9_), channel_id=1, source_target_pairs={{0,8},{4,36},{8,16},{12,44},{16,24},{20,52},{24,0},{28,60},{32,40}... | collective-permute-start | bytes 3145736 | tf_op jit(solution)/shard_map/ppermute | solution.py:498
  59.2 15.1 %collective-permute-start.2 = (bf16[16,128,256]{2,1,0:T(8,128)(2,1)}, bf16[16,128,256]{2,1,0:T(8,128)(2,1)}, u32[]{:S(2)}, u32[]{:S(2)}) collective-permute-start(bf16[16,128,256]{2,1,0:T(8,128)(2,1)} %pad_maximum_fusion.refs_8_), channel_id=1, source_target_pairs={{0,24},{4,100},{8,0},{12,108},{16,8},{20,116},{24,16},{28,124},{32... | collective-permute-start | bytes 3145736 | tf_op jit(solution)/shard_map/ppermute | solution.py:497
  60.8 24.7 %collective-permute-start.20 = (bf16[16,128,256]{2,1,0:T(8,128)(2,1)}, bf16[16,128,256]{2,1,0:T(8,128)(2,1)}, u32[]{:S(2)}, u32[]{:S(2)}) collective-permute-start(bf16[16,128,256]{2,1,0:T(8,128)(2,1)} %constant_dynamic-update-slice_fusion.refs_9_), channel_id=1, source_target_pairs={{0,24},{4,100},{8,0},{12,108},{16,8},{20,116},{24,16},{28,124},{32... | collective-permute-start | bytes 3145736 | tf_op jit(solution)/shard_map/ppermute | solution.py:500
  61.9 25.3 %collective-permute-start.26 = (bf16[16,128,256]{2,1,0:T(8,128)(2,1)}, bf16[16,128,256]{2,1,0:T(8,128)(2,1)}, u32[]{:S(2)}, u32[]{:S(2)}) collective-permute-start(bf16[16,128,256]{2,1,0:T(8,128)(2,1)} %constant_dynamic-update-slice_fusion.refs_9_), channel_id=1, source_target_pairs={{0,4},{4,0},{8,12},{12,8},{16,20},{20,16},{24,28},{28,24},{32,36},... | collective-permute-start | bytes 3145736 | tf_op jit(solution)/shard_map/ppermute | solution.py:509
  63.3 24.0 %collective-permute-start.24 = (bf16[16,128,256]{2,1,0:T(8,128)(2,1)}, bf16[16,128,256]{2,1,0:T(8,128)(2,1)}, u32[]{:S(2)}, u32[]{:S(2)}) collective-permute-start(bf16[16,128,256]{2,1,0:T(8,128)(2,1)} %pad_maximum_fusion.refs_8_), channel_id=1, source_target_pairs={{0,8},{4,36},{8,16},{12,44},{16,24},{20,52},{24,0},{28,60},{32,40}... | collective-permute-start | bytes 3145736 | tf_op jit(solution)/shard_map/ppermute | solution.py:499
  64.9 23.1 %collective-permute-start.25 = (bf16[16,128,256]{2,1,0:T(8,128)(2,1)}, bf16[16,128,256]{2,1,0:T(8,128)(2,1)}, u32[]{:S(2)}, u32[]{:S(2)}) collective-permute-start(bf16[16,128,256]{2,1,0:T(8,128)(2,1)} %pad_maximum_fusion.refs_8_), channel_id=1, source_target_pairs={{0,4},{4,0},{8,12},{12,8},{16,20},{20,16},{24,28},{28,24},{32,36},... | collective-permute-start | bytes 3145736 | tf_op jit(solution)/shard_map/ppermute | solution.py:509
  74.3 25.4 %collective-permute-start.8 = (bf16[1024,512]{1,0:T(8,128)(2,1)S(1)}, bf16[1024,512]{1,0:T(8,128)(2,1)S(1)}, u32[]{:S(2)}, u32[]{:S(2)}) collective-permute-start(bf16[1024,512]{1,0:T(8,128)(2,1)S(1)} %collective-permute-done.4.refs_2_), channel_id=1, source_target_pairs={{0,1},{1,2},{2,3},{3,0},{4,5},{5,6},{6,7},{7,4},{8,9},{9,10},{10,1... | collective-permute-start | bytes 3145736 | tf_op jit(solution)/shard_map/ppermute | solution.py:511
  85.5 24.4 %collective-permute-start.9 = (bf16[1024,512]{1,0:T(8,128)(2,1)}, bf16[1024,512]{1,0:T(8,128)(2,1)S(1)}, u32[]{:S(2)}, u32[]{:S(2)}) collective-permute-start(bf16[1024,512]{1,0:T(8,128)(2,1)} %collective-permute-done.7.refs_5_), channel_id=1, source_target_pairs={{0,3},{1,0},{2,1},{3,2},{4,7},{5,4},{6,5},{7,6},{8,11},{9,8},{10,9... | collective-permute-start | bytes 3145736 | tf_op jit(solution)/shard_map/ppermute | solution.py:512
  87.2 22.6 %collective-permute-start.12 = (bf16[1024,512]{1,0:T(8,128)(2,1)S(1)}, bf16[1024,512]{1,0:T(8,128)(2,1)}, u32[]{:S(2)}, u32[]{:S(2)}) collective-permute-start(bf16[1024,512]{1,0:T(8,128)(2,1)S(1)} %collective-permute-done.4.refs_2_), channel_id=1, source_target_pairs={{0,4},{4,0},{8,12},{12,8},{16,20},{20,16},{24,28},{28,24},{32,36},... | collective-permute-start | bytes 3145736 | tf_op jit(solution)/shard_map/ppermute | solution.py:514
  87.3 23.1 %collective-permute-start.23 = (bf16[16,128,256]{2,1,0:T(8,128)(2,1)}, bf16[16,128,256]{2,1,0:T(8,128)(2,1)}, u32[]{:S(2)}, u32[]{:S(2)}) collective-permute-start(bf16[16,128,256]{2,1,0:T(8,128)(2,1)} %collective-permute-done.22.refs_15_), channel_id=1, source_target_pairs={{0,8},{4,36},{8,16},{12,44},{16,24},{20,52},{24,0},{28,60},{32,40}... | collective-permute-start | bytes 3145736 | tf_op jit(solution)/shard_map/ppermute | solution.py:505
  87.9 22.6 %collective-permute-start.28 = (bf16[16,128,256]{2,1,0:T(8,128)(2,1)}, bf16[16,128,256]{2,1,0:T(8,128)(2,1)}, u32[]{:S(2)}, u32[]{:S(2)}) collective-permute-start(bf16[16,128,256]{2,1,0:T(8,128)(2,1)} %collective-permute-done.20.refs_11_), channel_id=1, source_target_pairs={{0,4},{4,0},{8,12},{12,8},{16,20},{20,16},{24,28},{28,24},{32,36},... | collective-permute-start | bytes 3145736 | tf_op jit(solution)/shard_map/ppermute | solution.py:509
  99.6 15.3 %collective-permute-start.21 = (bf16[16,128,256]{2,1,0:T(8,128)(2,1)}, bf16[16,128,256]{2,1,0:T(8,128)(2,1)}, u32[]{:S(2)}, u32[]{:S(2)}) collective-permute-start(bf16[16,128,256]{2,1,0:T(8,128)(2,1)} %collective-permute-done.2.refs_10_), channel_id=1, source_target_pairs={{0,24},{4,100},{8,0},{12,108},{16,8},{20,116},{24,16},{28,124},{32... | collective-permute-start | bytes 3145736 | tf_op jit(solution)/shard_map/ppermute | solution.py:504
  109.9 14.8 %collective-permute-start.27 = (bf16[16,128,256]{2,1,0:T(8,128)(2,1)}, bf16[16,128,256]{2,1,0:T(8,128)(2,1)}, u32[]{:S(2)}, u32[]{:S(2)}) collective-permute-start(bf16[16,128,256]{2,1,0:T(8,128)(2,1)} %collective-permute-done.2.refs_10_), channel_id=1, source_target_pairs={{0,4},{4,0},{8,12},{12,8},{16,20},{20,16},{24,28},{28,24},{32,36},... | collective-permute-start | bytes 3145736 | tf_op jit(solution)/shard_map/ppermute | solution.py:509
  109.9 14.3 %collective-permute-start.32 = (bf16[16,128,256]{2,1,0:T(8,128)(2,1)}, bf16[16,128,256]{2,1,0:T(8,128)(2,1)}, u32[]{:S(2)}, u32[]{:S(2)}) collective-permute-start(bf16[16,128,256]{2,1,0:T(8,128)(2,1)} %collective-permute-done.22.refs_15_), channel_id=1, source_target_pairs={{0,4},{4,0},{8,12},{12,8},{16,20},{20,16},{24,28},{28,24},{32,36},... | collective-permute-start | bytes 3145736 | tf_op jit(solution)/shard_map/ppermute | solution.py:509
  110.4 14.4 %collective-permute-start.31 = (bf16[16,128,256]{2,1,0:T(8,128)(2,1)}, bf16[16,128,256]{2,1,0:T(8,128)(2,1)}, u32[]{:S(2)}, u32[]{:S(2)}) collective-permute-start(bf16[16,128,256]{2,1,0:T(8,128)(2,1)} %collective-permute-done.24.refs_14_), channel_id=1, source_target_pairs={{0,4},{4,0},{8,12},{12,8},{16,20},{20,16},{24,28},{28,24},{32,36},... | collective-permute-start | bytes 3145736 | tf_op jit(solution)/shard_map/ppermute | solution.py:509
  110.5 14.7 %collective-permute-start.30 = (bf16[16,128,256]{2,1,0:T(8,128)(2,1)}, bf16[16,128,256]{2,1,0:T(8,128)(2,1)}, u32[]{:S(2)}, u32[]{:S(2)}) collective-permute-start(bf16[16,128,256]{2,1,0:T(8,128)(2,1)} %collective-permute-done.23.refs_13_), channel_id=1, source_target_pairs={{0,4},{4,0},{8,12},{12,8},{16,20},{20,16},{24,28},{28,24},{32,36},... | collective-permute-start | bytes 3145736 | tf_op jit(solution)/shard_map/ppermute | solution.py:509
  114.9 10.4 %collective-permute-start.29 = (bf16[16,128,256]{2,1,0:T(8,128)(2,1)}, bf16[16,128,256]{2,1,0:T(8,128)(2,1)}, u32[]{:S(2)}, u32[]{:S(2)}) collective-permute-start(bf16[16,128,256]{2,1,0:T(8,128)(2,1)} %collective-permute-done.21.refs_12_), channel_id=1, source_target_pairs={{0,4},{4,0},{8,12},{12,8},{16,20},{20,16},{24,28},{28,24},{32,36},... | collective-permute-start | bytes 3145736 | tf_op jit(solution)/shard_map/ppermute | solution.py:509
  124.2 51.1 %collective-permute-start.15 = (bf16[1024,512]{1,0:T(8,128)(2,1)}, bf16[1024,512]{1,0:T(8,128)(2,1)}, u32[]{:S(2)}, u32[]{:S(2)}) collective-permute-start(bf16[1024,512]{1,0:T(8,128)(2,1)} %collective-permute-done.7.refs_5_), channel_id=1, source_target_pairs={{0,4},{4,0},{8,12},{12,8},{16,20},{20,16},{24,28},{28,24},{32,36},... | collective-permute-start | bytes 3145736 | tf_op jit(solution)/shard_map/ppermute | solution.py:514
  124.7 51.6 %collective-permute-start.13 = (bf16[1024,512]{1,0:T(8,128)(2,1)}, bf16[1024,512]{1,0:T(8,128)(2,1)}, u32[]{:S(2)}, u32[]{:S(2)}) collective-permute-start(bf16[1024,512]{1,0:T(8,128)(2,1)} %collective-permute-done.5.refs_3_), channel_id=1, source_target_pairs={{0,4},{4,0},{8,12},{12,8},{16,20},{20,16},{24,28},{28,24},{32,36},... | collective-permute-start | bytes 3145736 | tf_op jit(solution)/shard_map/ppermute | solution.py:514
  124.8 51.5 %collective-permute-start.14 = (bf16[1024,512]{1,0:T(8,128)(2,1)}, bf16[1024,512]{1,0:T(8,128)(2,1)}, u32[]{:S(2)}, u32[]{:S(2)}) collective-permute-start(bf16[1024,512]{1,0:T(8,128)(2,1)} %collective-permute-done.6.refs_4_), channel_id=1, source_target_pairs={{0,4},{4,0},{8,12},{12,8},{16,20},{20,16},{24,28},{28,24},{32,36},... | collective-permute-start | bytes 3145736 | tf_op jit(solution)/shard_map/ppermute | solution.py:514
  125.2 51.1 %collective-permute-start.16 = (bf16[1024,512]{1,0:T(8,128)(2,1)S(1)}, bf16[1024,512]{1,0:T(8,128)(2,1)}, u32[]{:S(2)}, u32[]{:S(2)}) collective-permute-start(bf16[1024,512]{1,0:T(8,128)(2,1)S(1)} %collective-permute-done.8.refs_6_), channel_id=1, source_target_pairs={{0,4},{4,0},{8,12},{12,8},{16,20},{20,16},{24,28},{28,24},{32,36},... | collective-permute-start | bytes 3145736 | tf_op jit(solution)/shard_map/ppermute | solution.py:514
  125.3 51.0 %collective-permute-start.17 = (bf16[1024,512]{1,0:T(8,128)(2,1)S(1)}, bf16[1024,512]{1,0:T(8,128)(2,1)}, u32[]{:S(2)}, u32[]{:S(2)}) collective-permute-start(bf16[1024,512]{1,0:T(8,128)(2,1)S(1)} %collective-permute-done.9.refs_7_), channel_id=1, source_target_pairs={{0,4},{4,0},{8,12},{12,8},{16,20},{20,16},{24,28},{28,24},{32,36},... | collective-permute-start | bytes 3145736 | tf_op jit(solution)/shard_map/ppermute | solution.py:514
  147.7 18.7 %all-to-all-start = ((f32[32,24,128]{2,1,0:T(8,128)}), f32[32,24,128]{2,1,0:T(8,128)S(1)}, u32[]{:S(2)}, u32[]{:S(2)}) async-start(f32[32,24,128]{2,1,0:T(8,128)} %get-tuple-element.24), calls=%async_computation | async-start | bytes 786432 | tf_op jit(solution)/shard_map/all_to_all | solution.py:519
  175.3 1.5 collective-permute-start.33
  203.6 14.9 %collective-permute-start.38 = (f16[2,8,128,256]{3,2,1,0:T(8,128)(2,1)S(1)}, f16[2,8,128,256]{3,2,1,0:T(8,128)(2,1)S(1)}, u32[]{:S(2)}, u32[]{:S(2)}) collective-permute-start(f16[2,8,128,256]{3,2,1,0:T(8,128)(2,1)S(1)} %bitcast.96), channel_id=1, source_target_pairs={{0,96},{4,28},{8,104},{12,4},{16,112},{20,12},{24,120},{28,20},{32... | collective-permute-start | bytes 3145736 | tf_op jit(solution)/shard_map/ppermute | solution.py:384
  204.7 16.5 %collective-permute-start.34 = (f16[2,8,128,256]{3,2,1,0:T(8,128)(2,1)S(1)}, f16[2,8,128,256]{3,2,1,0:T(8,128)(2,1)S(1)}, u32[]{:S(2)}, u32[]{:S(2)}) collective-permute-start(f16[2,8,128,256]{3,2,1,0:T(8,128)(2,1)S(1)} %bitcast.95), channel_id=1, source_target_pairs={{0,32},{4,12},{8,40},{12,20},{16,48},{20,28},{24,56},{28,4},{32,64... | collective-permute-start | bytes 3145736 | tf_op jit(solution)/shard_map/ppermute | solution.py:383
  206.3 25.7 %collective-permute-start.37 = (f16[2,8,128,256]{3,2,1,0:T(8,128)(2,1)S(1)}, f16[2,8,128,256]{3,2,1,0:T(8,128)(2,1)S(1)}, u32[]{:S(2)}, u32[]{:S(2)}) collective-permute-start(f16[2,8,128,256]{3,2,1,0:T(8,128)(2,1)S(1)} %bitcast.98), channel_id=1, source_target_pairs={{0,32},{4,12},{8,40},{12,20},{16,48},{20,28},{24,56},{28,4},{32,64... | collective-permute-start | bytes 3145736 | tf_op jit(solution)/shard_map/ppermute | solution.py:385
  218.9 14.9 %collective-permute-start.39 = (f16[2,8,128,256]{3,2,1,0:T(8,128)(2,1)S(1)}, f16[2,8,128,256]{3,2,1,0:T(8,128)(2,1)S(1)}, u32[]{:S(2)}, u32[]{:S(2)}) collective-permute-start(f16[2,8,128,256]{3,2,1,0:T(8,128)(2,1)S(1)} %add_convert_fusion.1), channel_id=1, source_target_pairs={{0,96},{4,28},{8,104},{12,4},{16,112},{20,12},{24,120},{28,20},{32... | collective-permute-start | bytes 3145736 | tf_op jit(solution)/shard_map/ppermute | solution.py:388
  221.2 34.8 %collective-permute-start.36 = (f16[2,8,128,256]{3,2,1,0:T(8,128)(2,1)S(1)}, f16[2,8,128,256]{3,2,1,0:T(8,128)(2,1)S(1)}, u32[]{:S(2)}, u32[]{:S(2)}) collective-permute-start(f16[2,8,128,256]{3,2,1,0:T(8,128)(2,1)S(1)} %bitcast.97), channel_id=1, source_target_pairs={{0,96},{4,28},{8,104},{12,4},{16,112},{20,12},{24,120},{28,20},{32... | collective-permute-start | bytes 3145736 | tf_op jit(solution)/shard_map/ppermute | solution.py:386
  221.6 34.3 %collective-permute-start.35 = (f16[2,8,128,256]{3,2,1,0:T(8,128)(2,1)S(1)}, f16[2,8,128,256]{3,2,1,0:T(8,128)(2,1)S(1)}, u32[]{:S(2)}, u32[]{:S(2)}) collective-permute-start(f16[2,8,128,256]{3,2,1,0:T(8,128)(2,1)S(1)} %add_convert_fusion.2), channel_id=1, source_target_pairs={{0,32},{4,12},{8,40},{12,20},{16,48},{20,28},{24,56},{28,4},{32,64... | collective-permute-start | bytes 3145736 | tf_op jit(solution)/shard_map/ppermute | solution.py:387
  234.5 22.8 %collective-permute-start.40 = (f16[8,128,256]{2,1,0:T(8,128)(2,1)S(1)}, f16[8,128,256]{2,1,0:T(8,128)(2,1)S(1)}, u32[]{:S(2)}, u32[]{:S(2)}) collective-permute-start(f16[8,128,256]{2,1,0:T(8,128)(2,1)S(1)} %get-tuple-element.54), channel_id=1, source_target_pairs={{0,16},{4,68},{8,24},{12,76},{16,0},{20,84},{24,8},{28,92},{32,48}... | collective-permute-start | bytes 1572872 | tf_op jit(solution)/shard_map/ppermute | solution.py:396
  236.7 20.7 %collective-permute-start.42 = (f16[8,128,256]{2,1,0:T(8,128)(2,1)S(1)}, f16[8,128,256]{2,1,0:T(8,128)(2,1)S(1)}, u32[]{:S(2)}, u32[]{:S(2)}) collective-permute-start(f16[8,128,256]{2,1,0:T(8,128)(2,1)S(1)} %get-tuple-element.55), channel_id=1, source_target_pairs={{0,24},{4,100},{8,0},{12,108},{16,8},{20,116},{24,16},{28,124},{32... | collective-permute-start | bytes 1572872 | tf_op jit(solution)/shard_map/ppermute | solution.py:396
  256.5 10.5 %collective-permute-start.41 = (f16[8,128,256]{2,1,0:T(8,128)(2,1)S(1)}, f16[8,128,256]{2,1,0:T(8,128)(2,1)S(1)}, u32[]{:S(2)}, u32[]{:S(2)}) collective-permute-start(f16[8,128,256]{2,1,0:T(8,128)(2,1)S(1)} %fusion.6), channel_id=1, source_target_pairs={{0,8},{4,36},{8,16},{12,44},{16,24},{20,52},{24,0},{28,60},{32,40}... | collective-permute-start | bytes 1572872 | tf_op jit(solution)/shard_map/ppermute | solution.py:396
  267.3 1.6 collective-permute-start.43
  (18 other events, 335.0 us)

commit v9 on v8

--- a/solution.py
+++ b/solution.py
@@ -88,22 +88,11 @@
         lax.fori_loop(0, 32, fetch, 0)
 
 
-def density_steps(order, chunks, dmat, sem, table, weights, xc, rho, pacc, bufs, top):
+def density_steps(order, dmat, sem, table, weights, xc, rho, pacc, bufs, top):
     held, tbuf, psem, tsem = bufs
-    for i in range(CHUNKS):
-        pltpu.make_async_copy(chunks[i], held.at[i], psem.at[i]).start()
-    pltpu.make_async_copy(table.at[order[0]], tbuf.at[0], tsem.at[0]).start()
     pltpu.make_async_copy(dmat, dmat, sem).wait()
 
     def step(i, top):
-        slot = lax.rem(i, 2)
-
-        @pl.when(i + 1 < CHUNKS)
-        def _():
-            pltpu.make_async_copy(
-                table.at[order[i + 1]], tbuf.at[1 - slot], tsem.at[1 - slot]
-            ).start()
-
         pi = order[i]
         b = pi // 4
         pltpu.make_async_copy(held.at[i], held.at[i], psem.at[i]).wait()
@@ -117,31 +106,43 @@
             )
         rho[pi] = total
         weighted = weights[pi] * total
-        pltpu.make_async_copy(table.at[pi], tbuf.at[slot], tsem.at[slot]).wait()
+        pltpu.make_async_copy(table.at[pi], tbuf.at[i], tsem.at[i]).wait()
         for block in range(8):
             rows = pl.ds(block * 128, 128)
             part = pacc[b, rows, :]
             for lane in range(HALF // 128):
                 cols = slice(lane * 128, (lane + 1) * 128)
-                part = part + tbuf[slot, rows, cols] * weighted[:, cols]
+                part = part + tbuf[i, rows, cols] * weighted[:, cols]
             pacc[b, rows, :] = part
         return jnp.maximum(top, jnp.abs(xc[pi] * total))
 
     return lax.fori_loop(0, CHUNKS, step, top)
 
 
-def density_body(order, place, which, where, *refs):
+def assemble_body(place, which, where, *refs):
+    *sources, dmat, sem = refs
+    fetch_tiles(place[0], which, where, sources, dmat, sem)
+    pltpu.make_async_copy(dmat, dmat, sem).wait()
+
+
+def density_body(order, *refs):
     chunks = refs[:CHUNKS]
-    sources = refs[CHUNKS : CHUNKS + 2 * SOURCES]
-    table, weights, xc, home_rows, rho, sent, *rest = refs[CHUNKS + 2 * SOURCES :]
+    table, dmat_in, weights, xc, home_rows, rho, sent, *rest = refs[CHUNKS:]
     pacc, dmat, block_out, sem, *bufs = rest
-    fetch_tiles(place[0], which, where, sources, dmat, sem)
+    held, tbuf, psem, tsem = bufs
+
+    def load(i):
+        pltpu.make_async_copy(chunks[i], held.at[i], psem.at[i]).start()
+        pltpu.make_async_copy(table.at[order[i]], tbuf.at[i], tsem.at[i]).start()
+
+    pltpu.make_async_copy(dmat_in, dmat, sem).start()
+    for i in range(CHUNKS):
+        load(i)
     pacc[...] = jnp.zeros_like(pacc)
     block_out[...] = jnp.zeros_like(block_out)
     block_out[pl.ds(17, 2), :] = home_rows[...]
     top = density_steps(
-        order, chunks, dmat, sem, table, weights, xc, rho, pacc, bufs,
-        jnp.zeros((1, HALF), jnp.float32),
+        order, dmat, sem, table, weights, xc, rho, pacc, bufs, jnp.zeros((1, HALF), jnp.float32)
     )
     ones = jnp.ones((8, 128), jnp.bfloat16)
     for b in range(2):
@@ -159,7 +160,7 @@
 
 def potential_body(table, got, mine, weights, xc, rho, coeffs, pot, scale, bound, *scratch):
     tbuf, column, data, tsem = scratch
-    for i in range(2):
+    for i in range(PIECES):
         pltpu.make_async_copy(table.at[i], tbuf.at[i], tsem.at[i]).start()
     natoms = coeffs.shape[0]
     homes = []
@@ -197,20 +198,13 @@
     bound[...] = top + jnp.broadcast_to(heavy, (1, 128)) * (KERNEL_MAX * 16)
 
     def step(i, _):
-        slot = lax.rem(i, 3)
-
-        @pl.when(i + 2 < PIECES)
-        def _():
-            ahead = lax.rem(i + 2, 3)
-            pltpu.make_async_copy(table.at[i + 2], tbuf.at[ahead], tsem.at[ahead]).start()
-
         base = (i // 4) * 1024
-        pltpu.make_async_copy(table.at[i], tbuf.at[slot], tsem.at[slot]).wait()
+        pltpu.make_async_copy(table.at[i], tbuf.at[i], tsem.at[i]).wait()
         parts = [jnp.zeros((8, 128), jnp.float32) for _ in range(HALF // 128)]
         for block in range(16):
             factor = column[pl.ds(base + block * 64, 64), :]
             for lane in range(HALF // 128):
-                prod = tbuf[slot, block * 64 : (block + 1) * 64, lane * 128 : (lane + 1) * 128]
+                prod = tbuf[i, block * 64 : (block + 1) * 64, lane * 128 : (lane + 1) * 128]
                 parts[lane] = parts[lane] + jnp.sum((prod * factor).reshape(8, 8, 128), axis=0)
         hartree = jnp.concatenate([jnp.sum(p, axis=0, keepdims=True) for p in parts], axis=1)
         potential = hartree + xc[i] * rho[i]
@@ -235,7 +229,9 @@
             for half in range(2):
                 at = (1 - core) if half else core
                 pltpu.make_async_copy(
-                    ref.at[:, half], held.at[side, pi // 4, at, :, :, lanes], psem
+                    ref.at[:, half],
+                    held.at[side, pi // 4, at, :, :, lanes],
+                    psem.at[side * 2 + pi // 4],
                 ).start()
             i += width // HALF
     for b in range(2):
@@ -247,7 +243,6 @@
         return 0
 
     lax.fori_loop(0, dense.shape[0], clear, 0)
-    pltpu.make_async_copy(held, held, psem).wait()
 
     def product(side, b, col):
         left = held[side, b, 0].reshape(2 * BLK, 4 * HALF)
@@ -259,6 +254,12 @@
 
     def step(n, _):
         side, b, cols = n // 4, (n // 2) % 2, (n % 2) * 2
+
+        @pl.when(cols == 0)
+        def _():
+            batch = held.at[side, b]
+            pltpu.make_async_copy(batch, batch, psem.at[side * 2 + b]).wait()
+
         parts = [product(side, b, cols + k) for k in range(2)]
         for k in range(2):
             for row in range(NB):
@@ -285,7 +286,21 @@
     return pl.BlockSpec(memory_space=pltpu.SMEM)
 
 
-def density_call(order, place, which, where, chunks, sources, table, weights, xc, home_rows):
+def assemble_call(place, which, where, sources):
+    nbasis = NB * BLK
+    return pl.pallas_call(
+        assemble_body,
+        out_shape=jax.ShapeDtypeStruct((2, nbasis, nbasis), jnp.bfloat16),
+        in_specs=[smem_spec()] * 3 + [any_spec()] * (2 * SOURCES),
+        out_specs=vmem_spec(),
+        scratch_shapes=[pltpu.SemaphoreType.DMA],
+        compiler_params=pltpu.CompilerParams(vmem_limit_bytes=VMEM_GRANT),
+        cost_estimate=pl.CostEstimate(flops=0, bytes_accessed=8 << 20, transcendentals=0),
+        name="assemble",
+    )(place, which, where, *sources)
+
+
+def density_call(order, chunks, table, dmat, weights, xc, home_rows):
     nbasis = NB * BLK
     return pl.pallas_call(
         density_body,
@@ -293,9 +308,7 @@
             jax.ShapeDtypeStruct((PIECES, 1, HALF), jnp.float32),
             jax.ShapeDtypeStruct((32, PAY_ROWS, 128), jnp.float32),
         ),
-        in_specs=[smem_spec()] * 4
-        + [any_spec()] * (CHUNKS + 2 * SOURCES + 1)
-        + [vmem_spec()] * 3,
+        in_specs=[smem_spec()] + [any_spec()] * (CHUNKS + 2) + [vmem_spec()] * 3,
         out_specs=(vmem_spec(),) * 2,
         scratch_shapes=[
             pltpu.VMEM((2, nbasis, 128), jnp.float32),
@@ -303,16 +316,16 @@
             pltpu.VMEM((PAY_ROWS, 128), jnp.float32),
             pltpu.SemaphoreType.DMA,
             pltpu.VMEM((CHUNKS, nbasis, HALF), jnp.bfloat16),
-            pltpu.VMEM((2, nbasis, HALF), jnp.float32),
+            pltpu.VMEM((CHUNKS, nbasis, HALF), jnp.float32),
             pltpu.SemaphoreType.DMA((CHUNKS,)),
-            pltpu.SemaphoreType.DMA((2,)),
+            pltpu.SemaphoreType.DMA((CHUNKS,)),
         ],
         compiler_params=pltpu.CompilerParams(vmem_limit_bytes=VMEM_GRANT),
         cost_estimate=pl.CostEstimate(
             flops=2 * 4096 * 1024 * 1024, bytes_accessed=32 << 20, transcendentals=0
         ),
         name="density",
-    )(order, place, which, where, *chunks, *sources, table, weights, xc, home_rows)
+    )(order, *chunks, table, dmat, weights, xc, home_rows)
 
 
 def potential_call(table, got, mine, weights, xc, rho, natoms):
@@ -328,10 +341,10 @@
         in_specs=[any_spec()] + [vmem_spec()] * 5,
         out_specs=(vmem_spec(),) * 4,
         scratch_shapes=[
-            pltpu.VMEM((3, NB * BLK, HALF), jnp.float32),
+            pltpu.VMEM((PIECES, NB * BLK, HALF), jnp.float32),
             pltpu.VMEM((2048, 128), jnp.float32),
             pltpu.VMEM((512, 128), jnp.float32),
-            pltpu.SemaphoreType.DMA((3,)),
+            pltpu.SemaphoreType.DMA((PIECES,)),
         ],
         compiler_params=pltpu.CompilerParams(vmem_limit_bytes=VMEM_GRANT),
         cost_estimate=pl.CostEstimate(
@@ -351,7 +364,7 @@
             pltpu.VMEM((128, 128, BLK), jnp.float32),
             pltpu.VMEM((2, 2, 2, NB, 128, 4 * HALF), jnp.bfloat16),
             pltpu.VMEM((2, 2, 1, 4 * HALF), jnp.float32),
-            pltpu.SemaphoreType.DMA,
+            pltpu.SemaphoreType.DMA((4,)),
             pltpu.SemaphoreType.DMA((4,)),
         ],
         compiler_params=pltpu.CompilerParams(vmem_limit_bytes=VMEM_GRANT),
@@ -513,9 +526,8 @@
     chunks = [own0, own1, below0, below1, above0, above1, far0, far1]
     beside = [lax.ppermute(chunk, "grid", swap) for chunk in chunks]
 
-    rho, sent = density_call(
-        order, core_place, which, where, chunks, sources, gauss, weights, xc, home_rows
-    )
+    dmat = assemble_call(core_place, which, where, sources)
+    rho, sent = density_call(order, chunks, gauss, dmat, weights, xc, home_rows)
     got = lax.all_to_all(sent, "grid", split_axis=0, concat_axis=0, tiled=True)
     all_coeffs, pot, scale, bound = potential_call(
         hart, got.reshape(groups * PAY_ROWS, 128), my_homes, weights, xc, rho, natoms

time: 272 us -> 265 us (0.974)
  waiting for transfers between devices: 121 us -> 106 us
  Pallas kernels: 53.4 us -> 59.3 us
  starting transfers between devices: 50.1 us -> 54.6 us
    ppermute x1, waiting for transfers between devices: 0.01 us -> 10.7 us  [one_device(): other_far = lax.ppermute(other_behind, 'grid', forth)]
    ppermute x1, waiting for transfers between devices: 9.39 us -> 0.01 us  [one_device(): near_ahead = lax.ppermute(near, 'grid', back)]
    ppermute x1, waiting for transfers between devices: 0.01 us -> 9.31 us  [one_device(): near_behind = lax.ppermute(near, 'grid', forth)]
    pallas_call x0 -> x1, Pallas kernels: none -> 8.64 us  [assemble_call(): pl.pallas_call(assemble_body, out_shape=jax.ShapeDtypeStruct((2, nbasis,...]
    ppermute x1, waiting for transfers between devices: 7.77 us -> 0.01 us  [one_device(): other_ahead = lax.ppermute(other, 'grid', back)]
    ppermute x1, waiting for transfers between devices: 10.2 us -> 3.1 us  [one_device(): far0 = lax.ppermute(below0, 'pert', ring(1))]
    ppermute x3, waiting for transfers between devices: 5.15 us -> 12.2 us  [one_device(): lax.ppermute(base, 'grid', core_perm(-d, False))]
    ppermute x1, waiting for transfers between devices: 7.53 us -> 2.05 us  [one_device(): far1 = lax.ppermute(above1, 'pert', ring(3))]
  transfers between devices with their start and end apart: 45 -> 45, of which waited for: 19 -> 20; matrix products, arithmetic and copies ran while one was open for 13% -> 12% of each run, Pallas kernels for 11% -> 15%
where the time goes in v9:
time: 265 us; the launch traced here: 263 us
  waiting for transfers between devices  106 us (40%)
  Pallas kernels  59.3 us (22%)
  starting transfers between devices  54.6 us (21%)
  other arithmetic  31 us (12%)
  local copies, waits for them, and re-layouts  10.1 us (4%)
    pallas_call x1, Pallas kernels, density_call(): pl.pallas_call(density_body, out_shape=(jax.ShapeDtypeStruct((PIECES, 1,...  22.6 us
    pallas_call x1, Pallas kernels, ham_call(): pl.pallas_call(ham_body, out_shape=(jax.ShapeDtypeStruct((32, 128, BLK),...  20.3 us
    ppermute x1, waiting for transfers between devices, ring_sum(): above_low = lax.ppermute(cast(parts[3][:half] * factor), 'grid', down)  18 us
    ppermute x1, waiting for transfers between devices, one_device(): below1 = lax.ppermute(own1, 'pert', ring(1))  12.9 us
    ppermute x3, waiting for transfers between devices, one_device(): lax.ppermute(base, 'grid', core_perm(-d, False))  12.2 us
    ppermute x1, waiting for transfers between devices, one_device(): other_far = lax.ppermute(other_behind, 'grid', forth)  10.7 us
    ppermute x1, waiting for transfers between devices, ring_sum(): from_above = lax.ppermute(cast(parts[2][half:] * factor), 'grid', down)  10 us
    ppermute x3, waiting for transfers between devices, direct_sum(): lax.ppermute(cast(parts[d]), 'grid', core_perm(d, True))  9.57 us
  transfers between devices with their start and end apart: 45, of which 20 were waited for; matrix products, arithmetic and copies ran while one was open for 12% of the time, Pallas kernels for 15%

profile of v9, /device:TPU:0, one launch (start us, length us, event | category | flops | bytes accessed | tf_op | source)
XLA Modules:
  0.0 263.1 jit_solution(11297825982265350212)
XLA Ops:
  0.7 1.2 select_bitcast_fusion
  2.0 1.5 collective-permute-done
  5.5 4.1 %collective-permute-start.1 = (bf16[8,128,256]{2,1,0:T(8,128)(2,1)}, bf16[8,128,256]{2,1,0:T(8,128)(2,1)}, u32[]{:S(2)}, u32[]{:S(2)}) collective-permute-start(bf16[8,128,256]{2,1,0:T(8,128)(2,1)} %pad_maximum_fusion.1), channel_id=1, source_target_pairs={{0,96},{4,28},{8,104},{12,4},{16,112},{20,12},{24,120},{28,20},{32... | collective-permute-start | bytes 1572872 | tf_op jit(solution)/shard_map/ppermute | solution.py:456
  10.4 1.6 collective-permute-start.4
  12.7 1.7 collective-permute-start.7
  14.4 2.3 collective-permute-done.1
  17.9 2.8 %collective-permute-start.2 = (bf16[16,128,256]{2,1,0:T(8,128)(2,1)S(1)}, bf16[16,128,256]{2,1,0:T(8,128)(2,1)}, u32[]{:S(2)}, u32[]{:S(2)}) collective-permute-start(bf16[16,128,256]{2,1,0:T(8,128)(2,1)S(1)} %pad_maximum_fusion.refs_0_), channel_id=1, source_target_pairs={{0,24},{4,100},{8,0},{12,108},{16,8},{20,116},{24,16},{28,124},{32... | collective-permute-start | bytes 3145736 | tf_op jit(solution)/shard_map/ppermute | solution.py:510
  20.7 2.3 collective-permute-start.18
  23.0 2.2 collective-permute-start.19
  25.6 6.2 %collective-permute-done.18 = bf16[8,128,256]{2,1,0:T(8,128)(2,1)} collective-permute-done((bf16[8,128,256]{2,1,0:T(8,128)(2,1)}, bf16[8,128,256]{2,1,0:T(8,128)(2,1)}, u32[]{:S(2)}, u32[]{:S(2)}) %collective-permute-start.18) | collective-permute-done | bytes 524320 | tf_op jit(solution)/shard_map/ppermute | solution.py:456
  31.8 1.9 constant_dynamic-update-slice_fusion.1
  33.7 3.6 %collective-permute-done.19 = bf16[8,128,256]{2,1,0:T(8,128)(2,1)} collective-permute-done((bf16[8,128,256]{2,1,0:T(8,128)(2,1)}, bf16[8,128,256]{2,1,0:T(8,128)(2,1)}, u32[]{:S(2)}, u32[]{:S(2)}) %collective-permute-start.19) | collective-permute-done | bytes 524320 | tf_op jit(solution)/shard_map/ppermute | solution.py:456
  37.3 1.6 collective-permute-start.5
  38.9 1.9 constant_dynamic-update-slice_fusion.refs_1_
  40.8 1.7 collective-permute-start.6
  42.5 1.3 collective-permute-start.22
  43.7 2.2 collective-permute-start.20
  49.1 12.9 %collective-permute-done.5.refs_3_ = bf16[1024,512]{1,0:T(8,128)(2,1)} collective-permute-done((bf16[1024,512]{1,0:T(8,128)(2,1)S(1)}, bf16[1024,512]{1,0:T(8,128)(2,1)}, u32[]{:S(2)}, u32[]{:S(2)}) %collective-permute-start.5) | collective-permute-done | bytes 1048608 | tf_op jit(solution)/shard_map/ppermute | solution.py:442
  61.9 3.1 %collective-permute-start.24 = (bf16[16,128,256]{2,1,0:T(8,128)(2,1)S(1)}, bf16[16,128,256]{2,1,0:T(8,128)(2,1)S(1)}, u32[]{:S(2)}, u32[]{:S(2)}) collective-permute-start(bf16[16,128,256]{2,1,0:T(8,128)(2,1)S(1)} %pad_maximum_fusion.refs_0_), channel_id=1, source_target_pairs={{0,8},{4,36},{8,16},{12,44},{16,24},{20,52},{24,0},{28,60},{32,40}... | collective-permute-start | bytes 3145736 | tf_op jit(solution)/shard_map/ppermute | solution.py:512
  65.1 1.6 collective-permute-start.25
  67.0 2.4 collective-permute-start.28
  69.3 1.3 collective-permute-start.21
  70.7 9.3 %collective-permute-done.24.refs_6_ = bf16[16,128,256]{2,1,0:T(8,128)(2,1)S(1)} collective-permute-done((bf16[16,128,256]{2,1,0:T(8,128)(2,1)S(1)}, bf16[16,128,256]{2,1,0:T(8,128)(2,1)S(1)}, u32[]{:S(2)}, u32[]{:S(2)}) %collective-permute-start.24) | collective-permute-done | bytes 1048608 | tf_op jit(solution)/shard_map/ppermute | solution.py:512
  80.5 10.7 %collective-permute-done.23.refs_5_ = bf16[16,128,256]{2,1,0:T(8,128)(2,1)S(1)} collective-permute-done((bf16[16,128,256]{2,1,0:T(8,128)(2,1)}, bf16[16,128,256]{2,1,0:T(8,128)(2,1)S(1)}, u32[]{:S(2)}, u32[]{:S(2)}) %collective-permute-start.23) | collective-permute-done | bytes 1048608 | tf_op jit(solution)/shard_map/ppermute | solution.py:518
  92.5 1.4 collective-permute-done.31.refs_14_
  95.5 1.4 collective-permute-done.29.refs_12_
  96.9 2.0 collective-permute-start.9
  99.5 8.1 %fusion.refs_8_ = f32[8,1024,512]{2,1,0:T(8,128)} fusion(f32[1024]{0:T(1024)S(1)} %div.197, f32[8,16,512]{2,1,0:T(8,128)S(1)} %bitcast.91), kind=kLoop, calls=%fused_computation.3 | loop fusion | flops 4194304 | bytes 17043456 | tf_op jit(solution)/shard_map/exp | solution.py:493
  108.3 8.6 %assemble.1.refs_9_ = bf16[2,1024,1024]{2,1,0:T(8,128)(2,1)} custom-call(s32[1]{0:T(128)} %bitcast.3.place, s32[64]{0:T(128)} %get-tuple-element.20.which, s32[64]{0:T(128)} %get-tuple-element.21.where, bf16[16,128,256]{2,1,0:T(8,128)(2,1)} %copy-done.2, bf16[16,128,256]{2,1,0:T(8,128)(2,1)} %constant_dynamic-update-slice_fusion.refs_1_, ...), custom_call_target="tpu_custom_call" | custom-call | bytes 8388608 | tf_op jit(solution)/shard_map/assemble/pallas_call | solution.py:291
  117.5 3.1 %collective-permute-done.8.refs_6_ = bf16[1024,512]{1,0:T(8,128)(2,1)} collective-permute-done((bf16[1024,512]{1,0:T(8,128)(2,1)}, bf16[1024,512]{1,0:T(8,128)(2,1)}, u32[]{:S(2)}, u32[]{:S(2)}) %collective-permute-start.8) | collective-permute-done | bytes 1048608 | tf_op jit(solution)/shard_map/ppermute | solution.py:524
  120.6 2.1 collective-permute-done.9.refs_7_
  123.2 22.6 %density.1 = (f32[8,1,512]{2,1,0:T(1,128)}, f32[32,24,128]{2,1,0:T(8,128)}) custom-call(s32[8]{0:T(128)} %fusion.10.order, bf16[1024,512]{1,0:T(8,128)(2,1)} %bitcast.82, bf16[1024,512]{1,0:T(8,128)(2,1)} %bitcast.87, bf16[1024,512]{1,0:T(8,128)(2,1)} %collective-permute-done.4.refs_2_, bf16[1024,512]{1,0:T(8,128)(2,1)} %collective-permute-done.5.refs_3_, ...), custom_call_target="tpu_custom_call" | custom-call | flops 8589934592 | bytes 33554432 | tf_op jit(solution)/shard_map/density/pallas_call | solution.py:305
  145.8 6.6 %all-to-all-start = ((f32[32,24,128]{2,1,0:T(8,128)}), f32[32,24,128]{2,1,0:T(8,128)S(1)}, u32[]{:S(2)}, u32[]{:S(2)}) async-start(f32[32,24,128]{2,1,0:T(8,128)} %get-tuple-element.24), calls=%async_computation | async-start | bytes 786432 | tf_op jit(solution)/shard_map/all_to_all | solution.py:531
  152.5 7.4 %bitcast_divide_fusion.table = f32[8,1024,512]{2,1,0:T(8,128)} fusion(f32[1024]{0:T(1024)S(1)} %div.190, f32[8,16,512]{2,1,0:T(8,128)S(1)} %bitcast.90), kind=kLoop, calls=%fused_computation | loop fusion | flops 8388608 | bytes 17043456 | tf_op jit(solution)/shard_map/div | solution.py:495
  159.9 2.7 %all-to-all-done = f32[32,24,128]{2,1,0:T(8,128)S(1)} async-done(((f32[32,24,128]{2,1,0:T(8,128)}), f32[32,24,128]{2,1,0:T(8,128)S(1)}, u32[]{:S(2)}, u32[]{:S(2)}) %all-to-all-start) | async-done | bytes 393248 | tf_op jit(solution)/shard_map/all_to_all | solution.py:531
  163.4 7.7 %potential.1 = (f32[256,64]{1,0:T(8,128)}, f32[8,1,512]{2,1,0:T(1,128)}, f32[8,1,512]{2,1,0:T(1,128)}, f32[1,128]{1,0:T(1,128)}) custom-call(f32[8,1024,512]{2,1,0:T(8,128)} %bitcast_divide_fusion.table, f32[768,128]{1,0:T(8,128)} %bitcast.89, f32[32,128]{1,0:T(8,128)} %broadcast_in_dim.78.mine, f32[8,1,512]{2,1,0:T(1,128)} %bitcast.102, ...), custom_call_target="tpu_custom_call" | custom-call | flops 16777216 | bytes 16777216 | tf_op jit(solution)/shard_map/potential/pallas_call | solution.py:333
  173.2 20.3 %ham.1 = (f32[32,128,256]{2,1,0:T(8,128)}, f32[32,128,256]{2,1,0:T(8,128)}, f32[32,128,256]{2,1,0:T(8,128)}, f32[32,128,256]{2,1,0:T(8,128)}) custom-call(s32[8]{0:T(128)} %fusion.10.order, s32[64]{0:T(128)} %fusion.7.slots, s32[1]{0:T(128)} %bitcast.3.place, bf16[4,2,128,512]{3,2,1,0:T(8,128)(2,1)} %bitcast.83, bf16[4,2,128,512]{3,2,1,0:T(8,128)(2,1)} %bitcast.88, ...), custom_call_target="tpu_custom_call" | custom-call | flops 4294967296 | bytes 25165824 | tf_op jit(solution)/shard_map/ham/pallas_call | solution.py:358
  193.6 2.9 %multiply_convert_fusion = (f16[16,128,256]{2,1,0:T(8,128)(2,1)S(1)}, f16[16,128,256]{2,1,0:T(8,128)(2,1)S(1)}) fusion(f32[32,128,256]{2,1,0:T(8,128)} %get-tuple-element.31, f32[]{:T(128)} %bitcast.31), kind=kLoop, calls=%fused_computation.6 | loop fusion | flops 2097152 | bytes 6291460 | tf_op jit(solution)/shard_map/convert_element_type | solution.py:386
  201.3 10.0 %collective-permute-done.38 = f16[2,8,128,256]{3,2,1,0:T(8,128)(2,1)S(1)} collective-permute-done((f16[2,8,128,256]{3,2,1,0:T(8,128)(2,1)S(1)}, f16[2,8,128,256]{3,2,1,0:T(8,128)(2,1)S(1)}, u32[]{:S(2)}, u32[]{:S(2)}) %collective-permute-start.38) | collective-permute-done | bytes 1048608 | tf_op jit(solution)/shard_map/ppermute | solution.py:397
  211.7 2.4 collective-permute-start.39
  214.6 2.0 collective-permute-start.35
  217.0 7.9 %collective-permute-done.37 = f16[2,8,128,256]{3,2,1,0:T(8,128)(2,1)S(1)} collective-permute-done((f16[2,8,128,256]{3,2,1,0:T(8,128)(2,1)S(1)}, f16[2,8,128,256]{3,2,1,0:T(8,128)(2,1)S(1)}, u32[]{:S(2)}, u32[]{:S(2)}) %collective-permute-start.37) | collective-permute-done | bytes 1048608 | tf_op jit(solution)/shard_map/ppermute | solution.py:398
  224.9 1.7 collective-permute-done.39
  227.4 2.2 collective-permute-start.40
  229.6 1.4 collective-permute-start.42
  231.0 18.0 %collective-permute-done.36 = f16[2,8,128,256]{3,2,1,0:T(8,128)(2,1)S(1)} collective-permute-done((f16[2,8,128,256]{3,2,1,0:T(8,128)(2,1)S(1)}, f16[2,8,128,256]{3,2,1,0:T(8,128)(2,1)S(1)}, u32[]{:S(2)}, u32[]{:S(2)}) %collective-permute-start.36) | collective-permute-done | bytes 1048608 | tf_op jit(solution)/shard_map/ppermute | solution.py:399
  250.3 9.6 %collective-permute-done.41 = f16[8,128,256]{2,1,0:T(8,128)(2,1)S(1)} collective-permute-done((f16[8,128,256]{2,1,0:T(8,128)(2,1)S(1)}, f16[8,128,256]{2,1,0:T(8,128)(2,1)S(1)}, u32[]{:S(2)}, u32[]{:S(2)}) %collective-permute-start.41) | collective-permute-done | bytes 524320 | tf_op jit(solution)/shard_map/ppermute | solution.py:409
  260.4 1.3 dynamic-slice_bitcast_fusion
  (162 shorter events, 26.3 us)
Async XLA Ops:
  1.9 1.6 collective-permute-start
  5.5 11.2 %collective-permute-start.1 = (bf16[8,128,256]{2,1,0:T(8,128)(2,1)}, bf16[8,128,256]{2,1,0:T(8,128)(2,1)}, u32[]{:S(2)}, u32[]{:S(2)}) collective-permute-start(bf16[8,128,256]{2,1,0:T(8,128)(2,1)} %pad_maximum_fusion.1), channel_id=1, source_target_pairs={{0,96},{4,28},{8,104},{12,4},{16,112},{20,12},{24,120},{28,20},{32... | collective-permute-start | bytes 1572872 | tf_op jit(solution)/shard_map/ppermute | solution.py:456
  10.4 32.1 %collective-permute-start.4 = (bf16[1024,512]{1,0:T(8,128)(2,1)S(1)}, bf16[1024,512]{1,0:T(8,128)(2,1)}, u32[]{:S(2)}, u32[]{:S(2)}) collective-permute-start(bf16[1024,512]{1,0:T(8,128)(2,1)S(1)} %bitcast.79), channel_id=1, source_target_pairs={{0,1},{1,2},{2,3},{3,0},{4,5},{5,6},{6,7},{7,4},{8,9},{9,10},{10,1... | collective-permute-start | bytes 3145736 | tf_op jit(solution)/shard_map/ppermute | solution.py:440
  12.6 86.3 %copy-start.30 = (f32[64]{0:T(128)S(1)}, f32[64]{0:T(128)}, u32[]{:S(2)}) copy-start(f32[64]{0:T(128)} %param.17) | copy-start | bytes 772
  12.6 86.5 %copy-start.24 = (f32[3,256]{1,0:T(4,128)S(1)}, f32[3,256]{1,0:T(4,128)}, u32[]{:S(2)}) copy-start(f32[3,256]{1,0:T(4,128)} %param.18) | copy-start | bytes 9220
  12.7 31.1 %collective-permute-start.7 = (bf16[1024,512]{1,0:T(8,128)(2,1)S(1)}, bf16[1024,512]{1,0:T(8,128)(2,1)}, u32[]{:S(2)}, u32[]{:S(2)}) collective-permute-start(bf16[1024,512]{1,0:T(8,128)(2,1)S(1)} %bitcast.84), channel_id=1, source_target_pairs={{0,3},{1,0},{2,1},{3,2},{4,7},{5,4},{6,5},{7,6},{8,11},{9,8},{10,9... | collective-permute-start | bytes 3145736 | tf_op jit(solution)/shard_map/ppermute | solution.py:441
  17.9 89.8 %copy-start.2 = (bf16[16,128,256]{2,1,0:T(8,128)(2,1)}, bf16[16,128,256]{2,1,0:T(8,128)(2,1)S(1)}, u32[]{:S(2)}) copy-start(bf16[16,128,256]{2,1,0:T(8,128)(2,1)S(1)} %pad_maximum_fusion.refs_0_) | copy-start | bytes 3145732
  17.9 28.1 %collective-permute-start.2 = (bf16[16,128,256]{2,1,0:T(8,128)(2,1)S(1)}, bf16[16,128,256]{2,1,0:T(8,128)(2,1)}, u32[]{:S(2)}, u32[]{:S(2)}) collective-permute-start(bf16[16,128,256]{2,1,0:T(8,128)(2,1)S(1)} %pad_maximum_fusion.refs_0_), channel_id=1, source_target_pairs={{0,24},{4,100},{8,0},{12,108},{16,8},{20,116},{24,16},{28,124},{32... | collective-permute-start | bytes 3145736 | tf_op jit(solution)/shard_map/ppermute | solution.py:510
  20.7 11.1 %collective-permute-start.18 = (bf16[8,128,256]{2,1,0:T(8,128)(2,1)}, bf16[8,128,256]{2,1,0:T(8,128)(2,1)}, u32[]{:S(2)}, u32[]{:S(2)}) collective-permute-start(bf16[8,128,256]{2,1,0:T(8,128)(2,1)} %pad_maximum_fusion.1), channel_id=1, source_target_pairs={{0,64},{4,20},{8,72},{12,28},{16,80},{20,4},{24,88},{28,12},{32,96... | collective-permute-start | bytes 1572872 | tf_op jit(solution)/shard_map/ppermute | solution.py:456
  23.0 14.3 %collective-permute-start.19 = (bf16[8,128,256]{2,1,0:T(8,128)(2,1)}, bf16[8,128,256]{2,1,0:T(8,128)(2,1)}, u32[]{:S(2)}, u32[]{:S(2)}) collective-permute-start(bf16[8,128,256]{2,1,0:T(8,128)(2,1)} %pad_maximum_fusion.1), channel_id=1, source_target_pairs={{0,32},{4,12},{8,40},{12,20},{16,48},{20,28},{24,56},{28,4},{32,64... | collective-permute-start | bytes 1572872 | tf_op jit(solution)/shard_map/ppermute | solution.py:456
  31.8 9.0 %collective-permute-start.3 = (s32[32]{0:T(128)S(1)}, s32[32]{0:T(128)S(1)}, u32[]{:S(2)}, u32[]{:S(2)}) collective-permute-start(s32[32]{0:T(128)S(1)} %select_reduce_fusion.2), channel_id=1, source_target_pairs={{0,4},{4,0},{8,12},{12,8},{16,20},{20,16},{24,28},{28,24},{32,36},... | collective-permute-start | bytes 392 | tf_op jit(solution)/shard_map/ppermute | solution.py:461
  37.3 24.6 %collective-permute-start.5 = (bf16[1024,512]{1,0:T(8,128)(2,1)S(1)}, bf16[1024,512]{1,0:T(8,128)(2,1)}, u32[]{:S(2)}, u32[]{:S(2)}) collective-permute-start(bf16[1024,512]{1,0:T(8,128)(2,1)S(1)} %bitcast.85), channel_id=1, source_target_pairs={{0,1},{1,2},{2,3},{3,0},{4,5},{5,6},{6,7},{7,4},{8,9},{9,10},{10,1... | collective-permute-start | bytes 3145736 | tf_op jit(solution)/shard_map/ppermute | solution.py:442
  40.8 24.3 %collective-permute-start.6 = (bf16[1024,512]{1,0:T(8,128)(2,1)S(1)}, bf16[1024,512]{1,0:T(8,128)(2,1)}, u32[]{:S(2)}, u32[]{:S(2)}) collective-permute-start(bf16[1024,512]{1,0:T(8,128)(2,1)S(1)} %bitcast.80), channel_id=1, source_target_pairs={{0,3},{1,0},{2,1},{3,2},{4,7},{5,4},{6,5},{7,6},{8,11},{9,8},{10,9... | collective-permute-start | bytes 3145736 | tf_op jit(solution)/shard_map/ppermute | solution.py:443
  42.5 24.2 %collective-permute-start.22 = (bf16[16,128,256]{2,1,0:T(8,128)(2,1)}, bf16[16,128,256]{2,1,0:T(8,128)(2,1)}, u32[]{:S(2)}, u32[]{:S(2)}) collective-permute-start(bf16[16,128,256]{2,1,0:T(8,128)(2,1)} %constant_dynamic-update-slice_fusion.refs_1_), channel_id=1, source_target_pairs={{0,8},{4,36},{8,16},{12,44},{16,24},{20,52},{24,0},{28,60},{32,40}... | collective-permute-start | bytes 3145736 | tf_op jit(solution)/shard_map/ppermute | solution.py:511
  43.7 23.2 %collective-permute-start.20 = (bf16[16,128,256]{2,1,0:T(8,128)(2,1)}, bf16[16,128,256]{2,1,0:T(8,128)(2,1)}, u32[]{:S(2)}, u32[]{:S(2)}) collective-permute-start(bf16[16,128,256]{2,1,0:T(8,128)(2,1)} %constant_dynamic-update-slice_fusion.refs_1_), channel_id=1, source_target_pairs={{0,24},{4,100},{8,0},{12,108},{16,8},{20,116},{24,16},{28,124},{32... | collective-permute-start | bytes 3145736 | tf_op jit(solution)/shard_map/ppermute | solution.py:513
  46.0 23.4 %collective-permute-start.26 = (bf16[16,128,256]{2,1,0:T(8,128)(2,1)}, bf16[16,128,256]{2,1,0:T(8,128)(2,1)}, u32[]{:S(2)}, u32[]{:S(2)}) collective-permute-start(bf16[16,128,256]{2,1,0:T(8,128)(2,1)} %constant_dynamic-update-slice_fusion.refs_1_), channel_id=1, source_target_pairs={{0,4},{4,0},{8,12},{12,8},{16,20},{20,16},{24,28},{28,24},{32,36},... | collective-permute-start | bytes 3145736 | tf_op jit(solution)/shard_map/ppermute | solution.py:522
  61.9 18.1 %collective-permute-start.24 = (bf16[16,128,256]{2,1,0:T(8,128)(2,1)S(1)}, bf16[16,128,256]{2,1,0:T(8,128)(2,1)S(1)}, u32[]{:S(2)}, u32[]{:S(2)}) collective-permute-start(bf16[16,128,256]{2,1,0:T(8,128)(2,1)S(1)} %pad_maximum_fusion.refs_0_), channel_id=1, source_target_pairs={{0,8},{4,36},{8,16},{12,44},{16,24},{20,52},{24,0},{28,60},{32,40}... | collective-permute-start | bytes 3145736 | tf_op jit(solution)/shard_map/ppermute | solution.py:512
  65.1 14.9 %collective-permute-start.25 = (bf16[16,128,256]{2,1,0:T(8,128)(2,1)S(1)}, bf16[16,128,256]{2,1,0:T(8,128)(2,1)S(1)}, u32[]{:S(2)}, u32[]{:S(2)}) collective-permute-start(bf16[16,128,256]{2,1,0:T(8,128)(2,1)S(1)} %pad_maximum_fusion.refs_0_), channel_id=1, source_target_pairs={{0,4},{4,0},{8,12},{12,8},{16,20},{20,16},{24,28},{28,24},{32,36},... | collective-permute-start | bytes 3145736 | tf_op jit(solution)/shard_map/ppermute | solution.py:522
  66.6 24.6 %collective-permute-start.23 = (bf16[16,128,256]{2,1,0:T(8,128)(2,1)}, bf16[16,128,256]{2,1,0:T(8,128)(2,1)S(1)}, u32[]{:S(2)}, u32[]{:S(2)}) collective-permute-start(bf16[16,128,256]{2,1,0:T(8,128)(2,1)} %collective-permute-done.22.refs_7_), channel_id=1, source_target_pairs={{0,8},{4,36},{8,16},{12,44},{16,24},{20,52},{24,0},{28,60},{32,40}... | collective-permute-start | bytes 3145736 | tf_op jit(solution)/shard_map/ppermute | solution.py:518
  67.0 24.3 %collective-permute-start.28 = (bf16[16,128,256]{2,1,0:T(8,128)(2,1)}, bf16[16,128,256]{2,1,0:T(8,128)(2,1)S(1)}, u32[]{:S(2)}, u32[]{:S(2)}) collective-permute-start(bf16[16,128,256]{2,1,0:T(8,128)(2,1)} %collective-permute-done.20.refs_3_), channel_id=1, source_target_pairs={{0,4},{4,0},{8,12},{12,8},{16,20},{20,16},{24,28},{28,24},{32,36},... | collective-permute-start | bytes 3145736 | tf_op jit(solution)/shard_map/ppermute | solution.py:522
  69.3 22.4 %collective-permute-start.21 = (bf16[16,128,256]{2,1,0:T(8,128)(2,1)}, bf16[16,128,256]{2,1,0:T(8,128)(2,1)S(1)}, u32[]{:S(2)}, u32[]{:S(2)}) collective-permute-start(bf16[16,128,256]{2,1,0:T(8,128)(2,1)} %collective-permute-done.2.refs_2_), channel_id=1, source_target_pairs={{0,24},{4,100},{8,0},{12,108},{16,8},{20,116},{24,16},{28,124},{32... | collective-permute-start | bytes 3145736 | tf_op jit(solution)/shard_map/ppermute | solution.py:517
  80.0 11.9 %collective-permute-start.32 = (bf16[16,128,256]{2,1,0:T(8,128)(2,1)}, bf16[16,128,256]{2,1,0:T(8,128)(2,1)S(1)}, u32[]{:S(2)}, u32[]{:S(2)}) collective-permute-start(bf16[16,128,256]{2,1,0:T(8,128)(2,1)} %collective-permute-done.22.refs_7_), channel_id=1, source_target_pairs={{0,4},{4,0},{8,12},{12,8},{16,20},{20,16},{24,28},{28,24},{32,36},... | collective-permute-start | bytes 3145736 | tf_op jit(solution)/shard_map/ppermute | solution.py:522
  80.0 12.3 %collective-permute-start.27 = (bf16[16,128,256]{2,1,0:T(8,128)(2,1)}, bf16[16,128,256]{2,1,0:T(8,128)(2,1)S(1)}, u32[]{:S(2)}, u32[]{:S(2)}) collective-permute-start(bf16[16,128,256]{2,1,0:T(8,128)(2,1)} %collective-permute-done.2.refs_2_), channel_id=1, source_target_pairs={{0,4},{4,0},{8,12},{12,8},{16,20},{20,16},{24,28},{28,24},{32,36},... | collective-permute-start | bytes 3145736 | tf_op jit(solution)/shard_map/ppermute | solution.py:522
  91.2 2.7 %collective-permute-start.31 = (bf16[16,128,256]{2,1,0:T(8,128)(2,1)S(1)}, bf16[16,128,256]{2,1,0:T(8,128)(2,1)S(1)}, u32[]{:S(2)}, u32[]{:S(2)}) collective-permute-start(bf16[16,128,256]{2,1,0:T(8,128)(2,1)S(1)} %collective-permute-done.24.refs_6_), channel_id=1, source_target_pairs={{0,4},{4,0},{8,12},{12,8},{16,20},{20,16},{24,28},{28,24},{32,36},... | collective-permute-start | bytes 3145736 | tf_op jit(solution)/shard_map/ppermute | solution.py:522
  91.2 4.1 %collective-permute-start.30 = (bf16[16,128,256]{2,1,0:T(8,128)(2,1)S(1)}, bf16[16,128,256]{2,1,0:T(8,128)(2,1)S(1)}, u32[]{:S(2)}, u32[]{:S(2)}) collective-permute-start(bf16[16,128,256]{2,1,0:T(8,128)(2,1)S(1)} %collective-permute-done.23.refs_5_), channel_id=1, source_target_pairs={{0,4},{4,0},{8,12},{12,8},{16,20},{20,16},{24,28},{28,24},{32,36},... | collective-permute-start | bytes 3145736 | tf_op jit(solution)/shard_map/ppermute | solution.py:522
  91.7 5.1 %collective-permute-start.29 = (bf16[16,128,256]{2,1,0:T(8,128)(2,1)S(1)}, bf16[16,128,256]{2,1,0:T(8,128)(2,1)S(1)}, u32[]{:S(2)}, u32[]{:S(2)}) collective-permute-start(bf16[16,128,256]{2,1,0:T(8,128)(2,1)S(1)} %collective-permute-done.21.refs_4_), channel_id=1, source_target_pairs={{0,4},{4,0},{8,12},{12,8},{16,20},{20,16},{24,28},{28,24},{32,36},... | collective-permute-start | bytes 3145736 | tf_op jit(solution)/shard_map/ppermute | solution.py:522
  91.9 25.1 %collective-permute-start.10 = (bf16[1024,512]{1,0:T(8,128)(2,1)S(1)}, bf16[1024,512]{1,0:T(8,128)(2,1)}, u32[]{:S(2)}, u32[]{:S(2)}) collective-permute-start(bf16[1024,512]{1,0:T(8,128)(2,1)S(1)} %bitcast.81), channel_id=1, source_target_pairs={{0,4},{4,0},{8,12},{12,8},{16,20},{20,16},{24,28},{28,24},{32,36},... | collective-permute-start | bytes 3145736 | tf_op jit(solution)/shard_map/ppermute | solution.py:527
  92.4 24.7 %collective-permute-start.11 = (bf16[1024,512]{1,0:T(8,128)(2,1)S(1)}, bf16[1024,512]{1,0:T(8,128)(2,1)}, u32[]{:S(2)}, u32[]{:S(2)}) collective-permute-start(bf16[1024,512]{1,0:T(8,128)(2,1)S(1)} %bitcast.86), channel_id=1, source_target_pairs={{0,4},{4,0},{8,12},{12,8},{16,20},{20,16},{24,28},{28,24},{32,36},... | collective-permute-start | bytes 3145736 | tf_op jit(solution)/shard_map/ppermute | solution.py:527
  93.9 26.7 %collective-permute-start.8 = (bf16[1024,512]{1,0:T(8,128)(2,1)}, bf16[1024,512]{1,0:T(8,128)(2,1)}, u32[]{:S(2)}, u32[]{:S(2)}) collective-permute-start(bf16[1024,512]{1,0:T(8,128)(2,1)} %collective-permute-done.4.refs_2_), channel_id=1, source_target_pairs={{0,1},{1,2},{2,3},{3,0},{4,5},{5,6},{6,7},{7,4},{8,9},{9,10},{10,1... | collective-permute-start | bytes 3145736 | tf_op jit(solution)/shard_map/ppermute | solution.py:524
  95.4 27.3 %collective-permute-start.12 = (bf16[1024,512]{1,0:T(8,128)(2,1)}, bf16[1024,512]{1,0:T(8,128)(2,1)}, u32[]{:S(2)}, u32[]{:S(2)}) collective-permute-start(bf16[1024,512]{1,0:T(8,128)(2,1)} %collective-permute-done.4.refs_2_), channel_id=1, source_target_pairs={{0,4},{4,0},{8,12},{12,8},{16,20},{20,16},{24,28},{28,24},{32,36},... | collective-permute-start | bytes 3145736 | tf_op jit(solution)/shard_map/ppermute | solution.py:527
  96.9 25.8 %collective-permute-start.9 = (bf16[1024,512]{1,0:T(8,128)(2,1)}, bf16[1024,512]{1,0:T(8,128)(2,1)}, u32[]{:S(2)}, u32[]{:S(2)}) collective-permute-start(bf16[1024,512]{1,0:T(8,128)(2,1)} %collective-permute-done.7.refs_5_), channel_id=1, source_target_pairs={{0,3},{1,0},{2,1},{3,2},{4,7},{5,4},{6,5},{7,6},{8,11},{9,8},{10,9... | collective-permute-start | bytes 3145736 | tf_op jit(solution)/shard_map/ppermute | solution.py:525
  116.9 54.2 %collective-permute-start.15 = (bf16[1024,512]{1,0:T(8,128)(2,1)}, bf16[1024,512]{1,0:T(8,128)(2,1)S(1)}, u32[]{:S(2)}, u32[]{:S(2)}) collective-permute-start(bf16[1024,512]{1,0:T(8,128)(2,1)} %collective-permute-done.7.refs_5_), channel_id=1, source_target_pairs={{0,4},{4,0},{8,12},{12,8},{16,20},{20,16},{24,28},{28,24},{32,36},... | collective-permute-start | bytes 3145736 | tf_op jit(solution)/shard_map/ppermute | solution.py:527
  117.0 55.2 %collective-permute-start.13 = (bf16[1024,512]{1,0:T(8,128)(2,1)}, bf16[1024,512]{1,0:T(8,128)(2,1)S(1)}, u32[]{:S(2)}, u32[]{:S(2)}) collective-permute-start(bf16[1024,512]{1,0:T(8,128)(2,1)} %collective-permute-done.5.refs_3_), channel_id=1, source_target_pairs={{0,4},{4,0},{8,12},{12,8},{16,20},{20,16},{24,28},{28,24},{32,36},... | collective-permute-start | bytes 3145736 | tf_op jit(solution)/shard_map/ppermute | solution.py:527
  120.6 51.6 %collective-permute-start.14 = (bf16[1024,512]{1,0:T(8,128)(2,1)}, bf16[1024,512]{1,0:T(8,128)(2,1)}, u32[]{:S(2)}, u32[]{:S(2)}) collective-permute-start(bf16[1024,512]{1,0:T(8,128)(2,1)} %collective-permute-done.6.refs_4_), channel_id=1, source_target_pairs={{0,4},{4,0},{8,12},{12,8},{16,20},{20,16},{24,28},{28,24},{32,36},... | collective-permute-start | bytes 3145736 | tf_op jit(solution)/shard_map/ppermute | solution.py:527
  122.7 49.6 %collective-permute-start.16 = (bf16[1024,512]{1,0:T(8,128)(2,1)}, bf16[1024,512]{1,0:T(8,128)(2,1)}, u32[]{:S(2)}, u32[]{:S(2)}) collective-permute-start(bf16[1024,512]{1,0:T(8,128)(2,1)} %collective-permute-done.8.refs_6_), channel_id=1, source_target_pairs={{0,4},{4,0},{8,12},{12,8},{16,20},{20,16},{24,28},{28,24},{32,36},... | collective-permute-start | bytes 3145736 | tf_op jit(solution)/shard_map/ppermute | solution.py:527
  122.7 49.6 %collective-permute-start.17 = (bf16[1024,512]{1,0:T(8,128)(2,1)}, bf16[1024,512]{1,0:T(8,128)(2,1)}, u32[]{:S(2)}, u32[]{:S(2)}) collective-permute-start(bf16[1024,512]{1,0:T(8,128)(2,1)} %collective-permute-done.9.refs_7_), channel_id=1, source_target_pairs={{0,4},{4,0},{8,12},{12,8},{16,20},{20,16},{24,28},{28,24},{32,36},... | collective-permute-start | bytes 3145736 | tf_op jit(solution)/shard_map/ppermute | solution.py:527
  145.8 16.8 %all-to-all-start = ((f32[32,24,128]{2,1,0:T(8,128)}), f32[32,24,128]{2,1,0:T(8,128)S(1)}, u32[]{:S(2)}, u32[]{:S(2)}) async-start(f32[32,24,128]{2,1,0:T(8,128)} %get-tuple-element.24), calls=%async_computation | async-start | bytes 786432 | tf_op jit(solution)/shard_map/all_to_all | solution.py:531
  171.2 1.5 collective-permute-start.33
  196.5 14.9 %collective-permute-start.38 = (f16[2,8,128,256]{3,2,1,0:T(8,128)(2,1)S(1)}, f16[2,8,128,256]{3,2,1,0:T(8,128)(2,1)S(1)}, u32[]{:S(2)}, u32[]{:S(2)}) collective-permute-start(f16[2,8,128,256]{3,2,1,0:T(8,128)(2,1)S(1)} %bitcast.95), channel_id=1, source_target_pairs={{0,96},{4,28},{8,104},{12,4},{16,112},{20,12},{24,120},{28,20},{32... | collective-permute-start | bytes 3145736 | tf_op jit(solution)/shard_map/ppermute | solution.py:397
  197.7 16.5 %collective-permute-start.34 = (f16[2,8,128,256]{3,2,1,0:T(8,128)(2,1)S(1)}, f16[2,8,128,256]{3,2,1,0:T(8,128)(2,1)S(1)}, u32[]{:S(2)}, u32[]{:S(2)}) collective-permute-start(f16[2,8,128,256]{3,2,1,0:T(8,128)(2,1)S(1)} %bitcast.94), channel_id=1, source_target_pairs={{0,32},{4,12},{8,40},{12,20},{16,48},{20,28},{24,56},{28,4},{32,64... | collective-permute-start | bytes 3145736 | tf_op jit(solution)/shard_map/ppermute | solution.py:396
  199.1 25.8 %collective-permute-start.37 = (f16[2,8,128,256]{3,2,1,0:T(8,128)(2,1)S(1)}, f16[2,8,128,256]{3,2,1,0:T(8,128)(2,1)S(1)}, u32[]{:S(2)}, u32[]{:S(2)}) collective-permute-start(f16[2,8,128,256]{3,2,1,0:T(8,128)(2,1)S(1)} %bitcast.97), channel_id=1, source_target_pairs={{0,32},{4,12},{8,40},{12,20},{16,48},{20,28},{24,56},{28,4},{32,64... | collective-permute-start | bytes 3145736 | tf_op jit(solution)/shard_map/ppermute | solution.py:398
  211.7 14.9 %collective-permute-start.39 = (f16[2,8,128,256]{3,2,1,0:T(8,128)(2,1)S(1)}, f16[2,8,128,256]{3,2,1,0:T(8,128)(2,1)S(1)}, u32[]{:S(2)}, u32[]{:S(2)}) collective-permute-start(f16[2,8,128,256]{3,2,1,0:T(8,128)(2,1)S(1)} %add_convert_fusion.1), channel_id=1, source_target_pairs={{0,96},{4,28},{8,104},{12,4},{16,112},{20,12},{24,120},{28,20},{32... | collective-permute-start | bytes 3145736 | tf_op jit(solution)/shard_map/ppermute | solution.py:401
  214.1 34.8 %collective-permute-start.36 = (f16[2,8,128,256]{3,2,1,0:T(8,128)(2,1)S(1)}, f16[2,8,128,256]{3,2,1,0:T(8,128)(2,1)S(1)}, u32[]{:S(2)}, u32[]{:S(2)}) collective-permute-start(f16[2,8,128,256]{3,2,1,0:T(8,128)(2,1)S(1)} %bitcast.96), channel_id=1, source_target_pairs={{0,96},{4,28},{8,104},{12,4},{16,112},{20,12},{24,120},{28,20},{32... | collective-permute-start | bytes 3145736 | tf_op jit(solution)/shard_map/ppermute | solution.py:399
  214.6 34.3 %collective-permute-start.35 = (f16[2,8,128,256]{3,2,1,0:T(8,128)(2,1)S(1)}, f16[2,8,128,256]{3,2,1,0:T(8,128)(2,1)S(1)}, u32[]{:S(2)}, u32[]{:S(2)}) collective-permute-start(f16[2,8,128,256]{3,2,1,0:T(8,128)(2,1)S(1)} %add_convert_fusion.2), channel_id=1, source_target_pairs={{0,32},{4,12},{8,40},{12,20},{16,48},{20,28},{24,56},{28,4},{32,64... | collective-permute-start | bytes 3145736 | tf_op jit(solution)/shard_map/ppermute | solution.py:400
  227.4 22.9 %collective-permute-start.40 = (f16[8,128,256]{2,1,0:T(8,128)(2,1)S(1)}, f16[8,128,256]{2,1,0:T(8,128)(2,1)S(1)}, u32[]{:S(2)}, u32[]{:S(2)}) collective-permute-start(f16[8,128,256]{2,1,0:T(8,128)(2,1)S(1)} %get-tuple-element.54), channel_id=1, source_target_pairs={{0,16},{4,68},{8,24},{12,76},{16,0},{20,84},{24,8},{28,92},{32,48}... | collective-permute-start | bytes 1572872 | tf_op jit(solution)/shard_map/ppermute | solution.py:409
  229.6 20.7 %collective-permute-start.42 = (f16[8,128,256]{2,1,0:T(8,128)(2,1)S(1)}, f16[8,128,256]{2,1,0:T(8,128)(2,1)S(1)}, u32[]{:S(2)}, u32[]{:S(2)}) collective-permute-start(f16[8,128,256]{2,1,0:T(8,128)(2,1)S(1)} %get-tuple-element.55), channel_id=1, source_target_pairs={{0,24},{4,100},{8,0},{12,108},{16,8},{20,116},{24,16},{28,124},{32... | collective-permute-start | bytes 1572872 | tf_op jit(solution)/shard_map/ppermute | solution.py:409
  249.4 10.5 %collective-permute-start.41 = (f16[8,128,256]{2,1,0:T(8,128)(2,1)S(1)}, f16[8,128,256]{2,1,0:T(8,128)(2,1)S(1)}, u32[]{:S(2)}, u32[]{:S(2)}) collective-permute-start(f16[8,128,256]{2,1,0:T(8,128)(2,1)S(1)} %fusion.6), channel_id=1, source_target_pairs={{0,8},{4,36},{8,16},{12,44},{16,24},{20,52},{24,0},{28,60},{32,40}... | collective-permute-start | bytes 1572872 | tf_op jit(solution)/shard_map/ppermute | solution.py:409
  260.3 1.6 collective-permute-start.43
  (28 other events, 434.0 us)

commit v10 on v9

--- a/solution.py
+++ b/solution.py
@@ -119,15 +119,10 @@
     return lax.fori_loop(0, CHUNKS, step, top)
 
 
-def assemble_body(place, which, where, *refs):
-    *sources, dmat, sem = refs
-    fetch_tiles(place[0], which, where, sources, dmat, sem)
-    pltpu.make_async_copy(dmat, dmat, sem).wait()
-
-
-def density_body(order, *refs):
+def density_body(order, place, which, where, *refs):
     chunks = refs[:CHUNKS]
-    table, dmat_in, weights, xc, home_rows, rho, sent, *rest = refs[CHUNKS:]
+    sources = refs[CHUNKS : CHUNKS + 2 * SOURCES]
+    table, weights, xc, home_rows, rho, sent, *rest = refs[CHUNKS + 2 * SOURCES :]
     pacc, dmat, block_out, sem, *bufs = rest
     held, tbuf, psem, tsem = bufs
 
@@ -135,8 +130,9 @@
         pltpu.make_async_copy(chunks[i], held.at[i], psem.at[i]).start()
         pltpu.make_async_copy(table.at[order[i]], tbuf.at[i], tsem.at[i]).start()
 
-    pltpu.make_async_copy(dmat_in, dmat, sem).start()
-    for i in range(CHUNKS):
+    load(0)
+    fetch_tiles(place[0], which, where, sources, dmat, sem)
+    for i in range(1, CHUNKS):
         load(i)
     pacc[...] = jnp.zeros_like(pacc)
     block_out[...] = jnp.zeros_like(block_out)
@@ -286,21 +282,7 @@
     return pl.BlockSpec(memory_space=pltpu.SMEM)
 
 
-def assemble_call(place, which, where, sources):
-    nbasis = NB * BLK
-    return pl.pallas_call(
-        assemble_body,
-        out_shape=jax.ShapeDtypeStruct((2, nbasis, nbasis), jnp.bfloat16),
-        in_specs=[smem_spec()] * 3 + [any_spec()] * (2 * SOURCES),
-        out_specs=vmem_spec(),
-        scratch_shapes=[pltpu.SemaphoreType.DMA],
-        compiler_params=pltpu.CompilerParams(vmem_limit_bytes=VMEM_GRANT),
-        cost_estimate=pl.CostEstimate(flops=0, bytes_accessed=8 << 20, transcendentals=0),
-        name="assemble",
-    )(place, which, where, *sources)
-
-
-def density_call(order, chunks, table, dmat, weights, xc, home_rows):
+def density_call(order, place, which, where, chunks, sources, table, weights, xc, home_rows):
     nbasis = NB * BLK
     return pl.pallas_call(
         density_body,
@@ -308,7 +290,9 @@
             jax.ShapeDtypeStruct((PIECES, 1, HALF), jnp.float32),
             jax.ShapeDtypeStruct((32, PAY_ROWS, 128), jnp.float32),
         ),
-        in_specs=[smem_spec()] + [any_spec()] * (CHUNKS + 2) + [vmem_spec()] * 3,
+        in_specs=[smem_spec()] * 4
+        + [any_spec()] * (CHUNKS + 2 * SOURCES + 1)
+        + [vmem_spec()] * 3,
         out_specs=(vmem_spec(),) * 2,
         scratch_shapes=[
             pltpu.VMEM((2, nbasis, 128), jnp.float32),
@@ -325,7 +309,7 @@
             flops=2 * 4096 * 1024 * 1024, bytes_accessed=32 << 20, transcendentals=0
         ),
         name="density",
-    )(order, *chunks, table, dmat, weights, xc, home_rows)
+    )(order, place, which, where, *chunks, *sources, table, weights, xc, home_rows)
 
 
 def potential_call(table, got, mine, weights, xc, rho, natoms):
@@ -492,9 +476,6 @@
     erf_scale = (ROOT_TWO * gauss_widths)[None, None, :, None]
     gauss = jnp.exp(-dist_sq / spread).reshape(PIECES, neighbors * moments, HALF)
     distance = jnp.sqrt(dist_sq)
-    hart = (lax.erf(distance / erf_scale) / distance).reshape(
-        PIECES, neighbors * moments, HALF
-    )
     weights = point_weights.reshape(PIECES, 1, HALF)
     xc = xc_kernel.reshape(PIECES, 1, HALF)
 
@@ -524,10 +505,15 @@
     far0 = lax.ppermute(below0, "pert", ring(1))
     far1 = lax.ppermute(above1, "pert", ring(3))
     chunks = [own0, own1, below0, below1, above0, above1, far0, far1]
-    beside = [lax.ppermute(chunk, "grid", swap) for chunk in chunks]
-
-    dmat = assemble_call(core_place, which, where, sources)
-    rho, sent = density_call(order, chunks, gauss, dmat, weights, xc, home_rows)
+
+    rho, sent = density_call(
+        order, core_place, which, where, chunks, sources, gauss, weights, xc, home_rows
+    )
+    distance, sent, later = lax.optimization_barrier((distance, sent, chunks))
+    beside = [lax.ppermute(chunk, "grid", swap) for chunk in later]
+    hart = (lax.erf(distance / erf_scale) / distance).reshape(
+        PIECES, neighbors * moments, HALF
+    )
     got = lax.all_to_all(sent, "grid", split_axis=0, concat_axis=0, tiled=True)
     all_coeffs, pot, scale, bound = potential_call(
         hart, got.reshape(groups * PAY_ROWS, 128), my_homes, weights, xc, rho, natoms

time: 265 us -> 265 us (level)
  waiting for transfers between devices: 106 us -> 119 us
  Pallas kernels: 59.3 us -> 48.2 us
  starting transfers between devices: 54.6 us -> 47.8 us
  local copies, waits for them, and re-layouts: 10.1 us -> 13.2 us
  other arithmetic: 31 us -> 33.8 us
    pallas_call x1 -> x0, Pallas kernels: 8.64 us -> none  [assemble_call(): pl.pallas_call(assemble_body, out_shape=jax.ShapeDtypeStruct((2, nbasis,...]
    ppermute x1, waiting for transfers between devices: 10.7 us -> 2.76 us  [one_device(): other_far = lax.ppermute(other_behind, 'grid', forth)]
    ppermute x1, waiting for transfers between devices: 12.9 us -> 19.4 us  [one_device(): below1 = lax.ppermute(own1, 'pert', ring(1))]
    ppermute x1, waiting for transfers between devices: 3.1 us -> 9.37 us  [one_device(): far0 = lax.ppermute(below0, 'pert', ring(1))]
    ppermute x1, waiting for transfers between devices: 0.01 us -> 6.19 us  [one_device(): above1 = lax.ppermute(own1, 'pert', ring(3))]
    ppermute x3, waiting for transfers between devices: 12.2 us -> 6.16 us  [one_device(): lax.ppermute(base, 'grid', core_perm(-d, False))]
    ppermute x8, waiting for transfers between devices: 0.02 us -> 5.98 us  [one_device(): beside = [lax.ppermute(chunk, 'grid', swap) for chunk in later]]
    ppermute x1, waiting for transfers between devices: 18 us -> 13.2 us  [ring_sum(): above_low = lax.ppermute(cast(parts[3][:half] * factor), 'grid', down)]
  transfers between devices with their start and end apart: 45 -> 45, of which waited for: 20 -> 25; matrix products, arithmetic and copies ran while one was open for 12% -> 14% of each run, Pallas kernels for 15% -> 3%
where the time goes in v10:
time: 265 us; the launch traced here: 264 us
  waiting for transfers between devices  119 us (45%)
  Pallas kernels  48.2 us (18%)
  starting transfers between devices  47.8 us (18%)
  other arithmetic  33.8 us (13%)
  local copies, waits for them, and re-layouts  13.2 us (5%)
    pallas_call x1, Pallas kernels, ham_call(): pl.pallas_call(ham_body, out_shape=(jax.ShapeDtypeStruct((32, 128, BLK),...  20.3 us
    pallas_call x1, Pallas kernels, density_call(): pl.pallas_call(density_body, out_shape=(jax.ShapeDtypeStruct((PIECES, 1,...  20.1 us
    ppermute x1, waiting for transfers between devices, one_device(): below1 = lax.ppermute(own1, 'pert', ring(1))  19.4 us
    ppermute x1, waiting for transfers between devices, ring_sum(): above_low = lax.ppermute(cast(parts[3][:half] * factor), 'grid', down)  13.2 us
    ppermute x3, waiting for transfers between devices, direct_sum(): lax.ppermute(cast(parts[d]), 'grid', core_perm(d, True))  12.8 us
    ppermute x1, waiting for transfers between devices, ring_sum(): from_above = lax.ppermute(cast(parts[2][half:] * factor), 'grid', down)  10 us
    ppermute x1, waiting for transfers between devices, one_device(): near_behind = lax.ppermute(near, 'grid', forth)  9.49 us
    ppermute x1, waiting for transfers between devices, one_device(): far0 = lax.ppermute(below0, 'pert', ring(1))  9.37 us
  transfers between devices with their start and end apart: 45, of which 25 were waited for; matrix products, arithmetic and copies ran while one was open for 14% of the time, Pallas kernels for 3%

profile of v10, /device:TPU:0, one launch (start us, length us, event | category | flops | bytes accessed | tf_op | source)
XLA Modules:
  0.0 263.7 jit_solution(13395407450672457023)
XLA Ops:
  2.0 1.5 collective-permute-done
  6.2 4.1 %collective-permute-start.1 = (bf16[8,128,256]{2,1,0:T(8,128)(2,1)}, bf16[8,128,256]{2,1,0:T(8,128)(2,1)}, u32[]{:S(2)}, u32[]{:S(2)}) collective-permute-start(bf16[8,128,256]{2,1,0:T(8,128)(2,1)} %pad_maximum_fusion.1), channel_id=1, source_target_pairs={{0,96},{4,28},{8,104},{12,4},{16,112},{20,12},{24,120},{28,20},{32... | collective-permute-start | bytes 1572872 | tf_op jit(solution)/shard_map/ppermute | solution.py:440
  13.6 1.6 collective-permute-start.4
  15.3 1.5 copy.26
  16.8 6.2 %collective-permute-done.1 = bf16[8,128,256]{2,1,0:T(8,128)(2,1)} collective-permute-done((bf16[8,128,256]{2,1,0:T(8,128)(2,1)}, bf16[8,128,256]{2,1,0:T(8,128)(2,1)}, u32[]{:S(2)}, u32[]{:S(2)}) %collective-permute-start.1) | collective-permute-done | bytes 524320 | tf_op jit(solution)/shard_map/ppermute | solution.py:440
  23.0 1.6 collective-permute-start.5
  24.6 2.3 pad_maximum_fusion.refs_8_
  26.9 1.7 collective-permute-start.6
  28.6 1.8 collective-permute-start.7
  30.4 2.8 %collective-permute-start.2 = (bf16[16,128,256]{2,1,0:T(8,128)(2,1)}, bf16[16,128,256]{2,1,0:T(8,128)(2,1)}, u32[]{:S(2)}, u32[]{:S(2)}) collective-permute-start(bf16[16,128,256]{2,1,0:T(8,128)(2,1)} %pad_maximum_fusion.refs_8_), channel_id=1, source_target_pairs={{0,24},{4,100},{8,0},{12,108},{16,8},{20,116},{24,16},{28,124},{32... | collective-permute-start | bytes 3145736 | tf_op jit(solution)/shard_map/ppermute | solution.py:491
  33.2 1.9 constant_dynamic-update-slice_fusion.1
  35.0 1.9 constant_dynamic-update-slice_fusion.refs_9_
  36.9 4.0 %collective-permute-done.4.refs_2_ = bf16[1024,512]{1,0:T(8,128)(2,1)S(1)} collective-permute-done((bf16[1024,512]{1,0:T(8,128)(2,1)S(1)}, bf16[1024,512]{1,0:T(8,128)(2,1)S(1)}, u32[]{:S(2)}, u32[]{:S(2)}) %collective-permute-start.4) | collective-permute-done | bytes 1048608 | tf_op jit(solution)/shard_map/ppermute | solution.py:424
  40.9 2.8 %collective-permute-start.12 = (bf16[16,128,256]{2,1,0:T(8,128)(2,1)}, bf16[16,128,256]{2,1,0:T(8,128)(2,1)}, u32[]{:S(2)}, u32[]{:S(2)}) collective-permute-start(bf16[16,128,256]{2,1,0:T(8,128)(2,1)} %constant_dynamic-update-slice_fusion.refs_9_), channel_id=1, source_target_pairs={{0,24},{4,100},{8,0},{12,108},{16,8},{20,116},{24,16},{28,124},{32... | collective-permute-start | bytes 3145736 | tf_op jit(solution)/shard_map/ppermute | solution.py:494
  43.7 19.4 %collective-permute-done.5.refs_3_ = bf16[1024,512]{1,0:T(8,128)(2,1)} collective-permute-done((bf16[1024,512]{1,0:T(8,128)(2,1)S(1)}, bf16[1024,512]{1,0:T(8,128)(2,1)}, u32[]{:S(2)}, u32[]{:S(2)}) %collective-permute-start.5) | collective-permute-done | bytes 1048608 | tf_op jit(solution)/shard_map/ppermute | solution.py:426
  63.1 1.5 collective-permute-start.14
  64.6 1.5 collective-permute-start.16
  66.1 6.2 %collective-permute-done.7.refs_5_ = bf16[1024,512]{1,0:T(8,128)(2,1)} collective-permute-done((bf16[1024,512]{1,0:T(8,128)(2,1)S(1)}, bf16[1024,512]{1,0:T(8,128)(2,1)}, u32[]{:S(2)}, u32[]{:S(2)}) %collective-permute-start.7) | collective-permute-done | bytes 1048608 | tf_op jit(solution)/shard_map/ppermute | solution.py:425
  75.8 1.6 collective-permute-start.8
  77.4 2.0 collective-permute-done.14.refs_15_
  79.4 1.7 collective-permute-start.9
  81.2 9.5 %collective-permute-done.16.refs_14_ = bf16[16,128,256]{2,1,0:T(8,128)(2,1)} collective-permute-done((bf16[16,128,256]{2,1,0:T(8,128)(2,1)}, bf16[16,128,256]{2,1,0:T(8,128)(2,1)}, u32[]{:S(2)}, u32[]{:S(2)}) %collective-permute-start.16) | collective-permute-done | bytes 1048608 | tf_op jit(solution)/shard_map/ppermute | solution.py:493
  90.7 1.5 collective-permute-start.13
  92.8 9.4 %collective-permute-done.8.refs_6_ = bf16[1024,512]{1,0:T(8,128)(2,1)S(1)} collective-permute-done((bf16[1024,512]{1,0:T(8,128)(2,1)S(1)}, bf16[1024,512]{1,0:T(8,128)(2,1)S(1)}, u32[]{:S(2)}, u32[]{:S(2)}) %collective-permute-start.8) | collective-permute-done | bytes 1048608 | tf_op jit(solution)/shard_map/ppermute | solution.py:505
  103.6 2.2 collective-permute-done.13.refs_12_
  105.8 2.8 %collective-permute-done.15.refs_13_ = bf16[16,128,256]{2,1,0:T(8,128)(2,1)} collective-permute-done((bf16[16,128,256]{2,1,0:T(8,128)(2,1)}, bf16[16,128,256]{2,1,0:T(8,128)(2,1)}, u32[]{:S(2)}, u32[]{:S(2)}) %collective-permute-start.15) | collective-permute-done | bytes 1048608 | tf_op jit(solution)/shard_map/ppermute | solution.py:499
  110.3 8.1 %fusion.refs_24_ = f32[8,1024,512]{2,1,0:T(8,128)} fusion(f32[1024]{0:T(1024)S(1)} %div.192, f32[8,16,512]{2,1,0:T(8,128)S(1)} %bitcast.95), kind=kLoop, calls=%fused_computation.3 | loop fusion | flops 4194304 | bytes 17043456 | tf_op jit(solution)/shard_map/exp | solution.py:477
  119.1 20.1 %density.1 = (f32[8,1,512]{2,1,0:T(1,128)}, f32[32,24,128]{2,1,0:T(8,128)}) custom-call(s32[8]{0:T(128)} %fusion.10.order, s32[1]{0:T(128)} %bitcast.3.place, s32[64]{0:T(128)} %get-tuple-element.30.which, s32[64]{0:T(128)} %get-tuple-element.31.where, bf16[1024,512]{1,0:T(8,128)(2,1)} %bitcast.78, bf16[1024,512]{1,0:T(8,128)(2,1)} %bitcast.83, ...), custom_call_target="tpu_custom_call" | custom-call | flops 8589934592 | bytes 33554432 | tf_op jit(solution)/shard_map/density/pallas_call | solution.py:287
  139.9 4.0 %all-to-all-start = ((f32[32,24,128]{2,1,0:T(8,128)}), f32[32,24,128]{2,1,0:T(8,128)S(1)}, u32[]{:S(2)}, u32[]{:S(2)}) async-start(f32[32,24,128]{2,1,0:T(8,128)} %get-tuple-element.44), calls=%async_computation | async-start | bytes 786432 | tf_op jit(solution)/shard_map/all_to_all | solution.py:517
  143.9 8.4 %bitcast_divide_fusion.table = f32[8,1024,512]{2,1,0:T(8,128)} fusion(f32[1024]{0:T(1024)S(1)} %div.199, f32[8,16,512]{2,1,0:T(8,128)} %bitcast.94), kind=kLoop, calls=%fused_computation | loop fusion | flops 8388608 | bytes 17043456 | tf_op jit(solution)/shard_map/div | solution.py:514
  152.3 1.7 all-to-all-done
  154.8 7.7 %potential.1 = (f32[256,64]{1,0:T(8,128)}, f32[8,1,512]{2,1,0:T(1,128)}, f32[8,1,512]{2,1,0:T(1,128)}, f32[1,128]{1,0:T(1,128)}) custom-call(f32[8,1024,512]{2,1,0:T(8,128)} %bitcast_divide_fusion.table, f32[768,128]{1,0:T(8,128)} %bitcast.93, f32[32,128]{1,0:T(8,128)} %broadcast_in_dim.78.mine, f32[8,1,512]{2,1,0:T(1,128)} %bitcast.104, ...), custom_call_target="tpu_custom_call" | custom-call | flops 16777216 | bytes 16777216 | tf_op jit(solution)/shard_map/potential/pallas_call | solution.py:317
  165.8 1.5 collective-permute-done.29
  168.7 1.5 collective-permute-done.31
  170.2 1.5 collective-permute-done.32
  172.7 20.3 %ham.1 = (f32[32,128,256]{2,1,0:T(8,128)}, f32[32,128,256]{2,1,0:T(8,128)}, f32[32,128,256]{2,1,0:T(8,128)}, f32[32,128,256]{2,1,0:T(8,128)}) custom-call(s32[8]{0:T(128)} %fusion.10.order, s32[64]{0:T(128)} %fusion.7.slots, s32[1]{0:T(128)} %bitcast.3.place, bf16[4,2,128,512]{3,2,1,0:T(8,128)(2,1)} %bitcast.79, bf16[4,2,128,512]{3,2,1,0:T(8,128)(2,1)} %bitcast.84, ...), custom_call_target="tpu_custom_call" | custom-call | flops 4294967296 | bytes 25165824 | tf_op jit(solution)/shard_map/ham/pallas_call | solution.py:342
  193.0 3.0 %multiply_convert_fusion = (f16[16,128,256]{2,1,0:T(8,128)(2,1)S(1)}, f16[16,128,256]{2,1,0:T(8,128)(2,1)S(1)}) fusion(f32[32,128,256]{2,1,0:T(8,128)} %get-tuple-element.51, f32[]{:T(128)} %bitcast.32), kind=kLoop, calls=%fused_computation.6 | loop fusion | flops 2097152 | bytes 6291460 | tf_op jit(solution)/shard_map/convert_element_type | solution.py:370
  200.9 10.0 %collective-permute-done.38 = f16[2,8,128,256]{3,2,1,0:T(8,128)(2,1)S(1)} collective-permute-done((f16[2,8,128,256]{3,2,1,0:T(8,128)(2,1)S(1)}, f16[2,8,128,256]{3,2,1,0:T(8,128)(2,1)S(1)}, u32[]{:S(2)}, u32[]{:S(2)}) %collective-permute-start.38) | collective-permute-done | bytes 1048608 | tf_op jit(solution)/shard_map/ppermute | solution.py:381
  211.3 2.5 collective-permute-start.39
  214.3 2.0 collective-permute-start.35
  216.7 7.8 %collective-permute-done.37 = f16[2,8,128,256]{3,2,1,0:T(8,128)(2,1)S(1)} collective-permute-done((f16[2,8,128,256]{3,2,1,0:T(8,128)(2,1)S(1)}, f16[2,8,128,256]{3,2,1,0:T(8,128)(2,1)S(1)}, u32[]{:S(2)}, u32[]{:S(2)}) %collective-permute-start.37) | collective-permute-done | bytes 1048608 | tf_op jit(solution)/shard_map/ppermute | solution.py:382
  224.5 1.6 collective-permute-done.39
  227.1 2.7 %collective-permute-start.42 = (f16[8,128,256]{2,1,0:T(8,128)(2,1)S(1)}, f16[8,128,256]{2,1,0:T(8,128)(2,1)S(1)}, u32[]{:S(2)}, u32[]{:S(2)}) collective-permute-start(f16[8,128,256]{2,1,0:T(8,128)(2,1)S(1)} %get-tuple-element.75), channel_id=1, source_target_pairs={{0,24},{4,100},{8,0},{12,108},{16,8},{20,116},{24,16},{28,124},{32... | collective-permute-start | bytes 1572872 | tf_op jit(solution)/shard_map/ppermute | solution.py:393
  229.8 13.2 %collective-permute-done.36 = f16[2,8,128,256]{3,2,1,0:T(8,128)(2,1)S(1)} collective-permute-done((f16[2,8,128,256]{3,2,1,0:T(8,128)(2,1)S(1)}, f16[2,8,128,256]{3,2,1,0:T(8,128)(2,1)S(1)}, u32[]{:S(2)}, u32[]{:S(2)}) %collective-permute-start.36) | collective-permute-done | bytes 1048608 | tf_op jit(solution)/shard_map/ppermute | solution.py:383
  243.6 1.5 collective-permute-start.41
  245.1 2.7 %collective-permute-start.40 = (f16[8,128,256]{2,1,0:T(8,128)(2,1)S(1)}, f16[8,128,256]{2,1,0:T(8,128)(2,1)S(1)}, u32[]{:S(2)}, u32[]{:S(2)}) collective-permute-start(f16[8,128,256]{2,1,0:T(8,128)(2,1)S(1)} %get-tuple-element.74), channel_id=1, source_target_pairs={{0,16},{4,68},{8,24},{12,76},{16,0},{20,84},{24,8},{28,92},{32,48}... | collective-permute-start | bytes 1572872 | tf_op jit(solution)/shard_map/ppermute | solution.py:393
  247.8 6.3 %collective-permute-done.41 = f16[8,128,256]{2,1,0:T(8,128)(2,1)S(1)} collective-permute-done((f16[8,128,256]{2,1,0:T(8,128)(2,1)S(1)}, f16[8,128,256]{2,1,0:T(8,128)(2,1)S(1)}, u32[]{:S(2)}, u32[]{:S(2)}) %collective-permute-start.41) | collective-permute-done | bytes 524320 | tf_op jit(solution)/shard_map/ppermute | solution.py:393
  254.0 6.5 %collective-permute-done.40 = f16[8,128,256]{2,1,0:T(8,128)(2,1)S(1)} collective-permute-done((f16[8,128,256]{2,1,0:T(8,128)(2,1)S(1)}, f16[8,128,256]{2,1,0:T(8,128)(2,1)S(1)}, u32[]{:S(2)}, u32[]{:S(2)}) %collective-permute-start.40) | collective-permute-done | bytes 524320 | tf_op jit(solution)/shard_map/ppermute | solution.py:393
  (153 shorter events, 32.3 us)
Async XLA Ops:
  1.9 1.6 collective-permute-start
  6.2 16.8 %collective-permute-start.1 = (bf16[8,128,256]{2,1,0:T(8,128)(2,1)}, bf16[8,128,256]{2,1,0:T(8,128)(2,1)}, u32[]{:S(2)}, u32[]{:S(2)}) collective-permute-start(bf16[8,128,256]{2,1,0:T(8,128)(2,1)} %pad_maximum_fusion.1), channel_id=1, source_target_pairs={{0,96},{4,28},{8,104},{12,4},{16,112},{20,12},{24,120},{28,20},{32... | collective-permute-start | bytes 1572872 | tf_op jit(solution)/shard_map/ppermute | solution.py:440
  10.4 18.2 %collective-permute-start.10 = (bf16[8,128,256]{2,1,0:T(8,128)(2,1)}, bf16[8,128,256]{2,1,0:T(8,128)(2,1)}, u32[]{:S(2)}, u32[]{:S(2)}) collective-permute-start(bf16[8,128,256]{2,1,0:T(8,128)(2,1)} %pad_maximum_fusion.1), channel_id=1, source_target_pairs={{0,64},{4,20},{8,72},{12,28},{16,80},{20,4},{24,88},{28,12},{32,96... | collective-permute-start | bytes 1572872 | tf_op jit(solution)/shard_map/ppermute | solution.py:440
  10.4 19.9 %collective-permute-start.11 = (bf16[8,128,256]{2,1,0:T(8,128)(2,1)}, bf16[8,128,256]{2,1,0:T(8,128)(2,1)}, u32[]{:S(2)}, u32[]{:S(2)}) collective-permute-start(bf16[8,128,256]{2,1,0:T(8,128)(2,1)} %pad_maximum_fusion.1), channel_id=1, source_target_pairs={{0,32},{4,12},{8,40},{12,20},{16,48},{20,28},{24,56},{28,4},{32,64... | collective-permute-start | bytes 1572872 | tf_op jit(solution)/shard_map/ppermute | solution.py:440
  11.8 15.0 %collective-permute-start.3 = (s32[32]{0:T(128)S(1)}, s32[32]{0:T(128)S(1)}, u32[]{:S(2)}, u32[]{:S(2)}) collective-permute-start(s32[32]{0:T(128)S(1)} %select_reduce_fusion.2), channel_id=1, source_target_pairs={{0,4},{4,0},{8,12},{12,8},{16,20},{20,16},{24,28},{28,24},{32,36},... | collective-permute-start | bytes 392 | tf_op jit(solution)/shard_map/ppermute | solution.py:445
  13.6 27.3 %collective-permute-start.4 = (bf16[1024,512]{1,0:T(8,128)(2,1)S(1)}, bf16[1024,512]{1,0:T(8,128)(2,1)S(1)}, u32[]{:S(2)}, u32[]{:S(2)}) collective-permute-start(bf16[1024,512]{1,0:T(8,128)(2,1)S(1)} %bitcast.76), channel_id=1, source_target_pairs={{0,1},{1,2},{2,3},{3,0},{4,5},{5,6},{6,7},{7,4},{8,9},{9,10},{10,1... | collective-permute-start | bytes 3145736 | tf_op jit(solution)/shard_map/ppermute | solution.py:424
  22.9 86.1 %copy-start.26 = (f32[64]{0:T(128)S(1)}, f32[64]{0:T(128)}, u32[]{:S(2)}) copy-start(f32[64]{0:T(128)} %param.17) | copy-start | bytes 772
  23.0 86.3 %copy-start.20 = (f32[3,256]{1,0:T(4,128)S(1)}, f32[3,256]{1,0:T(4,128)}, u32[]{:S(2)}) copy-start(f32[3,256]{1,0:T(4,128)} %param.18) | copy-start | bytes 9220
  23.0 40.1 %collective-permute-start.5 = (bf16[1024,512]{1,0:T(8,128)(2,1)S(1)}, bf16[1024,512]{1,0:T(8,128)(2,1)}, u32[]{:S(2)}, u32[]{:S(2)}) collective-permute-start(bf16[1024,512]{1,0:T(8,128)(2,1)S(1)} %bitcast.81), channel_id=1, source_target_pairs={{0,1},{1,2},{2,3},{3,0},{4,5},{5,6},{6,7},{7,4},{8,9},{9,10},{10,1... | collective-permute-start | bytes 3145736 | tf_op jit(solution)/shard_map/ppermute | solution.py:426
  26.9 37.7 %collective-permute-start.6 = (bf16[1024,512]{1,0:T(8,128)(2,1)S(1)}, bf16[1024,512]{1,0:T(8,128)(2,1)}, u32[]{:S(2)}, u32[]{:S(2)}) collective-permute-start(bf16[1024,512]{1,0:T(8,128)(2,1)S(1)} %bitcast.77), channel_id=1, source_target_pairs={{0,3},{1,0},{2,1},{3,2},{4,7},{5,4},{6,5},{7,6},{8,11},{9,8},{10,9... | collective-permute-start | bytes 3145736 | tf_op jit(solution)/shard_map/ppermute | solution.py:427
  28.6 43.7 %collective-permute-start.7 = (bf16[1024,512]{1,0:T(8,128)(2,1)S(1)}, bf16[1024,512]{1,0:T(8,128)(2,1)}, u32[]{:S(2)}, u32[]{:S(2)}) collective-permute-start(bf16[1024,512]{1,0:T(8,128)(2,1)S(1)} %bitcast.82), channel_id=1, source_target_pairs={{0,3},{1,0},{2,1},{3,2},{4,7},{5,4},{6,5},{7,6},{8,11},{9,8},{10,9... | collective-permute-start | bytes 3145736 | tf_op jit(solution)/shard_map/ppermute | solution.py:425
  30.4 41.9 %collective-permute-start.2 = (bf16[16,128,256]{2,1,0:T(8,128)(2,1)}, bf16[16,128,256]{2,1,0:T(8,128)(2,1)}, u32[]{:S(2)}, u32[]{:S(2)}) collective-permute-start(bf16[16,128,256]{2,1,0:T(8,128)(2,1)} %pad_maximum_fusion.refs_8_), channel_id=1, source_target_pairs={{0,24},{4,100},{8,0},{12,108},{16,8},{20,116},{24,16},{28,124},{32... | collective-permute-start | bytes 3145736 | tf_op jit(solution)/shard_map/ppermute | solution.py:491
  40.9 77.5 %copy-start.4 = (bf16[1024,512]{1,0:T(8,128)(2,1)}, bf16[1024,512]{1,0:T(8,128)(2,1)S(1)}, u32[]{:S(2)}) copy-start(bf16[1024,512]{1,0:T(8,128)(2,1)S(1)} %collective-permute-done.4.refs_2_) | copy-start | bytes 3145732
  40.9 34.9 %collective-permute-start.12 = (bf16[16,128,256]{2,1,0:T(8,128)(2,1)}, bf16[16,128,256]{2,1,0:T(8,128)(2,1)}, u32[]{:S(2)}, u32[]{:S(2)}) collective-permute-start(bf16[16,128,256]{2,1,0:T(8,128)(2,1)} %constant_dynamic-update-slice_fusion.refs_9_), channel_id=1, source_target_pairs={{0,24},{4,100},{8,0},{12,108},{16,8},{20,116},{24,16},{28,124},{32... | collective-permute-start | bytes 3145736 | tf_op jit(solution)/shard_map/ppermute | solution.py:494
  63.1 16.3 %collective-permute-start.14 = (bf16[16,128,256]{2,1,0:T(8,128)(2,1)}, bf16[16,128,256]{2,1,0:T(8,128)(2,1)}, u32[]{:S(2)}, u32[]{:S(2)}) collective-permute-start(bf16[16,128,256]{2,1,0:T(8,128)(2,1)} %constant_dynamic-update-slice_fusion.refs_9_), channel_id=1, source_target_pairs={{0,8},{4,36},{8,16},{12,44},{16,24},{20,52},{24,0},{28,60},{32,40}... | collective-permute-start | bytes 3145736 | tf_op jit(solution)/shard_map/ppermute | solution.py:492
  64.6 26.1 %collective-permute-start.16 = (bf16[16,128,256]{2,1,0:T(8,128)(2,1)}, bf16[16,128,256]{2,1,0:T(8,128)(2,1)}, u32[]{:S(2)}, u32[]{:S(2)}) collective-permute-start(bf16[16,128,256]{2,1,0:T(8,128)(2,1)} %pad_maximum_fusion.refs_8_), channel_id=1, source_target_pairs={{0,8},{4,36},{8,16},{12,44},{16,24},{20,52},{24,0},{28,60},{32,40}... | collective-permute-start | bytes 3145736 | tf_op jit(solution)/shard_map/ppermute | solution.py:493
  72.3 19.9 %collective-permute-start.17 = (bf16[16,128,256]{2,1,0:T(8,128)(2,1)}, bf16[16,128,256]{2,1,0:T(8,128)(2,1)}, u32[]{:S(2)}, u32[]{:S(2)}) collective-permute-start(bf16[16,128,256]{2,1,0:T(8,128)(2,1)} %pad_maximum_fusion.refs_8_), channel_id=1, source_target_pairs={{0,4},{4,0},{8,12},{12,8},{16,20},{20,16},{24,28},{28,24},{32,36},... | collective-permute-start | bytes 3145736 | tf_op jit(solution)/shard_map/ppermute | solution.py:503
  72.3 20.4 %collective-permute-start.18 = (bf16[16,128,256]{2,1,0:T(8,128)(2,1)}, bf16[16,128,256]{2,1,0:T(8,128)(2,1)}, u32[]{:S(2)}, u32[]{:S(2)}) collective-permute-start(bf16[16,128,256]{2,1,0:T(8,128)(2,1)} %constant_dynamic-update-slice_fusion.refs_9_), channel_id=1, source_target_pairs={{0,4},{4,0},{8,12},{12,8},{16,20},{20,16},{24,28},{28,24},{32,36},... | collective-permute-start | bytes 3145736 | tf_op jit(solution)/shard_map/ppermute | solution.py:503
  75.8 26.3 %collective-permute-start.8 = (bf16[1024,512]{1,0:T(8,128)(2,1)S(1)}, bf16[1024,512]{1,0:T(8,128)(2,1)S(1)}, u32[]{:S(2)}, u32[]{:S(2)}) collective-permute-start(bf16[1024,512]{1,0:T(8,128)(2,1)S(1)} %collective-permute-done.4.refs_2_), channel_id=1, source_target_pairs={{0,1},{1,2},{2,3},{3,0},{4,5},{5,6},{6,7},{7,4},{8,9},{9,10},{10,1... | collective-permute-start | bytes 3145736 | tf_op jit(solution)/shard_map/ppermute | solution.py:505
  79.4 24.1 %collective-permute-start.9 = (bf16[1024,512]{1,0:T(8,128)(2,1)}, bf16[1024,512]{1,0:T(8,128)(2,1)S(1)}, u32[]{:S(2)}, u32[]{:S(2)}) collective-permute-start(bf16[1024,512]{1,0:T(8,128)(2,1)} %collective-permute-done.7.refs_5_), channel_id=1, source_target_pairs={{0,3},{1,0},{2,1},{3,2},{4,7},{5,4},{6,5},{7,6},{8,11},{9,8},{10,9... | collective-permute-start | bytes 3145736 | tf_op jit(solution)/shard_map/ppermute | solution.py:506
  90.7 15.1 %collective-permute-start.13 = (bf16[16,128,256]{2,1,0:T(8,128)(2,1)}, bf16[16,128,256]{2,1,0:T(8,128)(2,1)}, u32[]{:S(2)}, u32[]{:S(2)}) collective-permute-start(bf16[16,128,256]{2,1,0:T(8,128)(2,1)} %collective-permute-done.2.refs_10_), channel_id=1, source_target_pairs={{0,24},{4,100},{8,0},{12,108},{16,8},{20,116},{24,16},{28,124},{32... | collective-permute-start | bytes 3145736 | tf_op jit(solution)/shard_map/ppermute | solution.py:498
  92.2 16.3 %collective-permute-start.15 = (bf16[16,128,256]{2,1,0:T(8,128)(2,1)}, bf16[16,128,256]{2,1,0:T(8,128)(2,1)}, u32[]{:S(2)}, u32[]{:S(2)}) collective-permute-start(bf16[16,128,256]{2,1,0:T(8,128)(2,1)} %collective-permute-done.14.refs_15_), channel_id=1, source_target_pairs={{0,8},{4,36},{8,16},{12,44},{16,24},{20,52},{24,0},{28,60},{32,40}... | collective-permute-start | bytes 3145736 | tf_op jit(solution)/shard_map/ppermute | solution.py:499
  92.7 15.8 %collective-permute-start.19 = (bf16[16,128,256]{2,1,0:T(8,128)(2,1)}, bf16[16,128,256]{2,1,0:T(8,128)(2,1)}, u32[]{:S(2)}, u32[]{:S(2)}) collective-permute-start(bf16[16,128,256]{2,1,0:T(8,128)(2,1)} %collective-permute-done.2.refs_10_), channel_id=1, source_target_pairs={{0,4},{4,0},{8,12},{12,8},{16,20},{20,16},{24,28},{28,24},{32,36},... | collective-permute-start | bytes 3145736 | tf_op jit(solution)/shard_map/ppermute | solution.py:503
  102.1 16.9 %collective-permute-start.24 = (bf16[16,128,256]{2,1,0:T(8,128)(2,1)}, bf16[16,128,256]{2,1,0:T(8,128)(2,1)}, u32[]{:S(2)}, u32[]{:S(2)}) collective-permute-start(bf16[16,128,256]{2,1,0:T(8,128)(2,1)} %collective-permute-done.14.refs_15_), channel_id=1, source_target_pairs={{0,4},{4,0},{8,12},{12,8},{16,20},{20,16},{24,28},{28,24},{32,36},... | collective-permute-start | bytes 3145736 | tf_op jit(solution)/shard_map/ppermute | solution.py:503
  103.5 15.4 %collective-permute-start.20 = (bf16[16,128,256]{2,1,0:T(8,128)(2,1)}, bf16[16,128,256]{2,1,0:T(8,128)(2,1)}, u32[]{:S(2)}, u32[]{:S(2)}) collective-permute-start(bf16[16,128,256]{2,1,0:T(8,128)(2,1)} %collective-permute-done.12.refs_11_), channel_id=1, source_target_pairs={{0,4},{4,0},{8,12},{12,8},{16,20},{20,16},{24,28},{28,24},{32,36},... | collective-permute-start | bytes 3145736 | tf_op jit(solution)/shard_map/ppermute | solution.py:503
  105.8 13.2 %collective-permute-start.23 = (bf16[16,128,256]{2,1,0:T(8,128)(2,1)}, bf16[16,128,256]{2,1,0:T(8,128)(2,1)}, u32[]{:S(2)}, u32[]{:S(2)}) collective-permute-start(bf16[16,128,256]{2,1,0:T(8,128)(2,1)} %collective-permute-done.16.refs_14_), channel_id=1, source_target_pairs={{0,4},{4,0},{8,12},{12,8},{16,20},{20,16},{24,28},{28,24},{32,36},... | collective-permute-start | bytes 3145736 | tf_op jit(solution)/shard_map/ppermute | solution.py:503
  108.5 10.5 %collective-permute-start.21 = (bf16[16,128,256]{2,1,0:T(8,128)(2,1)}, bf16[16,128,256]{2,1,0:T(8,128)(2,1)}, u32[]{:S(2)}, u32[]{:S(2)}) collective-permute-start(bf16[16,128,256]{2,1,0:T(8,128)(2,1)} %collective-permute-done.13.refs_12_), channel_id=1, source_target_pairs={{0,4},{4,0},{8,12},{12,8},{16,20},{20,16},{24,28},{28,24},{32,36},... | collective-permute-start | bytes 3145736 | tf_op jit(solution)/shard_map/ppermute | solution.py:503
  108.6 10.5 %collective-permute-start.22 = (bf16[16,128,256]{2,1,0:T(8,128)(2,1)}, bf16[16,128,256]{2,1,0:T(8,128)(2,1)}, u32[]{:S(2)}, u32[]{:S(2)}) collective-permute-start(bf16[16,128,256]{2,1,0:T(8,128)(2,1)} %collective-permute-done.15.refs_13_), channel_id=1, source_target_pairs={{0,4},{4,0},{8,12},{12,8},{16,20},{20,16},{24,28},{28,24},{32,36},... | collective-permute-start | bytes 3145736 | tf_op jit(solution)/shard_map/ppermute | solution.py:503
  139.2 25.1 %collective-permute-start.25 = (bf16[1024,512]{1,0:T(8,128)(2,1)S(1)}, bf16[1024,512]{1,0:T(8,128)(2,1)}, u32[]{:S(2)}, u32[]{:S(2)}) collective-permute-start(bf16[1024,512]{1,0:T(8,128)(2,1)S(1)} %bitcast.80), channel_id=1, source_target_pairs={{0,4},{4,0},{8,12},{12,8},{16,20},{20,16},{24,28},{28,24},{32,36},... | collective-permute-start | bytes 3145736 | tf_op jit(solution)/shard_map/ppermute | solution.py:513
  139.3 25.2 %collective-permute-start.26 = (bf16[1024,512]{1,0:T(8,128)(2,1)S(1)}, bf16[1024,512]{1,0:T(8,128)(2,1)}, u32[]{:S(2)}, u32[]{:S(2)}) collective-permute-start(bf16[1024,512]{1,0:T(8,128)(2,1)S(1)} %bitcast.85), channel_id=1, source_target_pairs={{0,4},{4,0},{8,12},{12,8},{16,20},{20,16},{24,28},{28,24},{32,36},... | collective-permute-start | bytes 3145736 | tf_op jit(solution)/shard_map/ppermute | solution.py:513
  139.8 25.0 %collective-permute-start.27 = (bf16[1024,512]{1,0:T(8,128)(2,1)S(1)}, bf16[1024,512]{1,0:T(8,128)(2,1)}, u32[]{:S(2)}, u32[]{:S(2)}) collective-permute-start(bf16[1024,512]{1,0:T(8,128)(2,1)S(1)} %copy-done.5), channel_id=1, source_target_pairs={{0,4},{4,0},{8,12},{12,8},{16,20},{20,16},{24,28},{28,24},{32,36},... | collective-permute-start | bytes 3145736 | tf_op jit(solution)/shard_map/ppermute | solution.py:513
  139.9 14.2 %all-to-all-start = ((f32[32,24,128]{2,1,0:T(8,128)}), f32[32,24,128]{2,1,0:T(8,128)S(1)}, u32[]{:S(2)}, u32[]{:S(2)}) async-start(f32[32,24,128]{2,1,0:T(8,128)} %get-tuple-element.44), calls=%async_computation | async-start | bytes 786432 | tf_op jit(solution)/shard_map/all_to_all | solution.py:517
  162.5 1.5 collective-permute-start.33
  162.8 3.0 %collective-permute-start.28 = (bf16[1024,512]{1,0:T(8,128)(2,1)}, bf16[1024,512]{1,0:T(8,128)(2,1)}, u32[]{:S(2)}, u32[]{:S(2)}) collective-permute-start(bf16[1024,512]{1,0:T(8,128)(2,1)} %collective-permute-done.5.refs_3_), channel_id=1, source_target_pairs={{0,4},{4,0},{8,12},{12,8},{16,20},{20,16},{24,28},{28,24},{32,36},... | collective-permute-start | bytes 3145736 | tf_op jit(solution)/shard_map/ppermute | solution.py:513
  164.0 3.3 %collective-permute-start.29 = (bf16[1024,512]{1,0:T(8,128)(2,1)}, bf16[1024,512]{1,0:T(8,128)(2,1)}, u32[]{:S(2)}, u32[]{:S(2)}) collective-permute-start(bf16[1024,512]{1,0:T(8,128)(2,1)} %collective-permute-done.6.refs_4_), channel_id=1, source_target_pairs={{0,4},{4,0},{8,12},{12,8},{16,20},{20,16},{24,28},{28,24},{32,36},... | collective-permute-start | bytes 3145736 | tf_op jit(solution)/shard_map/ppermute | solution.py:513
  164.2 4.5 %collective-permute-start.30 = (bf16[1024,512]{1,0:T(8,128)(2,1)}, bf16[1024,512]{1,0:T(8,128)(2,1)S(1)}, u32[]{:S(2)}, u32[]{:S(2)}) collective-permute-start(bf16[1024,512]{1,0:T(8,128)(2,1)} %collective-permute-done.7.refs_5_), channel_id=1, source_target_pairs={{0,4},{4,0},{8,12},{12,8},{16,20},{20,16},{24,28},{28,24},{32,36},... | collective-permute-start | bytes 3145736 | tf_op jit(solution)/shard_map/ppermute | solution.py:513
  164.5 5.7 %collective-permute-start.31 = (bf16[1024,512]{1,0:T(8,128)(2,1)}, bf16[1024,512]{1,0:T(8,128)(2,1)S(1)}, u32[]{:S(2)}, u32[]{:S(2)}) collective-permute-start(bf16[1024,512]{1,0:T(8,128)(2,1)} %copy-done.6), channel_id=1, source_target_pairs={{0,4},{4,0},{8,12},{12,8},{16,20},{20,16},{24,28},{28,24},{32,36},... | collective-permute-start | bytes 3145736 | tf_op jit(solution)/shard_map/ppermute | solution.py:513
  164.8 7.0 %collective-permute-start.32 = (bf16[1024,512]{1,0:T(8,128)(2,1)}, bf16[1024,512]{1,0:T(8,128)(2,1)S(1)}, u32[]{:S(2)}, u32[]{:S(2)}) collective-permute-start(bf16[1024,512]{1,0:T(8,128)(2,1)} %copy-done.7), channel_id=1, source_target_pairs={{0,4},{4,0},{8,12},{12,8},{16,20},{20,16},{24,28},{28,24},{32,36},... | collective-permute-start | bytes 3145736 | tf_op jit(solution)/shard_map/ppermute | solution.py:513
  196.0 14.9 %collective-permute-start.38 = (f16[2,8,128,256]{3,2,1,0:T(8,128)(2,1)S(1)}, f16[2,8,128,256]{3,2,1,0:T(8,128)(2,1)S(1)}, u32[]{:S(2)}, u32[]{:S(2)}) collective-permute-start(f16[2,8,128,256]{3,2,1,0:T(8,128)(2,1)S(1)} %bitcast.100), channel_id=1, source_target_pairs={{0,96},{4,28},{8,104},{12,4},{16,112},{20,12},{24,120},{28,20},{32... | collective-permute-start | bytes 3145736 | tf_op jit(solution)/shard_map/ppermute | solution.py:381
  197.3 16.6 %collective-permute-start.34 = (f16[2,8,128,256]{3,2,1,0:T(8,128)(2,1)S(1)}, f16[2,8,128,256]{3,2,1,0:T(8,128)(2,1)S(1)}, u32[]{:S(2)}, u32[]{:S(2)}) collective-permute-start(f16[2,8,128,256]{3,2,1,0:T(8,128)(2,1)S(1)} %bitcast.99), channel_id=1, source_target_pairs={{0,32},{4,12},{8,40},{12,20},{16,48},{20,28},{24,56},{28,4},{32,64... | collective-permute-start | bytes 3145736 | tf_op jit(solution)/shard_map/ppermute | solution.py:380
  198.7 25.9 %collective-permute-start.37 = (f16[2,8,128,256]{3,2,1,0:T(8,128)(2,1)S(1)}, f16[2,8,128,256]{3,2,1,0:T(8,128)(2,1)S(1)}, u32[]{:S(2)}, u32[]{:S(2)}) collective-permute-start(f16[2,8,128,256]{3,2,1,0:T(8,128)(2,1)S(1)} %bitcast.102), channel_id=1, source_target_pairs={{0,32},{4,12},{8,40},{12,20},{16,48},{20,28},{24,56},{28,4},{32,64... | collective-permute-start | bytes 3145736 | tf_op jit(solution)/shard_map/ppermute | solution.py:382
  211.3 14.9 %collective-permute-start.39 = (f16[2,8,128,256]{3,2,1,0:T(8,128)(2,1)S(1)}, f16[2,8,128,256]{3,2,1,0:T(8,128)(2,1)S(1)}, u32[]{:S(2)}, u32[]{:S(2)}) collective-permute-start(f16[2,8,128,256]{3,2,1,0:T(8,128)(2,1)S(1)} %add_convert_fusion.1), channel_id=1, source_target_pairs={{0,96},{4,28},{8,104},{12,4},{16,112},{20,12},{24,120},{28,20},{32... | collective-permute-start | bytes 3145736 | tf_op jit(solution)/shard_map/ppermute | solution.py:385
  213.8 29.2 %collective-permute-start.36 = (f16[2,8,128,256]{3,2,1,0:T(8,128)(2,1)S(1)}, f16[2,8,128,256]{3,2,1,0:T(8,128)(2,1)S(1)}, u32[]{:S(2)}, u32[]{:S(2)}) collective-permute-start(f16[2,8,128,256]{3,2,1,0:T(8,128)(2,1)S(1)} %bitcast.101), channel_id=1, source_target_pairs={{0,96},{4,28},{8,104},{12,4},{16,112},{20,12},{24,120},{28,20},{32... | collective-permute-start | bytes 3145736 | tf_op jit(solution)/shard_map/ppermute | solution.py:383
  214.3 28.7 %collective-permute-start.35 = (f16[2,8,128,256]{3,2,1,0:T(8,128)(2,1)S(1)}, f16[2,8,128,256]{3,2,1,0:T(8,128)(2,1)S(1)}, u32[]{:S(2)}, u32[]{:S(2)}) collective-permute-start(f16[2,8,128,256]{3,2,1,0:T(8,128)(2,1)S(1)} %add_convert_fusion.2), channel_id=1, source_target_pairs={{0,32},{4,12},{8,40},{12,20},{16,48},{20,28},{24,56},{28,4},{32,64... | collective-permute-start | bytes 3145736 | tf_op jit(solution)/shard_map/ppermute | solution.py:384
  227.1 20.7 %collective-permute-start.42 = (f16[8,128,256]{2,1,0:T(8,128)(2,1)S(1)}, f16[8,128,256]{2,1,0:T(8,128)(2,1)S(1)}, u32[]{:S(2)}, u32[]{:S(2)}) collective-permute-start(f16[8,128,256]{2,1,0:T(8,128)(2,1)S(1)} %get-tuple-element.75), channel_id=1, source_target_pairs={{0,24},{4,100},{8,0},{12,108},{16,8},{20,116},{24,16},{28,124},{32... | collective-permute-start | bytes 1572872 | tf_op jit(solution)/shard_map/ppermute | solution.py:393
  243.6 10.5 %collective-permute-start.41 = (f16[8,128,256]{2,1,0:T(8,128)(2,1)S(1)}, f16[8,128,256]{2,1,0:T(8,128)(2,1)S(1)}, u32[]{:S(2)}, u32[]{:S(2)}) collective-permute-start(f16[8,128,256]{2,1,0:T(8,128)(2,1)S(1)} %fusion.6), channel_id=1, source_target_pairs={{0,8},{4,36},{8,16},{12,44},{16,24},{20,52},{24,0},{28,60},{32,40}... | collective-permute-start | bytes 1572872 | tf_op jit(solution)/shard_map/ppermute | solution.py:393
  245.1 15.5 %collective-permute-start.40 = (f16[8,128,256]{2,1,0:T(8,128)(2,1)S(1)}, f16[8,128,256]{2,1,0:T(8,128)(2,1)S(1)}, u32[]{:S(2)}, u32[]{:S(2)}) collective-permute-start(f16[8,128,256]{2,1,0:T(8,128)(2,1)S(1)} %get-tuple-element.74), channel_id=1, source_target_pairs={{0,16},{4,68},{8,24},{12,76},{16,0},{20,84},{24,8},{28,92},{32,48}... | collective-permute-start | bytes 1572872 | tf_op jit(solution)/shard_map/ppermute | solution.py:393
  260.9 1.6 collective-permute-start.43
  (24 other events, 367.9 us)

commit v11 on v10

--- a/solution.py
+++ b/solution.py
@@ -7,6 +7,7 @@
 
 
 SOFTEN = 0.25
+EARLY_SWAPS = (0, 1, 2, 5)
 ROOT_TWO = 1.4142135623730951
 HALF = 512
 PIECES = 8
@@ -476,6 +477,9 @@
     erf_scale = (ROOT_TWO * gauss_widths)[None, None, :, None]
     gauss = jnp.exp(-dist_sq / spread).reshape(PIECES, neighbors * moments, HALF)
     distance = jnp.sqrt(dist_sq)
+    hart = (lax.erf(distance / erf_scale) / distance).reshape(
+        PIECES, neighbors * moments, HALF
+    )
     weights = point_weights.reshape(PIECES, 1, HALF)
     xc = xc_kernel.reshape(PIECES, 1, HALF)
 
@@ -509,11 +513,11 @@
     rho, sent = density_call(
         order, core_place, which, where, chunks, sources, gauss, weights, xc, home_rows
     )
-    distance, sent, later = lax.optimization_barrier((distance, sent, chunks))
-    beside = [lax.ppermute(chunk, "grid", swap) for chunk in later]
-    hart = (lax.erf(distance / erf_scale) / distance).reshape(
-        PIECES, neighbors * moments, HALF
-    )
+    sent, later = lax.optimization_barrier((sent, chunks))
+    beside = [
+        lax.ppermute(chunks[i] if i in EARLY_SWAPS else later[i], "grid", swap)
+        for i in range(CHUNKS)
+    ]
     got = lax.all_to_all(sent, "grid", split_axis=0, concat_axis=0, tiled=True)
     all_coeffs, pot, scale, bound = potential_call(
         hart, got.reshape(groups * PAY_ROWS, 128), my_homes, weights, xc, rho, natoms

time: 265 us -> 263 us (level)
  waiting for transfers between devices: 119 us -> 116 us
    ppermute x1, waiting for transfers between devices: 4.02 us -> 33.3 us  [one_device(): below0 = lax.ppermute(own0, 'pert', ring(1))]
    ppermute x1, waiting for transfers between devices: 19.4 us -> 0.01 us  [one_device(): below1 = lax.ppermute(own1, 'pert', ring(1))]
    ppermute x1, waiting for transfers between devices: 9.49 us -> 0.01 us  [one_device(): near_behind = lax.ppermute(near, 'grid', forth)]
    ppermute x1, waiting for transfers between devices: 0.01 us -> 9.46 us  [one_device(): other_ahead = lax.ppermute(other, 'grid', back)]
    ppermute x1, waiting for transfers between devices: 0.01 us -> 7.99 us  [one_device(): near_ahead = lax.ppermute(near, 'grid', back)]
    ppermute x1, waiting for transfers between devices: 6.19 us -> 0.01 us  [one_device(): above1 = lax.ppermute(own1, 'pert', ring(3))]
    ppermute x8, waiting for transfers between devices: 5.98 us -> 0.02 us  [one_device(): lax.ppermute(chunks[i] if i in EARLY_SWAPS else later[i], 'grid', swap)]
    ppermute x3, waiting for transfers between devices: 6.16 us -> 0.67 us  [one_device(): lax.ppermute(base, 'grid', core_perm(-d, False))]
  transfers between devices with their start and end apart: 45 -> 45, of which waited for: 25 -> 17; matrix products, arithmetic and copies ran while one was open for 14% -> 14% of each run, Pallas kernels for 3% -> 11%
where the time goes in v11:
time: 263 us; the launch traced here: 261 us
  waiting for transfers between devices  116 us (44%)
  starting transfers between devices  49.2 us (19%)
  Pallas kernels  48 us (18%)
  other arithmetic  33.6 us (13%)
  local copies, waits for them, and re-layouts  12.3 us (5%)
    ppermute x1, waiting for transfers between devices, one_device(): below0 = lax.ppermute(own0, 'pert', ring(1))  33.3 us
    pallas_call x1, Pallas kernels, ham_call(): pl.pallas_call(ham_body, out_shape=(jax.ShapeDtypeStruct((32, 128, BLK),...  20.3 us
    pallas_call x1, Pallas kernels, density_call(): pl.pallas_call(density_body, out_shape=(jax.ShapeDtypeStruct((PIECES, 1,...  20 us
    ppermute x1, waiting for transfers between devices, ring_sum(): above_low = lax.ppermute(cast(parts[3][:half] * factor), 'grid', down)  18 us
    ppermute x1, waiting for transfers between devices, ring_sum(): from_above = lax.ppermute(cast(parts[2][half:] * factor), 'grid', down)  10 us
    ppermute x3, waiting for transfers between devices, direct_sum(): lax.ppermute(cast(parts[d]), 'grid', core_perm(d, True))  9.56 us
    ppermute x1, waiting for transfers between devices, one_device(): other_ahead = lax.ppermute(other, 'grid', back)  9.46 us
    exp x1, other arithmetic, one_device(): jnp.exp(-dist_sq / spread).reshape(PIECES, neighbors * moments, HALF)  9.18 us
  transfers between devices with their start and end apart: 45, of which 17 were waited for; matrix products, arithmetic and copies ran while one was open for 14% of the time, Pallas kernels for 11%

profile of v11, /device:TPU:0, one launch (start us, length us, event | category | flops | bytes accessed | tf_op | source)
XLA Modules:
  0.0 260.8 jit_solution(17164289438980008683)
XLA Ops:
  0.7 1.2 select_bitcast_fusion
  2.0 1.5 collective-permute-done
  3.5 1.1 bitcast_select_fusion.1
  4.6 0.9 pad_maximum_fusion.1
  5.5 4.0 %collective-permute-start.13 = (bf16[8,128,256]{2,1,0:T(8,128)(2,1)}, bf16[8,128,256]{2,1,0:T(8,128)(2,1)}, u32[]{:S(2)}, u32[]{:S(2)}) collective-permute-start(bf16[8,128,256]{2,1,0:T(8,128)(2,1)} %pad_maximum_fusion.1), channel_id=1, source_target_pairs={{0,64},{4,20},{8,72},{12,28},{16,80},{20,4},{24,88},{28,12},{32,96... | collective-permute-start | bytes 1572872 | tf_op jit(solution)/shard_map/ppermute | solution.py:441
  9.5 1.0 collective-permute-start.14
  10.5 2.2 collective-permute-start.1
  12.7 1.1 fusion.25
  14.4 3.1 %collective-permute-start.7 = (bf16[1024,512]{1,0:T(8,128)(2,1)S(1)}, bf16[1024,512]{1,0:T(8,128)(2,1)S(1)}, u32[]{:S(2)}, u32[]{:S(2)}) collective-permute-start(bf16[1024,512]{1,0:T(8,128)(2,1)S(1)} %bitcast.75), channel_id=1, source_target_pairs={{0,3},{1,0},{2,1},{3,2},{4,7},{5,4},{6,5},{7,6},{8,11},{9,8},{10,9... | collective-permute-start | bytes 3145736 | tf_op jit(solution)/shard_map/ppermute | solution.py:426
  17.6 1.5 copy.25
  20.0 1.9 constant_dynamic-update-slice_fusion.1
  22.6 1.8 constant_dynamic-update-slice_fusion.refs_9_
  24.4 3.0 %collective-permute-start.6 = (bf16[1024,512]{1,0:T(8,128)(2,1)S(1)}, bf16[1024,512]{1,0:T(8,128)(2,1)}, u32[]{:S(2)}, u32[]{:S(2)}) collective-permute-start(bf16[1024,512]{1,0:T(8,128)(2,1)S(1)} %bitcast.81), channel_id=1, source_target_pairs={{0,3},{1,0},{2,1},{3,2},{4,7},{5,4},{6,5},{7,6},{8,11},{9,8},{10,9... | collective-permute-start | bytes 3145736 | tf_op jit(solution)/shard_map/ppermute | solution.py:428
  27.4 1.5 collective-permute-start.17
  28.9 2.1 pad_maximum_fusion.refs_8_
  31.1 33.3 %collective-permute-done.4.refs_2_ = bf16[1024,512]{1,0:T(8,128)(2,1)S(1)} collective-permute-done((bf16[1024,512]{1,0:T(8,128)(2,1)S(1)}, bf16[1024,512]{1,0:T(8,128)(2,1)S(1)}, u32[]{:S(2)}, u32[]{:S(2)}) %collective-permute-start.4) | collective-permute-done | bytes 1048608 | tf_op jit(solution)/shard_map/ppermute | solution.py:425
  64.7 2.1 collective-permute-start.21
  67.4 1.5 collective-permute-start.19
  70.1 9.5 %collective-permute-done.15.refs_11_ = bf16[16,128,256]{2,1,0:T(8,128)(2,1)} collective-permute-done((bf16[16,128,256]{2,1,0:T(8,128)(2,1)}, bf16[16,128,256]{2,1,0:T(8,128)(2,1)}, u32[]{:S(2)}, u32[]{:S(2)}) %collective-permute-start.15) | collective-permute-done | bytes 1048608 | tf_op jit(solution)/shard_map/ppermute | solution.py:498
  79.5 3.2 %collective-permute-start.9 = (bf16[1024,512]{1,0:T(8,128)(2,1)S(1)}, bf16[1024,512]{1,0:T(8,128)(2,1)}, u32[]{:S(2)}, u32[]{:S(2)}) collective-permute-start(bf16[1024,512]{1,0:T(8,128)(2,1)S(1)} %collective-permute-done.7.refs_5_), channel_id=1, source_target_pairs={{0,3},{1,0},{2,1},{3,2},{4,7},{5,4},{6,5},{7,6},{8,11},{9,8},{10,9... | collective-permute-start | bytes 3145736 | tf_op jit(solution)/shard_map/ppermute | solution.py:510
  82.8 8.0 %collective-permute-done.2.refs_10_ = bf16[16,128,256]{2,1,0:T(8,128)(2,1)} collective-permute-done((bf16[16,128,256]{2,1,0:T(8,128)(2,1)}, bf16[16,128,256]{2,1,0:T(8,128)(2,1)}, u32[]{:S(2)}, u32[]{:S(2)}) %collective-permute-start.2) | collective-permute-done | bytes 1048608 | tf_op jit(solution)/shard_map/ppermute | solution.py:495
  93.2 3.1 %collective-permute-start.16 = (bf16[16,128,256]{2,1,0:T(8,128)(2,1)}, bf16[16,128,256]{2,1,0:T(8,128)(2,1)}, u32[]{:S(2)}, u32[]{:S(2)}) collective-permute-start(bf16[16,128,256]{2,1,0:T(8,128)(2,1)} %collective-permute-done.2.refs_10_), channel_id=1, source_target_pairs={{0,24},{4,100},{8,0},{12,108},{16,8},{20,116},{24,16},{28,124},{32... | collective-permute-start | bytes 3145736 | tf_op jit(solution)/shard_map/ppermute | solution.py:502
  96.3 9.1 %collective-permute-done.8.refs_6_ = bf16[1024,512]{1,0:T(8,128)(2,1)} collective-permute-done((bf16[1024,512]{1,0:T(8,128)(2,1)}, bf16[1024,512]{1,0:T(8,128)(2,1)}, u32[]{:S(2)}, u32[]{:S(2)}) %collective-permute-start.8) | collective-permute-done | bytes 1048608 | tf_op jit(solution)/shard_map/ppermute | solution.py:509
  105.9 1.2 collective-permute-done.18.refs_13_
  107.7 1.2 collective-permute-done.16.refs_12_
  111.6 9.2 %fusion.refs_24_ = f32[8,1024,512]{2,1,0:T(8,128)} fusion(f32[1024]{0:T(1024)S(1)} %div.190, f32[8,16,512]{2,1,0:T(8,128)} %bitcast.93), kind=kLoop, calls=%fused_computation.3 | loop fusion | flops 4194304 | bytes 17043456 | tf_op jit(solution)/shard_map/exp | solution.py:478
  121.8 20.0 %density.1 = (f32[8,1,512]{2,1,0:T(1,128)}, f32[32,24,128]{2,1,0:T(8,128)}) custom-call(s32[8]{0:T(128)} %fusion.10.order, s32[1]{0:T(128)} %bitcast.3.place, s32[64]{0:T(128)} %get-tuple-element.25.which, s32[64]{0:T(128)} %get-tuple-element.26.where, bf16[1024,512]{1,0:T(8,128)(2,1)} %bitcast.83, bf16[1024,512]{1,0:T(8,128)(2,1)} %bitcast.78, ...), custom_call_target="tpu_custom_call" | custom-call | flops 8589934592 | bytes 33554432 | tf_op jit(solution)/shard_map/density/pallas_call | solution.py:288
  142.9 7.0 %all-to-all-start = ((f32[32,24,128]{2,1,0:T(8,128)}), f32[32,24,128]{2,1,0:T(8,128)S(1)}, u32[]{:S(2)}, u32[]{:S(2)}) async-start(f32[32,24,128]{2,1,0:T(8,128)} %get-tuple-element.34), calls=%async_computation | async-start | bytes 786432 | tf_op jit(solution)/shard_map/all_to_all | solution.py:521
  150.0 7.4 %bitcast_divide_fusion.table = f32[8,1024,512]{2,1,0:T(8,128)} fusion(f32[1024]{0:T(1024)S(1)} %div.196, f32[8,16,512]{2,1,0:T(8,128)S(1)} %bitcast.92), kind=kLoop, calls=%fused_computation | loop fusion | flops 8388608 | bytes 17043456 | tf_op jit(solution)/shard_map/div | solution.py:480
  157.4 2.7 %all-to-all-done = f32[32,24,128]{2,1,0:T(8,128)S(1)} async-done(((f32[32,24,128]{2,1,0:T(8,128)}), f32[32,24,128]{2,1,0:T(8,128)S(1)}, u32[]{:S(2)}, u32[]{:S(2)}) %all-to-all-start) | async-done | bytes 393248 | tf_op jit(solution)/shard_map/all_to_all | solution.py:521
  160.8 7.7 %potential.1 = (f32[256,64]{1,0:T(8,128)}, f32[8,1,512]{2,1,0:T(1,128)}, f32[8,1,512]{2,1,0:T(1,128)}, f32[1,128]{1,0:T(1,128)}) custom-call(f32[8,1024,512]{2,1,0:T(8,128)} %bitcast_divide_fusion.table, f32[768,128]{1,0:T(8,128)} %bitcast.91, f32[32,128]{1,0:T(8,128)} %broadcast_in_dim.78.mine, f32[8,1,512]{2,1,0:T(1,128)} %bitcast.100, ...), custom_call_target="tpu_custom_call" | custom-call | flops 16777216 | bytes 16777216 | tf_op jit(solution)/shard_map/potential/pallas_call | solution.py:318
  171.1 20.3 %ham.1 = (f32[32,128,256]{2,1,0:T(8,128)}, f32[32,128,256]{2,1,0:T(8,128)}, f32[32,128,256]{2,1,0:T(8,128)}, f32[32,128,256]{2,1,0:T(8,128)}) custom-call(s32[8]{0:T(128)} %fusion.10.order, s32[64]{0:T(128)} %fusion.7.slots, s32[1]{0:T(128)} %bitcast.3.place, bf16[4,2,128,512]{3,2,1,0:T(8,128)(2,1)} %bitcast.84, bf16[4,2,128,512]{3,2,1,0:T(8,128)(2,1)} %bitcast.79, ...), custom_call_target="tpu_custom_call" | custom-call | flops 4294967296 | bytes 25165824 | tf_op jit(solution)/shard_map/ham/pallas_call | solution.py:343
  191.4 2.9 %multiply_convert_fusion = (f16[16,128,256]{2,1,0:T(8,128)(2,1)S(1)}, f16[16,128,256]{2,1,0:T(8,128)(2,1)S(1)}) fusion(f32[32,128,256]{2,1,0:T(8,128)} %get-tuple-element.41, f32[]{:T(128)} %bitcast.31), kind=kLoop, calls=%fused_computation.6 | loop fusion | flops 2097152 | bytes 6291460 | tf_op jit(solution)/shard_map/convert_element_type | solution.py:371
  194.3 1.1 collective-permute-start.38
  195.4 1.0 collective-permute-start.34
  197.8 0.8 copy-done.5
  199.1 10.0 %collective-permute-done.38 = f16[2,8,128,256]{3,2,1,0:T(8,128)(2,1)S(1)} collective-permute-done((f16[2,8,128,256]{3,2,1,0:T(8,128)(2,1)S(1)}, f16[2,8,128,256]{3,2,1,0:T(8,128)(2,1)S(1)}, u32[]{:S(2)}, u32[]{:S(2)}) %collective-permute-start.38) | collective-permute-done | bytes 1048608 | tf_op jit(solution)/shard_map/ppermute | solution.py:382
  209.6 2.3 collective-permute-start.39
  212.3 2.0 collective-permute-start.35
  214.8 7.9 %collective-permute-done.37 = f16[2,8,128,256]{3,2,1,0:T(8,128)(2,1)S(1)} collective-permute-done((f16[2,8,128,256]{3,2,1,0:T(8,128)(2,1)S(1)}, f16[2,8,128,256]{3,2,1,0:T(8,128)(2,1)S(1)}, u32[]{:S(2)}, u32[]{:S(2)}) %collective-permute-start.37) | collective-permute-done | bytes 1048608 | tf_op jit(solution)/shard_map/ppermute | solution.py:383
  222.7 1.8 collective-permute-done.39
  225.2 2.2 collective-permute-start.40
  227.4 1.3 collective-permute-start.42
  228.7 18.0 %collective-permute-done.36 = f16[2,8,128,256]{3,2,1,0:T(8,128)(2,1)S(1)} collective-permute-done((f16[2,8,128,256]{3,2,1,0:T(8,128)(2,1)S(1)}, f16[2,8,128,256]{3,2,1,0:T(8,128)(2,1)S(1)}, u32[]{:S(2)}, u32[]{:S(2)}) %collective-permute-start.36) | collective-permute-done | bytes 1048608 | tf_op jit(solution)/shard_map/ppermute | solution.py:384
  247.2 0.9 collective-permute-start.41
  248.1 9.6 %collective-permute-done.41 = f16[8,128,256]{2,1,0:T(8,128)(2,1)S(1)} collective-permute-done((f16[8,128,256]{2,1,0:T(8,128)(2,1)S(1)}, f16[8,128,256]{2,1,0:T(8,128)(2,1)S(1)}, u32[]{:S(2)}, u32[]{:S(2)}) %collective-permute-start.41) | collective-permute-done | bytes 524320 | tf_op jit(solution)/shard_map/ppermute | solution.py:394
  258.1 1.3 dynamic-slice_bitcast_fusion
  259.8 1.1 maximum_multiply_fusion
  (143 shorter events, 20.4 us)
Async XLA Ops:
  1.9 1.6 collective-permute-start
  5.5 13.6 %collective-permute-start.13 = (bf16[8,128,256]{2,1,0:T(8,128)(2,1)}, bf16[8,128,256]{2,1,0:T(8,128)(2,1)}, u32[]{:S(2)}, u32[]{:S(2)}) collective-permute-start(bf16[8,128,256]{2,1,0:T(8,128)(2,1)} %pad_maximum_fusion.1), channel_id=1, source_target_pairs={{0,64},{4,20},{8,72},{12,28},{16,80},{20,4},{24,88},{28,12},{32,96... | collective-permute-start | bytes 1572872 | tf_op jit(solution)/shard_map/ppermute | solution.py:441
  9.5 13.1 %collective-permute-start.14 = (bf16[8,128,256]{2,1,0:T(8,128)(2,1)}, bf16[8,128,256]{2,1,0:T(8,128)(2,1)}, u32[]{:S(2)}, u32[]{:S(2)}) collective-permute-start(bf16[8,128,256]{2,1,0:T(8,128)(2,1)} %pad_maximum_fusion.1), channel_id=1, source_target_pairs={{0,32},{4,12},{8,40},{12,20},{16,48},{20,28},{24,56},{28,4},{32,64... | collective-permute-start | bytes 1572872 | tf_op jit(solution)/shard_map/ppermute | solution.py:441
  10.5 16.9 %collective-permute-start.1 = (bf16[8,128,256]{2,1,0:T(8,128)(2,1)}, bf16[8,128,256]{2,1,0:T(8,128)(2,1)}, u32[]{:S(2)}, u32[]{:S(2)}) collective-permute-start(bf16[8,128,256]{2,1,0:T(8,128)(2,1)} %pad_maximum_fusion.1), channel_id=1, source_target_pairs={{0,96},{4,28},{8,104},{12,4},{16,112},{20,12},{24,120},{28,20},{32... | collective-permute-start | bytes 1572872 | tf_op jit(solution)/shard_map/ppermute | solution.py:441
  14.4 96.2 %copy-start = (bf16[512,1024]{0,1:T(8,128)(2,1)}, bf16[512,1024]{0,1:T(8,128)(2,1)S(1)}, u32[]{:S(2)}) copy-start(bf16[512,1024]{0,1:T(8,128)(2,1)S(1)} %copy.26) | copy-start | bytes 3145732
  14.4 50.3 %collective-permute-start.7 = (bf16[1024,512]{1,0:T(8,128)(2,1)S(1)}, bf16[1024,512]{1,0:T(8,128)(2,1)S(1)}, u32[]{:S(2)}, u32[]{:S(2)}) collective-permute-start(bf16[1024,512]{1,0:T(8,128)(2,1)S(1)} %bitcast.75), channel_id=1, source_target_pairs={{0,3},{1,0},{2,1},{3,2},{4,7},{5,4},{6,5},{7,6},{8,11},{9,8},{10,9... | collective-permute-start | bytes 3145736 | tf_op jit(solution)/shard_map/ppermute | solution.py:426
  17.5 49.3 %collective-permute-start.5 = (bf16[1024,512]{1,0:T(8,128)(2,1)S(1)}, bf16[1024,512]{1,0:T(8,128)(2,1)}, u32[]{:S(2)}, u32[]{:S(2)}) collective-permute-start(bf16[1024,512]{1,0:T(8,128)(2,1)S(1)} %bitcast.76), channel_id=1, source_target_pairs={{0,1},{1,2},{2,3},{3,0},{4,5},{5,6},{6,7},{7,4},{8,9},{9,10},{10,1... | collective-permute-start | bytes 3145736 | tf_op jit(solution)/shard_map/ppermute | solution.py:427
  19.1 91.0 %copy-start.1 = (bf16[512,1024]{0,1:T(8,128)(2,1)}, bf16[512,1024]{0,1:T(8,128)(2,1)S(1)}, u32[]{:S(2)}) copy-start(bf16[512,1024]{0,1:T(8,128)(2,1)S(1)} %copy.25) | copy-start | bytes 3145732
  19.1 45.3 %collective-permute-start.4 = (bf16[1024,512]{1,0:T(8,128)(2,1)S(1)}, bf16[1024,512]{1,0:T(8,128)(2,1)S(1)}, u32[]{:S(2)}, u32[]{:S(2)}) collective-permute-start(bf16[1024,512]{1,0:T(8,128)(2,1)S(1)} %bitcast.80), channel_id=1, source_target_pairs={{0,1},{1,2},{2,3},{3,0},{4,5},{5,6},{6,7},{7,4},{8,9},{9,10},{10,1... | collective-permute-start | bytes 3145736 | tf_op jit(solution)/shard_map/ppermute | solution.py:425
  21.9 89.7 %copy-start.21 = (f32[64]{0:T(128)S(1)}, f32[64]{0:T(128)}, u32[]{:S(2)}) copy-start(f32[64]{0:T(128)} %param.17) | copy-start | bytes 772
  22.6 1.9 collective-permute-start.3
  24.4 43.0 %collective-permute-start.6 = (bf16[1024,512]{1,0:T(8,128)(2,1)S(1)}, bf16[1024,512]{1,0:T(8,128)(2,1)}, u32[]{:S(2)}, u32[]{:S(2)}) collective-permute-start(bf16[1024,512]{1,0:T(8,128)(2,1)S(1)} %bitcast.81), channel_id=1, source_target_pairs={{0,3},{1,0},{2,1},{3,2},{4,7},{5,4},{6,5},{7,6},{8,11},{9,8},{10,9... | collective-permute-start | bytes 3145736 | tf_op jit(solution)/shard_map/ppermute | solution.py:428
  27.4 41.5 %collective-permute-start.17 = (bf16[16,128,256]{2,1,0:T(8,128)(2,1)}, bf16[16,128,256]{2,1,0:T(8,128)(2,1)}, u32[]{:S(2)}, u32[]{:S(2)}) collective-permute-start(bf16[16,128,256]{2,1,0:T(8,128)(2,1)} %constant_dynamic-update-slice_fusion.refs_9_), channel_id=1, source_target_pairs={{0,8},{4,36},{8,16},{12,44},{16,24},{20,52},{24,0},{28,60},{32,40}... | collective-permute-start | bytes 3145736 | tf_op jit(solution)/shard_map/ppermute | solution.py:496
  64.4 15.1 %collective-permute-start.15 = (bf16[16,128,256]{2,1,0:T(8,128)(2,1)}, bf16[16,128,256]{2,1,0:T(8,128)(2,1)}, u32[]{:S(2)}, u32[]{:S(2)}) collective-permute-start(bf16[16,128,256]{2,1,0:T(8,128)(2,1)} %constant_dynamic-update-slice_fusion.refs_9_), channel_id=1, source_target_pairs={{0,24},{4,100},{8,0},{12,108},{16,8},{20,116},{24,16},{28,124},{32... | collective-permute-start | bytes 3145736 | tf_op jit(solution)/shard_map/ppermute | solution.py:498
  64.7 14.8 %collective-permute-start.21 = (bf16[16,128,256]{2,1,0:T(8,128)(2,1)}, bf16[16,128,256]{2,1,0:T(8,128)(2,1)}, u32[]{:S(2)}, u32[]{:S(2)}) collective-permute-start(bf16[16,128,256]{2,1,0:T(8,128)(2,1)} %constant_dynamic-update-slice_fusion.refs_9_), channel_id=1, source_target_pairs={{0,4},{4,0},{8,12},{12,8},{16,20},{20,16},{24,28},{28,24},{32,36},... | collective-permute-start | bytes 3145736 | tf_op jit(solution)/shard_map/ppermute | solution.py:507
  66.8 24.0 %collective-permute-start.2 = (bf16[16,128,256]{2,1,0:T(8,128)(2,1)}, bf16[16,128,256]{2,1,0:T(8,128)(2,1)}, u32[]{:S(2)}, u32[]{:S(2)}) collective-permute-start(bf16[16,128,256]{2,1,0:T(8,128)(2,1)} %pad_maximum_fusion.refs_8_), channel_id=1, source_target_pairs={{0,24},{4,100},{8,0},{12,108},{16,8},{20,116},{24,16},{28,124},{32... | collective-permute-start | bytes 3145736 | tf_op jit(solution)/shard_map/ppermute | solution.py:495
  67.4 25.6 %collective-permute-start.19 = (bf16[16,128,256]{2,1,0:T(8,128)(2,1)}, bf16[16,128,256]{2,1,0:T(8,128)(2,1)}, u32[]{:S(2)}, u32[]{:S(2)}) collective-permute-start(bf16[16,128,256]{2,1,0:T(8,128)(2,1)} %pad_maximum_fusion.refs_8_), channel_id=1, source_target_pairs={{0,8},{4,36},{8,16},{12,44},{16,24},{20,52},{24,0},{28,60},{32,40}... | collective-permute-start | bytes 3145736 | tf_op jit(solution)/shard_map/ppermute | solution.py:497
  68.9 24.3 %collective-permute-start.20 = (bf16[16,128,256]{2,1,0:T(8,128)(2,1)}, bf16[16,128,256]{2,1,0:T(8,128)(2,1)}, u32[]{:S(2)}, u32[]{:S(2)}) collective-permute-start(bf16[16,128,256]{2,1,0:T(8,128)(2,1)} %pad_maximum_fusion.refs_8_), channel_id=1, source_target_pairs={{0,4},{4,0},{8,12},{12,8},{16,20},{20,16},{24,28},{28,24},{32,36},... | collective-permute-start | bytes 3145736 | tf_op jit(solution)/shard_map/ppermute | solution.py:507
  79.5 25.9 %collective-permute-start.8 = (bf16[1024,512]{1,0:T(8,128)(2,1)}, bf16[1024,512]{1,0:T(8,128)(2,1)}, u32[]{:S(2)}, u32[]{:S(2)}) collective-permute-start(bf16[1024,512]{1,0:T(8,128)(2,1)} %copy-done.3), channel_id=1, source_target_pairs={{0,1},{1,2},{2,3},{3,0},{4,5},{5,6},{6,7},{7,4},{8,9},{9,10},{10,1... | collective-permute-start | bytes 3145736 | tf_op jit(solution)/shard_map/ppermute | solution.py:509
  79.5 25.9 %collective-permute-start.9 = (bf16[1024,512]{1,0:T(8,128)(2,1)S(1)}, bf16[1024,512]{1,0:T(8,128)(2,1)}, u32[]{:S(2)}, u32[]{:S(2)}) collective-permute-start(bf16[1024,512]{1,0:T(8,128)(2,1)S(1)} %collective-permute-done.7.refs_5_), channel_id=1, source_target_pairs={{0,3},{1,0},{2,1},{3,2},{4,7},{5,4},{6,5},{7,6},{8,11},{9,8},{10,9... | collective-permute-start | bytes 3145736 | tf_op jit(solution)/shard_map/ppermute | solution.py:510
  90.8 16.3 %collective-permute-start.18 = (bf16[16,128,256]{2,1,0:T(8,128)(2,1)}, bf16[16,128,256]{2,1,0:T(8,128)(2,1)}, u32[]{:S(2)}, u32[]{:S(2)}) collective-permute-start(bf16[16,128,256]{2,1,0:T(8,128)(2,1)} %collective-permute-done.17.refs_15_), channel_id=1, source_target_pairs={{0,8},{4,36},{8,16},{12,44},{16,24},{20,52},{24,0},{28,60},{32,40}... | collective-permute-start | bytes 3145736 | tf_op jit(solution)/shard_map/ppermute | solution.py:503
  93.0 14.2 %collective-permute-start.23 = (bf16[16,128,256]{2,1,0:T(8,128)(2,1)}, bf16[16,128,256]{2,1,0:T(8,128)(2,1)}, u32[]{:S(2)}, u32[]{:S(2)}) collective-permute-start(bf16[16,128,256]{2,1,0:T(8,128)(2,1)} %collective-permute-done.15.refs_11_), channel_id=1, source_target_pairs={{0,4},{4,0},{8,12},{12,8},{16,20},{20,16},{24,28},{28,24},{32,36},... | collective-permute-start | bytes 3145736 | tf_op jit(solution)/shard_map/ppermute | solution.py:507
  93.2 15.7 %collective-permute-start.16 = (bf16[16,128,256]{2,1,0:T(8,128)(2,1)}, bf16[16,128,256]{2,1,0:T(8,128)(2,1)}, u32[]{:S(2)}, u32[]{:S(2)}) collective-permute-start(bf16[16,128,256]{2,1,0:T(8,128)(2,1)} %collective-permute-done.2.refs_10_), channel_id=1, source_target_pairs={{0,24},{4,100},{8,0},{12,108},{16,8},{20,116},{24,16},{28,124},{32... | collective-permute-start | bytes 3145736 | tf_op jit(solution)/shard_map/ppermute | solution.py:502
  105.4 4.6 %collective-permute-start.27 = (bf16[16,128,256]{2,1,0:T(8,128)(2,1)}, bf16[16,128,256]{2,1,0:T(8,128)(2,1)}, u32[]{:S(2)}, u32[]{:S(2)}) collective-permute-start(bf16[16,128,256]{2,1,0:T(8,128)(2,1)} %collective-permute-done.17.refs_15_), channel_id=1, source_target_pairs={{0,4},{4,0},{8,12},{12,8},{16,20},{20,16},{24,28},{28,24},{32,36},... | collective-permute-start | bytes 3145736 | tf_op jit(solution)/shard_map/ppermute | solution.py:507
  105.4 5.2 %collective-permute-start.22 = (bf16[16,128,256]{2,1,0:T(8,128)(2,1)}, bf16[16,128,256]{2,1,0:T(8,128)(2,1)}, u32[]{:S(2)}, u32[]{:S(2)}) collective-permute-start(bf16[16,128,256]{2,1,0:T(8,128)(2,1)} %collective-permute-done.2.refs_10_), channel_id=1, source_target_pairs={{0,4},{4,0},{8,12},{12,8},{16,20},{20,16},{24,28},{28,24},{32,36},... | collective-permute-start | bytes 3145736 | tf_op jit(solution)/shard_map/ppermute | solution.py:507
  107.1 4.3 %collective-permute-start.26 = (bf16[16,128,256]{2,1,0:T(8,128)(2,1)}, bf16[16,128,256]{2,1,0:T(8,128)(2,1)}, u32[]{:S(2)}, u32[]{:S(2)}) collective-permute-start(bf16[16,128,256]{2,1,0:T(8,128)(2,1)} %collective-permute-done.19.refs_14_), channel_id=1, source_target_pairs={{0,4},{4,0},{8,12},{12,8},{16,20},{20,16},{24,28},{28,24},{32,36},... | collective-permute-start | bytes 3145736 | tf_op jit(solution)/shard_map/ppermute | solution.py:507
  107.2 14.3 %collective-permute-start.25 = (bf16[16,128,256]{2,1,0:T(8,128)(2,1)}, bf16[16,128,256]{2,1,0:T(8,128)(2,1)}, u32[]{:S(2)}, u32[]{:S(2)}) collective-permute-start(bf16[16,128,256]{2,1,0:T(8,128)(2,1)} %collective-permute-done.18.refs_13_), channel_id=1, source_target_pairs={{0,4},{4,0},{8,12},{12,8},{16,20},{20,16},{24,28},{28,24},{32,36},... | collective-permute-start | bytes 3145736 | tf_op jit(solution)/shard_map/ppermute | solution.py:507
  108.9 12.8 %collective-permute-start.24 = (bf16[16,128,256]{2,1,0:T(8,128)(2,1)}, bf16[16,128,256]{2,1,0:T(8,128)(2,1)}, u32[]{:S(2)}, u32[]{:S(2)}) collective-permute-start(bf16[16,128,256]{2,1,0:T(8,128)(2,1)} %collective-permute-done.16.refs_12_), channel_id=1, source_target_pairs={{0,4},{4,0},{8,12},{12,8},{16,20},{20,16},{24,28},{28,24},{32,36},... | collective-permute-start | bytes 3145736 | tf_op jit(solution)/shard_map/ppermute | solution.py:507
  110.1 32.0 %collective-permute-start.10 = (bf16[1024,512]{1,0:T(8,128)(2,1)S(1)}, bf16[1024,512]{1,0:T(8,128)(2,1)}, u32[]{:S(2)}, u32[]{:S(2)}) collective-permute-start(bf16[1024,512]{1,0:T(8,128)(2,1)S(1)} %bitcast.82), channel_id=1, source_target_pairs={{0,4},{4,0},{8,12},{12,8},{16,20},{20,16},{24,28},{28,24},{32,36},... | collective-permute-start | bytes 3145736 | tf_op jit(solution)/shard_map/ppermute | solution.py:518
  110.6 31.8 %collective-permute-start.11 = (bf16[1024,512]{1,0:T(8,128)(2,1)S(1)}, bf16[1024,512]{1,0:T(8,128)(2,1)}, u32[]{:S(2)}, u32[]{:S(2)}) collective-permute-start(bf16[1024,512]{1,0:T(8,128)(2,1)S(1)} %bitcast.77), channel_id=1, source_target_pairs={{0,4},{4,0},{8,12},{12,8},{16,20},{20,16},{24,28},{28,24},{32,36},... | collective-permute-start | bytes 3145736 | tf_op jit(solution)/shard_map/ppermute | solution.py:518
  111.4 31.1 %collective-permute-start.12 = (bf16[1024,512]{1,0:T(8,128)(2,1)}, bf16[1024,512]{1,0:T(8,128)(2,1)}, u32[]{:S(2)}, u32[]{:S(2)}) collective-permute-start(bf16[1024,512]{1,0:T(8,128)(2,1)} %copy-done.3), channel_id=1, source_target_pairs={{0,4},{4,0},{8,12},{12,8},{16,20},{20,16},{24,28},{28,24},{32,36},... | collective-permute-start | bytes 3145736 | tf_op jit(solution)/shard_map/ppermute | solution.py:518
  121.4 47.2 %collective-permute-start.30 = (bf16[1024,512]{1,0:T(8,128)(2,1)S(1)}, bf16[1024,512]{1,0:T(8,128)(2,1)}, u32[]{:S(2)}, u32[]{:S(2)}) collective-permute-start(bf16[1024,512]{1,0:T(8,128)(2,1)S(1)} %collective-permute-done.7.refs_5_), channel_id=1, source_target_pairs={{0,4},{4,0},{8,12},{12,8},{16,20},{20,16},{24,28},{28,24},{32,36},... | collective-permute-start | bytes 3145736 | tf_op jit(solution)/shard_map/ppermute | solution.py:518
  141.8 28.3 %collective-permute-start.28 = (bf16[1024,512]{1,0:T(8,128)(2,1)}, bf16[1024,512]{1,0:T(8,128)(2,1)}, u32[]{:S(2)}, u32[]{:S(2)}) collective-permute-start(bf16[1024,512]{1,0:T(8,128)(2,1)} %collective-permute-done.5.refs_3_), channel_id=1, source_target_pairs={{0,4},{4,0},{8,12},{12,8},{16,20},{20,16},{24,28},{28,24},{32,36},... | collective-permute-start | bytes 3145736 | tf_op jit(solution)/shard_map/ppermute | solution.py:518
  142.0 28.1 %collective-permute-start.29 = (bf16[1024,512]{1,0:T(8,128)(2,1)}, bf16[1024,512]{1,0:T(8,128)(2,1)S(1)}, u32[]{:S(2)}, u32[]{:S(2)}) collective-permute-start(bf16[1024,512]{1,0:T(8,128)(2,1)} %collective-permute-done.6.refs_4_), channel_id=1, source_target_pairs={{0,4},{4,0},{8,12},{12,8},{16,20},{20,16},{24,28},{28,24},{32,36},... | collective-permute-start | bytes 3145736 | tf_op jit(solution)/shard_map/ppermute | solution.py:518
  142.4 27.7 %collective-permute-start.31 = (bf16[1024,512]{1,0:T(8,128)(2,1)}, bf16[1024,512]{1,0:T(8,128)(2,1)}, u32[]{:S(2)}, u32[]{:S(2)}) collective-permute-start(bf16[1024,512]{1,0:T(8,128)(2,1)} %collective-permute-done.8.refs_6_), channel_id=1, source_target_pairs={{0,4},{4,0},{8,12},{12,8},{16,20},{20,16},{24,28},{28,24},{32,36},... | collective-permute-start | bytes 3145736 | tf_op jit(solution)/shard_map/ppermute | solution.py:518
  142.5 27.6 %collective-permute-start.32 = (bf16[1024,512]{1,0:T(8,128)(2,1)}, bf16[1024,512]{1,0:T(8,128)(2,1)}, u32[]{:S(2)}, u32[]{:S(2)}) collective-permute-start(bf16[1024,512]{1,0:T(8,128)(2,1)} %collective-permute-done.9.refs_7_), channel_id=1, source_target_pairs={{0,4},{4,0},{8,12},{12,8},{16,20},{20,16},{24,28},{28,24},{32,36},... | collective-permute-start | bytes 3145736 | tf_op jit(solution)/shard_map/ppermute | solution.py:518
  142.9 17.2 %all-to-all-start = ((f32[32,24,128]{2,1,0:T(8,128)}), f32[32,24,128]{2,1,0:T(8,128)S(1)}, u32[]{:S(2)}, u32[]{:S(2)}) async-start(f32[32,24,128]{2,1,0:T(8,128)} %get-tuple-element.34), calls=%async_computation | async-start | bytes 786432 | tf_op jit(solution)/shard_map/all_to_all | solution.py:521
  168.6 1.5 collective-permute-start.33
  194.3 14.9 %collective-permute-start.38 = (f16[2,8,128,256]{3,2,1,0:T(8,128)(2,1)S(1)}, f16[2,8,128,256]{3,2,1,0:T(8,128)(2,1)S(1)}, u32[]{:S(2)}, u32[]{:S(2)}) collective-permute-start(f16[2,8,128,256]{3,2,1,0:T(8,128)(2,1)S(1)} %bitcast.96), channel_id=1, source_target_pairs={{0,96},{4,28},{8,104},{12,4},{16,112},{20,12},{24,120},{28,20},{32... | collective-permute-start | bytes 3145736 | tf_op jit(solution)/shard_map/ppermute | solution.py:382
  195.4 16.5 %collective-permute-start.34 = (f16[2,8,128,256]{3,2,1,0:T(8,128)(2,1)S(1)}, f16[2,8,128,256]{3,2,1,0:T(8,128)(2,1)S(1)}, u32[]{:S(2)}, u32[]{:S(2)}) collective-permute-start(f16[2,8,128,256]{3,2,1,0:T(8,128)(2,1)S(1)} %bitcast.95), channel_id=1, source_target_pairs={{0,32},{4,12},{8,40},{12,20},{16,48},{20,28},{24,56},{28,4},{32,64... | collective-permute-start | bytes 3145736 | tf_op jit(solution)/shard_map/ppermute | solution.py:381
  197.0 25.7 %collective-permute-start.37 = (f16[2,8,128,256]{3,2,1,0:T(8,128)(2,1)S(1)}, f16[2,8,128,256]{3,2,1,0:T(8,128)(2,1)S(1)}, u32[]{:S(2)}, u32[]{:S(2)}) collective-permute-start(f16[2,8,128,256]{3,2,1,0:T(8,128)(2,1)S(1)} %bitcast.98), channel_id=1, source_target_pairs={{0,32},{4,12},{8,40},{12,20},{16,48},{20,28},{24,56},{28,4},{32,64... | collective-permute-start | bytes 3145736 | tf_op jit(solution)/shard_map/ppermute | solution.py:383
  209.6 14.9 %collective-permute-start.39 = (f16[2,8,128,256]{3,2,1,0:T(8,128)(2,1)S(1)}, f16[2,8,128,256]{3,2,1,0:T(8,128)(2,1)S(1)}, u32[]{:S(2)}, u32[]{:S(2)}) collective-permute-start(f16[2,8,128,256]{3,2,1,0:T(8,128)(2,1)S(1)} %add_convert_fusion.1), channel_id=1, source_target_pairs={{0,96},{4,28},{8,104},{12,4},{16,112},{20,12},{24,120},{28,20},{32... | collective-permute-start | bytes 3145736 | tf_op jit(solution)/shard_map/ppermute | solution.py:386
  211.9 34.8 %collective-permute-start.36 = (f16[2,8,128,256]{3,2,1,0:T(8,128)(2,1)S(1)}, f16[2,8,128,256]{3,2,1,0:T(8,128)(2,1)S(1)}, u32[]{:S(2)}, u32[]{:S(2)}) collective-permute-start(f16[2,8,128,256]{3,2,1,0:T(8,128)(2,1)S(1)} %bitcast.97), channel_id=1, source_target_pairs={{0,96},{4,28},{8,104},{12,4},{16,112},{20,12},{24,120},{28,20},{32... | collective-permute-start | bytes 3145736 | tf_op jit(solution)/shard_map/ppermute | solution.py:384
  212.3 34.3 %collective-permute-start.35 = (f16[2,8,128,256]{3,2,1,0:T(8,128)(2,1)S(1)}, f16[2,8,128,256]{3,2,1,0:T(8,128)(2,1)S(1)}, u32[]{:S(2)}, u32[]{:S(2)}) collective-permute-start(f16[2,8,128,256]{3,2,1,0:T(8,128)(2,1)S(1)} %add_convert_fusion.2), channel_id=1, source_target_pairs={{0,32},{4,12},{8,40},{12,20},{16,48},{20,28},{24,56},{28,4},{32,64... | collective-permute-start | bytes 3145736 | tf_op jit(solution)/shard_map/ppermute | solution.py:385
  225.2 22.8 %collective-permute-start.40 = (f16[8,128,256]{2,1,0:T(8,128)(2,1)S(1)}, f16[8,128,256]{2,1,0:T(8,128)(2,1)S(1)}, u32[]{:S(2)}, u32[]{:S(2)}) collective-permute-start(f16[8,128,256]{2,1,0:T(8,128)(2,1)S(1)} %get-tuple-element.64), channel_id=1, source_target_pairs={{0,16},{4,68},{8,24},{12,76},{16,0},{20,84},{24,8},{28,92},{32,48}... | collective-permute-start | bytes 1572872 | tf_op jit(solution)/shard_map/ppermute | solution.py:394
  227.4 20.7 %collective-permute-start.42 = (f16[8,128,256]{2,1,0:T(8,128)(2,1)S(1)}, f16[8,128,256]{2,1,0:T(8,128)(2,1)S(1)}, u32[]{:S(2)}, u32[]{:S(2)}) collective-permute-start(f16[8,128,256]{2,1,0:T(8,128)(2,1)S(1)} %get-tuple-element.65), channel_id=1, source_target_pairs={{0,24},{4,100},{8,0},{12,108},{16,8},{20,116},{24,16},{28,124},{32... | collective-permute-start | bytes 1572872 | tf_op jit(solution)/shard_map/ppermute | solution.py:394
  247.2 10.5 %collective-permute-start.41 = (f16[8,128,256]{2,1,0:T(8,128)(2,1)S(1)}, f16[8,128,256]{2,1,0:T(8,128)(2,1)S(1)}, u32[]{:S(2)}, u32[]{:S(2)}) collective-permute-start(f16[8,128,256]{2,1,0:T(8,128)(2,1)S(1)} %fusion.6), channel_id=1, source_target_pairs={{0,8},{4,36},{8,16},{12,44},{16,24},{20,52},{24,0},{28,60},{32,40}... | collective-permute-start | bytes 1572872 | tf_op jit(solution)/shard_map/ppermute | solution.py:394
  258.0 1.6 collective-permute-start.43
  (19 other events, 401.5 us)

commit v12 on v10

--- a/solution.py
+++ b/solution.py
@@ -7,6 +7,7 @@
 
 
 SOFTEN = 0.25
+EARLY_SWAPS = (0, 1, 2, 5)
 ROOT_TWO = 1.4142135623730951
 HALF = 512
 PIECES = 8
@@ -214,7 +215,7 @@
 def ham_body(order, slots, place, *refs):
     chunks = refs[: 2 * CHUNKS]
     scale_mine, scale_beside, *rest = refs[2 * CHUNKS :]
-    outs, (dense, held, rows_of, psem, osem) = rest[:4], rest[4:]
+    outs, (dense, held, rows_of, psem, osem) = rest[:8], rest[8:]
     core = place[0]
     for side in range(2):
         i = 0
@@ -264,10 +265,10 @@
         return 0
 
     lax.fori_loop(0, 8, step, 0)
-    for d in range(4):
-        pltpu.make_async_copy(dense.at[pl.ds(d * 32, 32)], outs[d], osem.at[d]).start()
-    for d in range(4):
-        pltpu.make_async_copy(dense.at[pl.ds(d * 32, 32)], outs[d], osem.at[d]).wait()
+    for d in range(8):
+        pltpu.make_async_copy(dense.at[pl.ds(d * 16, 16)], outs[d], osem.at[d]).start()
+    for d in range(8):
+        pltpu.make_async_copy(dense.at[pl.ds(d * 16, 16)], outs[d], osem.at[d]).wait()
 
 
 def any_spec():
@@ -341,15 +342,15 @@
 def ham_call(order, slots, place, chunks, scale_mine, scale_beside):
     return pl.pallas_call(
         ham_body,
-        out_shape=(jax.ShapeDtypeStruct((32, 128, BLK), jnp.float32),) * 4,
+        out_shape=(jax.ShapeDtypeStruct((16, 128, BLK), jnp.float32),) * 8,
         in_specs=[smem_spec()] * 3 + [any_spec()] * (2 * CHUNKS) + [vmem_spec()] * 2,
-        out_specs=(any_spec(),) * 4,
+        out_specs=(any_spec(),) * 8,
         scratch_shapes=[
             pltpu.VMEM((128, 128, BLK), jnp.float32),
             pltpu.VMEM((2, 2, 2, NB, 128, 4 * HALF), jnp.bfloat16),
             pltpu.VMEM((2, 2, 1, 4 * HALF), jnp.float32),
             pltpu.SemaphoreType.DMA((4,)),
-            pltpu.SemaphoreType.DMA((4,)),
+            pltpu.SemaphoreType.DMA((8,)),
         ],
         compiler_params=pltpu.CompilerParams(vmem_limit_bytes=VMEM_GRANT),
         cost_estimate=pl.CostEstimate(
@@ -374,17 +375,16 @@
     return x.astype(jnp.float32)
 
 
-def ring_sum(parts, factor):
-    half = parts[2].shape[0] // 2
+def ring_sum(low, high, factor):
     up, down = core_perm(1, False), core_perm(-1, False)
-    from_below = lax.ppermute(cast(parts[2][:half] * factor), "grid", up)
-    from_above = lax.ppermute(cast(parts[2][half:] * factor), "grid", down)
-    below_high = lax.ppermute(cast(parts[1][half:] * factor), "grid", up)
-    above_low = lax.ppermute(cast(parts[3][:half] * factor), "grid", down)
-    below_low = lax.ppermute(cast(parts[1][:half] * factor + wide(from_below)), "grid", up)
-    above_high = lax.ppermute(cast(parts[3][half:] * factor + wide(from_above)), "grid", down)
-    low = parts[0][:half] * factor + wide(below_low) + wide(above_low)
-    high = parts[0][half:] * factor + wide(below_high) + wide(above_high)
+    from_below = lax.ppermute(cast(low[2] * factor), "grid", up)
+    from_above = lax.ppermute(cast(high[2] * factor), "grid", down)
+    below_high = lax.ppermute(cast(high[1] * factor), "grid", up)
+    above_low = lax.ppermute(cast(low[3] * factor), "grid", down)
+    below_low = lax.ppermute(cast(low[1] * factor + wide(from_below)), "grid", up)
+    above_high = lax.ppermute(cast(high[3] * factor + wide(from_above)), "grid", down)
+    low = low[0] * factor + wide(below_low) + wide(above_low)
+    high = high[0] * factor + wide(below_high) + wide(above_high)
     return [low[0], low[1], high[0], high[1]]
 
 
@@ -486,15 +486,15 @@
     my_homes = jnp.broadcast_to(home_floats[:, None], (slots_here, 128))
 
     back, forth = core_perm(-1, True), core_perm(1, True)
-    near = jnp.concatenate([base, ring_tiles[0]], axis=0)
+    first, slots, home_rows, my_homes, which, where = lax.optimization_barrier(
+        (ring_tiles[0], slots, home_rows, my_homes, which, where)
+    )
+    near = jnp.concatenate([base, first], axis=0)
     other = jnp.concatenate([ring_tiles[1], ring_tiles[2]], axis=0)
     near_ahead = lax.ppermute(near, "grid", back)
     other_behind = lax.ppermute(other, "grid", forth)
     near_behind = lax.ppermute(near, "grid", forth)
     other_ahead = lax.ppermute(other, "grid", back)
-    near_ahead, slots, home_rows, my_homes, which, where = lax.optimization_barrier(
-        (near_ahead, slots, home_rows, my_homes, which, where)
-    )
     near_far = lax.ppermute(near_ahead, "grid", back)
     other_far = lax.ppermute(other_behind, "grid", forth)
     sources = [
@@ -510,7 +510,10 @@
         order, core_place, which, where, chunks, sources, gauss, weights, xc, home_rows
     )
     distance, sent, later = lax.optimization_barrier((distance, sent, chunks))
-    beside = [lax.ppermute(chunk, "grid", swap) for chunk in later]
+    beside = [
+        lax.ppermute(chunks[i] if i in EARLY_SWAPS else later[i], "grid", swap)
+        for i in range(CHUNKS)
+    ]
     hart = (lax.erf(distance / erf_scale) / distance).reshape(
         PIECES, neighbors * moments, HALF
     )
@@ -532,8 +535,8 @@
         scale.reshape(2, 1, 4 * HALF),
         scale_beside.reshape(2, 1, 4 * HALF),
     )
-    dense = [d.reshape(4, 2 * tile_dev, 128, BLK) for d in dense]
-    chip = direct_sum(ring_sum(dense, factor))
+    dense = [d.reshape(2, 2 * tile_dev, 128, BLK) for d in dense]
+    chip = direct_sum(ring_sum(dense[0::2], dense[1::2], factor))
     chip = chip.reshape(2, tile_dev, 128, BLK)
     keep = jnp.where(first_core, chip[0], chip[1])
     give = jnp.where(first_core, chip[1], chip[0])

time: 265 us -> 265 us (level)
  local copies, waits for them, and re-layouts: 13.2 us -> 19 us
  other arithmetic: 33.8 us -> 30.6 us
    ppermute x1, waiting for transfers between devices: 19.4 us -> 0.01 us  [one_device(): below1 = lax.ppermute(own1, 'pert', ring(1))]
    ppermute x1, waiting for transfers between devices: 4.02 us -> 20.1 us  [one_device(): below0 = lax.ppermute(own0, 'pert', ring(1))]
    ppermute x1, waiting for transfers between devices: 0.01 us -> 11.3 us  [one_device(): other_ahead = lax.ppermute(other, 'grid', back)]
    ppermute x1, waiting for transfers between devices: 0.01 us -> 9.76 us  [one_device(): near_ahead = lax.ppermute(near, 'grid', back)]
    ppermute x1, waiting for transfers between devices: 9.49 us -> 0.01 us  [one_device(): near_behind = lax.ppermute(near, 'grid', forth)]
    ppermute x1, waiting for transfers between devices: 1.41 us -> 9.91 us  [one_device(): far1 = lax.ppermute(above1, 'pert', ring(3))]
    ppermute x1, waiting for transfers between devices: 6.19 us -> 0.01 us  [one_device(): above1 = lax.ppermute(own1, 'pert', ring(3))]
    unnamed x57 -> x63, local copies, waits for them, and re-layouts: 7.36 us -> 11.6 us
  transfers between devices with their start and end apart: 45 -> 45, of which waited for: 25 -> 15; matrix products, arithmetic and copies ran while one was open for 14% -> 14% of each run, Pallas kernels for 3% -> 11%
where the time goes in v12:
time: 265 us; the launch traced here: 263 us
  waiting for transfers between devices  117 us (44%)
  Pallas kernels  48.1 us (18%)
  starting transfers between devices  46.8 us (18%)
  other arithmetic  30.6 us (12%)
  local copies, waits for them, and re-layouts  19 us (7%)
    pallas_call x1, Pallas kernels, ham_call(): pl.pallas_call(ham_body, out_shape=(jax.ShapeDtypeStruct((16, 128, BLK),...  20.4 us
    ppermute x1, waiting for transfers between devices, one_device(): below0 = lax.ppermute(own0, 'pert', ring(1))  20.1 us
    pallas_call x1, Pallas kernels, density_call(): pl.pallas_call(density_body, out_shape=(jax.ShapeDtypeStruct((PIECES, 1,...  20 us
    ppermute x1, waiting for transfers between devices, ring_sum(): above_low = lax.ppermute(cast(low[3] * factor), 'grid', down)  15.9 us
    unnamed x63, local copies, waits for them, and re-layouts  11.6 us
    ppermute x1, waiting for transfers between devices, one_device(): other_ahead = lax.ppermute(other, 'grid', back)  11.3 us
    ppermute x1, waiting for transfers between devices, one_device(): far0 = lax.ppermute(below0, 'pert', ring(1))  11.1 us
    ppermute x1, waiting for transfers between devices, one_device(): far1 = lax.ppermute(above1, 'pert', ring(3))  9.91 us
  transfers between devices with their start and end apart: 45, of which 15 were waited for; matrix products, arithmetic and copies ran while one was open for 14% of the time, Pallas kernels for 11%

profile of v12, /device:TPU:0, one launch (start us, length us, event | category | flops | bytes accessed | tf_op | source)
XLA Modules:
  0.0 262.9 jit_solution(4463735394967069718)
XLA Ops:
  0.6 1.1 select_bitcast_fusion
  1.8 2.7 %fusion.25 = (bf16[512,1024]{1,0:T(8,128)(2,1)S(1)}, bf16[512,1024]{1,0:T(8,128)(2,1)}) fusion(bf16[1024,1024]{1,0:T(8,128)(2,1)} %param.13), kind=kLoop, calls=%fused_computation.138 | loop fusion | bytes 4194304 | tf_op jit(solution)/shard_map/slice | solution.py:423
  5.1 3.2 %collective-permute-start.6 = (bf16[1024,512]{1,0:T(8,128)(2,1)S(1)}, bf16[1024,512]{1,0:T(8,128)(2,1)S(1)}, u32[]{:S(2)}, u32[]{:S(2)}) collective-permute-start(bf16[1024,512]{1,0:T(8,128)(2,1)S(1)} %bitcast.76), channel_id=1, source_target_pairs={{0,3},{1,0},{2,1},{3,2},{4,7},{5,4},{6,5},{7,6},{8,11},{9,8},{10,9... | collective-permute-start | bytes 3145736 | tf_op jit(solution)/shard_map/ppermute | solution.py:425
  9.5 3.9 %collective-permute-start.12 = (bf16[8,128,256]{2,1,0:T(8,128)(2,1)}, bf16[8,128,256]{2,1,0:T(8,128)(2,1)}, u32[]{:S(2)}, u32[]{:S(2)}) collective-permute-start(bf16[8,128,256]{2,1,0:T(8,128)(2,1)} %pad_maximum_fusion.1), channel_id=1, source_target_pairs={{0,64},{4,20},{8,72},{12,28},{16,80},{20,4},{24,88},{28,12},{32,96... | collective-permute-start | bytes 1572872 | tf_op jit(solution)/shard_map/ppermute | solution.py:440
  13.4 1.1 collective-permute-start.13
  14.5 2.2 collective-permute-start.1
  16.8 1.5 copy.25
  18.3 2.6 %collective-permute-done.12 = bf16[8,128,256]{2,1,0:T(8,128)(2,1)} collective-permute-done((bf16[8,128,256]{2,1,0:T(8,128)(2,1)}, bf16[8,128,256]{2,1,0:T(8,128)(2,1)}, u32[]{:S(2)}, u32[]{:S(2)}) %collective-permute-start.12) | collective-permute-done | bytes 524320 | tf_op jit(solution)/shard_map/ppermute | solution.py:440
  21.5 1.9 constant_dynamic-update-slice_fusion.1
  23.4 3.0 %collective-permute-done.13 = bf16[8,128,256]{2,1,0:T(8,128)(2,1)} collective-permute-done((bf16[8,128,256]{2,1,0:T(8,128)(2,1)}, bf16[8,128,256]{2,1,0:T(8,128)(2,1)}, u32[]{:S(2)}, u32[]{:S(2)}) %collective-permute-start.13) | collective-permute-done | bytes 524320 | tf_op jit(solution)/shard_map/ppermute | solution.py:440
  26.5 1.8 constant_dynamic-update-slice_fusion.refs_9_
  28.3 3.2 %collective-permute-start.5 = (bf16[1024,512]{1,0:T(8,128)(2,1)S(1)}, bf16[1024,512]{1,0:T(8,128)(2,1)}, u32[]{:S(2)}, u32[]{:S(2)}) collective-permute-start(bf16[1024,512]{1,0:T(8,128)(2,1)S(1)} %bitcast.82), channel_id=1, source_target_pairs={{0,3},{1,0},{2,1},{3,2},{4,7},{5,4},{6,5},{7,6},{8,11},{9,8},{10,9... | collective-permute-start | bytes 3145736 | tf_op jit(solution)/shard_map/ppermute | solution.py:427
  31.6 1.5 collective-permute-start.17
  36.0 1.2 pad_maximum_fusion.refs_8_
  37.2 20.1 %collective-permute-done.3.refs_2_ = bf16[1024,512]{1,0:T(8,128)(2,1)} collective-permute-done((bf16[1024,512]{1,0:T(8,128)(2,1)S(1)}, bf16[1024,512]{1,0:T(8,128)(2,1)}, u32[]{:S(2)}, u32[]{:S(2)}) %collective-permute-start.3) | collective-permute-done | bytes 1048608 | tf_op jit(solution)/shard_map/ppermute | solution.py:424
  57.3 2.8 %collective-permute-start.14 = (bf16[16,128,256]{2,1,0:T(8,128)(2,1)S(1)}, bf16[16,128,256]{2,1,0:T(8,128)(2,1)}, u32[]{:S(2)}, u32[]{:S(2)}) collective-permute-start(bf16[16,128,256]{2,1,0:T(8,128)(2,1)S(1)} %pad_maximum_fusion.refs_8_), channel_id=1, source_target_pairs={{0,24},{4,100},{8,0},{12,108},{16,8},{20,116},{24,16},{28,124},{32... | collective-permute-start | bytes 3145736 | tf_op jit(solution)/shard_map/ppermute | solution.py:494
  60.9 1.2 collective-permute-start.19
  62.6 9.8 %collective-permute-done.14.refs_10_ = bf16[16,128,256]{2,1,0:T(8,128)(2,1)} collective-permute-done((bf16[16,128,256]{2,1,0:T(8,128)(2,1)S(1)}, bf16[16,128,256]{2,1,0:T(8,128)(2,1)}, u32[]{:S(2)}, u32[]{:S(2)}) %collective-permute-start.14) | collective-permute-done | bytes 1048608 | tf_op jit(solution)/shard_map/ppermute | solution.py:494
  72.4 11.3 %collective-permute-done.15.refs_11_ = bf16[16,128,256]{2,1,0:T(8,128)(2,1)} collective-permute-done((bf16[16,128,256]{2,1,0:T(8,128)(2,1)}, bf16[16,128,256]{2,1,0:T(8,128)(2,1)}, u32[]{:S(2)}, u32[]{:S(2)}) %collective-permute-start.15) | collective-permute-done | bytes 1048608 | tf_op jit(solution)/shard_map/ppermute | solution.py:497
  83.7 1.2 collective-permute-start.18
  85.0 2.6 collective-permute-start.16
  87.5 11.1 %collective-permute-done.7.refs_6_ = bf16[1024,512]{1,0:T(8,128)(2,1)S(1)} collective-permute-done((bf16[1024,512]{1,0:T(8,128)(2,1)}, bf16[1024,512]{1,0:T(8,128)(2,1)S(1)}, u32[]{:S(2)}, u32[]{:S(2)}) %collective-permute-start.7) | collective-permute-done | bytes 1048608 | tf_op jit(solution)/shard_map/ppermute | solution.py:505
  98.7 9.9 %collective-permute-done.8.refs_7_ = bf16[1024,512]{1,0:T(8,128)(2,1)S(1)} collective-permute-done((bf16[1024,512]{1,0:T(8,128)(2,1)S(1)}, bf16[1024,512]{1,0:T(8,128)(2,1)S(1)}, u32[]{:S(2)}, u32[]{:S(2)}) %collective-permute-start.8) | collective-permute-done | bytes 1048608 | tf_op jit(solution)/shard_map/ppermute | solution.py:506
  108.6 1.0 copy-done.4
  109.6 1.0 copy-done.18
  113.8 9.2 %fusion.refs_24_ = f32[8,1024,512]{2,1,0:T(8,128)} fusion(f32[1024]{0:T(1024)S(1)} %div.192, f32[8,16,512]{2,1,0:T(8,128)} %bitcast.95), kind=kLoop, calls=%fused_computation.3 | loop fusion | flops 4194304 | bytes 17043456 | tf_op jit(solution)/shard_map/exp | solution.py:477
  124.0 20.0 %density.1 = (f32[8,1,512]{2,1,0:T(1,128)}, f32[32,24,128]{2,1,0:T(8,128)}) custom-call(s32[8]{0:T(128)} %fusion.10.order, s32[1]{0:T(128)} %bitcast.3.place, s32[64]{0:T(128)} %get-tuple-element.30.which, s32[64]{0:T(128)} %get-tuple-element.31.where, bf16[1024,512]{1,0:T(8,128)(2,1)} %bitcast.84, bf16[1024,512]{1,0:T(8,128)(2,1)} %bitcast.79, ...), custom_call_target="tpu_custom_call" | custom-call | flops 8589934592 | bytes 33554432 | tf_op jit(solution)/shard_map/density/pallas_call | solution.py:288
  145.1 7.7 %all-to-all-start = ((f32[32,24,128]{2,1,0:T(8,128)}), f32[32,24,128]{2,1,0:T(8,128)S(1)}, u32[]{:S(2)}, u32[]{:S(2)}) async-start(f32[32,24,128]{2,1,0:T(8,128)} %get-tuple-element.40), calls=%async_computation | async-start | bytes 786432 | tf_op jit(solution)/shard_map/all_to_all | solution.py:520
  152.9 7.4 %bitcast_divide_fusion.table = f32[8,1024,512]{2,1,0:T(8,128)} fusion(f32[1024]{0:T(1024)S(1)} %div.199, f32[8,16,512]{2,1,0:T(8,128)S(1)} %bitcast.94), kind=kLoop, calls=%fused_computation | loop fusion | flops 8388608 | bytes 17043456 | tf_op jit(solution)/shard_map/div | solution.py:517
  160.3 2.7 %all-to-all-done = f32[32,24,128]{2,1,0:T(8,128)S(1)} async-done(((f32[32,24,128]{2,1,0:T(8,128)}), f32[32,24,128]{2,1,0:T(8,128)S(1)}, u32[]{:S(2)}, u32[]{:S(2)}) %all-to-all-start) | async-done | bytes 393248 | tf_op jit(solution)/shard_map/all_to_all | solution.py:520
  163.8 7.7 %potential.1 = (f32[256,64]{1,0:T(8,128)}, f32[8,1,512]{2,1,0:T(1,128)}, f32[8,1,512]{2,1,0:T(1,128)}, f32[1,128]{1,0:T(1,128)}) custom-call(f32[8,1024,512]{2,1,0:T(8,128)} %bitcast_divide_fusion.table, f32[768,128]{1,0:T(8,128)} %bitcast.93, f32[32,128]{1,0:T(8,128)} %broadcast_in_dim.78.mine, f32[8,1,512]{2,1,0:T(1,128)} %bitcast.102, ...), custom_call_target="tpu_custom_call" | custom-call | flops 16777216 | bytes 16777216 | tf_op jit(solution)/shard_map/potential/pallas_call | solution.py:318
  174.0 20.4 %ham.1 = (f32[16,128,256]{2,1,0:T(8,128)}, f32[16,128,256]{2,1,0:T(8,128)}, f32[16,128,256]{2,1,0:T(8,128)}, f32[16,128,256]{2,1,0:T(8,128)}, f32[16,128,256]{2,...) custom-call(s32[8]{0:T(128)} %fusion.10.order, s32[64]{0:T(128)} %fusion.7.slots, ...), custom_call_target="tpu_custom_call" | custom-call | flops 4294967296 | bytes 25165824 | tf_op jit(solution)/shard_map/ham/pallas_call | solution.py:343
  194.4 2.0 multiply_convert_fusion
  196.4 1.1 collective-permute-start.38
  197.8 1.0 collective-permute-start.37
  200.1 1.4 copy-done.10
  201.7 9.5 %collective-permute-done.38 = f16[2,8,128,256]{3,2,1,0:T(8,128)(2,1)S(1)} collective-permute-done((f16[2,8,128,256]{3,2,1,0:T(8,128)(2,1)S(1)}, f16[2,8,128,256]{3,2,1,0:T(8,128)(2,1)S(1)}, u32[]{:S(2)}, u32[]{:S(2)}) %collective-permute-start.38) | collective-permute-done | bytes 1048608 | tf_op jit(solution)/shard_map/ppermute | solution.py:381
  211.7 2.3 collective-permute-start.39
  214.3 1.2 collective-permute-start.36
  215.5 9.7 %collective-permute-done.34 = f16[2,8,128,256]{3,2,1,0:T(8,128)(2,1)S(1)} collective-permute-done((f16[2,8,128,256]{3,2,1,0:T(8,128)(2,1)S(1)}, f16[2,8,128,256]{3,2,1,0:T(8,128)(2,1)S(1)}, u32[]{:S(2)}, u32[]{:S(2)}) %collective-permute-start.34) | collective-permute-done | bytes 1048608 | tf_op jit(solution)/shard_map/ppermute | solution.py:380
  225.6 1.1 copy-done.8
  226.9 1.4 copy-done.7
  229.3 2.4 collective-permute-start.40
  231.7 1.2 collective-permute-start.42
  232.9 15.9 %collective-permute-done.36 = f16[2,8,128,256]{3,2,1,0:T(8,128)(2,1)S(1)} collective-permute-done((f16[2,8,128,256]{3,2,1,0:T(8,128)(2,1)S(1)}, f16[2,8,128,256]{3,2,1,0:T(8,128)(2,1)S(1)}, u32[]{:S(2)}, u32[]{:S(2)}) %collective-permute-start.36) | collective-permute-done | bytes 1048608 | tf_op jit(solution)/shard_map/ppermute | solution.py:383
  250.2 9.6 %collective-permute-done.41 = f16[8,128,256]{2,1,0:T(8,128)(2,1)S(1)} collective-permute-done((f16[8,128,256]{2,1,0:T(8,128)(2,1)S(1)}, f16[8,128,256]{2,1,0:T(8,128)(2,1)S(1)}, u32[]{:S(2)}, u32[]{:S(2)}) %collective-permute-start.41) | collective-permute-done | bytes 524320 | tf_op jit(solution)/shard_map/ppermute | solution.py:393
  260.2 1.3 dynamic-slice_bitcast_fusion
  261.9 1.1 maximum_multiply_fusion
  (163 shorter events, 20.9 us)
Async XLA Ops:
  1.7 6.8 %collective-permute-start = (bf16[4,128,256]{2,1,0:T(8,128)(2,1)S(1)}, bf16[4,128,256]{2,1,0:T(8,128)(2,1)S(1)}, u32[]{:S(2)}, u32[]{:S(2)}) collective-permute-start(bf16[4,128,256]{2,1,0:T(8,128)(2,1)S(1)} %select_bitcast_fusion), channel_id=1, source_target_pairs={{0,4},{4,0},{8,12},{12,8},{16,20},{20,16},{24,28},{28,24},{32,36},... | collective-permute-start | bytes 786440 | tf_op jit(solution)/shard_map/ppermute | solution.py:436
  5.0 107.8 %copy-start = (bf16[512,1024]{0,1:T(8,128)(2,1)}, bf16[512,1024]{0,1:T(8,128)(2,1)S(1)}, u32[]{:S(2)}) copy-start(bf16[512,1024]{0,1:T(8,128)(2,1)S(1)} %copy.26) | copy-start | bytes 3145732
  5.1 55.0 %collective-permute-start.6 = (bf16[1024,512]{1,0:T(8,128)(2,1)S(1)}, bf16[1024,512]{1,0:T(8,128)(2,1)S(1)}, u32[]{:S(2)}, u32[]{:S(2)}) collective-permute-start(bf16[1024,512]{1,0:T(8,128)(2,1)S(1)} %bitcast.76), channel_id=1, source_target_pairs={{0,3},{1,0},{2,1},{3,2},{4,7},{5,4},{6,5},{7,6},{8,11},{9,8},{10,9... | collective-permute-start | bytes 3145736 | tf_op jit(solution)/shard_map/ppermute | solution.py:425
  8.2 52.7 %collective-permute-start.4 = (bf16[1024,512]{1,0:T(8,128)(2,1)S(1)}, bf16[1024,512]{1,0:T(8,128)(2,1)}, u32[]{:S(2)}, u32[]{:S(2)}) collective-permute-start(bf16[1024,512]{1,0:T(8,128)(2,1)S(1)} %bitcast.77), channel_id=1, source_target_pairs={{0,1},{1,2},{2,3},{3,0},{4,5},{5,6},{6,7},{7,4},{8,9},{9,10},{10,1... | collective-permute-start | bytes 3145736 | tf_op jit(solution)/shard_map/ppermute | solution.py:426
  9.5 11.4 %collective-permute-start.12 = (bf16[8,128,256]{2,1,0:T(8,128)(2,1)}, bf16[8,128,256]{2,1,0:T(8,128)(2,1)}, u32[]{:S(2)}, u32[]{:S(2)}) collective-permute-start(bf16[8,128,256]{2,1,0:T(8,128)(2,1)} %pad_maximum_fusion.1), channel_id=1, source_target_pairs={{0,64},{4,20},{8,72},{12,28},{16,80},{20,4},{24,88},{28,12},{32,96... | collective-permute-start | bytes 1572872 | tf_op jit(solution)/shard_map/ppermute | solution.py:440
  13.4 13.0 %collective-permute-start.13 = (bf16[8,128,256]{2,1,0:T(8,128)(2,1)}, bf16[8,128,256]{2,1,0:T(8,128)(2,1)}, u32[]{:S(2)}, u32[]{:S(2)}) collective-permute-start(bf16[8,128,256]{2,1,0:T(8,128)(2,1)} %pad_maximum_fusion.1), channel_id=1, source_target_pairs={{0,32},{4,12},{8,40},{12,20},{16,48},{20,28},{24,56},{28,4},{32,64... | collective-permute-start | bytes 1572872 | tf_op jit(solution)/shard_map/ppermute | solution.py:440
  14.5 17.1 %collective-permute-start.1 = (bf16[8,128,256]{2,1,0:T(8,128)(2,1)}, bf16[8,128,256]{2,1,0:T(8,128)(2,1)}, u32[]{:S(2)}, u32[]{:S(2)}) collective-permute-start(bf16[8,128,256]{2,1,0:T(8,128)(2,1)} %pad_maximum_fusion.1), channel_id=1, source_target_pairs={{0,96},{4,28},{8,104},{12,4},{16,112},{20,12},{24,120},{28,20},{32... | collective-permute-start | bytes 1572872 | tf_op jit(solution)/shard_map/ppermute | solution.py:440
  18.3 94.2 %copy-start.1 = (bf16[512,1024]{0,1:T(8,128)(2,1)}, bf16[512,1024]{0,1:T(8,128)(2,1)S(1)}, u32[]{:S(2)}) copy-start(bf16[512,1024]{0,1:T(8,128)(2,1)S(1)} %copy.25) | copy-start | bytes 3145732
  21.0 90.5 %copy-start.23 = (f32[3,256]{1,0:T(4,128)S(1)}, f32[3,256]{1,0:T(4,128)}, u32[]{:S(2)}) copy-start(f32[3,256]{1,0:T(4,128)} %param.18) | copy-start | bytes 9220
  21.0 36.4 %collective-permute-start.3 = (bf16[1024,512]{1,0:T(8,128)(2,1)S(1)}, bf16[1024,512]{1,0:T(8,128)(2,1)}, u32[]{:S(2)}, u32[]{:S(2)}) collective-permute-start(bf16[1024,512]{1,0:T(8,128)(2,1)S(1)} %bitcast.81), channel_id=1, source_target_pairs={{0,1},{1,2},{2,3},{3,0},{4,5},{5,6},{6,7},{7,4},{8,9},{9,10},{10,1... | collective-permute-start | bytes 3145736 | tf_op jit(solution)/shard_map/ppermute | solution.py:424
  26.5 1.9 collective-permute-start.2
  28.3 33.8 %collective-permute-start.5 = (bf16[1024,512]{1,0:T(8,128)(2,1)S(1)}, bf16[1024,512]{1,0:T(8,128)(2,1)}, u32[]{:S(2)}, u32[]{:S(2)}) collective-permute-start(bf16[1024,512]{1,0:T(8,128)(2,1)S(1)} %bitcast.82), channel_id=1, source_target_pairs={{0,3},{1,0},{2,1},{3,2},{4,7},{5,4},{6,5},{7,6},{8,11},{9,8},{10,9... | collective-permute-start | bytes 3145736 | tf_op jit(solution)/shard_map/ppermute | solution.py:427
  31.6 30.6 %collective-permute-start.17 = (bf16[16,128,256]{2,1,0:T(8,128)(2,1)}, bf16[16,128,256]{2,1,0:T(8,128)(2,1)}, u32[]{:S(2)}, u32[]{:S(2)}) collective-permute-start(bf16[16,128,256]{2,1,0:T(8,128)(2,1)} %constant_dynamic-update-slice_fusion.refs_9_), channel_id=1, source_target_pairs={{0,8},{4,36},{8,16},{12,44},{16,24},{20,52},{24,0},{28,60},{32,40}... | collective-permute-start | bytes 3145736 | tf_op jit(solution)/shard_map/ppermute | solution.py:495
  57.3 15.1 %collective-permute-start.14 = (bf16[16,128,256]{2,1,0:T(8,128)(2,1)S(1)}, bf16[16,128,256]{2,1,0:T(8,128)(2,1)}, u32[]{:S(2)}, u32[]{:S(2)}) collective-permute-start(bf16[16,128,256]{2,1,0:T(8,128)(2,1)S(1)} %pad_maximum_fusion.refs_8_), channel_id=1, source_target_pairs={{0,24},{4,100},{8,0},{12,108},{16,8},{20,116},{24,16},{28,124},{32... | collective-permute-start | bytes 3145736 | tf_op jit(solution)/shard_map/ppermute | solution.py:494
  60.1 23.7 %collective-permute-start.15 = (bf16[16,128,256]{2,1,0:T(8,128)(2,1)}, bf16[16,128,256]{2,1,0:T(8,128)(2,1)}, u32[]{:S(2)}, u32[]{:S(2)}) collective-permute-start(bf16[16,128,256]{2,1,0:T(8,128)(2,1)} %constant_dynamic-update-slice_fusion.refs_9_), channel_id=1, source_target_pairs={{0,24},{4,100},{8,0},{12,108},{16,8},{20,116},{24,16},{28,124},{32... | collective-permute-start | bytes 3145736 | tf_op jit(solution)/shard_map/ppermute | solution.py:497
  60.9 22.8 %collective-permute-start.19 = (bf16[16,128,256]{2,1,0:T(8,128)(2,1)S(1)}, bf16[16,128,256]{2,1,0:T(8,128)(2,1)}, u32[]{:S(2)}, u32[]{:S(2)}) collective-permute-start(bf16[16,128,256]{2,1,0:T(8,128)(2,1)S(1)} %pad_maximum_fusion.refs_8_), channel_id=1, source_target_pairs={{0,8},{4,36},{8,16},{12,44},{16,24},{20,52},{24,0},{28,60},{32,40}... | collective-permute-start | bytes 3145736 | tf_op jit(solution)/shard_map/ppermute | solution.py:496
  62.1 22.8 %collective-permute-start.21 = (bf16[16,128,256]{2,1,0:T(8,128)(2,1)}, bf16[16,128,256]{2,1,0:T(8,128)(2,1)S(1)}, u32[]{:S(2)}, u32[]{:S(2)}) collective-permute-start(bf16[16,128,256]{2,1,0:T(8,128)(2,1)} %constant_dynamic-update-slice_fusion.refs_9_), channel_id=1, source_target_pairs={{0,4},{4,0},{8,12},{12,8},{16,20},{20,16},{24,28},{28,24},{32,36},... | collective-permute-start | bytes 3145736 | tf_op jit(solution)/shard_map/ppermute | solution.py:503
  62.1 25.4 %collective-permute-start.20 = (bf16[16,128,256]{2,1,0:T(8,128)(2,1)S(1)}, bf16[16,128,256]{2,1,0:T(8,128)(2,1)S(1)}, u32[]{:S(2)}, u32[]{:S(2)}) collective-permute-start(bf16[16,128,256]{2,1,0:T(8,128)(2,1)S(1)} %pad_maximum_fusion.refs_8_), channel_id=1, source_target_pairs={{0,4},{4,0},{8,12},{12,8},{16,20},{20,16},{24,28},{28,24},{32,36},... | collective-permute-start | bytes 3145736 | tf_op jit(solution)/shard_map/ppermute | solution.py:503
  72.4 26.3 %collective-permute-start.7 = (bf16[1024,512]{1,0:T(8,128)(2,1)}, bf16[1024,512]{1,0:T(8,128)(2,1)S(1)}, u32[]{:S(2)}, u32[]{:S(2)}) collective-permute-start(bf16[1024,512]{1,0:T(8,128)(2,1)} %collective-permute-done.3.refs_2_), channel_id=1, source_target_pairs={{0,1},{1,2},{2,3},{3,0},{4,5},{5,6},{6,7},{7,4},{8,9},{9,10},{10,1... | collective-permute-start | bytes 3145736 | tf_op jit(solution)/shard_map/ppermute | solution.py:505
  83.7 24.8 %collective-permute-start.8 = (bf16[1024,512]{1,0:T(8,128)(2,1)S(1)}, bf16[1024,512]{1,0:T(8,128)(2,1)S(1)}, u32[]{:S(2)}, u32[]{:S(2)}) collective-permute-start(bf16[1024,512]{1,0:T(8,128)(2,1)S(1)} %collective-permute-done.6.refs_5_), channel_id=1, source_target_pairs={{0,3},{1,0},{2,1},{3,2},{4,7},{5,4},{6,5},{7,6},{8,11},{9,8},{10,9... | collective-permute-start | bytes 3145736 | tf_op jit(solution)/shard_map/ppermute | solution.py:506
  83.7 25.8 %collective-permute-start.18 = (bf16[16,128,256]{2,1,0:T(8,128)(2,1)}, bf16[16,128,256]{2,1,0:T(8,128)(2,1)S(1)}, u32[]{:S(2)}, u32[]{:S(2)}) collective-permute-start(bf16[16,128,256]{2,1,0:T(8,128)(2,1)} %collective-permute-done.17.refs_15_), channel_id=1, source_target_pairs={{0,8},{4,36},{8,16},{12,44},{16,24},{20,52},{24,0},{28,60},{32,40}... | collective-permute-start | bytes 3145736 | tf_op jit(solution)/shard_map/ppermute | solution.py:499
  85.0 25.7 %collective-permute-start.16 = (bf16[16,128,256]{2,1,0:T(8,128)(2,1)}, bf16[16,128,256]{2,1,0:T(8,128)(2,1)}, u32[]{:S(2)}, u32[]{:S(2)}) collective-permute-start(bf16[16,128,256]{2,1,0:T(8,128)(2,1)} %collective-permute-done.14.refs_10_), channel_id=1, source_target_pairs={{0,24},{4,100},{8,0},{12,108},{16,8},{20,116},{24,16},{28,124},{32... | collective-permute-start | bytes 3145736 | tf_op jit(solution)/shard_map/ppermute | solution.py:498
  87.5 23.7 %collective-permute-start.23 = (bf16[16,128,256]{2,1,0:T(8,128)(2,1)}, bf16[16,128,256]{2,1,0:T(8,128)(2,1)}, u32[]{:S(2)}, u32[]{:S(2)}) collective-permute-start(bf16[16,128,256]{2,1,0:T(8,128)(2,1)} %collective-permute-done.15.refs_11_), channel_id=1, source_target_pairs={{0,4},{4,0},{8,12},{12,8},{16,20},{20,16},{24,28},{28,24},{32,36},... | collective-permute-start | bytes 3145736 | tf_op jit(solution)/shard_map/ppermute | solution.py:503
  98.7 13.8 %collective-permute-start.27 = (bf16[16,128,256]{2,1,0:T(8,128)(2,1)}, bf16[16,128,256]{2,1,0:T(8,128)(2,1)}, u32[]{:S(2)}, u32[]{:S(2)}) collective-permute-start(bf16[16,128,256]{2,1,0:T(8,128)(2,1)} %collective-permute-done.17.refs_15_), channel_id=1, source_target_pairs={{0,4},{4,0},{8,12},{12,8},{16,20},{20,16},{24,28},{28,24},{32,36},... | collective-permute-start | bytes 3145736 | tf_op jit(solution)/shard_map/ppermute | solution.py:503
  108.6 4.3 %collective-permute-start.22 = (bf16[16,128,256]{2,1,0:T(8,128)(2,1)}, bf16[16,128,256]{2,1,0:T(8,128)(2,1)}, u32[]{:S(2)}, u32[]{:S(2)}) collective-permute-start(bf16[16,128,256]{2,1,0:T(8,128)(2,1)} %collective-permute-done.14.refs_10_), channel_id=1, source_target_pairs={{0,4},{4,0},{8,12},{12,8},{16,20},{20,16},{24,28},{28,24},{32,36},... | collective-permute-start | bytes 3145736 | tf_op jit(solution)/shard_map/ppermute | solution.py:503
  110.6 3.0 %collective-permute-start.26 = (bf16[16,128,256]{2,1,0:T(8,128)(2,1)}, bf16[16,128,256]{2,1,0:T(8,128)(2,1)}, u32[]{:S(2)}, u32[]{:S(2)}) collective-permute-start(bf16[16,128,256]{2,1,0:T(8,128)(2,1)} %collective-permute-done.19.refs_14_), channel_id=1, source_target_pairs={{0,4},{4,0},{8,12},{12,8},{16,20},{20,16},{24,28},{28,24},{32,36},... | collective-permute-start | bytes 3145736 | tf_op jit(solution)/shard_map/ppermute | solution.py:503
  110.7 13.0 %collective-permute-start.25 = (bf16[16,128,256]{2,1,0:T(8,128)(2,1)}, bf16[16,128,256]{2,1,0:T(8,128)(2,1)}, u32[]{:S(2)}, u32[]{:S(2)}) collective-permute-start(bf16[16,128,256]{2,1,0:T(8,128)(2,1)} %copy-done.18), channel_id=1, source_target_pairs={{0,4},{4,0},{8,12},{12,8},{16,20},{20,16},{24,28},{28,24},{32,36},... | collective-permute-start | bytes 3145736 | tf_op jit(solution)/shard_map/ppermute | solution.py:503
  111.3 12.8 %collective-permute-start.24 = (bf16[16,128,256]{2,1,0:T(8,128)(2,1)}, bf16[16,128,256]{2,1,0:T(8,128)(2,1)}, u32[]{:S(2)}, u32[]{:S(2)}) collective-permute-start(bf16[16,128,256]{2,1,0:T(8,128)(2,1)} %collective-permute-done.16.refs_12_), channel_id=1, source_target_pairs={{0,4},{4,0},{8,12},{12,8},{16,20},{20,16},{24,28},{28,24},{32,36},... | collective-permute-start | bytes 3145736 | tf_op jit(solution)/shard_map/ppermute | solution.py:503
  112.5 31.8 %collective-permute-start.9 = (bf16[1024,512]{1,0:T(8,128)(2,1)S(1)}, bf16[1024,512]{1,0:T(8,128)(2,1)}, u32[]{:S(2)}, u32[]{:S(2)}) collective-permute-start(bf16[1024,512]{1,0:T(8,128)(2,1)S(1)} %bitcast.83), channel_id=1, source_target_pairs={{0,4},{4,0},{8,12},{12,8},{16,20},{20,16},{24,28},{28,24},{32,36},... | collective-permute-start | bytes 3145736 | tf_op jit(solution)/shard_map/ppermute | solution.py:514
  112.9 31.7 %collective-permute-start.10 = (bf16[1024,512]{1,0:T(8,128)(2,1)S(1)}, bf16[1024,512]{1,0:T(8,128)(2,1)}, u32[]{:S(2)}, u32[]{:S(2)}) collective-permute-start(bf16[1024,512]{1,0:T(8,128)(2,1)S(1)} %bitcast.78), channel_id=1, source_target_pairs={{0,4},{4,0},{8,12},{12,8},{16,20},{20,16},{24,28},{28,24},{32,36},... | collective-permute-start | bytes 3145736 | tf_op jit(solution)/shard_map/ppermute | solution.py:514
  113.6 31.2 %collective-permute-start.11 = (bf16[1024,512]{1,0:T(8,128)(2,1)}, bf16[1024,512]{1,0:T(8,128)(2,1)}, u32[]{:S(2)}, u32[]{:S(2)}) collective-permute-start(bf16[1024,512]{1,0:T(8,128)(2,1)} %collective-permute-done.3.refs_2_), channel_id=1, source_target_pairs={{0,4},{4,0},{8,12},{12,8},{16,20},{20,16},{24,28},{28,24},{32,36},... | collective-permute-start | bytes 3145736 | tf_op jit(solution)/shard_map/ppermute | solution.py:514
  123.6 47.9 %collective-permute-start.30 = (bf16[1024,512]{1,0:T(8,128)(2,1)S(1)}, bf16[1024,512]{1,0:T(8,128)(2,1)}, u32[]{:S(2)}, u32[]{:S(2)}) collective-permute-start(bf16[1024,512]{1,0:T(8,128)(2,1)S(1)} %collective-permute-done.6.refs_5_), channel_id=1, source_target_pairs={{0,4},{4,0},{8,12},{12,8},{16,20},{20,16},{24,28},{28,24},{32,36},... | collective-permute-start | bytes 3145736 | tf_op jit(solution)/shard_map/ppermute | solution.py:514
  144.0 29.0 %collective-permute-start.28 = (bf16[1024,512]{1,0:T(8,128)(2,1)}, bf16[1024,512]{1,0:T(8,128)(2,1)}, u32[]{:S(2)}, u32[]{:S(2)}) collective-permute-start(bf16[1024,512]{1,0:T(8,128)(2,1)} %collective-permute-done.4.refs_3_), channel_id=1, source_target_pairs={{0,4},{4,0},{8,12},{12,8},{16,20},{20,16},{24,28},{28,24},{32,36},... | collective-permute-start | bytes 3145736 | tf_op jit(solution)/shard_map/ppermute | solution.py:514
  144.3 28.8 %collective-permute-start.29 = (bf16[1024,512]{1,0:T(8,128)(2,1)}, bf16[1024,512]{1,0:T(8,128)(2,1)S(1)}, u32[]{:S(2)}, u32[]{:S(2)}) collective-permute-start(bf16[1024,512]{1,0:T(8,128)(2,1)} %collective-permute-done.5.refs_4_), channel_id=1, source_target_pairs={{0,4},{4,0},{8,12},{12,8},{16,20},{20,16},{24,28},{28,24},{32,36},... | collective-permute-start | bytes 3145736 | tf_op jit(solution)/shard_map/ppermute | solution.py:514
  144.6 28.4 %collective-permute-start.31 = (bf16[1024,512]{1,0:T(8,128)(2,1)}, bf16[1024,512]{1,0:T(8,128)(2,1)}, u32[]{:S(2)}, u32[]{:S(2)}) collective-permute-start(bf16[1024,512]{1,0:T(8,128)(2,1)} %copy-done.3), channel_id=1, source_target_pairs={{0,4},{4,0},{8,12},{12,8},{16,20},{20,16},{24,28},{28,24},{32,36},... | collective-permute-start | bytes 3145736 | tf_op jit(solution)/shard_map/ppermute | solution.py:514
  144.8 28.3 %collective-permute-start.32 = (bf16[1024,512]{1,0:T(8,128)(2,1)}, bf16[1024,512]{1,0:T(8,128)(2,1)}, u32[]{:S(2)}, u32[]{:S(2)}) collective-permute-start(bf16[1024,512]{1,0:T(8,128)(2,1)} %copy-done.4), channel_id=1, source_target_pairs={{0,4},{4,0},{8,12},{12,8},{16,20},{20,16},{24,28},{28,24},{32,36},... | collective-permute-start | bytes 3145736 | tf_op jit(solution)/shard_map/ppermute | solution.py:514
  145.1 17.9 %all-to-all-start = ((f32[32,24,128]{2,1,0:T(8,128)}), f32[32,24,128]{2,1,0:T(8,128)S(1)}, u32[]{:S(2)}, u32[]{:S(2)}) async-start(f32[32,24,128]{2,1,0:T(8,128)} %get-tuple-element.40), calls=%async_computation | async-start | bytes 786432 | tf_op jit(solution)/shard_map/all_to_all | solution.py:520
  171.5 1.5 collective-permute-start.33
  196.4 14.9 %collective-permute-start.38 = (f16[2,8,128,256]{3,2,1,0:T(8,128)(2,1)S(1)}, f16[2,8,128,256]{3,2,1,0:T(8,128)(2,1)S(1)}, u32[]{:S(2)}, u32[]{:S(2)}) collective-permute-start(f16[2,8,128,256]{3,2,1,0:T(8,128)(2,1)S(1)} %bitcast.100), channel_id=1, source_target_pairs={{0,96},{4,28},{8,104},{12,4},{16,112},{20,12},{24,120},{28,20},{32... | collective-permute-start | bytes 3145736 | tf_op jit(solution)/shard_map/ppermute | solution.py:381
  197.8 30.7 %collective-permute-start.37 = (f16[2,8,128,256]{3,2,1,0:T(8,128)(2,1)S(1)}, f16[2,8,128,256]{3,2,1,0:T(8,128)(2,1)S(1)}, u32[]{:S(2)}, u32[]{:S(2)}) collective-permute-start(f16[2,8,128,256]{3,2,1,0:T(8,128)(2,1)S(1)} %bitcast.97), channel_id=1, source_target_pairs={{0,32},{4,12},{8,40},{12,20},{16,48},{20,28},{24,56},{28,4},{32,64... | collective-permute-start | bytes 3145736 | tf_op jit(solution)/shard_map/ppermute | solution.py:382
  199.2 26.0 %collective-permute-start.34 = (f16[2,8,128,256]{3,2,1,0:T(8,128)(2,1)S(1)}, f16[2,8,128,256]{3,2,1,0:T(8,128)(2,1)S(1)}, u32[]{:S(2)}, u32[]{:S(2)}) collective-permute-start(f16[2,8,128,256]{3,2,1,0:T(8,128)(2,1)S(1)} %bitcast.99), channel_id=1, source_target_pairs={{0,32},{4,12},{8,40},{12,20},{16,48},{20,28},{24,56},{28,4},{32,64... | collective-permute-start | bytes 3145736 | tf_op jit(solution)/shard_map/ppermute | solution.py:380
  211.7 16.8 %collective-permute-start.39 = (f16[2,8,128,256]{3,2,1,0:T(8,128)(2,1)S(1)}, f16[2,8,128,256]{3,2,1,0:T(8,128)(2,1)S(1)}, u32[]{:S(2)}, u32[]{:S(2)}) collective-permute-start(f16[2,8,128,256]{3,2,1,0:T(8,128)(2,1)S(1)} %add_convert_fusion.1), channel_id=1, source_target_pairs={{0,96},{4,28},{8,104},{12,4},{16,112},{20,12},{24,120},{28,20},{32... | collective-permute-start | bytes 3145736 | tf_op jit(solution)/shard_map/ppermute | solution.py:385
  214.3 34.5 %collective-permute-start.36 = (f16[2,8,128,256]{3,2,1,0:T(8,128)(2,1)S(1)}, f16[2,8,128,256]{3,2,1,0:T(8,128)(2,1)S(1)}, u32[]{:S(2)}, u32[]{:S(2)}) collective-permute-start(f16[2,8,128,256]{3,2,1,0:T(8,128)(2,1)S(1)} %bitcast.98), channel_id=1, source_target_pairs={{0,96},{4,28},{8,104},{12,4},{16,112},{20,12},{24,120},{28,20},{32... | collective-permute-start | bytes 3145736 | tf_op jit(solution)/shard_map/ppermute | solution.py:383
  225.5 23.3 %collective-permute-start.35 = (f16[2,8,128,256]{3,2,1,0:T(8,128)(2,1)S(1)}, f16[2,8,128,256]{3,2,1,0:T(8,128)(2,1)S(1)}, u32[]{:S(2)}, u32[]{:S(2)}) collective-permute-start(f16[2,8,128,256]{3,2,1,0:T(8,128)(2,1)S(1)} %add_convert_fusion.2), channel_id=1, source_target_pairs={{0,32},{4,12},{8,40},{12,20},{16,48},{20,28},{24,56},{28,4},{32,64... | collective-permute-start | bytes 3145736 | tf_op jit(solution)/shard_map/ppermute | solution.py:384
  229.3 20.9 %collective-permute-start.40 = (f16[8,128,256]{2,1,0:T(8,128)(2,1)S(1)}, f16[8,128,256]{2,1,0:T(8,128)(2,1)S(1)}, u32[]{:S(2)}, u32[]{:S(2)}) collective-permute-start(f16[8,128,256]{2,1,0:T(8,128)(2,1)S(1)} %get-tuple-element.66), channel_id=1, source_target_pairs={{0,16},{4,68},{8,24},{12,76},{16,0},{20,84},{24,8},{28,92},{32,48}... | collective-permute-start | bytes 1572872 | tf_op jit(solution)/shard_map/ppermute | solution.py:393
  231.7 18.5 %collective-permute-start.42 = (f16[8,128,256]{2,1,0:T(8,128)(2,1)S(1)}, f16[8,128,256]{2,1,0:T(8,128)(2,1)S(1)}, u32[]{:S(2)}, u32[]{:S(2)}) collective-permute-start(f16[8,128,256]{2,1,0:T(8,128)(2,1)S(1)} %get-tuple-element.67), channel_id=1, source_target_pairs={{0,24},{4,100},{8,0},{12,108},{16,8},{20,116},{24,16},{28,124},{32... | collective-permute-start | bytes 1572872 | tf_op jit(solution)/shard_map/ppermute | solution.py:393
  249.3 10.5 %collective-permute-start.41 = (f16[8,128,256]{2,1,0:T(8,128)(2,1)S(1)}, f16[8,128,256]{2,1,0:T(8,128)(2,1)S(1)}, u32[]{:S(2)}, u32[]{:S(2)}) collective-permute-start(f16[8,128,256]{2,1,0:T(8,128)(2,1)S(1)} %fusion.6), channel_id=1, source_target_pairs={{0,8},{4,36},{8,16},{12,44},{16,24},{20,52},{24,0},{28,60},{32,40}... | collective-permute-start | bytes 1572872 | tf_op jit(solution)/shard_map/ppermute | solution.py:393
  260.1 1.6 collective-permute-start.43
  (27 other events, 463.0 us)

commit v13 on v12

--- a/solution.py
+++ b/solution.py
@@ -7,7 +7,7 @@
 
 
 SOFTEN = 0.25
-EARLY_SWAPS = (0, 1, 2, 5)
+EARLY_SWAPS = (0, 1, 2, 3, 4, 5)
 ROOT_TWO = 1.4142135623730951
 HALF = 512
 PIECES = 8
@@ -71,17 +71,17 @@
                 pl.ds(pl.multiple_of(row * BLK + half * 128, 128), 128),
                 pl.ds(pl.multiple_of(col * BLK, BLK), BLK),
             ]
-            at = side * 32 + n
+            kind, block = which[side * 32 + n], where[side * 32 + n]
 
             def pick(low, high):
                 if high - low == 1:
                     pltpu.make_async_copy(
-                        sources[side * SOURCES + low].at[where[at]], target, sem
+                        sources[side * SOURCES + low].at[block], target, sem
                     ).start()
                     return
                 middle = (low + high) // 2
-                pl.when(which[at] < middle)(lambda: pick(low, middle))
-                pl.when(which[at] >= middle)(lambda: pick(middle, high))
+                pl.when(kind < middle)(lambda: pick(low, middle))
+                pl.when(kind >= middle)(lambda: pick(middle, high))
 
             pick(0, SOURCES)
             return 0
@@ -155,10 +155,11 @@
         sent[dest] = block_out[...]
 
 
-def potential_body(table, got, mine, weights, xc, rho, coeffs, pot, scale, bound, *scratch):
+def potential_body(table0, table1, got, mine, weights, xc, rho, coeffs, pot, scale, bound, *scratch):
     tbuf, column, data, tsem = scratch
     for i in range(PIECES):
-        pltpu.make_async_copy(table.at[i], tbuf.at[i], tsem.at[i]).start()
+        table = table0 if i < PIECES // 2 else table1
+        pltpu.make_async_copy(table.at[i % (PIECES // 2)], tbuf.at[i], tsem.at[i]).start()
     natoms = coeffs.shape[0]
     homes = []
     for which in range(2):
@@ -196,7 +197,7 @@
 
     def step(i, _):
         base = (i // 4) * 1024
-        pltpu.make_async_copy(table.at[i], tbuf.at[i], tsem.at[i]).wait()
+        pltpu.make_async_copy(tbuf.at[i], tbuf.at[i], tsem.at[i]).wait()
         parts = [jnp.zeros((8, 128), jnp.float32) for _ in range(HALF // 128)]
         for block in range(16):
             factor = column[pl.ds(base + block * 64, 64), :]
@@ -313,7 +314,7 @@
     )(order, place, which, where, *chunks, *sources, table, weights, xc, home_rows)
 
 
-def potential_call(table, got, mine, weights, xc, rho, natoms):
+def potential_call(tables, got, mine, weights, xc, rho, natoms):
     row = jax.ShapeDtypeStruct((PIECES, 1, HALF), jnp.float32)
     return pl.pallas_call(
         potential_body,
@@ -323,7 +324,7 @@
             row,
             jax.ShapeDtypeStruct((1, 128), jnp.float32),
         ),
-        in_specs=[any_spec()] + [vmem_spec()] * 5,
+        in_specs=[any_spec()] * 2 + [vmem_spec()] * 5,
         out_specs=(vmem_spec(),) * 4,
         scratch_shapes=[
             pltpu.VMEM((PIECES, NB * BLK, HALF), jnp.float32),
@@ -336,7 +337,7 @@
             flops=16 << 20, bytes_accessed=16 << 20, transcendentals=0
         ),
         name="potential",
-    )(table, got, mine, weights, xc, rho)
+    )(*tables, got, mine, weights, xc, rho)
 
 
 def ham_call(order, slots, place, chunks, scale_mine, scale_beside):
@@ -476,6 +477,13 @@
     erf_scale = (ROOT_TWO * gauss_widths)[None, None, :, None]
     gauss = jnp.exp(-dist_sq / spread).reshape(PIECES, neighbors * moments, HALF)
     distance = jnp.sqrt(dist_sq)
+
+    def erf_table(part):
+        return (lax.erf(part / erf_scale) / part).reshape(
+            PIECES // 2, neighbors * moments, HALF
+        )
+
+    hart_first = erf_table(distance[: PIECES // 2])
     weights = point_weights.reshape(PIECES, 1, HALF)
     xc = xc_kernel.reshape(PIECES, 1, HALF)
 
@@ -506,17 +514,16 @@
     far1 = lax.ppermute(above1, "pert", ring(3))
     chunks = [own0, own1, below0, below1, above0, above1, far0, far1]
 
+    gauss, hart_first = lax.optimization_barrier((gauss, hart_first))
     rho, sent = density_call(
         order, core_place, which, where, chunks, sources, gauss, weights, xc, home_rows
     )
-    distance, sent, later = lax.optimization_barrier((distance, sent, chunks))
+    second, sent, later = lax.optimization_barrier((distance[PIECES // 2 :], sent, chunks))
     beside = [
         lax.ppermute(chunks[i] if i in EARLY_SWAPS else later[i], "grid", swap)
         for i in range(CHUNKS)
     ]
-    hart = (lax.erf(distance / erf_scale) / distance).reshape(
-        PIECES, neighbors * moments, HALF
-    )
+    hart = (hart_first, erf_table(second))
     got = lax.all_to_all(sent, "grid", split_axis=0, concat_axis=0, tiled=True)
     all_coeffs, pot, scale, bound = potential_call(
         hart, got.reshape(groups * PAY_ROWS, 128), my_homes, weights, xc, rho, natoms

time: 265 us -> 266 us (level)
    all_to_all x1, waiting for transfers between devices: 2.7 us -> 5.89 us  [one_device(): got = lax.all_to_all(sent, 'grid', split_axis=0, concat_axis=0, tiled=True)]
    div x1 -> x2, other arithmetic: 7.41 us -> 9.48 us  [erf_table(): lax.erf(part / erf_scale) / part]
  transfers between devices with their start and end apart: 45 -> 45, of which waited for: 15 -> 15; matrix products, arithmetic and copies ran while one was open for 14% -> 15% of each run, Pallas kernels for 11% -> 10%
where the time goes in v13:
time: 266 us; the launch traced here: 264 us
  waiting for transfers between devices  119 us (45%)
  starting transfers between devices  47 us (18%)
  Pallas kernels  45.7 us (17%)
  other arithmetic  31.1 us (12%)
  local copies, waits for them, and re-layouts  20 us (8%)
    pallas_call x1, Pallas kernels, ham_call(): pl.pallas_call(ham_body, out_shape=(jax.ShapeDtypeStruct((16, 128, BLK),...  20.4 us
    ppermute x1, waiting for transfers between devices, one_device(): below0 = lax.ppermute(own0, 'pert', ring(1))  19.5 us
    pallas_call x1, Pallas kernels, density_call(): pl.pallas_call(density_body, out_shape=(jax.ShapeDtypeStruct((PIECES, 1,...  17.4 us
    ppermute x1, waiting for transfers between devices, ring_sum(): above_low = lax.ppermute(cast(low[3] * factor), 'grid', down)  15.9 us
    unnamed x63, local copies, waits for them, and re-layouts  11.9 us
    ppermute x1, waiting for transfers between devices, one_device(): other_ahead = lax.ppermute(other, 'grid', back)  11.3 us
    ppermute x1, waiting for transfers between devices, one_device(): far0 = lax.ppermute(below0, 'pert', ring(1))  11.1 us
    ppermute x1, waiting for transfers between devices, one_device(): far1 = lax.ppermute(above1, 'pert', ring(3))  9.91 us
  transfers between devices with their start and end apart: 45, of which 15 were waited for; matrix products, arithmetic and copies ran while one was open for 15% of the time, Pallas kernels for 10%

profile of v13, /device:TPU:0, one launch (start us, length us, event | category | flops | bytes accessed | tf_op | source)
XLA Modules:
  0.0 264.5 jit_solution(1158141399210476103)
XLA Ops:
  0.6 1.1 select_bitcast_fusion
  1.8 2.7 %fusion.25 = (bf16[512,1024]{1,0:T(8,128)(2,1)S(1)}, bf16[512,1024]{1,0:T(8,128)(2,1)}) fusion(bf16[1024,1024]{1,0:T(8,128)(2,1)} %param.13), kind=kLoop, calls=%fused_computation.142 | loop fusion | bytes 4194304 | tf_op jit(solution)/shard_map/slice | solution.py:424
  5.1 3.2 %collective-permute-start.6 = (bf16[1024,512]{1,0:T(8,128)(2,1)S(1)}, bf16[1024,512]{1,0:T(8,128)(2,1)S(1)}, u32[]{:S(2)}, u32[]{:S(2)}) collective-permute-start(bf16[1024,512]{1,0:T(8,128)(2,1)S(1)} %bitcast.84), channel_id=1, source_target_pairs={{0,3},{1,0},{2,1},{3,2},{4,7},{5,4},{6,5},{7,6},{8,11},{9,8},{10,9... | collective-permute-start | bytes 3145736 | tf_op jit(solution)/shard_map/ppermute | solution.py:426
  10.2 3.9 %collective-permute-start.15 = (bf16[8,128,256]{2,1,0:T(8,128)(2,1)}, bf16[8,128,256]{2,1,0:T(8,128)(2,1)}, u32[]{:S(2)}, u32[]{:S(2)}) collective-permute-start(bf16[8,128,256]{2,1,0:T(8,128)(2,1)} %pad_maximum_fusion.1), channel_id=1, source_target_pairs={{0,64},{4,20},{8,72},{12,28},{16,80},{20,4},{24,88},{28,12},{32,96... | collective-permute-start | bytes 1572872 | tf_op jit(solution)/shard_map/ppermute | solution.py:441
  14.1 1.1 collective-permute-start.16
  15.2 1.5 copy.25
  16.7 2.3 collective-permute-start.1
  19.0 2.6 collective-permute-done.15
  22.4 1.9 constant_dynamic-update-slice_fusion.1
  24.3 2.8 %collective-permute-done.16 = bf16[8,128,256]{2,1,0:T(8,128)(2,1)} collective-permute-done((bf16[8,128,256]{2,1,0:T(8,128)(2,1)}, bf16[8,128,256]{2,1,0:T(8,128)(2,1)}, u32[]{:S(2)}, u32[]{:S(2)}) %collective-permute-start.16) | collective-permute-done | bytes 524320 | tf_op jit(solution)/shard_map/ppermute | solution.py:441
  27.1 1.9 constant_dynamic-update-slice_fusion.refs_9_
  29.0 3.2 %collective-permute-start.5 = (bf16[1024,512]{1,0:T(8,128)(2,1)S(1)}, bf16[1024,512]{1,0:T(8,128)(2,1)}, u32[]{:S(2)}, u32[]{:S(2)}) collective-permute-start(bf16[1024,512]{1,0:T(8,128)(2,1)S(1)} %bitcast.90), channel_id=1, source_target_pairs={{0,3},{1,0},{2,1},{3,2},{4,7},{5,4},{6,5},{7,6},{8,11},{9,8},{10,9... | collective-permute-start | bytes 3145736 | tf_op jit(solution)/shard_map/ppermute | solution.py:428
  32.3 1.5 collective-permute-start.20
  36.6 1.2 pad_maximum_fusion.refs_8_
  37.8 19.5 %collective-permute-done.3.refs_2_ = bf16[1024,512]{1,0:T(8,128)(2,1)} collective-permute-done((bf16[1024,512]{1,0:T(8,128)(2,1)S(1)}, bf16[1024,512]{1,0:T(8,128)(2,1)}, u32[]{:S(2)}, u32[]{:S(2)}) %collective-permute-start.3) | collective-permute-done | bytes 1048608 | tf_op jit(solution)/shard_map/ppermute | solution.py:425
  57.3 2.8 %collective-permute-start.17 = (bf16[16,128,256]{2,1,0:T(8,128)(2,1)S(1)}, bf16[16,128,256]{2,1,0:T(8,128)(2,1)}, u32[]{:S(2)}, u32[]{:S(2)}) collective-permute-start(bf16[16,128,256]{2,1,0:T(8,128)(2,1)S(1)} %pad_maximum_fusion.refs_8_), channel_id=1, source_target_pairs={{0,24},{4,100},{8,0},{12,108},{16,8},{20,116},{24,16},{28,124},{32... | collective-permute-start | bytes 3145736 | tf_op jit(solution)/shard_map/ppermute | solution.py:502
  60.9 1.2 collective-permute-start.22
  62.6 9.8 %collective-permute-done.17.refs_10_ = bf16[16,128,256]{2,1,0:T(8,128)(2,1)} collective-permute-done((bf16[16,128,256]{2,1,0:T(8,128)(2,1)S(1)}, bf16[16,128,256]{2,1,0:T(8,128)(2,1)}, u32[]{:S(2)}, u32[]{:S(2)}) %collective-permute-start.17) | collective-permute-done | bytes 1048608 | tf_op jit(solution)/shard_map/ppermute | solution.py:502
  72.4 11.3 %collective-permute-done.18.refs_11_ = bf16[16,128,256]{2,1,0:T(8,128)(2,1)} collective-permute-done((bf16[16,128,256]{2,1,0:T(8,128)(2,1)}, bf16[16,128,256]{2,1,0:T(8,128)(2,1)}, u32[]{:S(2)}, u32[]{:S(2)}) %collective-permute-start.18) | collective-permute-done | bytes 1048608 | tf_op jit(solution)/shard_map/ppermute | solution.py:505
  83.7 1.2 collective-permute-start.21
  85.0 2.6 collective-permute-start.19
  87.5 11.1 %collective-permute-done.7.refs_6_ = bf16[1024,512]{1,0:T(8,128)(2,1)S(1)} collective-permute-done((bf16[1024,512]{1,0:T(8,128)(2,1)}, bf16[1024,512]{1,0:T(8,128)(2,1)S(1)}, u32[]{:S(2)}, u32[]{:S(2)}) %collective-permute-start.7) | collective-permute-done | bytes 1048608 | tf_op jit(solution)/shard_map/ppermute | solution.py:513
  98.7 9.9 %collective-permute-done.8.refs_7_ = bf16[1024,512]{1,0:T(8,128)(2,1)S(1)} collective-permute-done((bf16[1024,512]{1,0:T(8,128)(2,1)S(1)}, bf16[1024,512]{1,0:T(8,128)(2,1)S(1)}, u32[]{:S(2)}, u32[]{:S(2)}) %collective-permute-start.8) | collective-permute-done | bytes 1048608 | tf_op jit(solution)/shard_map/ppermute | solution.py:514
  108.6 1.0 copy-done.4
  113.9 5.2 %bitcast_divide_fusion.3.table0 = f32[4,1024,512]{2,1,0:T(8,128)} fusion(f32[1024]{0:T(1024)S(1)} %div.222, f32[4,16,512]{2,1,0:T(8,128)} %get-tuple-element.70), kind=kLoop, calls=%fused_computation.4 | loop fusion | flops 4194304 | bytes 8523776 | tf_op jit(solution)/shard_map/div | solution.py:482
  119.0 8.2 %fusion.refs_24_ = f32[8,1024,512]{2,1,0:T(8,128)} fusion(f32[1024]{0:T(1024)S(1)} %div.215, f32[8,16,512]{2,1,0:T(8,128)S(1)} %bitcast.102), kind=kLoop, calls=%fused_computation.1 | loop fusion | flops 4194304 | bytes 17043456 | tf_op jit(solution)/shard_map/exp | solution.py:478
  128.3 17.4 %density.1 = (f32[8,1,512]{2,1,0:T(1,128)}, f32[32,24,128]{2,1,0:T(8,128)}) custom-call(s32[8]{0:T(128)} %fusion.10.order, s32[1]{0:T(128)} %bitcast.3.place, s32[64]{0:T(128)} %get-tuple-element.30.which, s32[64]{0:T(128)} %get-tuple-element.31.where, bf16[1024,512]{1,0:T(8,128)(2,1)} %bitcast.92, bf16[1024,512]{1,0:T(8,128)(2,1)} %bitcast.87, ...), custom_call_target="tpu_custom_call" | custom-call | flops 8589934592 | bytes 33554432 | tf_op jit(solution)/shard_map/density/pallas_call | solution.py:289
  146.7 7.7 %all-to-all-start = ((f32[32,24,128]{2,1,0:T(8,128)}), f32[32,24,128]{2,1,0:T(8,128)S(1)}, u32[]{:S(2)}, u32[]{:S(2)}) async-start(f32[32,24,128]{2,1,0:T(8,128)} %get-tuple-element.40), calls=%async_computation | async-start | bytes 786432 | tf_op jit(solution)/shard_map/all_to_all | solution.py:527
  154.4 4.3 %bitcast_divide_fusion.1.table1 = f32[4,1024,512]{2,1,0:T(8,128)} fusion(f32[4,16,512]{2,1,0:T(8,128)S(1)} %bitcast.108, f32[1024]{0:T(1024)S(1)} %div.222), kind=kLoop, calls=%fused_computation.2 | loop fusion | flops 4194304 | bytes 8523776 | tf_op jit(solution)/shard_map/div | solution.py:482
  158.7 5.9 %all-to-all-done = f32[32,24,128]{2,1,0:T(8,128)S(1)} async-done(((f32[32,24,128]{2,1,0:T(8,128)}), f32[32,24,128]{2,1,0:T(8,128)S(1)}, u32[]{:S(2)}, u32[]{:S(2)}) %all-to-all-start) | async-done | bytes 393248 | tf_op jit(solution)/shard_map/all_to_all | solution.py:527
  165.3 8.0 %potential.1 = (f32[256,64]{1,0:T(8,128)}, f32[8,1,512]{2,1,0:T(1,128)}, f32[8,1,512]{2,1,0:T(1,128)}, f32[1,128]{1,0:T(1,128)}) custom-call(f32[4,1024,512]{2,1,0:T(8,128)} %bitcast_divide_fusion.3.table0, f32[4,1024,512]{2,1,0:T(8,128)} %bitcast_divide_fusion.1.table1, f32[768,128]{1,0:T(8,128)} %bitcast.101, f32[32,128]{1,0:T(8,128)} %broadcast_in_dim.78.mine, ...), custom_call_target="tpu_custom_call" | custom-call | flops 16777216 | bytes 16777216 | tf_op jit(solution)/shard_map/potential/pallas_call | solution.py:319
  175.4 20.4 %ham.1 = (f32[16,128,256]{2,1,0:T(8,128)}, f32[16,128,256]{2,1,0:T(8,128)}, f32[16,128,256]{2,1,0:T(8,128)}, f32[16,128,256]{2,1,0:T(8,128)}, f32[16,128,256]{2,...) custom-call(s32[8]{0:T(128)} %fusion.10.order, s32[64]{0:T(128)} %fusion.7.slots, ...), custom_call_target="tpu_custom_call" | custom-call | flops 4294967296 | bytes 25165824 | tf_op jit(solution)/shard_map/ham/pallas_call | solution.py:344
  195.8 2.0 multiply_convert_fusion
  197.8 1.2 collective-permute-start.38
  199.3 1.0 collective-permute-start.37
  201.6 1.4 copy-done.10
  203.2 9.4 %collective-permute-done.38 = f16[2,8,128,256]{3,2,1,0:T(8,128)(2,1)S(1)} collective-permute-done((f16[2,8,128,256]{3,2,1,0:T(8,128)(2,1)S(1)}, f16[2,8,128,256]{3,2,1,0:T(8,128)(2,1)S(1)}, u32[]{:S(2)}, u32[]{:S(2)}) %collective-permute-start.38) | collective-permute-done | bytes 1048608 | tf_op jit(solution)/shard_map/ppermute | solution.py:382
  213.1 2.4 collective-permute-start.39
  215.8 1.2 collective-permute-start.36
  217.0 9.6 %collective-permute-done.34 = f16[2,8,128,256]{3,2,1,0:T(8,128)(2,1)S(1)} collective-permute-done((f16[2,8,128,256]{3,2,1,0:T(8,128)(2,1)S(1)}, f16[2,8,128,256]{3,2,1,0:T(8,128)(2,1)S(1)}, u32[]{:S(2)}, u32[]{:S(2)}) %collective-permute-start.34) | collective-permute-done | bytes 1048608 | tf_op jit(solution)/shard_map/ppermute | solution.py:381
  227.1 1.1 copy-done.8
  228.4 1.4 copy-done.7
  230.8 1.1 collective-permute-start.40
  231.9 2.5 collective-permute-start.42
  234.4 15.9 %collective-permute-done.36 = f16[2,8,128,256]{3,2,1,0:T(8,128)(2,1)S(1)} collective-permute-done((f16[2,8,128,256]{3,2,1,0:T(8,128)(2,1)S(1)}, f16[2,8,128,256]{3,2,1,0:T(8,128)(2,1)S(1)}, u32[]{:S(2)}, u32[]{:S(2)}) %collective-permute-start.36) | collective-permute-done | bytes 1048608 | tf_op jit(solution)/shard_map/ppermute | solution.py:384
  251.8 9.6 %collective-permute-done.41 = f16[8,128,256]{2,1,0:T(8,128)(2,1)S(1)} collective-permute-done((f16[8,128,256]{2,1,0:T(8,128)(2,1)S(1)}, f16[8,128,256]{2,1,0:T(8,128)(2,1)S(1)}, u32[]{:S(2)}, u32[]{:S(2)}) %collective-permute-start.41) | collective-permute-done | bytes 524320 | tf_op jit(solution)/shard_map/ppermute | solution.py:394
  261.8 1.3 dynamic-slice_bitcast_fusion
  263.4 1.1 maximum_multiply_fusion
  (165 shorter events, 22.5 us)
Async XLA Ops:
  1.7 6.8 %collective-permute-start = (bf16[4,128,256]{2,1,0:T(8,128)(2,1)S(1)}, bf16[4,128,256]{2,1,0:T(8,128)(2,1)S(1)}, u32[]{:S(2)}, u32[]{:S(2)}) collective-permute-start(bf16[4,128,256]{2,1,0:T(8,128)(2,1)S(1)} %select_bitcast_fusion), channel_id=1, source_target_pairs={{0,4},{4,0},{8,12},{12,8},{16,20},{20,16},{24,28},{28,24},{32,36},... | collective-permute-start | bytes 786440 | tf_op jit(solution)/shard_map/ppermute | solution.py:437
  5.0 107.8 %copy-start = (bf16[512,1024]{0,1:T(8,128)(2,1)}, bf16[512,1024]{0,1:T(8,128)(2,1)S(1)}, u32[]{:S(2)}) copy-start(bf16[512,1024]{0,1:T(8,128)(2,1)S(1)} %copy.26) | copy-start | bytes 3145732
  5.1 55.0 %collective-permute-start.6 = (bf16[1024,512]{1,0:T(8,128)(2,1)S(1)}, bf16[1024,512]{1,0:T(8,128)(2,1)S(1)}, u32[]{:S(2)}, u32[]{:S(2)}) collective-permute-start(bf16[1024,512]{1,0:T(8,128)(2,1)S(1)} %bitcast.84), channel_id=1, source_target_pairs={{0,3},{1,0},{2,1},{3,2},{4,7},{5,4},{6,5},{7,6},{8,11},{9,8},{10,9... | collective-permute-start | bytes 3145736 | tf_op jit(solution)/shard_map/ppermute | solution.py:426
  8.2 52.7 %collective-permute-start.4 = (bf16[1024,512]{1,0:T(8,128)(2,1)S(1)}, bf16[1024,512]{1,0:T(8,128)(2,1)}, u32[]{:S(2)}, u32[]{:S(2)}) collective-permute-start(bf16[1024,512]{1,0:T(8,128)(2,1)S(1)} %bitcast.85), channel_id=1, source_target_pairs={{0,1},{1,2},{2,3},{3,0},{4,5},{5,6},{6,7},{7,4},{8,9},{9,10},{10,1... | collective-permute-start | bytes 3145736 | tf_op jit(solution)/shard_map/ppermute | solution.py:427
  10.2 11.4 %collective-permute-start.15 = (bf16[8,128,256]{2,1,0:T(8,128)(2,1)}, bf16[8,128,256]{2,1,0:T(8,128)(2,1)}, u32[]{:S(2)}, u32[]{:S(2)}) collective-permute-start(bf16[8,128,256]{2,1,0:T(8,128)(2,1)} %pad_maximum_fusion.1), channel_id=1, source_target_pairs={{0,64},{4,20},{8,72},{12,28},{16,80},{20,4},{24,88},{28,12},{32,96... | collective-permute-start | bytes 1572872 | tf_op jit(solution)/shard_map/ppermute | solution.py:441
  14.1 13.0 %collective-permute-start.16 = (bf16[8,128,256]{2,1,0:T(8,128)(2,1)}, bf16[8,128,256]{2,1,0:T(8,128)(2,1)}, u32[]{:S(2)}, u32[]{:S(2)}) collective-permute-start(bf16[8,128,256]{2,1,0:T(8,128)(2,1)} %pad_maximum_fusion.1), channel_id=1, source_target_pairs={{0,32},{4,12},{8,40},{12,20},{16,48},{20,28},{24,56},{28,4},{32,64... | collective-permute-start | bytes 1572872 | tf_op jit(solution)/shard_map/ppermute | solution.py:441
  16.7 95.7 %copy-start.1 = (bf16[512,1024]{0,1:T(8,128)(2,1)}, bf16[512,1024]{0,1:T(8,128)(2,1)S(1)}, u32[]{:S(2)}) copy-start(bf16[512,1024]{0,1:T(8,128)(2,1)S(1)} %copy.25) | copy-start | bytes 3145732
  16.7 15.6 %collective-permute-start.1 = (bf16[8,128,256]{2,1,0:T(8,128)(2,1)}, bf16[8,128,256]{2,1,0:T(8,128)(2,1)}, u32[]{:S(2)}, u32[]{:S(2)}) collective-permute-start(bf16[8,128,256]{2,1,0:T(8,128)(2,1)} %pad_maximum_fusion.1), channel_id=1, source_target_pairs={{0,96},{4,28},{8,104},{12,4},{16,112},{20,12},{24,120},{28,20},{32... | collective-permute-start | bytes 1572872 | tf_op jit(solution)/shard_map/ppermute | solution.py:441
  21.6 35.7 %collective-permute-start.3 = (bf16[1024,512]{1,0:T(8,128)(2,1)S(1)}, bf16[1024,512]{1,0:T(8,128)(2,1)}, u32[]{:S(2)}, u32[]{:S(2)}) collective-permute-start(bf16[1024,512]{1,0:T(8,128)(2,1)S(1)} %bitcast.89), channel_id=1, source_target_pairs={{0,1},{1,2},{2,3},{3,0},{4,5},{5,6},{6,7},{7,4},{8,9},{9,10},{10,1... | collective-permute-start | bytes 3145736 | tf_op jit(solution)/shard_map/ppermute | solution.py:425
  22.4 88.3 %copy-start.23 = (f32[3,256]{1,0:T(4,128)S(1)}, f32[3,256]{1,0:T(4,128)}, u32[]{:S(2)}) copy-start(f32[3,256]{1,0:T(4,128)} %param.18) | copy-start | bytes 9220
  27.1 1.9 collective-permute-start.2
  29.0 33.1 %collective-permute-start.5 = (bf16[1024,512]{1,0:T(8,128)(2,1)S(1)}, bf16[1024,512]{1,0:T(8,128)(2,1)}, u32[]{:S(2)}, u32[]{:S(2)}) collective-permute-start(bf16[1024,512]{1,0:T(8,128)(2,1)S(1)} %bitcast.90), channel_id=1, source_target_pairs={{0,3},{1,0},{2,1},{3,2},{4,7},{5,4},{6,5},{7,6},{8,11},{9,8},{10,9... | collective-permute-start | bytes 3145736 | tf_op jit(solution)/shard_map/ppermute | solution.py:428
  32.3 29.8 %collective-permute-start.20 = (bf16[16,128,256]{2,1,0:T(8,128)(2,1)}, bf16[16,128,256]{2,1,0:T(8,128)(2,1)}, u32[]{:S(2)}, u32[]{:S(2)}) collective-permute-start(bf16[16,128,256]{2,1,0:T(8,128)(2,1)} %constant_dynamic-update-slice_fusion.refs_9_), channel_id=1, source_target_pairs={{0,8},{4,36},{8,16},{12,44},{16,24},{20,52},{24,0},{28,60},{32,40}... | collective-permute-start | bytes 3145736 | tf_op jit(solution)/shard_map/ppermute | solution.py:503
  57.3 15.1 %collective-permute-start.17 = (bf16[16,128,256]{2,1,0:T(8,128)(2,1)S(1)}, bf16[16,128,256]{2,1,0:T(8,128)(2,1)}, u32[]{:S(2)}, u32[]{:S(2)}) collective-permute-start(bf16[16,128,256]{2,1,0:T(8,128)(2,1)S(1)} %pad_maximum_fusion.refs_8_), channel_id=1, source_target_pairs={{0,24},{4,100},{8,0},{12,108},{16,8},{20,116},{24,16},{28,124},{32... | collective-permute-start | bytes 3145736 | tf_op jit(solution)/shard_map/ppermute | solution.py:502
  60.1 23.7 %collective-permute-start.18 = (bf16[16,128,256]{2,1,0:T(8,128)(2,1)}, bf16[16,128,256]{2,1,0:T(8,128)(2,1)}, u32[]{:S(2)}, u32[]{:S(2)}) collective-permute-start(bf16[16,128,256]{2,1,0:T(8,128)(2,1)} %constant_dynamic-update-slice_fusion.refs_9_), channel_id=1, source_target_pairs={{0,24},{4,100},{8,0},{12,108},{16,8},{20,116},{24,16},{28,124},{32... | collective-permute-start | bytes 3145736 | tf_op jit(solution)/shard_map/ppermute | solution.py:505
  60.9 22.8 %collective-permute-start.22 = (bf16[16,128,256]{2,1,0:T(8,128)(2,1)S(1)}, bf16[16,128,256]{2,1,0:T(8,128)(2,1)}, u32[]{:S(2)}, u32[]{:S(2)}) collective-permute-start(bf16[16,128,256]{2,1,0:T(8,128)(2,1)S(1)} %pad_maximum_fusion.refs_8_), channel_id=1, source_target_pairs={{0,8},{4,36},{8,16},{12,44},{16,24},{20,52},{24,0},{28,60},{32,40}... | collective-permute-start | bytes 3145736 | tf_op jit(solution)/shard_map/ppermute | solution.py:504
  62.1 22.8 %collective-permute-start.24 = (bf16[16,128,256]{2,1,0:T(8,128)(2,1)}, bf16[16,128,256]{2,1,0:T(8,128)(2,1)S(1)}, u32[]{:S(2)}, u32[]{:S(2)}) collective-permute-start(bf16[16,128,256]{2,1,0:T(8,128)(2,1)} %constant_dynamic-update-slice_fusion.refs_9_), channel_id=1, source_target_pairs={{0,4},{4,0},{8,12},{12,8},{16,20},{20,16},{24,28},{28,24},{32,36},... | collective-permute-start | bytes 3145736 | tf_op jit(solution)/shard_map/ppermute | solution.py:511
  62.1 25.4 %collective-permute-start.23 = (bf16[16,128,256]{2,1,0:T(8,128)(2,1)S(1)}, bf16[16,128,256]{2,1,0:T(8,128)(2,1)S(1)}, u32[]{:S(2)}, u32[]{:S(2)}) collective-permute-start(bf16[16,128,256]{2,1,0:T(8,128)(2,1)S(1)} %pad_maximum_fusion.refs_8_), channel_id=1, source_target_pairs={{0,4},{4,0},{8,12},{12,8},{16,20},{20,16},{24,28},{28,24},{32,36},... | collective-permute-start | bytes 3145736 | tf_op jit(solution)/shard_map/ppermute | solution.py:511
  72.4 26.3 %collective-permute-start.7 = (bf16[1024,512]{1,0:T(8,128)(2,1)}, bf16[1024,512]{1,0:T(8,128)(2,1)S(1)}, u32[]{:S(2)}, u32[]{:S(2)}) collective-permute-start(bf16[1024,512]{1,0:T(8,128)(2,1)} %collective-permute-done.3.refs_2_), channel_id=1, source_target_pairs={{0,1},{1,2},{2,3},{3,0},{4,5},{5,6},{6,7},{7,4},{8,9},{9,10},{10,1... | collective-permute-start | bytes 3145736 | tf_op jit(solution)/shard_map/ppermute | solution.py:513
  83.7 24.8 %collective-permute-start.8 = (bf16[1024,512]{1,0:T(8,128)(2,1)S(1)}, bf16[1024,512]{1,0:T(8,128)(2,1)S(1)}, u32[]{:S(2)}, u32[]{:S(2)}) collective-permute-start(bf16[1024,512]{1,0:T(8,128)(2,1)S(1)} %collective-permute-done.6.refs_5_), channel_id=1, source_target_pairs={{0,3},{1,0},{2,1},{3,2},{4,7},{5,4},{6,5},{7,6},{8,11},{9,8},{10,9... | collective-permute-start | bytes 3145736 | tf_op jit(solution)/shard_map/ppermute | solution.py:514
  83.7 25.8 %collective-permute-start.21 = (bf16[16,128,256]{2,1,0:T(8,128)(2,1)}, bf16[16,128,256]{2,1,0:T(8,128)(2,1)S(1)}, u32[]{:S(2)}, u32[]{:S(2)}) collective-permute-start(bf16[16,128,256]{2,1,0:T(8,128)(2,1)} %collective-permute-done.20.refs_15_), channel_id=1, source_target_pairs={{0,8},{4,36},{8,16},{12,44},{16,24},{20,52},{24,0},{28,60},{32,40}... | collective-permute-start | bytes 3145736 | tf_op jit(solution)/shard_map/ppermute | solution.py:507
  85.0 25.8 %collective-permute-start.19 = (bf16[16,128,256]{2,1,0:T(8,128)(2,1)}, bf16[16,128,256]{2,1,0:T(8,128)(2,1)}, u32[]{:S(2)}, u32[]{:S(2)}) collective-permute-start(bf16[16,128,256]{2,1,0:T(8,128)(2,1)} %collective-permute-done.17.refs_10_), channel_id=1, source_target_pairs={{0,24},{4,100},{8,0},{12,108},{16,8},{20,116},{24,16},{28,124},{32... | collective-permute-start | bytes 3145736 | tf_op jit(solution)/shard_map/ppermute | solution.py:506
  87.5 23.9 %collective-permute-start.26 = (bf16[16,128,256]{2,1,0:T(8,128)(2,1)}, bf16[16,128,256]{2,1,0:T(8,128)(2,1)}, u32[]{:S(2)}, u32[]{:S(2)}) collective-permute-start(bf16[16,128,256]{2,1,0:T(8,128)(2,1)} %collective-permute-done.18.refs_11_), channel_id=1, source_target_pairs={{0,4},{4,0},{8,12},{12,8},{16,20},{20,16},{24,28},{28,24},{32,36},... | collective-permute-start | bytes 3145736 | tf_op jit(solution)/shard_map/ppermute | solution.py:511
  98.7 13.8 %collective-permute-start.30 = (bf16[16,128,256]{2,1,0:T(8,128)(2,1)}, bf16[16,128,256]{2,1,0:T(8,128)(2,1)}, u32[]{:S(2)}, u32[]{:S(2)}) collective-permute-start(bf16[16,128,256]{2,1,0:T(8,128)(2,1)} %collective-permute-done.20.refs_15_), channel_id=1, source_target_pairs={{0,4},{4,0},{8,12},{12,8},{16,20},{20,16},{24,28},{28,24},{32,36},... | collective-permute-start | bytes 3145736 | tf_op jit(solution)/shard_map/ppermute | solution.py:511
  108.6 4.3 %collective-permute-start.25 = (bf16[16,128,256]{2,1,0:T(8,128)(2,1)}, bf16[16,128,256]{2,1,0:T(8,128)(2,1)}, u32[]{:S(2)}, u32[]{:S(2)}) collective-permute-start(bf16[16,128,256]{2,1,0:T(8,128)(2,1)} %collective-permute-done.17.refs_10_), channel_id=1, source_target_pairs={{0,4},{4,0},{8,12},{12,8},{16,20},{20,16},{24,28},{28,24},{32,36},... | collective-permute-start | bytes 3145736 | tf_op jit(solution)/shard_map/ppermute | solution.py:511
  110.6 3.0 %collective-permute-start.29 = (bf16[16,128,256]{2,1,0:T(8,128)(2,1)}, bf16[16,128,256]{2,1,0:T(8,128)(2,1)}, u32[]{:S(2)}, u32[]{:S(2)}) collective-permute-start(bf16[16,128,256]{2,1,0:T(8,128)(2,1)} %collective-permute-done.22.refs_14_), channel_id=1, source_target_pairs={{0,4},{4,0},{8,12},{12,8},{16,20},{20,16},{24,28},{28,24},{32,36},... | collective-permute-start | bytes 3145736 | tf_op jit(solution)/shard_map/ppermute | solution.py:511
  110.8 17.0 %collective-permute-start.28 = (bf16[16,128,256]{2,1,0:T(8,128)(2,1)}, bf16[16,128,256]{2,1,0:T(8,128)(2,1)}, u32[]{:S(2)}, u32[]{:S(2)}) collective-permute-start(bf16[16,128,256]{2,1,0:T(8,128)(2,1)} %copy-done.18), channel_id=1, source_target_pairs={{0,4},{4,0},{8,12},{12,8},{16,20},{20,16},{24,28},{28,24},{32,36},... | collective-permute-start | bytes 3145736 | tf_op jit(solution)/shard_map/ppermute | solution.py:511
  111.4 16.8 %collective-permute-start.27 = (bf16[16,128,256]{2,1,0:T(8,128)(2,1)}, bf16[16,128,256]{2,1,0:T(8,128)(2,1)}, u32[]{:S(2)}, u32[]{:S(2)}) collective-permute-start(bf16[16,128,256]{2,1,0:T(8,128)(2,1)} %collective-permute-done.19.refs_12_), channel_id=1, source_target_pairs={{0,4},{4,0},{8,12},{12,8},{16,20},{20,16},{24,28},{28,24},{32,36},... | collective-permute-start | bytes 3145736 | tf_op jit(solution)/shard_map/ppermute | solution.py:511
  112.4 33.3 %collective-permute-start.9 = (bf16[1024,512]{1,0:T(8,128)(2,1)S(1)}, bf16[1024,512]{1,0:T(8,128)(2,1)}, u32[]{:S(2)}, u32[]{:S(2)}) collective-permute-start(bf16[1024,512]{1,0:T(8,128)(2,1)S(1)} %bitcast.91), channel_id=1, source_target_pairs={{0,4},{4,0},{8,12},{12,8},{16,20},{20,16},{24,28},{28,24},{32,36},... | collective-permute-start | bytes 3145736 | tf_op jit(solution)/shard_map/ppermute | solution.py:523
  112.8 33.3 %collective-permute-start.10 = (bf16[1024,512]{1,0:T(8,128)(2,1)S(1)}, bf16[1024,512]{1,0:T(8,128)(2,1)}, u32[]{:S(2)}, u32[]{:S(2)}) collective-permute-start(bf16[1024,512]{1,0:T(8,128)(2,1)S(1)} %bitcast.86), channel_id=1, source_target_pairs={{0,4},{4,0},{8,12},{12,8},{16,20},{20,16},{24,28},{28,24},{32,36},... | collective-permute-start | bytes 3145736 | tf_op jit(solution)/shard_map/ppermute | solution.py:523
  113.6 32.7 %collective-permute-start.11 = (bf16[1024,512]{1,0:T(8,128)(2,1)}, bf16[1024,512]{1,0:T(8,128)(2,1)}, u32[]{:S(2)}, u32[]{:S(2)}) collective-permute-start(bf16[1024,512]{1,0:T(8,128)(2,1)} %collective-permute-done.3.refs_2_), channel_id=1, source_target_pairs={{0,4},{4,0},{8,12},{12,8},{16,20},{20,16},{24,28},{28,24},{32,36},... | collective-permute-start | bytes 3145736 | tf_op jit(solution)/shard_map/ppermute | solution.py:523
  127.8 45.5 %collective-permute-start.14 = (bf16[1024,512]{1,0:T(8,128)(2,1)S(1)}, bf16[1024,512]{1,0:T(8,128)(2,1)}, u32[]{:S(2)}, u32[]{:S(2)}) collective-permute-start(bf16[1024,512]{1,0:T(8,128)(2,1)S(1)} %collective-permute-done.6.refs_5_), channel_id=1, source_target_pairs={{0,4},{4,0},{8,12},{12,8},{16,20},{20,16},{24,28},{28,24},{32,36},... | collective-permute-start | bytes 3145736 | tf_op jit(solution)/shard_map/ppermute | solution.py:523
  128.2 46.2 %collective-permute-start.12 = (bf16[1024,512]{1,0:T(8,128)(2,1)}, bf16[1024,512]{1,0:T(8,128)(2,1)}, u32[]{:S(2)}, u32[]{:S(2)}) collective-permute-start(bf16[1024,512]{1,0:T(8,128)(2,1)} %collective-permute-done.4.refs_3_), channel_id=1, source_target_pairs={{0,4},{4,0},{8,12},{12,8},{16,20},{20,16},{24,28},{28,24},{32,36},... | collective-permute-start | bytes 3145736 | tf_op jit(solution)/shard_map/ppermute | solution.py:523
  145.7 28.6 %collective-permute-start.13 = (bf16[1024,512]{1,0:T(8,128)(2,1)}, bf16[1024,512]{1,0:T(8,128)(2,1)S(1)}, u32[]{:S(2)}, u32[]{:S(2)}) collective-permute-start(bf16[1024,512]{1,0:T(8,128)(2,1)} %collective-permute-done.5.refs_4_), channel_id=1, source_target_pairs={{0,4},{4,0},{8,12},{12,8},{16,20},{20,16},{24,28},{28,24},{32,36},... | collective-permute-start | bytes 3145736 | tf_op jit(solution)/shard_map/ppermute | solution.py:523
  146.2 28.6 %collective-permute-start.31 = (bf16[1024,512]{1,0:T(8,128)(2,1)}, bf16[1024,512]{1,0:T(8,128)(2,1)}, u32[]{:S(2)}, u32[]{:S(2)}) collective-permute-start(bf16[1024,512]{1,0:T(8,128)(2,1)} %copy-done.3), channel_id=1, source_target_pairs={{0,4},{4,0},{8,12},{12,8},{16,20},{20,16},{24,28},{28,24},{32,36},... | collective-permute-start | bytes 3145736 | tf_op jit(solution)/shard_map/ppermute | solution.py:523
  146.3 28.5 %collective-permute-start.32 = (bf16[1024,512]{1,0:T(8,128)(2,1)}, bf16[1024,512]{1,0:T(8,128)(2,1)}, u32[]{:S(2)}, u32[]{:S(2)}) collective-permute-start(bf16[1024,512]{1,0:T(8,128)(2,1)} %copy-done.4), channel_id=1, source_target_pairs={{0,4},{4,0},{8,12},{12,8},{16,20},{20,16},{24,28},{28,24},{32,36},... | collective-permute-start | bytes 3145736 | tf_op jit(solution)/shard_map/ppermute | solution.py:523
  146.7 17.9 %all-to-all-start = ((f32[32,24,128]{2,1,0:T(8,128)}), f32[32,24,128]{2,1,0:T(8,128)S(1)}, u32[]{:S(2)}, u32[]{:S(2)}) async-start(f32[32,24,128]{2,1,0:T(8,128)} %get-tuple-element.40), calls=%async_computation | async-start | bytes 786432 | tf_op jit(solution)/shard_map/all_to_all | solution.py:527
  173.3 1.5 collective-permute-start.33
  197.8 14.9 %collective-permute-start.38 = (f16[2,8,128,256]{3,2,1,0:T(8,128)(2,1)S(1)}, f16[2,8,128,256]{3,2,1,0:T(8,128)(2,1)S(1)}, u32[]{:S(2)}, u32[]{:S(2)}) collective-permute-start(f16[2,8,128,256]{3,2,1,0:T(8,128)(2,1)S(1)} %bitcast.107), channel_id=1, source_target_pairs={{0,96},{4,28},{8,104},{12,4},{16,112},{20,12},{24,120},{28,20},{32... | collective-permute-start | bytes 3145736 | tf_op jit(solution)/shard_map/ppermute | solution.py:382
  199.3 30.7 %collective-permute-start.37 = (f16[2,8,128,256]{3,2,1,0:T(8,128)(2,1)S(1)}, f16[2,8,128,256]{3,2,1,0:T(8,128)(2,1)S(1)}, u32[]{:S(2)}, u32[]{:S(2)}) collective-permute-start(f16[2,8,128,256]{3,2,1,0:T(8,128)(2,1)S(1)} %bitcast.104), channel_id=1, source_target_pairs={{0,32},{4,12},{8,40},{12,20},{16,48},{20,28},{24,56},{28,4},{32,64... | collective-permute-start | bytes 3145736 | tf_op jit(solution)/shard_map/ppermute | solution.py:383
  200.5 26.0 %collective-permute-start.34 = (f16[2,8,128,256]{3,2,1,0:T(8,128)(2,1)S(1)}, f16[2,8,128,256]{3,2,1,0:T(8,128)(2,1)S(1)}, u32[]{:S(2)}, u32[]{:S(2)}) collective-permute-start(f16[2,8,128,256]{3,2,1,0:T(8,128)(2,1)S(1)} %bitcast.106), channel_id=1, source_target_pairs={{0,32},{4,12},{8,40},{12,20},{16,48},{20,28},{24,56},{28,4},{32,64... | collective-permute-start | bytes 3145736 | tf_op jit(solution)/shard_map/ppermute | solution.py:381
  213.1 16.9 %collective-permute-start.39 = (f16[2,8,128,256]{3,2,1,0:T(8,128)(2,1)S(1)}, f16[2,8,128,256]{3,2,1,0:T(8,128)(2,1)S(1)}, u32[]{:S(2)}, u32[]{:S(2)}) collective-permute-start(f16[2,8,128,256]{3,2,1,0:T(8,128)(2,1)S(1)} %add_convert_fusion.1), channel_id=1, source_target_pairs={{0,96},{4,28},{8,104},{12,4},{16,112},{20,12},{24,120},{28,20},{32... | collective-permute-start | bytes 3145736 | tf_op jit(solution)/shard_map/ppermute | solution.py:386
  215.8 34.5 %collective-permute-start.36 = (f16[2,8,128,256]{3,2,1,0:T(8,128)(2,1)S(1)}, f16[2,8,128,256]{3,2,1,0:T(8,128)(2,1)S(1)}, u32[]{:S(2)}, u32[]{:S(2)}) collective-permute-start(f16[2,8,128,256]{3,2,1,0:T(8,128)(2,1)S(1)} %bitcast.105), channel_id=1, source_target_pairs={{0,96},{4,28},{8,104},{12,4},{16,112},{20,12},{24,120},{28,20},{32... | collective-permute-start | bytes 3145736 | tf_op jit(solution)/shard_map/ppermute | solution.py:384
  227.0 23.2 %collective-permute-start.35 = (f16[2,8,128,256]{3,2,1,0:T(8,128)(2,1)S(1)}, f16[2,8,128,256]{3,2,1,0:T(8,128)(2,1)S(1)}, u32[]{:S(2)}, u32[]{:S(2)}) collective-permute-start(f16[2,8,128,256]{3,2,1,0:T(8,128)(2,1)S(1)} %add_convert_fusion.2), channel_id=1, source_target_pairs={{0,32},{4,12},{8,40},{12,20},{16,48},{20,28},{24,56},{28,4},{32,64... | collective-permute-start | bytes 3145736 | tf_op jit(solution)/shard_map/ppermute | solution.py:385
  230.8 21.0 %collective-permute-start.40 = (f16[8,128,256]{2,1,0:T(8,128)(2,1)S(1)}, f16[8,128,256]{2,1,0:T(8,128)(2,1)S(1)}, u32[]{:S(2)}, u32[]{:S(2)}) collective-permute-start(f16[8,128,256]{2,1,0:T(8,128)(2,1)S(1)} %get-tuple-element.66), channel_id=1, source_target_pairs={{0,16},{4,68},{8,24},{12,76},{16,0},{20,84},{24,8},{28,92},{32,48}... | collective-permute-start | bytes 1572872 | tf_op jit(solution)/shard_map/ppermute | solution.py:394
  231.9 19.9 %collective-permute-start.42 = (f16[8,128,256]{2,1,0:T(8,128)(2,1)S(1)}, f16[8,128,256]{2,1,0:T(8,128)(2,1)S(1)}, u32[]{:S(2)}, u32[]{:S(2)}) collective-permute-start(f16[8,128,256]{2,1,0:T(8,128)(2,1)S(1)} %get-tuple-element.67), channel_id=1, source_target_pairs={{0,24},{4,100},{8,0},{12,108},{16,8},{20,116},{24,16},{28,124},{32... | collective-permute-start | bytes 1572872 | tf_op jit(solution)/shard_map/ppermute | solution.py:394
  250.9 10.5 %collective-permute-start.41 = (f16[8,128,256]{2,1,0:T(8,128)(2,1)S(1)}, f16[8,128,256]{2,1,0:T(8,128)(2,1)S(1)}, u32[]{:S(2)}, u32[]{:S(2)}) collective-permute-start(f16[8,128,256]{2,1,0:T(8,128)(2,1)S(1)} %fusion.6), channel_id=1, source_target_pairs={{0,8},{4,36},{8,16},{12,44},{16,24},{20,52},{24,0},{28,60},{32,40}... | collective-permute-start | bytes 1572872 | tf_op jit(solution)/shard_map/ppermute | solution.py:394
  261.7 1.6 collective-permute-start.43
  (27 other events, 444.9 us)
